TPU v7x, 32 devices: a whole 2x2x4 slice. The times are simulated.
32 devices in a mesh: seq: 4 (over y, core), tensor: 8 (over z, x).
Axes of the slice: x: 2, y: 2, z: 4, core: 2. Of those that a mesh axis runs over, the one named last changes fastest.
Arguments:
- tokens: bfloat16 [128, 12288], P('tensor', 'seq'), may hold values from -6 to 6
- in_blocks: bfloat16 [4, 8, 288, 128, 128], P('seq', 'tensor'), may hold values from -0.109375 to 0.109375
- in_slots: int32 [4, 8, 288], P('seq', 'tensor'), may hold values from -1 to 575, as said below
- out_blocks: bfloat16 [8, 4, 288, 128, 128], P('tensor', 'seq'), may hold values from -0.078125 to 0.078125
- out_slots: int32 [8, 4, 288], P('tensor', 'seq'), may hold values from -1 to 575, as said below
- cotangent: bfloat16 [128, 12288], P('tensor', 'seq'), may hold values from -6 to 6
Outputs:
- output: bfloat16 [128, 12288], P('tensor', 'seq')
- grad_tokens: bfloat16 [128, 12288], P('tensor', 'seq')
- grad_in: float32 [4, 8, 288, 128, 128], P('seq', 'tensor')
- grad_out: float32 [8, 4, 288, 128, 128], P('tensor', 'seq')
Inputs may be any that keep to these rules, and one draw needn't show every extreme that they name: `in_slots`: on every shard the 288 slots hold distinct block positions below 576, the filled slots first and -1 after them; every shard has at least one filled slot and some shard has all 288 filled. `out_slots`: on every shard the 288 slots hold distinct block positions below 576, the filled slots first and -1 after them; every shard has at least one filled slot and some shard has all 288 filled.
All inputs are finite; a program needn't handle non-finite values.
Results may differ from a plain program's by a relative error of at most 0.019.
Values may be sent and summed in bfloat16 or wider, within the bound.
No kernel may reach another device: no remote copies, remote signals or barrier semaphores. Data moves between devices by JAX's collectives and lax.ppermute only.
A program may use at most 192 MiB of HBM per device.

v0:
```python
import functools

import jax
import jax.numpy as jnp
from jax import lax
from jax.experimental import pallas as pl
from jax.experimental.pallas import tpu as pltpu
from jax.sharding import PartitionSpec as P

GELU_SCALE = 0.7978845608028654
GELU_CUBE = 0.044715


def gelu_value(values):
    return (
        0.5
        * values
        * (1.0 + jnp.tanh(GELU_SCALE * (values + GELU_CUBE * values * values * values)))
    )


def gelu_slope(values):
    tangent = jnp.tanh(GELU_SCALE * (values + GELU_CUBE * values * values * values))
    return 0.5 * (1.0 + tangent) + 0.5 * values * (1.0 - tangent * tangent) * GELU_SCALE * (
        1.0 + 3.0 * GELU_CUBE * values * values
    )


def largest_divisor(number, limit):
    return max(d for d in range(1, limit + 1) if number % d == 0)


def load_pieces(piece_refs, offsets, store, width):
    for i, piece in enumerate(piece_refs):
        length = piece.shape[0]
        start = offsets(i, length)
        for b in range(piece.shape[1] // width):
            store[b, pl.ds(start, length), :] = piece[:, b * width : (b + 1) * width]


def block_product(pieces, in_rows, blocks, src, dst, info, n_dst, out_lengths, out_rows, transposed):
    cap, width = blocks.shape[0], blocks.shape[1]
    n_src = pieces[0].shape[1] // width
    tokens = sum(piece.shape[0] for piece in pieces)
    chunk = largest_divisor(cap, 32)
    unroll = largest_divisor(chunk, 8)
    steps = cap // chunk
    dims = (((1,), (1 if transposed else 0,)), ((), ()))
    zero_rows = jnp.zeros((1,), jnp.int32)
    in_arr = zero_rows if in_rows is None else in_rows
    out_arr = zero_rows if out_rows is None else out_rows
    n_in, n_out = len(pieces), len(out_lengths)

    def body(src_s, dst_s, info_s, in_s, out_s, *refs):
        piece_refs = refs[:n_in]
        w_ref = refs[n_in]
        out_refs = refs[n_in + 1 : n_in + 1 + n_out]
        xs, acc = refs[n_in + 1 + n_out :]
        step = pl.program_id(0)

        @pl.when(step == 0)
        def _():
            if in_rows is None:
                place = lambda i, length: i * length
            else:
                place = lambda i, length: pl.multiple_of(in_s[i], length)
            load_pieces(piece_refs, place, xs, width)
            acc[...] = jnp.zeros_like(acc)

        @pl.when(step <= info_s[0])
        def _():
            def some(g, carry):
                base = g * unroll
                terms = []
                for u in range(unroll):
                    k = step * chunk + base + u
                    terms.append(
                        lax.dot_general(
                            xs[src_s[k]], w_ref[base + u], dims, preferred_element_type=jnp.float32
                        )
                    )
                for u in range(unroll):
                    k = step * chunk + base + u
                    acc[dst_s[k]] += terms[u]
                return carry

            lax.fori_loop(0, chunk // unroll, some, 0)

        @pl.when(step == steps - 1)
        def _():
            at = 0
            for i, ref in enumerate(out_refs):
                lead = ref.shape[:-2]
                length = ref.shape[-2]
                for j in range(lead[0] if lead else 1):
                    start = at * length if out_rows is None else pl.multiple_of(out_s[at], length)
                    at += 1
                    for b in range(n_dst):
                        val = acc[b, pl.ds(start, length), :].astype(jnp.bfloat16)
                        if lead:
                            ref[j, :, b * width : (b + 1) * width] = val
                        else:
                            ref[:, b * width : (b + 1) * width] = val

    whole = lambda shape: pl.BlockSpec(shape, lambda i, *s: (0,) * len(shape))
    out_shapes = [shape + (n_dst * width,) for shape in out_lengths]
    return pl.pallas_call(
        body,
        grid_spec=pltpu.PrefetchScalarGridSpec(
            num_scalar_prefetch=5,
            grid=(steps,),
            in_specs=[whole(piece.shape) for piece in pieces]
            + [
                pl.BlockSpec(
                    (chunk, width, width), lambda i, s, d, info_s, a, b: (jnp.minimum(i, info_s[0]), 0, 0)
                )
            ],
            out_specs=[whole(shape) for shape in out_shapes],
            scratch_shapes=[
                pltpu.VMEM((n_src, tokens, width), jnp.bfloat16),
                pltpu.VMEM((n_dst + 1, tokens, width), jnp.float32),
            ],
        ),
        out_shape=[jax.ShapeDtypeStruct(shape, jnp.bfloat16) for shape in out_shapes],
        compiler_params=pltpu.CompilerParams(dimension_semantics=("arbitrary",)),
        cost_estimate=pl.CostEstimate(
            flops=2 * cap * tokens * width * width,
            bytes_accessed=cap * width * width * 2 + tokens * width * 2 * (n_src + n_dst),
            transcendentals=0,
        ),
        name="block_product",
    )(src, dst, info, in_arr, out_arr, *pieces, blocks)


def block_grads(left, left_rows, right, right_rows, rows, cols, cap):
    width = 128
    n_left, n_right = left[0].shape[1] // width, right[0].shape[1] // width
    tokens = sum(piece.shape[0] for piece in left)
    chunk = largest_divisor(cap, 32)
    unroll = largest_divisor(chunk, 8)
    steps = cap // chunk
    n_l, n_r = len(left), len(right)
    dims = (((1,), (0,)), ((), ()))
    zero_rows = jnp.zeros((1,), jnp.int32)
    left_arr = zero_rows if left_rows is None else left_rows
    right_arr = zero_rows if right_rows is None else right_rows

    def body(row_s, col_s, left_s, right_s, *refs):
        l_refs = refs[:n_l]
        r_refs = refs[n_l : n_l + n_r]
        out = refs[n_l + n_r]
        ls, lt, rs = refs[n_l + n_r + 1 :]
        step = pl.program_id(0)

        @pl.when(step == 0)
        def _():
            def place(given, table):
                if given is None:
                    return lambda i, length: i * length
                return lambda i, length: pl.multiple_of(table[i], length)

            load_pieces(l_refs, place(left_rows, left_s), ls, width)
            load_pieces(r_refs, place(right_rows, right_s), rs, width)
            rs[n_right] = jnp.zeros((tokens, width), rs.dtype)
            for b in range(n_left):
                lt[b] = ls[b].T

        def some(g, carry):
            base = g * unroll
            for u in range(unroll):
                k = step * chunk + base + u
                out[base + u] = lax.dot_general(
                    lt[row_s[k]], rs[col_s[k]], dims, preferred_element_type=jnp.float32
                )
            return carry

        lax.fori_loop(0, chunk // unroll, some, 0)

    whole = lambda shape: pl.BlockSpec(shape, lambda i, *s: (0,) * len(shape))
    return pl.pallas_call(
        body,
        grid_spec=pltpu.PrefetchScalarGridSpec(
            num_scalar_prefetch=4,
            grid=(steps,),
            in_specs=[whole(piece.shape) for piece in left] + [whole(piece.shape) for piece in right],
            out_specs=pl.BlockSpec((chunk, width, width), lambda i, *s: (i, 0, 0)),
            scratch_shapes=[
                pltpu.VMEM((n_left, tokens, width), jnp.bfloat16),
                pltpu.VMEM((n_left, width, tokens), jnp.bfloat16),
                pltpu.VMEM((n_right + 1, tokens, width), jnp.bfloat16),
            ],
        ),
        out_shape=jax.ShapeDtypeStruct((cap, width, width), jnp.float32),
        compiler_params=pltpu.CompilerParams(dimension_semantics=("arbitrary",)),
        cost_estimate=pl.CostEstimate(
            flops=2 * cap * tokens * width * width,
            bytes_accessed=cap * width * width * 4 + tokens * width * 2 * (n_left + n_right),
            transcendentals=0,
        ),
        name="block_grads",
    )(rows, cols, left_arr, right_arr, *left, *right)


def on_device(tokens, in_blocks, in_slots, out_blocks, out_slots, cotangent, *, hidden_total):
    w_in = in_blocks.reshape(in_blocks.shape[2:])
    w_out = out_blocks.reshape(out_blocks.shape[2:])
    slots_in = in_slots.reshape(-1)
    slots_out = out_slots.reshape(-1)
    width = w_in.shape[-1]
    cap = w_in.shape[0]
    tensor_count = lax.axis_size("tensor")
    seq_count = lax.axis_size("seq")
    feat_blocks = tokens.shape[1] // width
    hid_blocks = hidden_total // tensor_count // width
    tensor_rows = tokens.shape[0]
    token_count = tensor_rows * tensor_count
    seq_rows = token_count // seq_count
    far_t, far_s = tensor_count // 2, seq_count // 2

    def near_move(v, axis, count):
        return lax.ppermute(v, axis, [(i, i ^ 1) for i in range(count)])

    def far_move(v, axis, count, shift):
        half = count // 2
        pairs = [(o * 2 + c, ((o + shift) % half) * 2 + c) for o in range(half) for c in range(2)]
        return lax.ppermute(v, axis, pairs)

    me = lax.axis_index("seq")
    shifts = jnp.arange(seq_count, dtype=jnp.int32)
    far_of = (me // 2 + far_s - shifts // 2) % far_s
    seq_part = (far_of * 2 + (me % 2 + shifts % 2) % 2) * seq_rows
    near_order = jnp.concatenate([seq_part[0::2], seq_part[1::2]])

    def tables(slot_list, col_blocks, row_blocks):
        filled = slot_list >= 0
        safe = jnp.where(filled, slot_list, 0)
        row, col = safe // col_blocks, safe % col_blocks
        count = jnp.sum(filled.astype(jnp.int32))
        last = (count - 1) // largest_divisor(cap, 32)
        return (
            row,
            col,
            jnp.where(filled, row, row_blocks),
            jnp.where(filled, col, col_blocks),
            last[None],
        )

    in_row, in_col, in_row_dst, in_col_dst, in_last = tables(slots_in, hid_blocks, feat_blocks)
    out_row, out_col, out_row_dst, out_col_dst, out_last = tables(slots_out, feat_blocks, hid_blocks)

    def gather_panel(own):
        far = [own] + [far_move(own, "tensor", tensor_count, k) for k in range(1, far_t)]
        pieces = []
        for piece in far:
            pieces += [piece, near_move(piece, "tensor", tensor_count)]
        return pieces

    def sum_out(terms):
        keep, send = terms[0::2], terms[1::2]
        order = list(range(1, far_t)) + [0]
        got = {k: near_move(send[k], "tensor", tensor_count) for k in order}
        pair = {k: keep[k].astype(jnp.float32) + got[k].astype(jnp.float32) for k in order}
        total = pair[0]
        for k in range(1, far_t):
            moved = far_move(pair[k].astype(jnp.bfloat16), "tensor", tensor_count, far_t - k)
            total = total + moved.astype(jnp.float32)
        return total.astype(jnp.bfloat16)

    def sum_hidden(keep, send):
        got = near_move(send, "seq", seq_count)
        total = keep[0].astype(jnp.float32) + got[0].astype(jnp.float32)
        for k in range(1, far_s):
            pair = (keep[k].astype(jnp.float32) + got[k].astype(jnp.float32)).astype(jnp.bfloat16)
            total = total + far_move(pair, "seq", seq_count, far_s - k).astype(jnp.float32)
        return total

    def spread_hidden(own):
        pieces = []
        far = [own] + [far_move(own, "seq", seq_count, k) for k in range(1, far_s)]
        for piece in far:
            pieces += [piece, near_move(piece, "seq", seq_count)]
        return pieces

    hidden_lengths = [(far_s, seq_rows)] * 2
    token_lengths = [(tensor_rows,)] * tensor_count

    tok = gather_panel(tokens)
    cot = gather_panel(cotangent)
    keep_h, send_h = block_product(
        tok, None, w_in, in_row, in_col_dst, in_last, hid_blocks, hidden_lengths, near_order, False
    )
    keep_g, send_g = block_product(
        cot, None, w_out, out_col, out_row_dst, out_last, hid_blocks, hidden_lengths, near_order, True
    )
    hidden = sum_hidden(keep_h, send_h)
    activated = spread_hidden(gelu_value(hidden).astype(jnp.bfloat16))
    grad_act = sum_hidden(keep_g, send_g)
    grad_hidden = spread_hidden((grad_act * gelu_slope(hidden)).astype(jnp.bfloat16))

    output = sum_out(
        block_product(
            activated, seq_part, w_out, out_row, out_col_dst, out_last, feat_blocks, token_lengths, None, False
        )
    )
    grad_tokens = sum_out(
        block_product(
            grad_hidden, seq_part, w_in, in_col, in_row_dst, in_last, feat_blocks, token_lengths, None, True
        )
    )
    grad_out = block_grads(activated, seq_part, cot, None, out_row, out_col_dst, cap)
    grad_in = block_grads(tok, None, grad_hidden, seq_part, in_row, in_col_dst, cap)
    return (
        output,
        grad_tokens,
        grad_in.reshape(in_blocks.shape),
        grad_out.reshape(out_blocks.shape),
    )


HIDDEN_TOTAL = 24576


def solution(mesh):
    return jax.shard_map(
        functools.partial(on_device, hidden_total=HIDDEN_TOTAL),
        mesh=mesh,
        in_specs=(
            P("tensor", "seq"),
            P("seq", "tensor", None, None, None),
            P("seq", "tensor", None),
            P("tensor", "seq", None, None, None),
            P("tensor", "seq", None),
            P("tensor", "seq"),
        ),
        out_specs=(
            P("tensor", "seq"),
            P("tensor", "seq"),
            P("seq", "tensor", None, None, None),
            P("tensor", "seq", None, None, None),
        ),
        check_vma=False,
    )
```

profile of v0, /device:TPU:1, one launch (start us, length us, event | category | flops | bytes accessed | tf_op | source)
XLA Modules:
  0.0 169.2 jit_solution(14603919812708315326)
XLA Ops:
  0.6 4.2 %collective-permute-start.24 = (bf16[16,3072]{1,0:T(8,128)(2,1)}, bf16[16,3072]{1,0:T(8,128)(2,1)S(1)}, u32[]{:S(2)}, u32[]{:S(2)}) collective-permute-start(bf16[16,3072]{1,0:T(8,128)(2,1)} %refs_4_.1), channel_id=1, source_target_pairs={{0,6},{1,7},{2,0},{3,1},{4,2},{5,3},{6,4},{7,5},{8,14},{9,15},{10,... | collective-permute-start | bytes 294920 | tf_op jit(solution)/shard_map/ppermute | solution.py:226
  5.3 1.2 collective-permute-start.19
  6.5 2.8 %collective-permute-start.5 = (bf16[16,3072]{1,0:T(8,128)(2,1)}, bf16[16,3072]{1,0:T(8,128)(2,1)S(1)}, u32[]{:S(2)}, u32[]{:S(2)}) collective-permute-start(bf16[16,3072]{1,0:T(8,128)(2,1)} %refs_0_.5), channel_id=1, source_target_pairs={{0,6},{1,7},{2,0},{3,1},{4,2},{5,3},{6,4},{7,5},{8,14},{9,15},{10,... | collective-permute-start | bytes 294920 | tf_op jit(solution)/shard_map/ppermute | solution.py:226
  9.3 0.7 reduce
  10.0 0.6 broadcast_select_fusion.1
  10.6 1.2 add_select_fusion.2
  12.7 0.7 reduce.1
  13.9 1.2 collective-permute-start.23
  15.9 3.5 %collective-permute-start.3 = (bf16[16,3072]{1,0:T(8,128)(2,1)}, bf16[16,3072]{1,0:T(8,128)(2,1)S(1)}, u32[]{:S(2)}, u32[]{:S(2)}) collective-permute-start(bf16[16,3072]{1,0:T(8,128)(2,1)} %refs_0_.5), channel_id=1, source_target_pairs={{0,4},{1,5},{2,6},{3,7},{4,0},{5,1},{6,2},{7,3},{8,12},{9,13},{10,... | collective-permute-start | bytes 294920 | tf_op jit(solution)/shard_map/ppermute | solution.py:226
  20.9 13.8 %block_product.6 = (bf16[2,32,3072]{2,1,0:T(8,128)(2,1)}, bf16[2,32,3072]{2,1,0:T(8,128)(2,1)}) custom-call(s32[288]{0:T(512)} %get-tuple-element.52.src_s, s32[288]{0:T(512)} %get-tuple-element.44.dst_s, s32[1]{0:T(128)} %bitcast.info_s, s32[1]{0:T(128)} %constant.114.clone.1.in_s.out_s.left_s.right_s, s32[4]{0:T(128)} %pad_add_fusion.out_s, ...), custom_call_target="tpu_custom_call" | custom-call | flops 1207959552 | bytes 11010048 | tf_op jit(solution)/shard_map/block_product/pallas_call | solution.py:107
  34.7 0.7 collective-permute-start.26
  35.4 0.6 broadcast_select_fusion.3
  36.0 2.7 %collective-permute-start.6 = (bf16[16,3072]{1,0:T(8,128)(2,1)S(1)}, bf16[16,3072]{1,0:T(8,128)(2,1)S(1)}, u32[]{:S(2)}, u32[]{:S(2)}) collective-permute-start(bf16[16,3072]{1,0:T(8,128)(2,1)S(1)} %collective-permute-done.5.refs_6_), channel_id=1, source_target_pairs={{0,1},{1,0},{2,3},{3,2},{4,5},{5,4},{6,7},{7,6},{8,9},{9,8},{10,11... | collective-permute-start | bytes 294920 | tf_op jit(solution)/shard_map/ppermute | solution.py:221
  38.8 1.4 collective-permute-start.2
  40.2 1.3 add_select_fusion
  42.2 1.8 %collective-permute-done.4.refs_5_ = bf16[16,3072]{1,0:T(8,128)(2,1)S(1)} collective-permute-done((bf16[16,3072]{1,0:T(8,128)(2,1)S(1)}, bf16[16,3072]{1,0:T(8,128)(2,1)S(1)}, u32[]{:S(2)}, u32[]{:S(2)}) %collective-permute-start.4) | collective-permute-done | bytes 98336 | tf_op jit(solution)/shard_map/ppermute | solution.py:221
  44.0 2.1 %collective-permute-done.2.refs_3_ = bf16[16,3072]{1,0:T(8,128)(2,1)S(1)} collective-permute-done((bf16[16,3072]{1,0:T(8,128)(2,1)S(1)}, bf16[16,3072]{1,0:T(8,128)(2,1)S(1)}, u32[]{:S(2)}, u32[]{:S(2)}) %collective-permute-start.2) | collective-permute-done | bytes 98336 | tf_op jit(solution)/shard_map/ppermute | solution.py:221
  46.7 4.8 %block_product.4 = (bf16[2,32,3072]{2,1,0:T(8,128)(2,1)}, bf16[2,32,3072]{2,1,0:T(8,128)(2,1)}) custom-call(s32[288]{0:T(512)} %get-tuple-element.48.src_s.row_s, s32[288]{0:T(512)} %get-tuple-element.55.dst_s.col_s, s32[1]{0:T(128)} %bitcast.1.info_s, s32[1]{0:T(128)} %constant.114.clone.1.in_s.out_s.left_s.right_s, s32[4]{0:T(128)} %pad_add_fusion.out_s, ...), custom_call_target="tpu_custom_call" | custom-call | flops 1207959552 | bytes 11010048 | tf_op jit(solution)/shard_map/block_product/pallas_call | solution.py:107
  51.5 3.6 %collective-permute-start.7 = (bf16[2,32,3072]{2,1,0:T(8,128)(2,1)}, bf16[2,32,3072]{2,1,0:T(8,128)(2,1)S(1)}, u32[]{:S(2)}, u32[]{:S(2)}) collective-permute-start(bf16[2,32,3072]{2,1,0:T(8,128)(2,1)} %get-tuple-element.25), channel_id=1, source_target_pairs={{0,8},{8,0},{16,24},{24,16},{1,9},{9,1},{17,25},{25,17},{2,10},{10... | collective-permute-start | bytes 1179656 | tf_op jit(solution)/shard_map/ppermute | solution.py:221
  55.1 1.0 fusion.8
  56.1 2.9 %collective-permute-start.27 = (bf16[32,3072]{1,0:T(8,128)(2,1)S(1)}, bf16[32,3072]{1,0:T(8,128)(2,1)S(1)}, u32[]{:S(2)}, u32[]{:S(2)}) collective-permute-start(bf16[32,3072]{1,0:T(8,128)(2,1)S(1)} %fusion.8), channel_id=1, source_target_pairs={{0,16},{8,24},{16,0},{24,8},{1,17},{9,25},{17,1},{25,9},{2,18},{10... | collective-permute-start | bytes 589832 | tf_op jit(solution)/shard_map/ppermute | solution.py:226
  59.0 1.0 fusion.7
  60.6 3.7 %collective-permute-done.27 = bf16[32,3072]{1,0:T(8,128)(2,1)S(1)} collective-permute-done((bf16[32,3072]{1,0:T(8,128)(2,1)S(1)}, bf16[32,3072]{1,0:T(8,128)(2,1)S(1)}, u32[]{:S(2)}, u32[]{:S(2)}) %collective-permute-start.27) | collective-permute-done | bytes 196640 | tf_op jit(solution)/shard_map/ppermute | solution.py:226
  64.3 4.2 %collective-permute-done.8 = bf16[32,3072]{1,0:T(8,128)(2,1)S(1)} collective-permute-done((bf16[32,3072]{1,0:T(8,128)(2,1)S(1)}, bf16[32,3072]{1,0:T(8,128)(2,1)S(1)}, u32[]{:S(2)}, u32[]{:S(2)}) %collective-permute-start.8) | collective-permute-done | bytes 196640 | tf_op jit(solution)/shard_map/ppermute | solution.py:226
  68.5 1.4 fusion.6
  70.0 1.2 collective-permute-start.29
  71.5 1.1 collective-permute-start.28
  72.6 3.3 %collective-permute-done.29.refs_2_.refs_10_ = bf16[32,3072]{1,0:T(8,128)(2,1)S(1)} collective-permute-done((bf16[32,3072]{1,0:T(8,128)(2,1)S(1)}, bf16[32,3072]{1,0:T(8,128)(2,1)S(1)}, u32[]{:S(2)}, u32[]{:S(2)}) %collective-permute-start.29) | collective-permute-done | bytes 196640 | tf_op jit(solution)/shard_map/ppermute | solution.py:226
  75.9 2.5 %collective-permute-start.30 = (bf16[32,3072]{1,0:T(8,128)(2,1)S(1)}, bf16[32,3072]{1,0:T(8,128)(2,1)S(1)}, u32[]{:S(2)}, u32[]{:S(2)}) collective-permute-start(bf16[32,3072]{1,0:T(8,128)(2,1)S(1)} %collective-permute-done.29.refs_2_.refs_10_), channel_id=1, source_target_pairs={{0,8},{8,0},{16,24},{24,16},{1,9},{9,1},{17,25},{25,17},{2,10},{10... | collective-permute-start | bytes 589832 | tf_op jit(solution)/shard_map/ppermute | solution.py:221
  78.4 1.7 %collective-permute-done.10.refs_2_ = bf16[32,3072]{1,0:T(8,128)(2,1)S(1)} collective-permute-done((bf16[32,3072]{1,0:T(8,128)(2,1)S(1)}, bf16[32,3072]{1,0:T(8,128)(2,1)S(1)}, u32[]{:S(2)}, u32[]{:S(2)}) %collective-permute-start.10) | collective-permute-done | bytes 196640 | tf_op jit(solution)/shard_map/ppermute | solution.py:226
  80.1 1.4 collective-permute-start.11
  81.6 0.6 copy-done.3
  82.3 5.1 %block_product.7 = (bf16[16,3072]{1,0:T(8,128)(2,1)}, bf16[16,3072]{1,0:T(8,128)(2,1)}, bf16[16,3072]{1,0:T(8,128)(2,1)}, bf16[16,3072]{1,0:T(8,128)(2,1)}, bf16...) custom-call(s32[288]{0:T(512)} %get-tuple-element.54.src_s, ...), custom_call_target="tpu_custom_call" | custom-call | flops 1207959552 | bytes 11010048 | tf_op jit(solution)/shard_map/block_product/pallas_call | solution.py:107
  87.4 12.6 %collective-permute-start.31 = (bf16[16,3072]{1,0:T(8,128)(2,1)}, bf16[16,3072]{1,0:T(8,128)(2,1)S(1)}, u32[]{:S(2)}, u32[]{:S(2)}) collective-permute-start(bf16[16,3072]{1,0:T(8,128)(2,1)} %get-tuple-element.37), channel_id=1, source_target_pairs={{0,1},{1,0},{2,3},{3,2},{4,5},{5,4},{6,7},{7,6},{8,9},{9,8},{10,11... | collective-permute-start | bytes 294920 | tf_op jit(solution)/shard_map/ppermute | solution.py:221
  100.1 1.4 collective-permute-start.34
  101.6 0.6 copy-done.6
  102.3 12.1 %block_product.5 = (bf16[16,3072]{1,0:T(8,128)(2,1)}, bf16[16,3072]{1,0:T(8,128)(2,1)}, bf16[16,3072]{1,0:T(8,128)(2,1)}, bf16[16,3072]{1,0:T(8,128)(2,1)}, bf16...) custom-call(s32[288]{0:T(512)} %get-tuple-element.45.src_s.row_s, ...), custom_call_target="tpu_custom_call" | custom-call | flops 1207959552 | bytes 11010048 | tf_op jit(solution)/shard_map/block_product/pallas_call | solution.py:107
  114.5 13.8 %block_grads.3 = f32[288,128,128]{2,1,0:T(8,128)} custom-call(s32[288]{0:T(512)} %get-tuple-element.45.src_s.row_s, s32[288]{0:T(512)} %get-tuple-element.53.dst_s.col_s, s32[4]{0:T(128)} %copy-done.30, s32[1]{0:T(128)} %constant.114.clone.1.in_s.out_s.left_s.right_s, bf16[32,3072]{1,0:T(8,128)(2,1)} %copy-done.1, bf16[32,3072]{1,0:T(8,128)(2,1)} %copy-done.6, ...), custom_call_target="tpu_custom_call" | custom-call | flops 1207959552 | bytes 20447232 | tf_op jit(solution)/shard_map/block_grads/pallas_call | solution.py:180
  128.3 13.5 %block_grads.2 = f32[288,128,128]{2,1,0:T(8,128)} custom-call(s32[288]{0:T(512)} %get-tuple-element.48.src_s.row_s, s32[288]{0:T(512)} %get-tuple-element.55.dst_s.col_s, s32[1]{0:T(128)} %constant.114.clone.1.in_s.out_s.left_s.right_s, s32[4]{0:T(128)} %copy-done.30, bf16[16,3072]{1,0:T(8,128)(2,1)} %refs_0_.5, bf16[16,3072]{1,0:T(8,128)(2,1)} %copy-done.18, ...), custom_call_target="tpu_custom_call" | custom-call | flops 1207959552 | bytes 20447232 | tf_op jit(solution)/shard_map/block_grads/pallas_call | solution.py:180
  141.9 1.4 collective-permute-start.13
  143.6 1.4 collective-permute-start.17
  145.4 5.3 %collective-permute-start.33 = (bf16[16,3072]{1,0:T(8,128)(2,1)S(1)}, bf16[16,3072]{1,0:T(8,128)(2,1)S(1)}, u32[]{:S(2)}, u32[]{:S(2)}) collective-permute-start(bf16[16,3072]{1,0:T(8,128)(2,1)S(1)} %add_convert_fusion.5), channel_id=1, source_target_pairs={{0,6},{1,7},{2,0},{3,1},{4,2},{5,3},{6,4},{7,5},{8,14},{9,15},{10,... | collective-permute-start | bytes 294920 | tf_op jit(solution)/shard_map/ppermute | solution.py:226
  151.0 1.3 collective-permute-start.37
  152.3 2.1 %collective-permute-start.14 = (bf16[16,3072]{1,0:T(8,128)(2,1)S(1)}, bf16[16,3072]{1,0:T(8,128)(2,1)S(1)}, u32[]{:S(2)}, u32[]{:S(2)}) collective-permute-start(bf16[16,3072]{1,0:T(8,128)(2,1)S(1)} %add_convert_fusion.9), channel_id=1, source_target_pairs={{0,6},{1,7},{2,0},{3,1},{4,2},{5,3},{6,4},{7,5},{8,14},{9,15},{10,... | collective-permute-start | bytes 294920 | tf_op jit(solution)/shard_map/ppermute | solution.py:226
  154.9 5.4 %collective-permute-done.35 = bf16[16,3072]{1,0:T(8,128)(2,1)S(1)} collective-permute-done((bf16[16,3072]{1,0:T(8,128)(2,1)S(1)}, bf16[16,3072]{1,0:T(8,128)(2,1)S(1)}, u32[]{:S(2)}, u32[]{:S(2)}) %collective-permute-start.35) | collective-permute-done | bytes 98336 | tf_op jit(solution)/shard_map/ppermute | solution.py:226
  160.3 0.7 add_convert_fusion.2
  161.0 7.4 %collective-permute-done.16 = bf16[16,3072]{1,0:T(8,128)(2,1)S(1)} collective-permute-done((bf16[16,3072]{1,0:T(8,128)(2,1)S(1)}, bf16[16,3072]{1,0:T(8,128)(2,1)S(1)}, u32[]{:S(2)}, u32[]{:S(2)}) %collective-permute-start.16) | collective-permute-done | bytes 98336 | tf_op jit(solution)/shard_map/ppermute | solution.py:226
  168.5 0.7 add_convert_fusion.6
  (123 shorter events, 6.9 us)
Async XLA Ops:
  0.6 12.8 %collective-permute-start.24 = (bf16[16,3072]{1,0:T(8,128)(2,1)}, bf16[16,3072]{1,0:T(8,128)(2,1)S(1)}, u32[]{:S(2)}, u32[]{:S(2)}) collective-permute-start(bf16[16,3072]{1,0:T(8,128)(2,1)} %refs_4_.1), channel_id=1, source_target_pairs={{0,6},{1,7},{2,0},{3,1},{4,2},{5,3},{6,4},{7,5},{8,14},{9,15},{10,... | collective-permute-start | bytes 294920 | tf_op jit(solution)/shard_map/ppermute | solution.py:226
  4.8 9.0 %collective-permute-start.22 = (bf16[16,3072]{1,0:T(8,128)(2,1)}, bf16[16,3072]{1,0:T(8,128)(2,1)S(1)}, u32[]{:S(2)}, u32[]{:S(2)}) collective-permute-start(bf16[16,3072]{1,0:T(8,128)(2,1)} %refs_4_.1), channel_id=1, source_target_pairs={{0,4},{1,5},{2,6},{3,7},{4,0},{5,1},{6,2},{7,3},{8,12},{9,13},{10,... | collective-permute-start | bytes 294920 | tf_op jit(solution)/shard_map/ppermute | solution.py:226
  4.8 10.2 %collective-permute-start.20 = (bf16[16,3072]{1,0:T(8,128)(2,1)}, bf16[16,3072]{1,0:T(8,128)(2,1)S(1)}, u32[]{:S(2)}, u32[]{:S(2)}) collective-permute-start(bf16[16,3072]{1,0:T(8,128)(2,1)} %refs_4_.1), channel_id=1, source_target_pairs={{0,2},{1,3},{2,4},{3,5},{4,6},{5,7},{6,0},{7,1},{8,10},{9,11},{10,... | collective-permute-start | bytes 294920 | tf_op jit(solution)/shard_map/ppermute | solution.py:226
  5.3 10.7 %collective-permute-start.19 = (bf16[16,3072]{1,0:T(8,128)(2,1)}, bf16[16,3072]{1,0:T(8,128)(2,1)S(1)}, u32[]{:S(2)}, u32[]{:S(2)}) collective-permute-start(bf16[16,3072]{1,0:T(8,128)(2,1)} %refs_4_.1), channel_id=1, source_target_pairs={{0,1},{1,0},{2,3},{3,2},{4,5},{5,4},{6,7},{7,6},{8,9},{9,8},{10,11... | collective-permute-start | bytes 294920 | tf_op jit(solution)/shard_map/ppermute | solution.py:221
  6.5 29.5 %collective-permute-start.5 = (bf16[16,3072]{1,0:T(8,128)(2,1)}, bf16[16,3072]{1,0:T(8,128)(2,1)S(1)}, u32[]{:S(2)}, u32[]{:S(2)}) collective-permute-start(bf16[16,3072]{1,0:T(8,128)(2,1)} %refs_0_.5), channel_id=1, source_target_pairs={{0,6},{1,7},{2,0},{3,1},{4,2},{5,3},{6,4},{7,5},{8,14},{9,15},{10,... | collective-permute-start | bytes 294920 | tf_op jit(solution)/shard_map/ppermute | solution.py:226
  11.9 69.7 %copy-start.30 = (s32[4]{0:T(128)}, s32[4]{0:T(128)S(1)}, u32[]{:S(2)}) copy-start(s32[4]{0:T(128)S(1)} %fusion.16.in_s.right_s.left_s) | copy-start | bytes 52
  13.5 6.0 %collective-permute-start.25 = (bf16[16,3072]{1,0:T(8,128)(2,1)S(1)}, bf16[16,3072]{1,0:T(8,128)(2,1)S(1)}, u32[]{:S(2)}, u32[]{:S(2)}) collective-permute-start(bf16[16,3072]{1,0:T(8,128)(2,1)S(1)} %collective-permute-done.24.refs_6_.refs_10_), channel_id=1, source_target_pairs={{0,1},{1,0},{2,3},{3,2},{4,5},{5,4},{6,7},{7,6},{8,9},{9,8},{10,11... | collective-permute-start | bytes 294920 | tf_op jit(solution)/shard_map/ppermute | solution.py:221
  13.9 5.6 %collective-permute-start.23 = (bf16[16,3072]{1,0:T(8,128)(2,1)S(1)}, bf16[16,3072]{1,0:T(8,128)(2,1)S(1)}, u32[]{:S(2)}, u32[]{:S(2)}) collective-permute-start(bf16[16,3072]{1,0:T(8,128)(2,1)S(1)} %collective-permute-done.22.refs_4_.refs_8_), channel_id=1, source_target_pairs={{0,1},{1,0},{2,3},{3,2},{4,5},{5,4},{6,7},{7,6},{8,9},{9,8},{10,11... | collective-permute-start | bytes 294920 | tf_op jit(solution)/shard_map/ppermute | solution.py:221
  15.0 5.3 %collective-permute-start.21 = (bf16[16,3072]{1,0:T(8,128)(2,1)S(1)}, bf16[16,3072]{1,0:T(8,128)(2,1)S(1)}, u32[]{:S(2)}, u32[]{:S(2)}) collective-permute-start(bf16[16,3072]{1,0:T(8,128)(2,1)S(1)} %collective-permute-done.20.refs_2_.refs_6_), channel_id=1, source_target_pairs={{0,1},{1,0},{2,3},{3,2},{4,5},{5,4},{6,7},{7,6},{8,9},{9,8},{10,11... | collective-permute-start | bytes 294920 | tf_op jit(solution)/shard_map/ppermute | solution.py:221
  15.9 22.8 %collective-permute-start.3 = (bf16[16,3072]{1,0:T(8,128)(2,1)}, bf16[16,3072]{1,0:T(8,128)(2,1)S(1)}, u32[]{:S(2)}, u32[]{:S(2)}) collective-permute-start(bf16[16,3072]{1,0:T(8,128)(2,1)} %refs_0_.5), channel_id=1, source_target_pairs={{0,4},{1,5},{2,6},{3,7},{4,0},{5,1},{6,2},{7,3},{8,12},{9,13},{10,... | collective-permute-start | bytes 294920 | tf_op jit(solution)/shard_map/ppermute | solution.py:226
  19.4 19.4 %collective-permute-start.1 = (bf16[16,3072]{1,0:T(8,128)(2,1)}, bf16[16,3072]{1,0:T(8,128)(2,1)S(1)}, u32[]{:S(2)}, u32[]{:S(2)}) collective-permute-start(bf16[16,3072]{1,0:T(8,128)(2,1)} %refs_0_.5), channel_id=1, source_target_pairs={{0,2},{1,3},{2,4},{3,5},{4,6},{5,7},{6,0},{7,1},{8,10},{9,11},{10,... | collective-permute-start | bytes 294920 | tf_op jit(solution)/shard_map/ppermute | solution.py:226
  19.5 22.7 %collective-permute-start = (bf16[16,3072]{1,0:T(8,128)(2,1)}, bf16[16,3072]{1,0:T(8,128)(2,1)S(1)}, u32[]{:S(2)}, u32[]{:S(2)}) collective-permute-start(bf16[16,3072]{1,0:T(8,128)(2,1)} %refs_0_.5), channel_id=1, source_target_pairs={{0,1},{1,0},{2,3},{3,2},{4,5},{5,4},{6,7},{7,6},{8,9},{9,8},{10,11... | collective-permute-start | bytes 294920 | tf_op jit(solution)/shard_map/ppermute | solution.py:221
  34.7 20.5 %collective-permute-start.26 = (bf16[2,32,3072]{2,1,0:T(8,128)(2,1)}, bf16[2,32,3072]{2,1,0:T(8,128)(2,1)S(1)}, u32[]{:S(2)}, u32[]{:S(2)}) collective-permute-start(bf16[2,32,3072]{2,1,0:T(8,128)(2,1)} %get-tuple-element.35), channel_id=1, source_target_pairs={{0,8},{8,0},{16,24},{24,16},{1,9},{9,1},{17,25},{25,17},{2,10},{10... | collective-permute-start | bytes 1179656 | tf_op jit(solution)/shard_map/ppermute | solution.py:221
  36.0 6.2 %collective-permute-start.6 = (bf16[16,3072]{1,0:T(8,128)(2,1)S(1)}, bf16[16,3072]{1,0:T(8,128)(2,1)S(1)}, u32[]{:S(2)}, u32[]{:S(2)}) collective-permute-start(bf16[16,3072]{1,0:T(8,128)(2,1)S(1)} %collective-permute-done.5.refs_6_), channel_id=1, source_target_pairs={{0,1},{1,0},{2,3},{3,2},{4,5},{5,4},{6,7},{7,6},{8,9},{9,8},{10,11... | collective-permute-start | bytes 294920 | tf_op jit(solution)/shard_map/ppermute | solution.py:221
  38.7 5.3 %collective-permute-start.4 = (bf16[16,3072]{1,0:T(8,128)(2,1)S(1)}, bf16[16,3072]{1,0:T(8,128)(2,1)S(1)}, u32[]{:S(2)}, u32[]{:S(2)}) collective-permute-start(bf16[16,3072]{1,0:T(8,128)(2,1)S(1)} %collective-permute-done.3.refs_4_), channel_id=1, source_target_pairs={{0,1},{1,0},{2,3},{3,2},{4,5},{5,4},{6,7},{7,6},{8,9},{9,8},{10,11... | collective-permute-start | bytes 294920 | tf_op jit(solution)/shard_map/ppermute | solution.py:221
  38.8 7.3 %collective-permute-start.2 = (bf16[16,3072]{1,0:T(8,128)(2,1)S(1)}, bf16[16,3072]{1,0:T(8,128)(2,1)S(1)}, u32[]{:S(2)}, u32[]{:S(2)}) collective-permute-start(bf16[16,3072]{1,0:T(8,128)(2,1)S(1)} %collective-permute-done.1.refs_2_), channel_id=1, source_target_pairs={{0,1},{1,0},{2,3},{3,2},{4,5},{5,4},{6,7},{7,6},{8,9},{9,8},{10,11... | collective-permute-start | bytes 294920 | tf_op jit(solution)/shard_map/ppermute | solution.py:221
  51.5 7.5 %collective-permute-start.7 = (bf16[2,32,3072]{2,1,0:T(8,128)(2,1)}, bf16[2,32,3072]{2,1,0:T(8,128)(2,1)S(1)}, u32[]{:S(2)}, u32[]{:S(2)}) collective-permute-start(bf16[2,32,3072]{2,1,0:T(8,128)(2,1)} %get-tuple-element.25), channel_id=1, source_target_pairs={{0,8},{8,0},{16,24},{24,16},{1,9},{9,1},{17,25},{25,17},{2,10},{10... | collective-permute-start | bytes 1179656 | tf_op jit(solution)/shard_map/ppermute | solution.py:221
  56.1 8.2 %collective-permute-start.27 = (bf16[32,3072]{1,0:T(8,128)(2,1)S(1)}, bf16[32,3072]{1,0:T(8,128)(2,1)S(1)}, u32[]{:S(2)}, u32[]{:S(2)}) collective-permute-start(bf16[32,3072]{1,0:T(8,128)(2,1)S(1)} %fusion.8), channel_id=1, source_target_pairs={{0,16},{8,24},{16,0},{24,8},{1,17},{9,25},{17,1},{25,9},{2,18},{10... | collective-permute-start | bytes 589832 | tf_op jit(solution)/shard_map/ppermute | solution.py:226
  60.0 8.5 %collective-permute-start.8 = (bf16[32,3072]{1,0:T(8,128)(2,1)S(1)}, bf16[32,3072]{1,0:T(8,128)(2,1)S(1)}, u32[]{:S(2)}, u32[]{:S(2)}) collective-permute-start(bf16[32,3072]{1,0:T(8,128)(2,1)S(1)} %fusion.7), channel_id=1, source_target_pairs={{0,16},{8,24},{16,0},{24,8},{1,17},{9,25},{17,1},{25,9},{2,18},{10... | collective-permute-start | bytes 589832 | tf_op jit(solution)/shard_map/ppermute | solution.py:226
  70.0 31.7 %copy-start.1 = (bf16[32,3072]{1,0:T(8,128)(2,1)}, bf16[32,3072]{1,0:T(8,128)(2,1)S(1)}, u32[]{:S(2)}) copy-start(bf16[32,3072]{1,0:T(8,128)(2,1)S(1)} %get-tuple-element.51.refs_0_) | copy-start | bytes 589828
  70.0 5.9 %collective-permute-start.29 = (bf16[32,3072]{1,0:T(8,128)(2,1)S(1)}, bf16[32,3072]{1,0:T(8,128)(2,1)S(1)}, u32[]{:S(2)}, u32[]{:S(2)}) collective-permute-start(bf16[32,3072]{1,0:T(8,128)(2,1)S(1)} %get-tuple-element.50.refs_0_.refs_8_), channel_id=1, source_target_pairs={{0,16},{8,24},{16,0},{24,8},{1,17},{9,25},{17,1},{25,9},{2,18},{10... | collective-permute-start | bytes 589832 | tf_op jit(solution)/shard_map/ppermute | solution.py:226
  71.2 8.9 %collective-permute-start.10 = (bf16[32,3072]{1,0:T(8,128)(2,1)S(1)}, bf16[32,3072]{1,0:T(8,128)(2,1)S(1)}, u32[]{:S(2)}, u32[]{:S(2)}) collective-permute-start(bf16[32,3072]{1,0:T(8,128)(2,1)S(1)} %get-tuple-element.51.refs_0_), channel_id=1, source_target_pairs={{0,16},{8,24},{16,0},{24,8},{1,17},{9,25},{17,1},{25,9},{2,18},{10... | collective-permute-start | bytes 589832 | tf_op jit(solution)/shard_map/ppermute | solution.py:226
  71.5 10.1 %collective-permute-start.28 = (bf16[32,3072]{1,0:T(8,128)(2,1)S(1)}, bf16[32,3072]{1,0:T(8,128)(2,1)S(1)}, u32[]{:S(2)}, u32[]{:S(2)}) collective-permute-start(bf16[32,3072]{1,0:T(8,128)(2,1)S(1)} %get-tuple-element.50.refs_0_.refs_8_), channel_id=1, source_target_pairs={{0,8},{8,0},{16,24},{24,16},{1,9},{9,1},{17,25},{25,17},{2,10},{10... | collective-permute-start | bytes 589832 | tf_op jit(solution)/shard_map/ppermute | solution.py:221
  75.9 5.7 %collective-permute-start.30 = (bf16[32,3072]{1,0:T(8,128)(2,1)S(1)}, bf16[32,3072]{1,0:T(8,128)(2,1)S(1)}, u32[]{:S(2)}, u32[]{:S(2)}) collective-permute-start(bf16[32,3072]{1,0:T(8,128)(2,1)S(1)} %collective-permute-done.29.refs_2_.refs_10_), channel_id=1, source_target_pairs={{0,8},{8,0},{16,24},{24,16},{1,9},{9,1},{17,25},{25,17},{2,10},{10... | collective-permute-start | bytes 589832 | tf_op jit(solution)/shard_map/ppermute | solution.py:221
  78.4 23.1 %collective-permute-start.9 = (bf16[32,3072]{1,0:T(8,128)(2,1)S(1)}, bf16[32,3072]{1,0:T(8,128)(2,1)S(1)}, u32[]{:S(2)}, u32[]{:S(2)}) collective-permute-start(bf16[32,3072]{1,0:T(8,128)(2,1)S(1)} %get-tuple-element.51.refs_0_), channel_id=1, source_target_pairs={{0,8},{8,0},{16,24},{24,16},{1,9},{9,1},{17,25},{25,17},{2,10},{10... | collective-permute-start | bytes 589832 | tf_op jit(solution)/shard_map/ppermute | solution.py:221
  80.1 21.5 %collective-permute-start.11 = (bf16[32,3072]{1,0:T(8,128)(2,1)S(1)}, bf16[32,3072]{1,0:T(8,128)(2,1)S(1)}, u32[]{:S(2)}, u32[]{:S(2)}) collective-permute-start(bf16[32,3072]{1,0:T(8,128)(2,1)S(1)} %collective-permute-done.10.refs_2_), channel_id=1, source_target_pairs={{0,8},{8,0},{16,24},{24,16},{1,9},{9,1},{17,25},{25,17},{2,10},{10... | collective-permute-start | bytes 589832 | tf_op jit(solution)/shard_map/ppermute | solution.py:221
  87.4 64.8 %collective-permute-start.31 = (bf16[16,3072]{1,0:T(8,128)(2,1)}, bf16[16,3072]{1,0:T(8,128)(2,1)S(1)}, u32[]{:S(2)}, u32[]{:S(2)}) collective-permute-start(bf16[16,3072]{1,0:T(8,128)(2,1)} %get-tuple-element.37), channel_id=1, source_target_pairs={{0,1},{1,0},{2,3},{3,2},{4,5},{5,4},{6,7},{7,6},{8,9},{9,8},{10,11... | collective-permute-start | bytes 294920 | tf_op jit(solution)/shard_map/ppermute | solution.py:221
  100.1 41.8 %collective-permute-start.32 = (bf16[16,3072]{1,0:T(8,128)(2,1)}, bf16[16,3072]{1,0:T(8,128)(2,1)S(1)}, u32[]{:S(2)}, u32[]{:S(2)}) collective-permute-start(bf16[16,3072]{1,0:T(8,128)(2,1)} %get-tuple-element.39), channel_id=1, source_target_pairs={{0,1},{1,0},{2,3},{3,2},{4,5},{5,4},{6,7},{7,6},{8,9},{9,8},{10,11... | collective-permute-start | bytes 294920 | tf_op jit(solution)/shard_map/ppermute | solution.py:221
  100.1 43.2 %collective-permute-start.34 = (bf16[16,3072]{1,0:T(8,128)(2,1)}, bf16[16,3072]{1,0:T(8,128)(2,1)S(1)}, u32[]{:S(2)}, u32[]{:S(2)}) collective-permute-start(bf16[16,3072]{1,0:T(8,128)(2,1)} %get-tuple-element.41), channel_id=1, source_target_pairs={{0,1},{1,0},{2,3},{3,2},{4,5},{5,4},{6,7},{7,6},{8,9},{9,8},{10,11... | collective-permute-start | bytes 294920 | tf_op jit(solution)/shard_map/ppermute | solution.py:221
  101.5 42.0 %collective-permute-start.36 = (bf16[16,3072]{1,0:T(8,128)(2,1)}, bf16[16,3072]{1,0:T(8,128)(2,1)S(1)}, u32[]{:S(2)}, u32[]{:S(2)}) collective-permute-start(bf16[16,3072]{1,0:T(8,128)(2,1)} %get-tuple-element.43), channel_id=1, source_target_pairs={{0,1},{1,0},{2,3},{3,2},{4,5},{5,4},{6,7},{7,6},{8,9},{9,8},{10,11... | collective-permute-start | bytes 294920 | tf_op jit(solution)/shard_map/ppermute | solution.py:221
  114.4 29.2 %copy-start.26 = (bf16[16,3072]{1,0:T(8,128)(2,1)S(1)}, bf16[16,3072]{1,0:T(8,128)(2,1)}, u32[]{:S(2)}) copy-start(bf16[16,3072]{1,0:T(8,128)(2,1)} %get-tuple-element.40) | copy-start | bytes 294916
  114.4 29.2 %copy-start.31 = (bf16[16,3072]{1,0:T(8,128)(2,1)S(1)}, bf16[16,3072]{1,0:T(8,128)(2,1)}, u32[]{:S(2)}) copy-start(bf16[16,3072]{1,0:T(8,128)(2,1)} %get-tuple-element.33) | copy-start | bytes 294916
  114.4 30.6 %copy-start.24 = (bf16[16,3072]{1,0:T(8,128)(2,1)S(1)}, bf16[16,3072]{1,0:T(8,128)(2,1)}, u32[]{:S(2)}) copy-start(bf16[16,3072]{1,0:T(8,128)(2,1)} %get-tuple-element.42) | copy-start | bytes 294916
  114.4 36.4 %copy-start.29 = (bf16[16,3072]{1,0:T(8,128)(2,1)S(1)}, bf16[16,3072]{1,0:T(8,128)(2,1)}, u32[]{:S(2)}) copy-start(bf16[16,3072]{1,0:T(8,128)(2,1)} %get-tuple-element.28) | copy-start | bytes 294916
  114.4 36.5 %copy-start.27 = (bf16[16,3072]{1,0:T(8,128)(2,1)S(1)}, bf16[16,3072]{1,0:T(8,128)(2,1)}, u32[]{:S(2)}) copy-start(bf16[16,3072]{1,0:T(8,128)(2,1)} %get-tuple-element.30) | copy-start | bytes 294916
  114.4 37.8 %copy-start.25 = (bf16[16,3072]{1,0:T(8,128)(2,1)S(1)}, bf16[16,3072]{1,0:T(8,128)(2,1)}, u32[]{:S(2)}) copy-start(bf16[16,3072]{1,0:T(8,128)(2,1)} %get-tuple-element.32) | copy-start | bytes 294916
  114.4 45.9 %copy-start.22 = (bf16[16,3072]{1,0:T(8,128)(2,1)S(1)}, bf16[16,3072]{1,0:T(8,128)(2,1)}, u32[]{:S(2)}) copy-start(bf16[16,3072]{1,0:T(8,128)(2,1)} %get-tuple-element.36) | copy-start | bytes 294916
  114.5 54.0 %copy-start.23 = (bf16[16,3072]{1,0:T(8,128)(2,1)S(1)}, bf16[16,3072]{1,0:T(8,128)(2,1)}, u32[]{:S(2)}) copy-start(bf16[16,3072]{1,0:T(8,128)(2,1)} %get-tuple-element.26) | copy-start | bytes 294916
  114.5 46.6 %collective-permute-start.12 = (bf16[16,3072]{1,0:T(8,128)(2,1)}, bf16[16,3072]{1,0:T(8,128)(2,1)S(1)}, u32[]{:S(2)}, u32[]{:S(2)}) collective-permute-start(bf16[16,3072]{1,0:T(8,128)(2,1)} %get-tuple-element.27), channel_id=1, source_target_pairs={{0,1},{1,0},{2,3},{3,2},{4,5},{5,4},{6,7},{7,6},{8,9},{9,8},{10,11... | collective-permute-start | bytes 294920 | tf_op jit(solution)/shard_map/ppermute | solution.py:221
  141.9 3.5 %collective-permute-start.13 = (bf16[16,3072]{1,0:T(8,128)(2,1)S(1)}, bf16[16,3072]{1,0:T(8,128)(2,1)S(1)}, u32[]{:S(2)}, u32[]{:S(2)}) collective-permute-start(bf16[16,3072]{1,0:T(8,128)(2,1)S(1)} %copy-done.33), channel_id=1, source_target_pairs={{0,1},{1,0},{2,3},{3,2},{4,5},{5,4},{6,7},{7,6},{8,9},{9,8},{10,11... | collective-permute-start | bytes 294920 | tf_op jit(solution)/shard_map/ppermute | solution.py:221
  143.3 7.5 %collective-permute-start.15 = (bf16[16,3072]{1,0:T(8,128)(2,1)S(1)}, bf16[16,3072]{1,0:T(8,128)(2,1)S(1)}, u32[]{:S(2)}, u32[]{:S(2)}) collective-permute-start(bf16[16,3072]{1,0:T(8,128)(2,1)S(1)} %copy-done.32), channel_id=1, source_target_pairs={{0,1},{1,0},{2,3},{3,2},{4,5},{5,4},{6,7},{7,6},{8,9},{9,8},{10,11... | collective-permute-start | bytes 294920 | tf_op jit(solution)/shard_map/ppermute | solution.py:221
  143.6 7.3 %collective-permute-start.17 = (bf16[16,3072]{1,0:T(8,128)(2,1)S(1)}, bf16[16,3072]{1,0:T(8,128)(2,1)S(1)}, u32[]{:S(2)}, u32[]{:S(2)}) collective-permute-start(bf16[16,3072]{1,0:T(8,128)(2,1)S(1)} %copy-done.31), channel_id=1, source_target_pairs={{0,1},{1,0},{2,3},{3,2},{4,5},{5,4},{6,7},{7,6},{8,9},{9,8},{10,11... | collective-permute-start | bytes 294920 | tf_op jit(solution)/shard_map/ppermute | solution.py:221
  145.4 8.9 %collective-permute-start.33 = (bf16[16,3072]{1,0:T(8,128)(2,1)S(1)}, bf16[16,3072]{1,0:T(8,128)(2,1)S(1)}, u32[]{:S(2)}, u32[]{:S(2)}) collective-permute-start(bf16[16,3072]{1,0:T(8,128)(2,1)S(1)} %add_convert_fusion.5), channel_id=1, source_target_pairs={{0,6},{1,7},{2,0},{3,1},{4,2},{5,3},{6,4},{7,5},{8,14},{9,15},{10,... | collective-permute-start | bytes 294920 | tf_op jit(solution)/shard_map/ppermute | solution.py:226
  150.8 9.5 %collective-permute-start.35 = (bf16[16,3072]{1,0:T(8,128)(2,1)S(1)}, bf16[16,3072]{1,0:T(8,128)(2,1)S(1)}, u32[]{:S(2)}, u32[]{:S(2)}) collective-permute-start(bf16[16,3072]{1,0:T(8,128)(2,1)S(1)} %add_convert_fusion.4), channel_id=1, source_target_pairs={{0,4},{1,5},{2,6},{3,7},{4,0},{5,1},{6,2},{7,3},{8,12},{9,13},{10,... | collective-permute-start | bytes 294920 | tf_op jit(solution)/shard_map/ppermute | solution.py:226
  151.0 9.4 %collective-permute-start.37 = (bf16[16,3072]{1,0:T(8,128)(2,1)S(1)}, bf16[16,3072]{1,0:T(8,128)(2,1)S(1)}, u32[]{:S(2)}, u32[]{:S(2)}) collective-permute-start(bf16[16,3072]{1,0:T(8,128)(2,1)S(1)} %add_convert_fusion.3), channel_id=1, source_target_pairs={{0,2},{1,3},{2,4},{3,5},{4,6},{5,7},{6,0},{7,1},{8,10},{9,11},{10,... | collective-permute-start | bytes 294920 | tf_op jit(solution)/shard_map/ppermute | solution.py:226
  152.3 8.8 %collective-permute-start.14 = (bf16[16,3072]{1,0:T(8,128)(2,1)S(1)}, bf16[16,3072]{1,0:T(8,128)(2,1)S(1)}, u32[]{:S(2)}, u32[]{:S(2)}) collective-permute-start(bf16[16,3072]{1,0:T(8,128)(2,1)S(1)} %add_convert_fusion.9), channel_id=1, source_target_pairs={{0,6},{1,7},{2,0},{3,1},{4,2},{5,3},{6,4},{7,5},{8,14},{9,15},{10,... | collective-permute-start | bytes 294920 | tf_op jit(solution)/shard_map/ppermute | solution.py:226
  154.4 14.1 %collective-permute-start.16 = (bf16[16,3072]{1,0:T(8,128)(2,1)S(1)}, bf16[16,3072]{1,0:T(8,128)(2,1)S(1)}, u32[]{:S(2)}, u32[]{:S(2)}) collective-permute-start(bf16[16,3072]{1,0:T(8,128)(2,1)S(1)} %add_convert_fusion.8), channel_id=1, source_target_pairs={{0,4},{1,5},{2,6},{3,7},{4,0},{5,1},{6,2},{7,3},{8,12},{9,13},{10,... | collective-permute-start | bytes 294920 | tf_op jit(solution)/shard_map/ppermute | solution.py:226
  160.3 8.1 %collective-permute-start.18 = (bf16[16,3072]{1,0:T(8,128)(2,1)S(1)}, bf16[16,3072]{1,0:T(8,128)(2,1)S(1)}, u32[]{:S(2)}, u32[]{:S(2)}) collective-permute-start(bf16[16,3072]{1,0:T(8,128)(2,1)S(1)} %add_convert_fusion.7), channel_id=1, source_target_pairs={{0,2},{1,3},{2,4},{3,5},{4,6},{5,7},{6,0},{7,1},{8,10},{9,11},{10,... | collective-permute-start | bytes 294920 | tf_op jit(solution)/shard_map/ppermute | solution.py:226
  (24 other events, 187.8 us)
where the time goes:
time: 170 us; the launch traced here: 169 us
  Pallas kernels  63.1 us (37%)
  starting transfers between devices  59.4 us (35%)
  waiting for transfers between devices  30.7 us (18%)
  other arithmetic  10.7 us (6%)
  local copies, waits for them, and re-layouts  2.85 us (2%)
  between operations  2.41 us (1%)
    pallas_call x4, Pallas kernels, block_product(): pl.pallas_call(body, grid_spec=pltpu.PrefetchScalarGridSpec(num_scalar_pr...  35.8 us
    ppermute x22, starting transfers between devices, near_move(): return lax.ppermute(v, axis, [(i, i ^ 1) for i in range(count)])  34.1 us
    pallas_call x2, Pallas kernels, block_grads(): pl.pallas_call(body, grid_spec=pltpu.PrefetchScalarGridSpec(num_scalar_pr...  27.3 us
    ppermute x16, waiting for transfers between devices, far_move(): return lax.ppermute(v, axis, pairs)  25.8 us
    ppermute x16, starting transfers between devices, far_move(): return lax.ppermute(v, axis, pairs)  25.3 us
    ppermute x22, waiting for transfers between devices, near_move(): return lax.ppermute(v, axis, [(i, i ^ 1) for i in range(count)])  4.88 us
  transfers between devices with their start and end apart: 38, of which 11 were waited for; matrix products, arithmetic and copies ran while one was open for 5% of the time, Pallas kernels for 37%

commit v1 on v0

v1 whole, which is shorter than its diff:
```python
import jax
import jax.numpy as jnp
from jax import lax
from jax.experimental import pallas as pl
from jax.experimental.pallas import tpu as pltpu
from jax.sharding import PartitionSpec as P


GELU_SCALE = 0.7978845608028654
GELU_CUBE = 0.044715


def gelu_value(values):
    return (
        0.5
        * values
        * (1.0 + jnp.tanh(GELU_SCALE * (values + GELU_CUBE * values * values * values)))
    )


def gelu_slope(values):
    tangent = jnp.tanh(GELU_SCALE * (values + GELU_CUBE * values * values * values))
    return 0.5 * (1.0 + tangent) + 0.5 * values * (1.0 - tangent * tangent) * GELU_SCALE * (
        1.0 + 3.0 * GELU_CUBE * values * values
    )


def after(values, *earlier):
    return lax.optimization_barrier((values, earlier))[0]


def largest_divisor(number, limit):
    return max(d for d in range(1, limit + 1) if number % d == 0)


def load_pieces(piece_refs, offsets, store, width):
    for i, piece in enumerate(piece_refs):
        length = piece.shape[0]
        start = offsets(i, length)
        for b in range(piece.shape[1] // width):
            store[b, pl.ds(start, length), :] = piece[:, b * width : (b + 1) * width]


def pair_tables(jobs, weights):
    cap = jobs[0][0].shape[0]
    specs = [job[1:] for job in jobs]
    n = len(jobs)
    limits = [pair_limit(cap, rows if by_row else cols) for rows, cols, by_row in specs]

    def body(*refs):
        refs = refs[:n] + refs[n + len(weights) :]
        slot_refs, tables, pending = refs[:n], refs[n : 2 * n], refs[2 * n :]
        for (rows, cols, by_row), pend in zip(specs, pending):

            def clear(i, carry, pend=pend):
                pend[i] = -1
                return carry

            lax.fori_loop(0, (rows if by_row else cols) + 1, clear, 0)

        def one(k, counts):
            counts = list(counts)
            for t, (rows, cols, by_row) in enumerate(specs):
                pos = slot_refs[t][k]
                filled = pos >= 0
                safe = jnp.maximum(pos, 0)
                row = (safe * (-(-65536 // cols))) >> 16
                col = safe - row * cols
                key, src, end = (row, col, rows) if by_row else (col, row, cols)
                table, pend, limit = tables[t], pending[t], limits[t]
                key = jnp.where(filled, key, end)
                first = pend[key]
                word = k + src * 4096
                paired = jnp.logical_and(first >= 0, filled)
                at = counts[t]
                table[at] = first
                table[limit + at] = word
                table[2 * limit + at] = key
                pend[key] = jnp.where(first >= 0, -1, word)
                counts[t] = at + paired.astype(jnp.int32)
            return tuple(counts)

        counts = lax.fori_loop(0, cap, one, (jnp.int32(0),) * n)
        for t, (rows, cols, by_row) in enumerate(specs):
            table, pend, limit = tables[t], pending[t], limits[t]
            n_dst, n_src = (rows, cols) if by_row else (cols, rows)

            def rest(d, at, table=table, pend=pend, limit=limit, n_src=n_src):
                first = pend[d]
                table[at] = first
                table[limit + at] = n_src * 4096
                table[2 * limit + at] = d
                return at + (first >= 0).astype(jnp.int32)

            at = lax.fori_loop(0, n_dst, rest, counts[t])
            for u in range(PAIR_UNROLL):
                table[at + u] = n_src * 4096
                table[limit + at + u] = n_src * 4096
                table[2 * limit + at + u] = n_dst
            table[3 * limit] = (at + (PAIR_UNROLL - 1)) >> PAIR_SHIFT

    smem = pl.BlockSpec(memory_space=pltpu.SMEM)
    return pl.pallas_call(
        body,
        in_specs=[smem] * n + [pl.BlockSpec(memory_space=pltpu.VMEM)] * len(weights),
        out_specs=[smem] * n,
        out_shape=[jax.ShapeDtypeStruct((3 * limit + 1,), jnp.int32) for limit in limits],
        scratch_shapes=[pltpu.SMEM(((rows if by_row else cols) + 1,), jnp.int32) for rows, cols, by_row in specs],
        compiler_params=pltpu.CompilerParams(vmem_limit_bytes=1024 * 1024),
        name="pair_tables",
    )(*[job[0] for job in jobs], *weights)


PAIR_SHIFT = 4
PAIR_UNROLL = 1 << PAIR_SHIFT


def pair_limit(cap, n_dst):
    return (cap + n_dst) // 2 + PAIR_UNROLL + 1


def block_product(pieces, in_rows, blocks, table, n_dst, out_lengths, out_rows, transposed):
    cap, width = blocks.shape[0], blocks.shape[1]
    n_src = pieces[0].shape[1] // width
    tokens = sum(piece.shape[0] for piece in pieces)
    limit = pair_limit(cap, n_dst)
    dims = (((1,), (1 if transposed else 0,)), ((), ()))
    zero_rows = jnp.zeros((1,), jnp.int32)
    in_arr = zero_rows if in_rows is None else in_rows
    out_arr = zero_rows if out_rows is None else out_rows
    n_in, n_out = len(pieces), len(out_lengths)

    def body(table_s, in_s, out_s, *refs):
        piece_refs = refs[:n_in]
        w_ref = refs[n_in]
        out_refs = refs[n_in + 1 : n_in + 1 + n_out]
        xs, acc = refs[n_in + 1 + n_out :]
        if in_rows is None:
            place = lambda i, length: i * length
        else:
            place = lambda i, length: pl.multiple_of(in_s[i], length)
        load_pieces(piece_refs, place, xs, width)
        xs[n_src] = jnp.zeros((tokens, width), xs.dtype)
        acc[...] = jnp.zeros_like(acc)

        def some(g, carry):
            terms = []
            for u in range(PAIR_UNROLL):
                n = g * PAIR_UNROLL + u
                one, two = table_s[n], table_s[limit + n]
                left = jnp.concatenate([xs[one >> 12], xs[two >> 12]], axis=1)
                right = jnp.concatenate(
                    [w_ref[one & 4095], w_ref[two & 4095]], axis=1 if transposed else 0
                )
                terms.append(lax.dot_general(left, right, dims, preferred_element_type=jnp.float32))
            for u in range(PAIR_UNROLL):
                acc[table_s[2 * limit + g * PAIR_UNROLL + u]] += terms[u]
            return carry

        lax.fori_loop(0, table_s[3 * limit], some, 0)
        at = 0
        for ref in out_refs:
            lead = ref.shape[:-2]
            length = ref.shape[-2]
            for j in range(lead[0] if lead else 1):
                start = at * length if out_rows is None else pl.multiple_of(out_s[at], length)
                at += 1
                for b in range(n_dst):
                    val = acc[b, pl.ds(start, length), :].astype(jnp.bfloat16)
                    if lead:
                        ref[j, :, b * width : (b + 1) * width] = val
                    else:
                        ref[:, b * width : (b + 1) * width] = val

    smem = pl.BlockSpec(memory_space=pltpu.SMEM)
    vmem = pl.BlockSpec(memory_space=pltpu.VMEM)
    out_shapes = [shape + (n_dst * width,) for shape in out_lengths]
    return pl.pallas_call(
        body,
        in_specs=[smem] * 3 + [vmem] * (n_in + 1),
        out_specs=[vmem] * n_out,
        scratch_shapes=[
            pltpu.VMEM((n_src + 1, tokens, width), jnp.bfloat16),
            pltpu.VMEM((n_dst + 1, tokens, width), jnp.float32),
        ],
        out_shape=[jax.ShapeDtypeStruct(shape, jnp.bfloat16) for shape in out_shapes],
        compiler_params=pltpu.CompilerParams(vmem_limit_bytes=8 * 1024 * 1024),
        cost_estimate=pl.CostEstimate(
            flops=2 * cap * tokens * width * width,
            bytes_accessed=cap * width * width * 2 + tokens * width * 2 * (n_src + n_dst),
            transcendentals=0,
        ),
        name="block_product",
    )(table, in_arr, out_arr, *pieces, blocks)


def block_grads(left, left_rows, right, right_rows, rows, cols, cap):
    width = 128
    n_left, n_right = left[0].shape[1] // width, right[0].shape[1] // width
    tokens = sum(piece.shape[0] for piece in left)
    chunk = largest_divisor(cap, 48)
    unroll = chunk
    steps = cap // chunk
    n_l, n_r = len(left), len(right)
    dims = (((1,), (0,)), ((), ()))
    zero_rows = jnp.zeros((1,), jnp.int32)
    left_arr = zero_rows if left_rows is None else left_rows
    right_arr = zero_rows if right_rows is None else right_rows

    def body(row_s, col_s, left_s, right_s, *refs):
        l_refs = refs[:n_l]
        r_refs = refs[n_l : n_l + n_r]
        out = refs[n_l + n_r]
        ls, lt, rs = refs[n_l + n_r + 1 :]
        step = pl.program_id(0)

        @pl.when(step == 0)
        def _():
            def place(given, table):
                if given is None:
                    return lambda i, length: i * length
                return lambda i, length: pl.multiple_of(table[i], length)

            load_pieces(l_refs, place(left_rows, left_s), ls, width)
            load_pieces(r_refs, place(right_rows, right_s), rs, width)
            rs[n_right] = jnp.zeros((tokens, width), rs.dtype)
            for b in range(n_left):
                lt[b] = ls[b].T

        def some(g, carry):
            base = g * unroll
            for u in range(unroll):
                k = step * chunk + base + u
                out[base + u] = lax.dot_general(
                    lt[row_s[k]], rs[col_s[k]], dims, preferred_element_type=jnp.float32
                )
            return carry

        lax.fori_loop(0, chunk // unroll, some, 0)

    whole = lambda shape: pl.BlockSpec(shape, lambda i, *s: (0,) * len(shape))
    return pl.pallas_call(
        body,
        grid_spec=pltpu.PrefetchScalarGridSpec(
            num_scalar_prefetch=4,
            grid=(steps,),
            in_specs=[whole(piece.shape) for piece in left] + [whole(piece.shape) for piece in right],
            out_specs=pl.BlockSpec((chunk, width, width), lambda i, *s: (i, 0, 0)),
            scratch_shapes=[
                pltpu.VMEM((n_left, tokens, width), jnp.bfloat16),
                pltpu.VMEM((n_left, width, tokens), jnp.bfloat16),
                pltpu.VMEM((n_right + 1, tokens, width), jnp.bfloat16),
            ],
        ),
        out_shape=jax.ShapeDtypeStruct((cap, width, width), jnp.float32),
        compiler_params=pltpu.CompilerParams(
            dimension_semantics=("arbitrary",), vmem_limit_bytes=16 * 1024 * 1024
        ),
        cost_estimate=pl.CostEstimate(
            flops=2 * cap * tokens * width * width,
            bytes_accessed=cap * width * width * 4 + tokens * width * 2 * (n_left + n_right),
            transcendentals=0,
        ),
        name="block_grads",
    )(rows, cols, left_arr, right_arr, *left, *right)


def on_device(tokens, in_blocks, in_slots, out_blocks, out_slots, cotangent, *, hidden_total):
    w_in = in_blocks.reshape(in_blocks.shape[2:])
    w_out = out_blocks.reshape(out_blocks.shape[2:])
    slots_in = in_slots.reshape(-1)
    slots_out = out_slots.reshape(-1)
    width = w_in.shape[-1]
    cap = w_in.shape[0]
    tensor_count = lax.axis_size("tensor")
    seq_count = lax.axis_size("seq")
    feat_blocks = tokens.shape[1] // width
    hid_blocks = hidden_total // tensor_count // width
    tensor_rows = tokens.shape[0]
    token_count = tensor_rows * tensor_count
    seq_rows = token_count // seq_count
    far_t, far_s = tensor_count // 2, seq_count // 2

    def near_move(v, axis, count):
        return lax.ppermute(v, axis, [(i, i ^ 1) for i in range(count)])

    def far_move(v, axis, count, shift):
        half = count // 2
        pairs = [(o * 2 + c, ((o + shift) % half) * 2 + c) for o in range(half) for c in range(2)]
        return lax.ppermute(v, axis, pairs)

    me = lax.axis_index("seq")
    shifts = jnp.arange(seq_count, dtype=jnp.int32)
    far_of = (me // 2 + far_s - shifts // 2) % far_s
    seq_part = (far_of * 2 + (me % 2 + shifts % 2) % 2) * seq_rows
    near_order = jnp.concatenate([seq_part[0::2], seq_part[1::2]])

    def positions(slot_list, cols):
        filled = slot_list >= 0
        safe = jnp.where(filled, slot_list, 0)
        return safe // cols, jnp.where(filled, safe % cols, cols)

    in_row, in_col = positions(slots_in, hid_blocks)
    out_row, out_col = positions(slots_out, feat_blocks)

    def gather_far(own):
        return [own] + [far_move(own, "tensor", tensor_count, k) for k in range(1, far_t)]

    def gather_near(far):
        pieces = []
        for piece in far:
            pieces += [piece, near_move(piece, "tensor", tensor_count)]
        return pieces

    def send_near(terms):
        order = list(range(1, far_t)) + [0]
        got = {k: near_move(terms[2 * k + 1], "tensor", tensor_count) for k in order}
        return [got[k] for k in range(far_t)]

    def pair_out(terms, got):
        pair = [terms[2 * k].astype(jnp.float32) + got[k].astype(jnp.float32) for k in range(far_t)]
        return pair[0], [value.astype(jnp.bfloat16) for value in pair[1:]]

    def total_out(own, pairs):
        moved = [far_move(pairs[k - 1], "tensor", tensor_count, far_t - k) for k in range(1, far_t)]
        total = own
        for value in moved:
            total = total + value.astype(jnp.float32)
        return total.astype(jnp.bfloat16)

    def pair_hidden(keep, send):
        got = near_move(send, "seq", seq_count)
        pair = [keep[k].astype(jnp.float32) + got[k].astype(jnp.float32) for k in range(far_s)]
        return pair[0], [value.astype(jnp.bfloat16) for value in pair[1:]]

    def total_hidden(own, pairs, *earlier):
        moved = [far_move(pairs[k - 1], "seq", seq_count, far_s - k) for k in range(1, far_s)]
        total = own
        for value in moved:
            total = total + after(value, *earlier).astype(jnp.float32)
        return total

    def spread_far(own):
        return [own] + [far_move(own, "seq", seq_count, k) for k in range(1, far_s)]

    def spread_near(far):
        pieces = []
        for piece in far:
            pieces += [piece, near_move(piece, "seq", seq_count)]
        return pieces

    hidden_lengths = [(far_s, seq_rows)] * 2
    token_lengths = [(tensor_rows,)] * tensor_count

    tok_far = gather_far(tokens)
    (in_by_col,) = pair_tables([(slots_in, feat_blocks, hid_blocks, False)], [w_in])
    cot_far = gather_far(after(cotangent, tok_far[1:]))
    tok = gather_near(tok_far)
    cot = gather_near(cot_far)
    later_in, later_out = after((slots_in, slots_out), tok_far[1:])
    out_by_row, out_by_col, in_by_row = pair_tables(
        [
            (later_out, hid_blocks, feat_blocks, True),
            (later_out, hid_blocks, feat_blocks, False),
            (later_in, feat_blocks, hid_blocks, True),
        ],
        [w_out],
    )
    keep_h, send_h = block_product(
        tok, None, w_in, in_by_col, hid_blocks, hidden_lengths, near_order, False
    )
    own_h, pairs_h = pair_hidden(keep_h, send_h)
    keep_g, send_g = block_product(
        after(cot, pairs_h), None, w_out, out_by_row, hid_blocks, hidden_lengths, near_order, True
    )
    hidden = total_hidden(own_h, pairs_h)
    own_act = gelu_value(hidden).astype(jnp.bfloat16)
    act_far = spread_far(own_act)
    activated = spread_near(act_far)
    own_g, pairs_g = pair_hidden(keep_g, send_g)
    grad_act = total_hidden(own_g, pairs_g, own_act)
    own_gh = (grad_act * gelu_slope(hidden)).astype(jnp.bfloat16)
    gh_far = spread_far(own_gh)
    grad_hidden = spread_near(gh_far)

    terms_o = block_product(
        after(activated, own_gh), seq_part, w_out, out_by_col, feat_blocks, token_lengths, None, False
    )
    got_o = send_near(terms_o)
    terms_t = block_product(
        after(grad_hidden, terms_o), seq_part, w_in, in_by_row, feat_blocks, token_lengths, None, True
    )
    got_t = send_near(terms_t)
    own_o, pairs_o = pair_out(terms_o, after(got_o, terms_t))
    grad_out = block_grads(after(activated, pairs_o), seq_part, cot, None, out_row, out_col, cap)
    own_t, pairs_t = pair_out(terms_t, after(got_t, grad_out))
    grad_in = block_grads(tok, None, after(grad_hidden, pairs_t), seq_part, in_row, in_col, cap)
    output = total_out(own_o, pairs_o)
    grad_tokens = total_out(own_t, pairs_t)
    return (
        output,
        grad_tokens,
        grad_in.reshape(in_blocks.shape),
        grad_out.reshape(out_blocks.shape),
    )


HIDDEN_TOTAL = 24576


def solution(mesh):
    def program(*args):
        return on_device(*args, hidden_total=HIDDEN_TOTAL)

    return jax.shard_map(
        program,
        mesh=mesh,
        in_specs=(
            P("tensor", "seq"),
            P("seq", "tensor", None, None, None),
            P("seq", "tensor", None),
            P("tensor", "seq", None, None, None),
            P("tensor", "seq", None),
            P("tensor", "seq"),
        ),
        out_specs=(
            P("tensor", "seq"),
            P("tensor", "seq"),
            P("seq", "tensor", None, None, None),
            P("tensor", "seq", None, None, None),
        ),
        check_vma=False,
    )
```

time: 170 us -> 146 us (0.86)
  the two profiles are of different devices: /device:TPU:1 before, /device:TPU:18 now
where the time goes in v1:
time: 146 us
  Pallas kernels  55.6 us (38%)
  waiting for transfers between devices  36.1 us (25%)
  starting transfers between devices  34.1 us (23%)
  local copies, waits for them, and re-layouts  15.8 us (11%)
  other arithmetic  3.1 us (2%)
    ppermute x16, waiting for transfers between devices, far_move(): return lax.ppermute(v, axis, pairs)  25.3 us
    pallas_call x4, Pallas kernels, block_product(): pl.pallas_call(body, in_specs=[smem] * 3 + [vmem] * (n_in + 1), out_specs...  21.6 us
    ppermute x22, starting transfers between devices, near_move(): return lax.ppermute(v, axis, [(i, i ^ 1) for i in range(count)])  18.5 us
    pallas_call x2, Pallas kernels, block_grads(): pl.pallas_call(body, grid_spec=pltpu.PrefetchScalarGridSpec(num_scalar_pr...  17.5 us
    pallas_call x2, Pallas kernels, pair_tables(): pl.pallas_call(body, in_specs=[smem] * n + [pl.BlockSpec(memory_space=plt...  16.5 us
    unnamed x28, local copies, waits for them, and re-layouts  15.6 us
    ppermute x16, starting transfers between devices, far_move(): return lax.ppermute(v, axis, pairs)  15.6 us
    ppermute x22, waiting for transfers between devices, near_move(): return lax.ppermute(v, axis, [(i, i ^ 1) for i in range(count)])  10.8 us
  transfers between devices with their start and end apart: 38, of which 12 were waited for; matrix products, arithmetic and copies ran while one was open for 2% of the time, Pallas kernels for 31%

profile of v1, /device:TPU:18, one launch (start us, length us, event | category | flops | bytes accessed | tf_op | source)
XLA Modules:
  0.0 145.8 jit_solution(16117211037660038684)
XLA Ops:
  0.6 0.6 collective-permute-start.3
  1.2 0.4 collective-permute-start.2
  1.7 3.5 %collective-permute-start.1 = (bf16[16,3072]{1,0:T(8,128)(2,1)}, bf16[16,3072]{1,0:T(8,128)(2,1)S(1)}, u32[]{:S(2)}, u32[]{:S(2)}) collective-permute-start(bf16[16,3072]{1,0:T(8,128)(2,1)} %refs_0_.4), channel_id=1, source_target_pairs={{0,4},{1,5},{2,6},{3,7},{4,0},{5,1},{6,2},{7,3},{8,12},{9,13},{10,... | collective-permute-start | bytes 294920 | tf_op jit(solution)/shard_map/ppermute | solution.py:290
  5.4 0.7 reduce.refs_2_.refs_0_
  6.1 3.7 %copy-done.2 = bf16[1,1,288,128,128]{4,3,2,1,0:T(8,128)(2,1)S(1)} copy-done((bf16[1,1,288,128,128]{4,3,2,1,0:T(8,128)(2,1)S(1)}, bf16[1,1,288,128,128]{4,3,2,1,0:T(8,128)(2,1)}, u32[]{:S(2)}) %copy-start.2) | copy-done | bytes 9437208
  9.8 6.1 %pair_tables.3.table_s = s32[520]{0:T(1024)S(1)} custom-call(s32[288]{0:T(512)S(1)} %reduce.refs_2_.refs_0_, bf16[288,128,128]{2,1,0:T(8,128)(2,1)S(1)} %bitcast.23), custom_call_target="tpu_custom_call" | custom-call | tf_op jit(solution)/shard_map/pair_tables/pallas_call | solution.py:103
  15.9 1.6 %collective-permute-start.6 = (bf16[16,3072]{1,0:T(8,128)(2,1)S(1)}, bf16[16,3072]{1,0:T(8,128)(2,1)S(1)}, u32[]{:S(2)}, u32[]{:S(2)}) collective-permute-start(bf16[16,3072]{1,0:T(8,128)(2,1)S(1)} %collective-permute-done.2.refs_6_), channel_id=1, source_target_pairs={{0,1},{1,0},{2,3},{3,2},{4,5},{5,4},{6,7},{7,6},{8,9},{9,8},{10,11... | collective-permute-start | bytes 294920 | tf_op jit(solution)/shard_map/ppermute | solution.py:285
  17.5 0.5 collective-permute-start.5
  18.0 1.5 %collective-permute-start.4 = (bf16[16,3072]{1,0:T(8,128)(2,1)S(1)}, bf16[16,3072]{1,0:T(8,128)(2,1)S(1)}, u32[]{:S(2)}, u32[]{:S(2)}) collective-permute-start(bf16[16,3072]{1,0:T(8,128)(2,1)S(1)} %collective-permute-done.refs_2_), channel_id=1, source_target_pairs={{0,1},{1,0},{2,3},{3,2},{4,5},{5,4},{6,7},{7,6},{8,9},{9,8},{10,11... | collective-permute-start | bytes 294920 | tf_op jit(solution)/shard_map/ppermute | solution.py:285
  19.6 2.1 %collective-permute-done.6.refs_7_ = bf16[16,3072]{1,0:T(8,128)(2,1)S(1)} collective-permute-done((bf16[16,3072]{1,0:T(8,128)(2,1)S(1)}, bf16[16,3072]{1,0:T(8,128)(2,1)S(1)}, u32[]{:S(2)}, u32[]{:S(2)}) %collective-permute-start.6) | collective-permute-done | bytes 98336 | tf_op jit(solution)/shard_map/ppermute | solution.py:285
  21.6 1.3 collective-permute-done.5.refs_5_
  23.0 1.1 collective-permute-done.4.refs_3_
  24.0 3.7 %copy-done.3 = bf16[1,1,288,128,128]{4,3,2,1,0:T(8,128)(2,1)S(1)} copy-done((bf16[1,1,288,128,128]{4,3,2,1,0:T(8,128)(2,1)S(1)}, bf16[1,1,288,128,128]{4,3,2,1,0:T(8,128)(2,1)}, u32[]{:S(2)}) %copy-start.3) | copy-done | bytes 9437208
  27.7 0.9 copy-done.5
  28.6 5.3 %block_product.4 = (bf16[2,32,3072]{2,1,0:T(8,128)(2,1)S(1)}, bf16[2,32,3072]{2,1,0:T(8,128)(2,1)S(1)}) custom-call(s32[520]{0:T(1024)S(1)} %pair_tables.3.table_s, s32[1]{0:T(128)} %constant.92.clone.1.in_s.out_s.right_s.left_s, s32[4]{0:T(128)S(1)} %pad_add_fusion.out_s, bf16[16,3072]{1,0:T(8,128)(2,1)S(1)} %copy-done.5, ...), custom_call_target="tpu_custom_call" | custom-call | flops 1207959552 | bytes 11010048 | tf_op jit(solution)/shard_map/block_product/pallas_call | solution.py:178
  34.2 1.9 %collective-permute-start.13 = (bf16[16,3072]{1,0:T(8,128)(2,1)S(1)}, bf16[16,3072]{1,0:T(8,128)(2,1)S(1)}, u32[]{:S(2)}, u32[]{:S(2)}) collective-permute-start(bf16[16,3072]{1,0:T(8,128)(2,1)S(1)} %copy-done.4), channel_id=1, source_target_pairs={{0,2},{1,3},{2,4},{3,5},{4,6},{5,7},{6,0},{7,1},{8,10},{9,11},{10,... | collective-permute-start | bytes 294920 | tf_op jit(solution)/shard_map/ppermute | solution.py:290
  36.2 3.2 %collective-permute-start.12 = (bf16[16,3072]{1,0:T(8,128)(2,1)S(1)}, bf16[16,3072]{1,0:T(8,128)(2,1)S(1)}, u32[]{:S(2)}, u32[]{:S(2)}) collective-permute-start(bf16[16,3072]{1,0:T(8,128)(2,1)S(1)} %copy-done.4), channel_id=1, source_target_pairs={{0,1},{1,0},{2,3},{3,2},{4,5},{5,4},{6,7},{7,6},{8,9},{9,8},{10,11... | collective-permute-start | bytes 294920 | tf_op jit(solution)/shard_map/ppermute | solution.py:285
  39.4 3.7 %copy-done = bf16[1,1,288,128,128]{4,3,2,1,0:T(8,128)(2,1)S(1)} copy-done((bf16[1,1,288,128,128]{4,3,2,1,0:T(8,128)(2,1)S(1)}, bf16[1,1,288,128,128]{4,3,2,1,0:T(8,128)(2,1)}, u32[]{:S(2)}) %copy-start) | copy-done | bytes 9437208
  43.0 10.4 %pair_tables.2 = (s32[520]{0:T(1024)S(1)}, s32[520]{0:T(1024)S(1)}, s32[520]{0:T(1024)S(1)}) custom-call(s32[288]{0:T(512)S(1)} %reduce.1.refs_0_.refs_1_, s32[288]{0:T(512)S(1)} %reduce.1.refs_0_.refs_1_, s32[288]{0:T(512)S(1)} %reduce.refs_2_.refs_0_, bf16[288,128,128]{2,1,0:T(8,128)(2,1)S(1)} %bitcast.18), custom_call_target="tpu_custom_call" | custom-call | tf_op jit(solution)/shard_map/pair_tables/pallas_call | solution.py:103
  53.6 2.0 %collective-permute-start.16 = (bf16[16,3072]{1,0:T(8,128)(2,1)S(1)}, bf16[16,3072]{1,0:T(8,128)(2,1)S(1)}, u32[]{:S(2)}, u32[]{:S(2)}) collective-permute-start(bf16[16,3072]{1,0:T(8,128)(2,1)S(1)} %collective-permute-done.15.refs_4_.refs_8_), channel_id=1, source_target_pairs={{0,1},{1,0},{2,3},{3,2},{4,5},{5,4},{6,7},{7,6},{8,9},{9,8},{10,11... | collective-permute-start | bytes 294920 | tf_op jit(solution)/shard_map/ppermute | solution.py:285
  55.7 3.5 %collective-permute-done.18.refs_7_.refs_11_ = bf16[16,3072]{1,0:T(8,128)(2,1)S(1)} collective-permute-done((bf16[16,3072]{1,0:T(8,128)(2,1)S(1)}, bf16[16,3072]{1,0:T(8,128)(2,1)S(1)}, u32[]{:S(2)}, u32[]{:S(2)}) %collective-permute-start.18) | collective-permute-done | bytes 98336 | tf_op jit(solution)/shard_map/ppermute | solution.py:285
  59.2 1.8 %collective-permute-done.16.refs_5_.refs_9_ = bf16[16,3072]{1,0:T(8,128)(2,1)S(1)} collective-permute-done((bf16[16,3072]{1,0:T(8,128)(2,1)S(1)}, bf16[16,3072]{1,0:T(8,128)(2,1)S(1)}, u32[]{:S(2)}, u32[]{:S(2)}) %collective-permute-start.16) | collective-permute-done | bytes 98336 | tf_op jit(solution)/shard_map/ppermute | solution.py:285
  61.0 1.1 collective-permute-done.14.refs_3_.refs_7_
  62.0 3.7 %copy-done.1 = bf16[1,1,288,128,128]{4,3,2,1,0:T(8,128)(2,1)S(1)} copy-done((bf16[1,1,288,128,128]{4,3,2,1,0:T(8,128)(2,1)S(1)}, bf16[1,1,288,128,128]{4,3,2,1,0:T(8,128)(2,1)}, u32[]{:S(2)}) %copy-start.1) | copy-done | bytes 9437208
  65.7 5.4 %block_product.5 = (bf16[2,32,3072]{2,1,0:T(8,128)(2,1)S(1)}, bf16[2,32,3072]{2,1,0:T(8,128)(2,1)S(1)}) custom-call(s32[520]{0:T(1024)S(1)} %get-tuple-element.68.table_s, s32[1]{0:T(128)} %constant.92.clone.1.in_s.out_s.right_s.left_s, s32[4]{0:T(128)S(1)} %pad_add_fusion.out_s, bf16[16,3072]{1,0:T(8,128)(2,1)S(1)} %copy-done.4, ...), custom_call_target="tpu_custom_call" | custom-call | flops 1207959552 | bytes 11010048 | tf_op jit(solution)/shard_map/block_product/pallas_call | solution.py:178
  71.3 7.2 %collective-permute-done.8 = bf16[32,3072]{1,0:T(8,128)(2,1)S(1)} collective-permute-done((bf16[32,3072]{1,0:T(8,128)(2,1)S(1)}, bf16[32,3072]{1,0:T(8,128)(2,1)S(1)}, u32[]{:S(2)}, u32[]{:S(2)}) %collective-permute-start.8) | collective-permute-done | bytes 196640 | tf_op jit(solution)/shard_map/ppermute | solution.py:290
  79.1 1.8 %collective-permute-start.10 = (bf16[32,3072]{1,0:T(8,128)(2,1)S(1)}, bf16[32,3072]{1,0:T(8,128)(2,1)S(1)}, u32[]{:S(2)}, u32[]{:S(2)}) collective-permute-start(bf16[32,3072]{1,0:T(8,128)(2,1)S(1)} %multiply_convert_fusion.refs_0_), channel_id=1, source_target_pairs={{0,16},{8,24},{16,0},{24,8},{1,17},{9,25},{17,1},{25,9},{2,18},{10... | collective-permute-start | bytes 589832 | tf_op jit(solution)/shard_map/ppermute | solution.py:290
  80.9 5.5 %collective-permute-done.20 = bf16[32,3072]{1,0:T(8,128)(2,1)S(1)} collective-permute-done((bf16[32,3072]{1,0:T(8,128)(2,1)S(1)}, bf16[32,3072]{1,0:T(8,128)(2,1)S(1)}, u32[]{:S(2)}, u32[]{:S(2)}) %collective-permute-start.20) | collective-permute-done | bytes 196640 | tf_op jit(solution)/shard_map/ppermute | solution.py:290
  86.4 0.4 fusion.6.refs_0_.refs_8_
  87.2 3.4 %collective-permute-done.10.refs_2_ = bf16[32,3072]{1,0:T(8,128)(2,1)S(1)} collective-permute-done((bf16[32,3072]{1,0:T(8,128)(2,1)S(1)}, bf16[32,3072]{1,0:T(8,128)(2,1)S(1)}, u32[]{:S(2)}, u32[]{:S(2)}) %collective-permute-start.10) | collective-permute-done | bytes 196640 | tf_op jit(solution)/shard_map/ppermute | solution.py:290
  90.6 0.5 collective-permute-start.25
  91.1 2.3 %collective-permute-done.26.refs_2_.refs_10_ = bf16[32,3072]{1,0:T(8,128)(2,1)S(1)} collective-permute-done((bf16[32,3072]{1,0:T(8,128)(2,1)S(1)}, bf16[32,3072]{1,0:T(8,128)(2,1)S(1)}, u32[]{:S(2)}, u32[]{:S(2)}) %collective-permute-start.26) | collective-permute-done | bytes 196640 | tf_op jit(solution)/shard_map/ppermute | solution.py:290
  93.5 5.3 %block_product.6 = (bf16[16,3072]{1,0:T(8,128)(2,1)S(1)}, bf16[16,3072]{1,0:T(8,128)(2,1)S(1)}, bf16[16,3072]{1,0:T(8,128)(2,1)S(1)}, bf16[16,3072]{1,0:T(8,128)...) custom-call(s32[520]{0:T(1024)S(1)} %get-tuple-element.65.table_s, ...), custom_call_target="tpu_custom_call" | custom-call | flops 1207959552 | bytes 11010048 | tf_op jit(solution)/shard_map/block_product/pallas_call | solution.py:178
  99.0 2.0 %collective-permute-start.22 = (bf16[16,3072]{1,0:T(8,128)(2,1)S(1)}, bf16[16,3072]{1,0:T(8,128)(2,1)S(1)}, u32[]{:S(2)}, u32[]{:S(2)}) collective-permute-start(bf16[16,3072]{1,0:T(8,128)(2,1)S(1)} %get-tuple-element.87), channel_id=1, source_target_pairs={{0,1},{1,0},{2,3},{3,2},{4,5},{5,4},{6,7},{7,6},{8,9},{9,8},{10,11... | collective-permute-start | bytes 294920 | tf_op jit(solution)/shard_map/ppermute | solution.py:285
  101.1 1.9 %collective-permute-start.24 = (bf16[16,3072]{1,0:T(8,128)(2,1)S(1)}, bf16[16,3072]{1,0:T(8,128)(2,1)S(1)}, u32[]{:S(2)}, u32[]{:S(2)}) collective-permute-start(bf16[16,3072]{1,0:T(8,128)(2,1)S(1)} %get-tuple-element.89), channel_id=1, source_target_pairs={{0,1},{1,0},{2,3},{3,2},{4,5},{5,4},{6,7},{7,6},{8,9},{9,8},{10,11... | collective-permute-start | bytes 294920 | tf_op jit(solution)/shard_map/ppermute | solution.py:285
  103.1 5.5 %block_product.7 = (bf16[16,3072]{1,0:T(8,128)(2,1)S(1)}, bf16[16,3072]{1,0:T(8,128)(2,1)S(1)}, bf16[16,3072]{1,0:T(8,128)(2,1)S(1)}, bf16[16,3072]{1,0:T(8,128)...) custom-call(s32[520]{0:T(1024)S(1)} %get-tuple-element.90.table_s, ...), custom_call_target="tpu_custom_call" | custom-call | flops 1207959552 | bytes 11010048 | tf_op jit(solution)/shard_map/block_product/pallas_call | solution.py:178
  108.6 2.0 %collective-permute-start.32 = (bf16[16,3072]{1,0:T(8,128)(2,1)S(1)}, bf16[16,3072]{1,0:T(8,128)(2,1)S(1)}, u32[]{:S(2)}, u32[]{:S(2)}) collective-permute-start(bf16[16,3072]{1,0:T(8,128)(2,1)S(1)} %get-tuple-element.101), channel_id=1, source_target_pairs={{0,1},{1,0},{2,3},{3,2},{4,5},{5,4},{6,7},{7,6},{8,9},{9,8},{10,11... | collective-permute-start | bytes 294920 | tf_op jit(solution)/shard_map/ppermute | solution.py:285
  110.7 1.9 %collective-permute-start.34 = (bf16[16,3072]{1,0:T(8,128)(2,1)S(1)}, bf16[16,3072]{1,0:T(8,128)(2,1)S(1)}, u32[]{:S(2)}, u32[]{:S(2)}) collective-permute-start(bf16[16,3072]{1,0:T(8,128)(2,1)S(1)} %get-tuple-element.105), channel_id=1, source_target_pairs={{0,1},{1,0},{2,3},{3,2},{4,5},{5,4},{6,7},{7,6},{8,9},{9,8},{10,11... | collective-permute-start | bytes 294920 | tf_op jit(solution)/shard_map/ppermute | solution.py:285
  112.8 8.8 %block_grads.2 = f32[288,128,128]{2,1,0:T(8,128)} custom-call(s32[288]{0:T(512)S(1)} %get-tuple-element.125.row_s, s32[288]{0:T(512)S(1)} %get-tuple-element.124.col_s, s32[4]{0:T(128)S(1)} %fusion.16.in_s.left_s.right_s, s32[1]{0:T(128)} %constant.92.clone.1.in_s.out_s.right_s.left_s, bf16[32,3072]{1,0:T(8,128)(2,1)S(1)} %multiply_convert_fusion.refs_0_, ...), custom_call_target="tpu_custom_call" | custom-call | flops 1207959552 | bytes 20447232 | tf_op jit(solution)/shard_map/block_grads/pallas_call | solution.py:242
  121.7 1.2 collective-permute-start.29
  122.9 0.9 collective-permute-start.30
  123.9 1.5 %collective-permute-start.35 = (bf16[16,3072]{1,0:T(8,128)(2,1)S(1)}, bf16[16,3072]{1,0:T(8,128)(2,1)S(1)}, u32[]{:S(2)}, u32[]{:S(2)}) collective-permute-start(bf16[16,3072]{1,0:T(8,128)(2,1)S(1)} %add_convert_fusion.5), channel_id=1, source_target_pairs={{0,6},{1,7},{2,0},{3,1},{4,2},{5,3},{6,4},{7,5},{8,14},{9,15},{10,... | collective-permute-start | bytes 294920 | tf_op jit(solution)/shard_map/ppermute | solution.py:290
  125.3 3.3 %collective-permute-start.36 = (bf16[16,3072]{1,0:T(8,128)(2,1)S(1)}, bf16[16,3072]{1,0:T(8,128)(2,1)S(1)}, u32[]{:S(2)}, u32[]{:S(2)}) collective-permute-start(bf16[16,3072]{1,0:T(8,128)(2,1)S(1)} %add_convert_fusion.4), channel_id=1, source_target_pairs={{0,4},{1,5},{2,6},{3,7},{4,0},{5,1},{6,2},{7,3},{8,12},{9,13},{10,... | collective-permute-start | bytes 294920 | tf_op jit(solution)/shard_map/ppermute | solution.py:290
  128.8 0.4 collective-permute-done.29
  129.2 6.5 %collective-permute-done.30 = bf16[16,3072]{1,0:T(8,128)(2,1)S(1)} collective-permute-done((bf16[16,3072]{1,0:T(8,128)(2,1)S(1)}, bf16[16,3072]{1,0:T(8,128)(2,1)S(1)}, u32[]{:S(2)}, u32[]{:S(2)}) %collective-permute-start.30) | collective-permute-done | bytes 98336 | tf_op jit(solution)/shard_map/ppermute | solution.py:290
  135.7 0.7 add_convert_fusion.6
  136.4 8.7 %block_grads.3 = f32[288,128,128]{2,1,0:T(8,128)} custom-call(s32[288]{0:T(512)S(1)} %get-tuple-element.123.row_s, s32[288]{0:T(512)S(1)} %get-tuple-element.122.col_s, s32[1]{0:T(128)} %constant.92.clone.1.in_s.out_s.right_s.left_s, s32[4]{0:T(128)S(1)} %fusion.16.in_s.left_s.right_s, bf16[16,3072]{1,0:T(8,128)(2,1)S(1)} %copy-done.6, ...), custom_call_target="tpu_custom_call" | custom-call | flops 1207959552 | bytes 20447232 | tf_op jit(solution)/shard_map/block_grads/pallas_call | solution.py:242
  145.1 0.7 add_convert_fusion.2
  (86 shorter events, 2.8 us)
Async XLA Ops:
  0.6 35.5 %copy-start.7 = (s32[1,1,288]{2,1,0:T(1,128)S(1)}, s32[1,1,288]{2,1,0:T(1,128)}, u32[]{:S(2)}) copy-start(s32[1,1,288]{2,1,0:T(1,128)} %param.10) | copy-start | bytes 3460
  0.6 18.9 %collective-permute-start.3 = (bf16[16,3072]{1,0:T(8,128)(2,1)}, bf16[16,3072]{1,0:T(8,128)(2,1)S(1)}, u32[]{:S(2)}, u32[]{:S(2)}) collective-permute-start(bf16[16,3072]{1,0:T(8,128)(2,1)} %refs_0_.4), channel_id=1, source_target_pairs={{0,1},{1,0},{2,3},{3,2},{4,5},{5,4},{6,7},{7,6},{8,9},{9,8},{10,11... | collective-permute-start | bytes 294920 | tf_op jit(solution)/shard_map/ppermute | solution.py:285
  1.2 14.7 %collective-permute-start.2 = (bf16[16,3072]{1,0:T(8,128)(2,1)}, bf16[16,3072]{1,0:T(8,128)(2,1)S(1)}, u32[]{:S(2)}, u32[]{:S(2)}) collective-permute-start(bf16[16,3072]{1,0:T(8,128)(2,1)} %refs_0_.4), channel_id=1, source_target_pairs={{0,6},{1,7},{2,0},{3,1},{4,2},{5,3},{6,4},{7,5},{8,14},{9,15},{10,... | collective-permute-start | bytes 294920 | tf_op jit(solution)/shard_map/ppermute | solution.py:290
  1.7 15.8 %collective-permute-start.1 = (bf16[16,3072]{1,0:T(8,128)(2,1)}, bf16[16,3072]{1,0:T(8,128)(2,1)S(1)}, u32[]{:S(2)}, u32[]{:S(2)}) collective-permute-start(bf16[16,3072]{1,0:T(8,128)(2,1)} %refs_0_.4), channel_id=1, source_target_pairs={{0,4},{1,5},{2,6},{3,7},{4,0},{5,1},{6,2},{7,3},{8,12},{9,13},{10,... | collective-permute-start | bytes 294920 | tf_op jit(solution)/shard_map/ppermute | solution.py:290
  5.2 12.8 %collective-permute-start = (bf16[16,3072]{1,0:T(8,128)(2,1)}, bf16[16,3072]{1,0:T(8,128)(2,1)S(1)}, u32[]{:S(2)}, u32[]{:S(2)}) collective-permute-start(bf16[16,3072]{1,0:T(8,128)(2,1)} %refs_0_.4), channel_id=1, source_target_pairs={{0,2},{1,3},{2,4},{3,5},{4,6},{5,7},{6,0},{7,1},{8,10},{9,11},{10,... | collective-permute-start | bytes 294920 | tf_op jit(solution)/shard_map/ppermute | solution.py:290
  6.1 3.7 %copy-start.2 = (bf16[1,1,288,128,128]{4,3,2,1,0:T(8,128)(2,1)S(1)}, bf16[1,1,288,128,128]{4,3,2,1,0:T(8,128)(2,1)}, u32[]{:S(2)}) copy-start(bf16[1,1,288,128,128]{4,3,2,1,0:T(8,128)(2,1)} %param.7) | copy-start | bytes 28311556
  9.8 24.3 %copy-start.4 = (bf16[16,3072]{1,0:T(8,128)(2,1)S(1)}, bf16[16,3072]{1,0:T(8,128)(2,1)}, u32[]{:S(2)}) copy-start(bf16[16,3072]{1,0:T(8,128)(2,1)} %refs_4_) | copy-start | bytes 294916
  15.9 77.6 %slice-start = ((s8[9437184]{0:T(1024)(128)(4,1)}), s8[1048576]{0:T(1024)(128)(4,1)S(1)}, s32[]{:S(2)}) async-start(s8[9437184]{0:T(1024)(128)(4,1)} %bitcast.20), calls=%async_computation | async-start | bytes 2097152
  15.9 5.7 %collective-permute-start.6 = (bf16[16,3072]{1,0:T(8,128)(2,1)S(1)}, bf16[16,3072]{1,0:T(8,128)(2,1)S(1)}, u32[]{:S(2)}, u32[]{:S(2)}) collective-permute-start(bf16[16,3072]{1,0:T(8,128)(2,1)S(1)} %collective-permute-done.2.refs_6_), channel_id=1, source_target_pairs={{0,1},{1,0},{2,3},{3,2},{4,5},{5,4},{6,7},{7,6},{8,9},{9,8},{10,11... | collective-permute-start | bytes 294920 | tf_op jit(solution)/shard_map/ppermute | solution.py:285
  17.5 5.5 %collective-permute-start.5 = (bf16[16,3072]{1,0:T(8,128)(2,1)S(1)}, bf16[16,3072]{1,0:T(8,128)(2,1)S(1)}, u32[]{:S(2)}, u32[]{:S(2)}) collective-permute-start(bf16[16,3072]{1,0:T(8,128)(2,1)S(1)} %collective-permute-done.1.refs_4_), channel_id=1, source_target_pairs={{0,1},{1,0},{2,3},{3,2},{4,5},{5,4},{6,7},{7,6},{8,9},{9,8},{10,11... | collective-permute-start | bytes 294920 | tf_op jit(solution)/shard_map/ppermute | solution.py:285
  18.0 6.0 %collective-permute-start.4 = (bf16[16,3072]{1,0:T(8,128)(2,1)S(1)}, bf16[16,3072]{1,0:T(8,128)(2,1)S(1)}, u32[]{:S(2)}, u32[]{:S(2)}) collective-permute-start(bf16[16,3072]{1,0:T(8,128)(2,1)S(1)} %collective-permute-done.refs_2_), channel_id=1, source_target_pairs={{0,1},{1,0},{2,3},{3,2},{4,5},{5,4},{6,7},{7,6},{8,9},{9,8},{10,11... | collective-permute-start | bytes 294920 | tf_op jit(solution)/shard_map/ppermute | solution.py:285
  34.0 21.7 %collective-permute-start.7 = (bf16[2,32,3072]{2,1,0:T(8,128)(2,1)S(1)}, bf16[2,32,3072]{2,1,0:T(8,128)(2,1)S(1)}, u32[]{:S(2)}, u32[]{:S(2)}) collective-permute-start(bf16[2,32,3072]{2,1,0:T(8,128)(2,1)S(1)} %get-tuple-element.67), channel_id=1, source_target_pairs={{0,8},{8,0},{16,24},{24,16},{1,9},{9,1},{17,25},{25,17},{2,10},{10... | collective-permute-start | bytes 1179656 | tf_op jit(solution)/shard_map/ppermute | solution.py:285
  34.0 19.4 %collective-permute-start.17 = (bf16[16,3072]{1,0:T(8,128)(2,1)S(1)}, bf16[16,3072]{1,0:T(8,128)(2,1)S(1)}, u32[]{:S(2)}, u32[]{:S(2)}) collective-permute-start(bf16[16,3072]{1,0:T(8,128)(2,1)S(1)} %copy-done.4), channel_id=1, source_target_pairs={{0,6},{1,7},{2,0},{3,1},{4,2},{5,3},{6,4},{7,5},{8,14},{9,15},{10,... | collective-permute-start | bytes 294920 | tf_op jit(solution)/shard_map/ppermute | solution.py:290
  34.1 19.4 %collective-permute-start.15 = (bf16[16,3072]{1,0:T(8,128)(2,1)S(1)}, bf16[16,3072]{1,0:T(8,128)(2,1)S(1)}, u32[]{:S(2)}, u32[]{:S(2)}) collective-permute-start(bf16[16,3072]{1,0:T(8,128)(2,1)S(1)} %copy-done.4), channel_id=1, source_target_pairs={{0,4},{1,5},{2,6},{3,7},{4,0},{5,1},{6,2},{7,3},{8,12},{9,13},{10,... | collective-permute-start | bytes 294920 | tf_op jit(solution)/shard_map/ppermute | solution.py:290
  34.2 21.4 %collective-permute-start.13 = (bf16[16,3072]{1,0:T(8,128)(2,1)S(1)}, bf16[16,3072]{1,0:T(8,128)(2,1)S(1)}, u32[]{:S(2)}, u32[]{:S(2)}) collective-permute-start(bf16[16,3072]{1,0:T(8,128)(2,1)S(1)} %copy-done.4), channel_id=1, source_target_pairs={{0,2},{1,3},{2,4},{3,5},{4,6},{5,7},{6,0},{7,1},{8,10},{9,11},{10,... | collective-permute-start | bytes 294920 | tf_op jit(solution)/shard_map/ppermute | solution.py:290
  36.2 19.6 %collective-permute-start.12 = (bf16[16,3072]{1,0:T(8,128)(2,1)S(1)}, bf16[16,3072]{1,0:T(8,128)(2,1)S(1)}, u32[]{:S(2)}, u32[]{:S(2)}) collective-permute-start(bf16[16,3072]{1,0:T(8,128)(2,1)S(1)} %copy-done.4), channel_id=1, source_target_pairs={{0,1},{1,0},{2,3},{3,2},{4,5},{5,4},{6,7},{7,6},{8,9},{9,8},{10,11... | collective-permute-start | bytes 294920 | tf_op jit(solution)/shard_map/ppermute | solution.py:285
  43.0 50.5 %slice-start.1 = ((s8[9437184]{0:T(1024)(128)(4,1)}), s8[4194304]{0:T(1024)(128)(4,1)S(1)}, s32[]{:S(2)}) async-start(s8[9437184]{0:T(1024)(128)(4,1)} %bitcast.20), calls=%async_computation.1 | async-start | bytes 8388608
  53.5 5.7 %collective-permute-start.18 = (bf16[16,3072]{1,0:T(8,128)(2,1)S(1)}, bf16[16,3072]{1,0:T(8,128)(2,1)S(1)}, u32[]{:S(2)}, u32[]{:S(2)}) collective-permute-start(bf16[16,3072]{1,0:T(8,128)(2,1)S(1)} %collective-permute-done.17.refs_6_.refs_10_), channel_id=1, source_target_pairs={{0,1},{1,0},{2,3},{3,2},{4,5},{5,4},{6,7},{7,6},{8,9},{9,8},{10,11... | collective-permute-start | bytes 294920 | tf_op jit(solution)/shard_map/ppermute | solution.py:285
  53.6 7.4 %collective-permute-start.16 = (bf16[16,3072]{1,0:T(8,128)(2,1)S(1)}, bf16[16,3072]{1,0:T(8,128)(2,1)S(1)}, u32[]{:S(2)}, u32[]{:S(2)}) collective-permute-start(bf16[16,3072]{1,0:T(8,128)(2,1)S(1)} %collective-permute-done.15.refs_4_.refs_8_), channel_id=1, source_target_pairs={{0,1},{1,0},{2,3},{3,2},{4,5},{5,4},{6,7},{7,6},{8,9},{9,8},{10,11... | collective-permute-start | bytes 294920 | tf_op jit(solution)/shard_map/ppermute | solution.py:285
  55.6 6.5 %collective-permute-start.14 = (bf16[16,3072]{1,0:T(8,128)(2,1)S(1)}, bf16[16,3072]{1,0:T(8,128)(2,1)S(1)}, u32[]{:S(2)}, u32[]{:S(2)}) collective-permute-start(bf16[16,3072]{1,0:T(8,128)(2,1)S(1)} %collective-permute-done.13.refs_2_.refs_6_), channel_id=1, source_target_pairs={{0,1},{1,0},{2,3},{3,2},{4,5},{5,4},{6,7},{7,6},{8,9},{9,8},{10,11... | collective-permute-start | bytes 294920 | tf_op jit(solution)/shard_map/ppermute | solution.py:285
  65.7 27.8 %slice-start.2 = ((s8[9437184]{0:T(1024)(128)(4,1)}), s8[4194304]{0:T(1024)(128)(4,1)S(1)}, s32[]{:S(2)}) async-start(s8[9437184]{0:T(1024)(128)(4,1)} %bitcast.20), calls=%async_computation.2 | async-start | bytes 8388608
  65.7 37.3 %slice-start.3 = ((s8[9437184]{0:T(1024)(128)(4,1)}), s8[4194304]{0:T(1024)(128)(4,1)S(1)}, s32[]{:S(2)}) async-start(s8[9437184]{0:T(1024)(128)(4,1)} %bitcast.25), calls=%async_computation.3 | async-start | bytes 8388608
  65.7 37.3 %slice-start.4 = ((s8[9437184]{0:T(1024)(128)(4,1)}), s8[4194304]{0:T(1024)(128)(4,1)S(1)}, s32[]{:S(2)}) async-start(s8[9437184]{0:T(1024)(128)(4,1)} %bitcast.25), calls=%async_computation.4 | async-start | bytes 8388608
  71.1 7.4 %collective-permute-start.19 = (bf16[2,32,3072]{2,1,0:T(8,128)(2,1)S(1)}, bf16[2,32,3072]{2,1,0:T(8,128)(2,1)S(1)}, u32[]{:S(2)}, u32[]{:S(2)}) collective-permute-start(bf16[2,32,3072]{2,1,0:T(8,128)(2,1)S(1)} %get-tuple-element.79), channel_id=1, source_target_pairs={{0,8},{8,0},{16,24},{24,16},{1,9},{9,1},{17,25},{25,17},{2,10},{10... | collective-permute-start | bytes 1179656 | tf_op jit(solution)/shard_map/ppermute | solution.py:285
  71.2 7.3 %collective-permute-start.8 = (bf16[32,3072]{1,0:T(8,128)(2,1)S(1)}, bf16[32,3072]{1,0:T(8,128)(2,1)S(1)}, u32[]{:S(2)}, u32[]{:S(2)}) collective-permute-start(bf16[32,3072]{1,0:T(8,128)(2,1)S(1)} %fusion.7), channel_id=1, source_target_pairs={{0,16},{8,24},{16,0},{24,8},{1,17},{9,25},{17,1},{25,9},{2,18},{10... | collective-permute-start | bytes 589832 | tf_op jit(solution)/shard_map/ppermute | solution.py:290
  78.6 7.8 %collective-permute-start.20 = (bf16[32,3072]{1,0:T(8,128)(2,1)S(1)}, bf16[32,3072]{1,0:T(8,128)(2,1)S(1)}, u32[]{:S(2)}, u32[]{:S(2)}) collective-permute-start(bf16[32,3072]{1,0:T(8,128)(2,1)S(1)} %fusion.8), channel_id=1, source_target_pairs={{0,16},{8,24},{16,0},{24,8},{1,17},{9,25},{17,1},{25,9},{2,18},{10... | collective-permute-start | bytes 589832 | tf_op jit(solution)/shard_map/ppermute | solution.py:290
  79.1 11.5 %collective-permute-start.10 = (bf16[32,3072]{1,0:T(8,128)(2,1)S(1)}, bf16[32,3072]{1,0:T(8,128)(2,1)S(1)}, u32[]{:S(2)}, u32[]{:S(2)}) collective-permute-start(bf16[32,3072]{1,0:T(8,128)(2,1)S(1)} %multiply_convert_fusion.refs_0_), channel_id=1, source_target_pairs={{0,16},{8,24},{16,0},{24,8},{1,17},{9,25},{17,1},{25,9},{2,18},{10... | collective-permute-start | bytes 589832 | tf_op jit(solution)/shard_map/ppermute | solution.py:290
  86.8 6.6 %collective-permute-start.26 = (bf16[32,3072]{1,0:T(8,128)(2,1)S(1)}, bf16[32,3072]{1,0:T(8,128)(2,1)S(1)}, u32[]{:S(2)}, u32[]{:S(2)}) collective-permute-start(bf16[32,3072]{1,0:T(8,128)(2,1)S(1)} %fusion.6.refs_0_.refs_8_), channel_id=1, source_target_pairs={{0,16},{8,24},{16,0},{24,8},{1,17},{9,25},{17,1},{25,9},{2,18},{10... | collective-permute-start | bytes 589832 | tf_op jit(solution)/shard_map/ppermute | solution.py:290
  87.2 6.3 %collective-permute-start.9 = (bf16[32,3072]{1,0:T(8,128)(2,1)S(1)}, bf16[32,3072]{1,0:T(8,128)(2,1)S(1)}, u32[]{:S(2)}, u32[]{:S(2)}) collective-permute-start(bf16[32,3072]{1,0:T(8,128)(2,1)S(1)} %multiply_convert_fusion.refs_0_), channel_id=1, source_target_pairs={{0,8},{8,0},{16,24},{24,16},{1,9},{9,1},{17,25},{25,17},{2,10},{10... | collective-permute-start | bytes 589832 | tf_op jit(solution)/shard_map/ppermute | solution.py:285
  90.6 2.9 %collective-permute-start.11 = (bf16[32,3072]{1,0:T(8,128)(2,1)S(1)}, bf16[32,3072]{1,0:T(8,128)(2,1)S(1)}, u32[]{:S(2)}, u32[]{:S(2)}) collective-permute-start(bf16[32,3072]{1,0:T(8,128)(2,1)S(1)} %collective-permute-done.10.refs_2_), channel_id=1, source_target_pairs={{0,8},{8,0},{16,24},{24,16},{1,9},{9,1},{17,25},{25,17},{2,10},{10... | collective-permute-start | bytes 589832 | tf_op jit(solution)/shard_map/ppermute | solution.py:285
  90.6 10.4 %collective-permute-start.25 = (bf16[32,3072]{1,0:T(8,128)(2,1)S(1)}, bf16[32,3072]{1,0:T(8,128)(2,1)S(1)}, u32[]{:S(2)}, u32[]{:S(2)}) collective-permute-start(bf16[32,3072]{1,0:T(8,128)(2,1)S(1)} %fusion.6.refs_0_.refs_8_), channel_id=1, source_target_pairs={{0,8},{8,0},{16,24},{24,16},{1,9},{9,1},{17,25},{25,17},{2,10},{10... | collective-permute-start | bytes 589832 | tf_op jit(solution)/shard_map/ppermute | solution.py:285
  93.4 9.6 %collective-permute-start.27 = (bf16[32,3072]{1,0:T(8,128)(2,1)S(1)}, bf16[32,3072]{1,0:T(8,128)(2,1)S(1)}, u32[]{:S(2)}, u32[]{:S(2)}) collective-permute-start(bf16[32,3072]{1,0:T(8,128)(2,1)S(1)} %collective-permute-done.26.refs_2_.refs_10_), channel_id=1, source_target_pairs={{0,8},{8,0},{16,24},{24,16},{1,9},{9,1},{17,25},{25,17},{2,10},{10... | collective-permute-start | bytes 589832 | tf_op jit(solution)/shard_map/ppermute | solution.py:285
  93.5 9.5 %slice-start.5 = ((s8[9437184]{0:T(1024)(128)(4,1)}), s8[1048576]{0:T(1024)(128)(4,1)S(1)}, s32[]{:S(2)}) async-start(s8[9437184]{0:T(1024)(128)(4,1)} %bitcast.25), calls=%async_computation.5 | async-start | bytes 2097152
  98.9 37.5 %copy-start.6 = (bf16[16,3072]{1,0:T(8,128)(2,1)S(1)}, bf16[16,3072]{1,0:T(8,128)(2,1)}, u32[]{:S(2)}) copy-start(bf16[16,3072]{1,0:T(8,128)(2,1)} %refs_0_.4) | copy-start | bytes 294916
  98.9 9.7 %collective-permute-start.21 = (bf16[16,3072]{1,0:T(8,128)(2,1)S(1)}, bf16[16,3072]{1,0:T(8,128)(2,1)S(1)}, u32[]{:S(2)}, u32[]{:S(2)}) collective-permute-start(bf16[16,3072]{1,0:T(8,128)(2,1)S(1)} %get-tuple-element.86), channel_id=1, source_target_pairs={{0,1},{1,0},{2,3},{3,2},{4,5},{5,4},{6,7},{7,6},{8,9},{9,8},{10,11... | collective-permute-start | bytes 294920 | tf_op jit(solution)/shard_map/ppermute | solution.py:285
  99.0 11.7 %collective-permute-start.22 = (bf16[16,3072]{1,0:T(8,128)(2,1)S(1)}, bf16[16,3072]{1,0:T(8,128)(2,1)S(1)}, u32[]{:S(2)}, u32[]{:S(2)}) collective-permute-start(bf16[16,3072]{1,0:T(8,128)(2,1)S(1)} %get-tuple-element.87), channel_id=1, source_target_pairs={{0,1},{1,0},{2,3},{3,2},{4,5},{5,4},{6,7},{7,6},{8,9},{9,8},{10,11... | collective-permute-start | bytes 294920 | tf_op jit(solution)/shard_map/ppermute | solution.py:285
  101.0 9.7 %collective-permute-start.23 = (bf16[16,3072]{1,0:T(8,128)(2,1)S(1)}, bf16[16,3072]{1,0:T(8,128)(2,1)S(1)}, u32[]{:S(2)}, u32[]{:S(2)}) collective-permute-start(bf16[16,3072]{1,0:T(8,128)(2,1)S(1)} %get-tuple-element.88), channel_id=1, source_target_pairs={{0,1},{1,0},{2,3},{3,2},{4,5},{5,4},{6,7},{7,6},{8,9},{9,8},{10,11... | collective-permute-start | bytes 294920 | tf_op jit(solution)/shard_map/ppermute | solution.py:285
  101.1 11.6 %collective-permute-start.24 = (bf16[16,3072]{1,0:T(8,128)(2,1)S(1)}, bf16[16,3072]{1,0:T(8,128)(2,1)S(1)}, u32[]{:S(2)}, u32[]{:S(2)}) collective-permute-start(bf16[16,3072]{1,0:T(8,128)(2,1)S(1)} %get-tuple-element.89), channel_id=1, source_target_pairs={{0,1},{1,0},{2,3},{3,2},{4,5},{5,4},{6,7},{7,6},{8,9},{9,8},{10,11... | collective-permute-start | bytes 294920 | tf_op jit(solution)/shard_map/ppermute | solution.py:285
  108.5 13.1 %collective-permute-start.31 = (bf16[16,3072]{1,0:T(8,128)(2,1)S(1)}, bf16[16,3072]{1,0:T(8,128)(2,1)S(1)}, u32[]{:S(2)}, u32[]{:S(2)}) collective-permute-start(bf16[16,3072]{1,0:T(8,128)(2,1)S(1)} %get-tuple-element.99), channel_id=1, source_target_pairs={{0,1},{1,0},{2,3},{3,2},{4,5},{5,4},{6,7},{7,6},{8,9},{9,8},{10,11... | collective-permute-start | bytes 294920 | tf_op jit(solution)/shard_map/ppermute | solution.py:285
  108.6 14.2 %collective-permute-start.32 = (bf16[16,3072]{1,0:T(8,128)(2,1)S(1)}, bf16[16,3072]{1,0:T(8,128)(2,1)S(1)}, u32[]{:S(2)}, u32[]{:S(2)}) collective-permute-start(bf16[16,3072]{1,0:T(8,128)(2,1)S(1)} %get-tuple-element.101), channel_id=1, source_target_pairs={{0,1},{1,0},{2,3},{3,2},{4,5},{5,4},{6,7},{7,6},{8,9},{9,8},{10,11... | collective-permute-start | bytes 294920 | tf_op jit(solution)/shard_map/ppermute | solution.py:285
  110.6 13.1 %collective-permute-start.33 = (bf16[16,3072]{1,0:T(8,128)(2,1)S(1)}, bf16[16,3072]{1,0:T(8,128)(2,1)S(1)}, u32[]{:S(2)}, u32[]{:S(2)}) collective-permute-start(bf16[16,3072]{1,0:T(8,128)(2,1)S(1)} %get-tuple-element.103), channel_id=1, source_target_pairs={{0,1},{1,0},{2,3},{3,2},{4,5},{5,4},{6,7},{7,6},{8,9},{9,8},{10,11... | collective-permute-start | bytes 294920 | tf_op jit(solution)/shard_map/ppermute | solution.py:285
  110.7 13.0 %collective-permute-start.34 = (bf16[16,3072]{1,0:T(8,128)(2,1)S(1)}, bf16[16,3072]{1,0:T(8,128)(2,1)S(1)}, u32[]{:S(2)}, u32[]{:S(2)}) collective-permute-start(bf16[16,3072]{1,0:T(8,128)(2,1)S(1)} %get-tuple-element.105), channel_id=1, source_target_pairs={{0,1},{1,0},{2,3},{3,2},{4,5},{5,4},{6,7},{7,6},{8,9},{9,8},{10,11... | collective-permute-start | bytes 294920 | tf_op jit(solution)/shard_map/ppermute | solution.py:285
  112.8 15.8 %collective-permute-start.28 = (bf16[16,3072]{1,0:T(8,128)(2,1)S(1)}, bf16[16,3072]{1,0:T(8,128)(2,1)S(1)}, u32[]{:S(2)}, u32[]{:S(2)}) collective-permute-start(bf16[16,3072]{1,0:T(8,128)(2,1)S(1)} %add_convert_fusion.9), channel_id=1, source_target_pairs={{0,6},{1,7},{2,0},{3,1},{4,2},{5,3},{6,4},{7,5},{8,14},{9,15},{10,... | collective-permute-start | bytes 294920 | tf_op jit(solution)/shard_map/ppermute | solution.py:290
  121.7 7.5 %collective-permute-start.29 = (bf16[16,3072]{1,0:T(8,128)(2,1)S(1)}, bf16[16,3072]{1,0:T(8,128)(2,1)S(1)}, u32[]{:S(2)}, u32[]{:S(2)}) collective-permute-start(bf16[16,3072]{1,0:T(8,128)(2,1)S(1)} %add_convert_fusion.8), channel_id=1, source_target_pairs={{0,4},{1,5},{2,6},{3,7},{4,0},{5,1},{6,2},{7,3},{8,12},{9,13},{10,... | collective-permute-start | bytes 294920 | tf_op jit(solution)/shard_map/ppermute | solution.py:290
  122.9 12.8 %collective-permute-start.30 = (bf16[16,3072]{1,0:T(8,128)(2,1)S(1)}, bf16[16,3072]{1,0:T(8,128)(2,1)S(1)}, u32[]{:S(2)}, u32[]{:S(2)}) collective-permute-start(bf16[16,3072]{1,0:T(8,128)(2,1)S(1)} %add_convert_fusion.7), channel_id=1, source_target_pairs={{0,2},{1,3},{2,4},{3,5},{4,6},{5,7},{6,0},{7,1},{8,10},{9,11},{10,... | collective-permute-start | bytes 294920 | tf_op jit(solution)/shard_map/ppermute | solution.py:290
  123.9 21.3 %collective-permute-start.35 = (bf16[16,3072]{1,0:T(8,128)(2,1)S(1)}, bf16[16,3072]{1,0:T(8,128)(2,1)S(1)}, u32[]{:S(2)}, u32[]{:S(2)}) collective-permute-start(bf16[16,3072]{1,0:T(8,128)(2,1)S(1)} %add_convert_fusion.5), channel_id=1, source_target_pairs={{0,6},{1,7},{2,0},{3,1},{4,2},{5,3},{6,4},{7,5},{8,14},{9,15},{10,... | collective-permute-start | bytes 294920 | tf_op jit(solution)/shard_map/ppermute | solution.py:290
  125.3 19.8 %collective-permute-start.36 = (bf16[16,3072]{1,0:T(8,128)(2,1)S(1)}, bf16[16,3072]{1,0:T(8,128)(2,1)S(1)}, u32[]{:S(2)}, u32[]{:S(2)}) collective-permute-start(bf16[16,3072]{1,0:T(8,128)(2,1)S(1)} %add_convert_fusion.4), channel_id=1, source_target_pairs={{0,4},{1,5},{2,6},{3,7},{4,0},{5,1},{6,2},{7,3},{8,12},{9,13},{10,... | collective-permute-start | bytes 294920 | tf_op jit(solution)/shard_map/ppermute | solution.py:290
  128.6 16.5 %collective-permute-start.37 = (bf16[16,3072]{1,0:T(8,128)(2,1)S(1)}, bf16[16,3072]{1,0:T(8,128)(2,1)S(1)}, u32[]{:S(2)}, u32[]{:S(2)}) collective-permute-start(bf16[16,3072]{1,0:T(8,128)(2,1)S(1)} %add_convert_fusion.3), channel_id=1, source_target_pairs={{0,2},{1,3},{2,4},{3,5},{4,6},{5,7},{6,0},{7,1},{8,10},{9,11},{10,... | collective-permute-start | bytes 294920 | tf_op jit(solution)/shard_map/ppermute | solution.py:290
  (4 other events, 11.9 us)

commit v2 on v1

--- a/solution.py
+++ b/solution.py
@@ -41,15 +41,18 @@
             store[b, pl.ds(start, length), :] = piece[:, b * width : (b + 1) * width]
 
 
-def pair_tables(jobs, weights):
+def pair_tables(jobs, weights=()):
     cap = jobs[0][0].shape[0]
     specs = [job[1:] for job in jobs]
-    n = len(jobs)
+    n, m = len(jobs), len(weights)
     limits = [pair_limit(cap, rows if by_row else cols) for rows, cols, by_row in specs]
 
     def body(*refs):
-        refs = refs[:n] + refs[n + len(weights) :]
-        slot_refs, tables, pending = refs[:n], refs[n : 2 * n], refs[2 * n :]
+        slot_refs, far, tables, near = refs[:n], refs[n : n + m], refs[n + m : 2 * n + m], refs[2 * n + m : 2 * n + 2 * m]
+        pending, sems = refs[2 * n + 2 * m : 3 * n + 2 * m], refs[3 * n + 2 * m :]
+        copies = [pltpu.make_async_copy(*copy) for copy in zip(far, near, sems)]
+        for copy in copies:
+            copy.start()
         for (rows, cols, by_row), pend in zip(specs, pending):
 
             def clear(i, carry, pend=pend):
@@ -58,29 +61,33 @@
 
             lax.fori_loop(0, (rows if by_row else cols) + 1, clear, 0)
 
-        def one(k, counts):
+        step = largest_divisor(cap, 8)
+
+        def some(g, counts):
             counts = list(counts)
             for t, (rows, cols, by_row) in enumerate(specs):
-                pos = slot_refs[t][k]
-                filled = pos >= 0
-                safe = jnp.maximum(pos, 0)
-                row = (safe * (-(-65536 // cols))) >> 16
-                col = safe - row * cols
-                key, src, end = (row, col, rows) if by_row else (col, row, cols)
                 table, pend, limit = tables[t], pending[t], limits[t]
-                key = jnp.where(filled, key, end)
-                first = pend[key]
-                word = k + src * 4096
-                paired = jnp.logical_and(first >= 0, filled)
-                at = counts[t]
-                table[at] = first
-                table[limit + at] = word
-                table[2 * limit + at] = key
-                pend[key] = jnp.where(first >= 0, -1, word)
-                counts[t] = at + paired.astype(jnp.int32)
+                entries = []
+                for u in range(step):
+                    k = g * step + u
+                    pos = slot_refs[t][k]
+                    filled = pos >= 0
+                    safe = jnp.maximum(pos, 0)
+                    row = (safe * (-(-65536 // cols))) >> 16
+                    col = safe - row * cols
+                    key, src, end = (row, col, rows) if by_row else (col, row, cols)
+                    entries.append((jnp.where(filled, key, end), k + src * 4096, filled))
+                for key, word, filled in entries:
+                    first = pend[key]
+                    at = counts[t]
+                    table[at] = first
+                    table[limit + at] = word
+                    table[2 * limit + at] = key
+                    pend[key] = jnp.where(first >= 0, -1, word)
+                    counts[t] = at + jnp.logical_and(first >= 0, filled).astype(jnp.int32)
             return tuple(counts)
 
-        counts = lax.fori_loop(0, cap, one, (jnp.int32(0),) * n)
+        counts = lax.fori_loop(0, cap // step, some, (jnp.int32(0),) * n)
         for t, (rows, cols, by_row) in enumerate(specs):
             table, pend, limit = tables[t], pending[t], limits[t]
             n_dst, n_src = (rows, cols) if by_row else (cols, rows)
@@ -97,15 +104,20 @@
                 table[at + u] = n_src * 4096
                 table[limit + at + u] = n_src * 4096
                 table[2 * limit + at + u] = n_dst
-            table[3 * limit] = (at + (PAIR_UNROLL - 1)) >> PAIR_SHIFT
+            table[3 * limit] = counts[t]
+            table[3 * limit + 1] = (at + (PAIR_UNROLL - 1)) >> PAIR_SHIFT
+        for copy in copies:
+            copy.wait()
 
     smem = pl.BlockSpec(memory_space=pltpu.SMEM)
     return pl.pallas_call(
         body,
-        in_specs=[smem] * n + [pl.BlockSpec(memory_space=pltpu.VMEM)] * len(weights),
-        out_specs=[smem] * n,
-        out_shape=[jax.ShapeDtypeStruct((3 * limit + 1,), jnp.int32) for limit in limits],
-        scratch_shapes=[pltpu.SMEM(((rows if by_row else cols) + 1,), jnp.int32) for rows, cols, by_row in specs],
+        in_specs=[smem] * n + [pl.BlockSpec(memory_space=pltpu.HBM)] * m,
+        out_specs=[smem] * n + [pl.BlockSpec(memory_space=pltpu.VMEM)] * m,
+        out_shape=[jax.ShapeDtypeStruct((3 * limit + 2,), jnp.int32) for limit in limits]
+        + [jax.ShapeDtypeStruct(weight.shape, weight.dtype) for weight in weights],
+        scratch_shapes=[pltpu.SMEM(((rows if by_row else cols) + 1,), jnp.int32) for rows, cols, by_row in specs]
+        + [pltpu.SemaphoreType.DMA] * m,
         compiler_params=pltpu.CompilerParams(vmem_limit_bytes=1024 * 1024),
         name="pair_tables",
     )(*[job[0] for job in jobs], *weights)
@@ -119,7 +131,7 @@
     return (cap + n_dst) // 2 + PAIR_UNROLL + 1
 
 
-def block_product(pieces, in_rows, blocks, table, n_dst, out_lengths, out_rows, transposed):
+def block_product(pieces, in_rows, blocks, table, n_dst, out_lengths, out_rows, transposed, stage=()):
     cap, width = blocks.shape[0], blocks.shape[1]
     n_src = pieces[0].shape[1] // width
     tokens = sum(piece.shape[0] for piece in pieces)
@@ -127,14 +139,20 @@
     dims = (((1,), (1 if transposed else 0,)), ((), ()))
     zero_rows = jnp.zeros((1,), jnp.int32)
     in_arr = zero_rows if in_rows is None else in_rows
-    out_arr = zero_rows if out_rows is None else out_rows
-    n_in, n_out = len(pieces), len(out_lengths)
+    static_out = isinstance(out_rows, list)
+    out_arr = zero_rows if static_out else out_rows
+    n_in, n_out, m = len(pieces), len(out_lengths), len(stage)
 
     def body(table_s, in_s, out_s, *refs):
         piece_refs = refs[:n_in]
         w_ref = refs[n_in]
-        out_refs = refs[n_in + 1 : n_in + 1 + n_out]
-        xs, acc = refs[n_in + 1 + n_out :]
+        far = refs[n_in + 1 : n_in + 1 + m]
+        refs = refs[n_in + 1 + m :]
+        out_refs, near = refs[:n_out], refs[n_out : n_out + m]
+        xs, acc = refs[n_out + m : n_out + m + 2]
+        copies = [pltpu.make_async_copy(*copy) for copy in zip(far, near, refs[n_out + m + 2 :])]
+        for copy in copies:
+            copy.start()
         if in_rows is None:
             place = lambda i, length: i * length
         else:
@@ -157,13 +175,13 @@
                 acc[table_s[2 * limit + g * PAIR_UNROLL + u]] += terms[u]
             return carry
 
-        lax.fori_loop(0, table_s[3 * limit], some, 0)
+        lax.fori_loop(0, table_s[3 * limit + 1], some, 0)
         at = 0
         for ref in out_refs:
             lead = ref.shape[:-2]
             length = ref.shape[-2]
             for j in range(lead[0] if lead else 1):
-                start = at * length if out_rows is None else pl.multiple_of(out_s[at], length)
+                start = out_rows[at] if static_out else pl.multiple_of(out_s[at], length)
                 at += 1
                 for b in range(n_dst):
                     val = acc[b, pl.ds(start, length), :].astype(jnp.bfloat16)
@@ -171,19 +189,23 @@
                         ref[j, :, b * width : (b + 1) * width] = val
                     else:
                         ref[:, b * width : (b + 1) * width] = val
+        for copy in copies:
+            copy.wait()
 
     smem = pl.BlockSpec(memory_space=pltpu.SMEM)
     vmem = pl.BlockSpec(memory_space=pltpu.VMEM)
     out_shapes = [shape + (n_dst * width,) for shape in out_lengths]
     return pl.pallas_call(
         body,
-        in_specs=[smem] * 3 + [vmem] * (n_in + 1),
-        out_specs=[vmem] * n_out,
+        in_specs=[smem] * 3 + [vmem] * (n_in + 1) + [pl.BlockSpec(memory_space=pltpu.HBM)] * m,
+        out_specs=[vmem] * (n_out + m),
         scratch_shapes=[
             pltpu.VMEM((n_src + 1, tokens, width), jnp.bfloat16),
             pltpu.VMEM((n_dst + 1, tokens, width), jnp.float32),
-        ],
-        out_shape=[jax.ShapeDtypeStruct(shape, jnp.bfloat16) for shape in out_shapes],
+        ]
+        + [pltpu.SemaphoreType.DMA] * m,
+        out_shape=[jax.ShapeDtypeStruct(shape, jnp.bfloat16) for shape in out_shapes]
+        + [jax.ShapeDtypeStruct(array.shape, array.dtype) for array in stage],
         compiler_params=pltpu.CompilerParams(vmem_limit_bytes=8 * 1024 * 1024),
         cost_estimate=pl.CostEstimate(
             flops=2 * cap * tokens * width * width,
@@ -191,7 +213,7 @@
             transcendentals=0,
         ),
         name="block_product",
-    )(table, in_arr, out_arr, *pieces, blocks)
+    )(table, in_arr, out_arr, *pieces, blocks, *stage)
 
 
 def block_grads(left, left_rows, right, right_rows, rows, cols, cap):
@@ -268,6 +290,8 @@
 def on_device(tokens, in_blocks, in_slots, out_blocks, out_slots, cotangent, *, hidden_total):
     w_in = in_blocks.reshape(in_blocks.shape[2:])
     w_out = out_blocks.reshape(out_blocks.shape[2:])
+    w_in = pltpu.with_memory_space_constraint(w_in, pltpu.HBM)
+    w_out = pltpu.with_memory_space_constraint(w_out, pltpu.HBM)
     slots_in = in_slots.reshape(-1)
     slots_out = out_slots.reshape(-1)
     width = w_in.shape[-1]
@@ -312,13 +336,8 @@
             pieces += [piece, near_move(piece, "tensor", tensor_count)]
         return pieces
 
-    def send_near(terms):
-        order = list(range(1, far_t)) + [0]
-        got = {k: near_move(terms[2 * k + 1], "tensor", tensor_count) for k in order}
-        return [got[k] for k in range(far_t)]
-
-    def pair_out(terms, got):
-        pair = [terms[2 * k].astype(jnp.float32) + got[k].astype(jnp.float32) for k in range(far_t)]
+    def pair_out(keep, got):
+        pair = [keep[k].astype(jnp.float32) + got[k].astype(jnp.float32) for k in range(far_t)]
         return pair[0], [value.astype(jnp.bfloat16) for value in pair[1:]]
 
     def total_out(own, pairs):
@@ -350,28 +369,27 @@
         return pieces
 
     hidden_lengths = [(far_s, seq_rows)] * 2
-    token_lengths = [(tensor_rows,)] * tensor_count
+    token_lengths = [(far_t, tensor_rows)] * 2
+    token_rows = [(2 * k + flip) * tensor_rows for flip in range(2) for k in range(far_t)]
 
     tok_far = gather_far(tokens)
-    (in_by_col,) = pair_tables([(slots_in, feat_blocks, hid_blocks, False)], [w_in])
-    cot_far = gather_far(after(cotangent, tok_far[1:]))
+    in_by_col, w_in_near = pair_tables([(slots_in, feat_blocks, hid_blocks, False)], [w_in])
+    cot_far = gather_far(cotangent)
     tok = gather_near(tok_far)
     cot = gather_near(cot_far)
-    later_in, later_out = after((slots_in, slots_out), tok_far[1:])
-    out_by_row, out_by_col, in_by_row = pair_tables(
-        [
-            (later_out, hid_blocks, feat_blocks, True),
-            (later_out, hid_blocks, feat_blocks, False),
-            (later_in, feat_blocks, hid_blocks, True),
-        ],
-        [w_out],
+    out_by_row, w_out_near = pair_tables(
+        [(after(slots_out, tok_far[1:]), hid_blocks, feat_blocks, True)], [w_out]
     )
     keep_h, send_h = block_product(
-        tok, None, w_in, in_by_col, hid_blocks, hidden_lengths, near_order, False
+        after(tok, out_by_row), None, w_in_near, in_by_col, hid_blocks, hidden_lengths, near_order, False
     )
     own_h, pairs_h = pair_hidden(keep_h, send_h)
     keep_g, send_g = block_product(
-        after(cot, pairs_h), None, w_out, out_by_row, hid_blocks, hidden_lengths, near_order, True
+        after(cot, pairs_h), None, w_out_near, out_by_row, hid_blocks, hidden_lengths, near_order, True
+    )
+    later_in, later_out = after((slots_in, slots_out), keep_g)
+    out_by_col, in_by_row = pair_tables(
+        [(later_out, hid_blocks, feat_blocks, False), (later_in, feat_blocks, hid_blocks, True)]
     )
     hidden = total_hidden(own_h, pairs_h)
     own_act = gelu_value(hidden).astype(jnp.bfloat16)
@@ -383,17 +401,25 @@
     gh_far = spread_far(own_gh)
     grad_hidden = spread_near(gh_far)
 
-    terms_o = block_product(
-        after(activated, own_gh), seq_part, w_out, out_by_col, feat_blocks, token_lengths, None, False
-    )
-    got_o = send_near(terms_o)
-    terms_t = block_product(
-        after(grad_hidden, terms_o), seq_part, w_in, in_by_row, feat_blocks, token_lengths, None, True
-    )
-    got_t = send_near(terms_t)
-    own_o, pairs_o = pair_out(terms_o, after(got_o, terms_t))
+    keep_o, send_o, w_in_near = block_product(
+        after(activated, own_gh),
+        seq_part,
+        w_out_near,
+        out_by_col,
+        feat_blocks,
+        token_lengths,
+        token_rows,
+        False,
+        [w_in],
+    )
+    got_o = near_move(send_o, "tensor", tensor_count)
+    keep_t, send_t = block_product(
+        after(grad_hidden, keep_o), seq_part, w_in_near, in_by_row, feat_blocks, token_lengths, token_rows, True
+    )
+    got_t = near_move(send_t, "tensor", tensor_count)
+    own_o, pairs_o = pair_out(keep_o, after(got_o, keep_t))
     grad_out = block_grads(after(activated, pairs_o), seq_part, cot, None, out_row, out_col, cap)
-    own_t, pairs_t = pair_out(terms_t, after(got_t, grad_out))
+    own_t, pairs_t = pair_out(keep_t, after(got_t, grad_out))
     grad_in = block_grads(tok, None, after(grad_hidden, pairs_t), seq_part, in_row, in_col, cap)
     output = total_out(own_o, pairs_o)
     grad_tokens = total_out(own_t, pairs_t)

time: 146 us -> 107 us (0.73)
  the two profiles are of different devices: /device:TPU:18 before, /device:TPU:0 now
where the time goes in v2:
time: 107 us
  Pallas kernels  45.4 us (42%)
  starting transfers between devices  37.6 us (35%)
  waiting for transfers between devices  19 us (18%)
  other arithmetic  3.75 us (4%)
    ppermute x16, starting transfers between devices, far_move(): return lax.ppermute(v, axis, pairs)  22.6 us
    pallas_call x2, Pallas kernels, block_grads(): pl.pallas_call(body, grid_spec=pltpu.PrefetchScalarGridSpec(num_scalar_pr...  17.5 us
    pallas_call x3, Pallas kernels, pair_tables(): pl.pallas_call(body, in_specs=[smem] * n + [pl.BlockSpec(memory_space=plt...  16.5 us
    ppermute x16, starting transfers between devices, near_move(): return lax.ppermute(v, axis, [(i, i ^ 1) for i in range(count)])  15 us
    pallas_call x4, Pallas kernels, block_product(): pl.pallas_call(body, in_specs=[smem] * 3 + [vmem] * (n_in + 1) + [pl.Bloc...  11.4 us
    ppermute x16, waiting for transfers between devices, far_move(): return lax.ppermute(v, axis, pairs)  10 us
    ppermute x16, waiting for transfers between devices, near_move(): return lax.ppermute(v, axis, [(i, i ^ 1) for i in range(count)])  8.94 us
  transfers between devices with their start and end apart: 32, of which 12 were waited for; matrix products, arithmetic and copies ran while one was open for 3% of the time, Pallas kernels for 41%

profile of v2, /device:TPU:0, one launch (start us, length us, event | category | flops | bytes accessed | tf_op | source)
XLA Modules:
  0.0 106.7 jit_solution(5137894917224389958)
XLA Ops:
  0.6 3.0 %collective-permute-start.10 = (bf16[16,3072]{1,0:T(8,128)(2,1)}, bf16[16,3072]{1,0:T(8,128)(2,1)S(1)}, u32[]{:S(2)}, u32[]{:S(2)}) collective-permute-start(bf16[16,3072]{1,0:T(8,128)(2,1)} %refs_0_.3), channel_id=1, source_target_pairs={{0,1},{1,0},{2,3},{3,2},{4,5},{5,4},{6,7},{7,6},{8,9},{9,8},{10,11... | collective-permute-start | bytes 294920 | tf_op jit(solution)/shard_map/ppermute | solution.py:309
  3.7 3.6 %collective-permute-start.2 = (bf16[16,3072]{1,0:T(8,128)(2,1)}, bf16[16,3072]{1,0:T(8,128)(2,1)S(1)}, u32[]{:S(2)}, u32[]{:S(2)}) collective-permute-start(bf16[16,3072]{1,0:T(8,128)(2,1)} %refs_0_.3), channel_id=1, source_target_pairs={{0,6},{1,7},{2,0},{3,1},{4,2},{5,3},{6,4},{7,5},{8,14},{9,15},{10,... | collective-permute-start | bytes 294920 | tf_op jit(solution)/shard_map/ppermute | solution.py:314
  7.3 1.0 collective-permute-start
  8.5 0.7 reduce.refs_0_.refs_1_
  9.2 0.7 reduce.1.refs_0_
  9.9 4.9 %pair_tables.4 = (s32[521]{0:T(1024)S(1)}, bf16[288,128,128]{2,1,0:T(8,128)(2,1)S(1)}) custom-call(s32[288]{0:T(512)S(1)} %reduce.refs_0_.refs_1_, bf16[288,128,128]{2,1,0:T(8,128)(2,1)} %bitcast.46), custom_call_target="tpu_custom_call" | custom-call | tf_op jit(solution)/shard_map/pair_tables/pallas_call | solution.py:113
  14.8 0.6 collective-permute-start.13
  15.4 0.4 collective-permute-done.1.refs_4_
  15.8 1.1 collective-permute-start.12
  16.9 1.0 collective-permute-start.11
  17.9 4.9 %pair_tables.3 = (s32[521]{0:T(1024)S(1)}, bf16[288,128,128]{2,1,0:T(8,128)(2,1)S(1)}) custom-call(s32[288]{0:T(512)S(1)} %reduce.1.refs_0_, bf16[288,128,128]{2,1,0:T(8,128)(2,1)} %bitcast.50), custom_call_target="tpu_custom_call" | custom-call | tf_op jit(solution)/shard_map/pair_tables/pallas_call | solution.py:113
  22.8 0.3 collective-permute-done.11.refs_3_
  23.1 1.8 %block_product.4 = (bf16[2,32,3072]{2,1,0:T(8,128)(2,1)S(1)}, bf16[2,32,3072]{2,1,0:T(8,128)(2,1)S(1)}) custom-call(s32[521]{0:T(1024)S(1)} %get-tuple-element.59.table_s, s32[1]{0:T(128)} %constant.86.clone.1.in_s.out_s.right_s.left_s, s32[4]{0:T(128)S(1)} %pad_add_fusion.out_s, bf16[16,3072]{1,0:T(8,128)(2,1)S(1)} %copy-done.1, ...), custom_call_target="tpu_custom_call" | custom-call | flops 1207959552 | bytes 11010048 | tf_op jit(solution)/shard_map/block_product/pallas_call | solution.py:198
  25.1 6.2 %collective-permute-start.8 = (bf16[16,3072]{1,0:T(8,128)(2,1)S(1)}, bf16[16,3072]{1,0:T(8,128)(2,1)S(1)}, u32[]{:S(2)}, u32[]{:S(2)}) collective-permute-start(bf16[16,3072]{1,0:T(8,128)(2,1)S(1)} %copy-done), channel_id=1, source_target_pairs={{0,6},{1,7},{2,0},{3,1},{4,2},{5,3},{6,4},{7,5},{8,14},{9,15},{10,... | collective-permute-start | bytes 294920 | tf_op jit(solution)/shard_map/ppermute | solution.py:314
  31.3 0.6 collective-permute-start.4
  31.9 1.6 %collective-permute-start.3 = (bf16[16,3072]{1,0:T(8,128)(2,1)S(1)}, bf16[16,3072]{1,0:T(8,128)(2,1)S(1)}, u32[]{:S(2)}, u32[]{:S(2)}) collective-permute-start(bf16[16,3072]{1,0:T(8,128)(2,1)S(1)} %copy-done), channel_id=1, source_target_pairs={{0,1},{1,0},{2,3},{3,2},{4,5},{5,4},{6,7},{7,6},{8,9},{9,8},{10,11... | collective-permute-start | bytes 294920 | tf_op jit(solution)/shard_map/ppermute | solution.py:309
  33.5 0.9 collective-permute-done.8.refs_6_.refs_10_
  34.5 6.5 %collective-permute-done.6.refs_4_.refs_8_ = bf16[16,3072]{1,0:T(8,128)(2,1)S(1)} collective-permute-done((bf16[16,3072]{1,0:T(8,128)(2,1)S(1)}, bf16[16,3072]{1,0:T(8,128)(2,1)S(1)}, u32[]{:S(2)}, u32[]{:S(2)}) %collective-permute-start.6) | collective-permute-done | bytes 98336 | tf_op jit(solution)/shard_map/ppermute | solution.py:314
  41.2 1.8 %collective-permute-start.5 = (bf16[16,3072]{1,0:T(8,128)(2,1)S(1)}, bf16[16,3072]{1,0:T(8,128)(2,1)S(1)}, u32[]{:S(2)}, u32[]{:S(2)}) collective-permute-start(bf16[16,3072]{1,0:T(8,128)(2,1)S(1)} %collective-permute-done.4.refs_2_.refs_6_), channel_id=1, source_target_pairs={{0,1},{1,0},{2,3},{3,2},{4,5},{5,4},{6,7},{7,6},{8,9},{9,8},{10,11... | collective-permute-start | bytes 294920 | tf_op jit(solution)/shard_map/ppermute | solution.py:309
  43.0 2.1 %collective-permute-start.15 = (bf16[32,3072]{1,0:T(8,128)(2,1)S(1)}, bf16[32,3072]{1,0:T(8,128)(2,1)S(1)}, u32[]{:S(2)}, u32[]{:S(2)}) collective-permute-start(bf16[32,3072]{1,0:T(8,128)(2,1)S(1)} %fusion.7), channel_id=1, source_target_pairs={{0,16},{8,24},{16,0},{24,8},{1,17},{9,25},{17,1},{25,9},{2,18},{10... | collective-permute-start | bytes 589832 | tf_op jit(solution)/shard_map/ppermute | solution.py:314
  45.2 1.4 %collective-permute-done.7.refs_5_.refs_9_ = bf16[16,3072]{1,0:T(8,128)(2,1)S(1)} collective-permute-done((bf16[16,3072]{1,0:T(8,128)(2,1)S(1)}, bf16[16,3072]{1,0:T(8,128)(2,1)S(1)}, u32[]{:S(2)}, u32[]{:S(2)}) %collective-permute-start.7) | collective-permute-done | bytes 98336 | tf_op jit(solution)/shard_map/ppermute | solution.py:309
  46.6 1.2 %collective-permute-done.5.refs_3_.refs_7_ = bf16[16,3072]{1,0:T(8,128)(2,1)S(1)} collective-permute-done((bf16[16,3072]{1,0:T(8,128)(2,1)S(1)}, bf16[16,3072]{1,0:T(8,128)(2,1)S(1)}, u32[]{:S(2)}, u32[]{:S(2)}) %collective-permute-start.5) | collective-permute-done | bytes 98336 | tf_op jit(solution)/shard_map/ppermute | solution.py:309
  47.8 3.2 %block_product.5 = (bf16[2,32,3072]{2,1,0:T(8,128)(2,1)S(1)}, bf16[2,32,3072]{2,1,0:T(8,128)(2,1)S(1)}) custom-call(s32[521]{0:T(1024)S(1)} %get-tuple-element.58.table_s, s32[1]{0:T(128)} %constant.86.clone.1.in_s.out_s.right_s.left_s, s32[4]{0:T(128)S(1)} %pad_add_fusion.out_s, bf16[16,3072]{1,0:T(8,128)(2,1)S(1)} %copy-done, ...), custom_call_target="tpu_custom_call" | custom-call | flops 1207959552 | bytes 11010048 | tf_op jit(solution)/shard_map/block_product/pallas_call | solution.py:198
  51.6 1.2 %collective-permute-done.19 = bf16[2,32,3072]{2,1,0:T(8,128)(2,1)S(1)} collective-permute-done((bf16[2,32,3072]{2,1,0:T(8,128)(2,1)S(1)}, bf16[2,32,3072]{2,1,0:T(8,128)(2,1)S(1)}, u32[]{:S(2)}, u32[]{:S(2)}) %collective-permute-start.19) | collective-permute-done | bytes 393248 | tf_op jit(solution)/shard_map/ppermute | solution.py:309
  52.9 0.7 collective-permute-start.20
  53.6 6.7 %pair_tables.5 = (s32[521]{0:T(1024)S(1)}, s32[521]{0:T(1024)S(1)}) custom-call(s32[288]{0:T(512)S(1)} %reduce.1.refs_0_, s32[288]{0:T(512)S(1)} %reduce.refs_0_.refs_1_), custom_call_target="tpu_custom_call" | custom-call | tf_op jit(solution)/shard_map/pair_tables/pallas_call | solution.py:113
  60.4 0.5 collective-permute-start.18
  60.9 2.0 %collective-permute-done.20 = bf16[32,3072]{1,0:T(8,128)(2,1)S(1)} collective-permute-done((bf16[32,3072]{1,0:T(8,128)(2,1)S(1)}, bf16[32,3072]{1,0:T(8,128)(2,1)S(1)}, u32[]{:S(2)}, u32[]{:S(2)}) %collective-permute-start.20) | collective-permute-done | bytes 196640 | tf_op jit(solution)/shard_map/ppermute | solution.py:314
  62.9 0.4 fusion.6.refs_0_.refs_8_
  63.3 0.4 collective-permute-start.23
  63.6 4.5 %block_product.6 = (bf16[4,16,3072]{2,1,0:T(8,128)(2,1)S(1)}, bf16[4,16,3072]{2,1,0:T(8,128)(2,1)S(1)}, bf16[288,128,128]{2,1,0:T(8,128)(2,1)S(1)}) custom-call(s32[521]{0:T(1024)S(1)} %get-tuple-element.83.table_s, s32[4]{0:T(128)S(1)} %fusion.28.in_s.left_s.right_s, s32[1]{0:T(128)} %constant.86.clone.1.in_s.out_s.right_s.left_s, ...), custom_call_target="tpu_custom_call" | custom-call | flops 1207959552 | bytes 11010048 | tf_op jit(solution)/shard_map/block_product/pallas_call | solution.py:198
  68.1 1.3 %collective-permute-start.21 = (bf16[4,16,3072]{2,1,0:T(8,128)(2,1)S(1)}, bf16[4,16,3072]{2,1,0:T(8,128)(2,1)S(1)}, u32[]{:S(2)}, u32[]{:S(2)}) collective-permute-start(bf16[4,16,3072]{2,1,0:T(8,128)(2,1)S(1)} %get-tuple-element.91), channel_id=1, source_target_pairs={{0,1},{1,0},{2,3},{3,2},{4,5},{5,4},{6,7},{7,6},{8,9},{9,8},{10,11... | collective-permute-start | bytes 1179656 | tf_op jit(solution)/shard_map/ppermute | solution.py:309
  69.7 0.3 collective-permute-start.24
  70.1 0.9 collective-permute-done.22.refs_1_.refs_9_
  71.0 0.3 collective-permute-done.24.refs_3_.refs_11_
  71.2 1.8 %block_product.7 = (bf16[4,16,3072]{2,1,0:T(8,128)(2,1)S(1)}, bf16[4,16,3072]{2,1,0:T(8,128)(2,1)S(1)}) custom-call(s32[521]{0:T(1024)S(1)} %get-tuple-element.92.table_s, s32[4]{0:T(128)S(1)} %fusion.28.in_s.left_s.right_s, s32[1]{0:T(128)} %constant.86.clone.1.in_s.out_s.right_s.left_s, bf16[32,3072]{1,0:T(8,128)(2,1)S(1)} %fusion.6.refs_0_.refs_8_, ...), custom_call_target="tpu_custom_call" | custom-call | flops 1207959552 | bytes 11010048 | tf_op jit(solution)/shard_map/block_product/pallas_call | solution.py:198
  73.1 3.1 %collective-permute-start.28 = (bf16[4,16,3072]{2,1,0:T(8,128)(2,1)S(1)}, bf16[4,16,3072]{2,1,0:T(8,128)(2,1)S(1)}, u32[]{:S(2)}, u32[]{:S(2)}) collective-permute-start(bf16[4,16,3072]{2,1,0:T(8,128)(2,1)S(1)} %get-tuple-element.100), channel_id=1, source_target_pairs={{0,1},{1,0},{2,3},{3,2},{4,5},{5,4},{6,7},{7,6},{8,9},{9,8},{10,11... | collective-permute-start | bytes 1179656 | tf_op jit(solution)/shard_map/ppermute | solution.py:309
  76.2 3.6 %collective-permute-done.21 = bf16[4,16,3072]{2,1,0:T(8,128)(2,1)S(1)} collective-permute-done((bf16[4,16,3072]{2,1,0:T(8,128)(2,1)S(1)}, bf16[4,16,3072]{2,1,0:T(8,128)(2,1)S(1)}, u32[]{:S(2)}, u32[]{:S(2)}) %collective-permute-start.21) | collective-permute-done | bytes 393248 | tf_op jit(solution)/shard_map/ppermute | solution.py:309
  79.9 1.8 %collective-permute-start.25 = (bf16[16,3072]{1,0:T(8,128)(2,1)S(1)}, bf16[16,3072]{1,0:T(8,128)(2,1)S(1)}, u32[]{:S(2)}, u32[]{:S(2)}) collective-permute-start(bf16[16,3072]{1,0:T(8,128)(2,1)S(1)} %get-tuple-element.113), channel_id=1, source_target_pairs={{0,6},{1,7},{2,0},{3,1},{4,2},{5,3},{6,4},{7,5},{8,14},{9,15},{10,... | collective-permute-start | bytes 294920 | tf_op jit(solution)/shard_map/ppermute | solution.py:314
  81.7 0.3 collective-permute-start.27
  82.0 3.0 %collective-permute-start.26 = (bf16[16,3072]{1,0:T(8,128)(2,1)S(1)}, bf16[16,3072]{1,0:T(8,128)(2,1)S(1)}, u32[]{:S(2)}, u32[]{:S(2)}) collective-permute-start(bf16[16,3072]{1,0:T(8,128)(2,1)S(1)} %get-tuple-element.115), channel_id=1, source_target_pairs={{0,4},{1,5},{2,6},{3,7},{4,0},{5,1},{6,2},{7,3},{8,12},{9,13},{10,... | collective-permute-start | bytes 294920 | tf_op jit(solution)/shard_map/ppermute | solution.py:314
  85.0 8.8 %block_grads.2 = f32[288,128,128]{2,1,0:T(8,128)} custom-call(s32[288]{0:T(512)S(1)} %get-tuple-element.119.row_s, s32[288]{0:T(512)S(1)} %get-tuple-element.118.col_s, s32[4]{0:T(128)S(1)} %fusion.28.in_s.left_s.right_s, s32[1]{0:T(128)} %constant.86.clone.1.in_s.out_s.right_s.left_s, bf16[32,3072]{1,0:T(8,128)(2,1)S(1)} %multiply_convert_fusion.refs_0_, ...), custom_call_target="tpu_custom_call" | custom-call | flops 1207959552 | bytes 20447232 | tf_op jit(solution)/shard_map/block_grads/pallas_call | solution.py:264
  93.8 0.7 fusion.14
  94.6 1.0 collective-permute-start.29
  95.6 1.1 collective-permute-start.31
  96.7 0.6 collective-permute-start.30
  97.3 8.7 %block_grads.3 = f32[288,128,128]{2,1,0:T(8,128)} custom-call(s32[288]{0:T(512)S(1)} %get-tuple-element.117.row_s, s32[288]{0:T(512)S(1)} %get-tuple-element.116.col_s, s32[1]{0:T(128)} %constant.86.clone.1.in_s.out_s.right_s.left_s, s32[4]{0:T(128)S(1)} %fusion.28.in_s.left_s.right_s, bf16[16,3072]{1,0:T(8,128)(2,1)S(1)} %copy-done.1, ...), custom_call_target="tpu_custom_call" | custom-call | flops 1207959552 | bytes 20447232 | tf_op jit(solution)/shard_map/block_grads/pallas_call | solution.py:264
  106.0 0.7 fusion.11
  (45 shorter events, 1.9 us)
Async XLA Ops:
  0.6 22.2 %collective-permute-start.10 = (bf16[16,3072]{1,0:T(8,128)(2,1)}, bf16[16,3072]{1,0:T(8,128)(2,1)S(1)}, u32[]{:S(2)}, u32[]{:S(2)}) collective-permute-start(bf16[16,3072]{1,0:T(8,128)(2,1)} %refs_0_.3), channel_id=1, source_target_pairs={{0,1},{1,0},{2,3},{3,2},{4,5},{5,4},{6,7},{7,6},{8,9},{9,8},{10,11... | collective-permute-start | bytes 294920 | tf_op jit(solution)/shard_map/ppermute | solution.py:309
  3.7 11.1 %collective-permute-start.2 = (bf16[16,3072]{1,0:T(8,128)(2,1)}, bf16[16,3072]{1,0:T(8,128)(2,1)S(1)}, u32[]{:S(2)}, u32[]{:S(2)}) collective-permute-start(bf16[16,3072]{1,0:T(8,128)(2,1)} %refs_0_.3), channel_id=1, source_target_pairs={{0,6},{1,7},{2,0},{3,1},{4,2},{5,3},{6,4},{7,5},{8,14},{9,15},{10,... | collective-permute-start | bytes 294920 | tf_op jit(solution)/shard_map/ppermute | solution.py:314
  7.3 8.6 %collective-permute-start.1 = (bf16[16,3072]{1,0:T(8,128)(2,1)}, bf16[16,3072]{1,0:T(8,128)(2,1)S(1)}, u32[]{:S(2)}, u32[]{:S(2)}) collective-permute-start(bf16[16,3072]{1,0:T(8,128)(2,1)} %refs_0_.3), channel_id=1, source_target_pairs={{0,4},{1,5},{2,6},{3,7},{4,0},{5,1},{6,2},{7,3},{8,12},{9,13},{10,... | collective-permute-start | bytes 294920 | tf_op jit(solution)/shard_map/ppermute | solution.py:314
  7.3 9.6 %collective-permute-start = (bf16[16,3072]{1,0:T(8,128)(2,1)}, bf16[16,3072]{1,0:T(8,128)(2,1)S(1)}, u32[]{:S(2)}, u32[]{:S(2)}) collective-permute-start(bf16[16,3072]{1,0:T(8,128)(2,1)} %refs_0_.3), channel_id=1, source_target_pairs={{0,2},{1,3},{2,4},{3,5},{4,6},{5,7},{6,0},{7,1},{8,10},{9,11},{10,... | collective-permute-start | bytes 294920 | tf_op jit(solution)/shard_map/ppermute | solution.py:314
  9.9 13.3 %copy-start.1 = (bf16[16,3072]{1,0:T(8,128)(2,1)S(1)}, bf16[16,3072]{1,0:T(8,128)(2,1)}, u32[]{:S(2)}) copy-start(bf16[16,3072]{1,0:T(8,128)(2,1)} %refs_0_.3) | copy-start | bytes 294916
  14.8 8.0 %collective-permute-start.13 = (bf16[16,3072]{1,0:T(8,128)(2,1)S(1)}, bf16[16,3072]{1,0:T(8,128)(2,1)S(1)}, u32[]{:S(2)}, u32[]{:S(2)}) collective-permute-start(bf16[16,3072]{1,0:T(8,128)(2,1)S(1)} %collective-permute-done.2.refs_6_), channel_id=1, source_target_pairs={{0,1},{1,0},{2,3},{3,2},{4,5},{5,4},{6,7},{7,6},{8,9},{9,8},{10,11... | collective-permute-start | bytes 294920 | tf_op jit(solution)/shard_map/ppermute | solution.py:309
  15.8 7.0 %collective-permute-start.12 = (bf16[16,3072]{1,0:T(8,128)(2,1)S(1)}, bf16[16,3072]{1,0:T(8,128)(2,1)S(1)}, u32[]{:S(2)}, u32[]{:S(2)}) collective-permute-start(bf16[16,3072]{1,0:T(8,128)(2,1)S(1)} %collective-permute-done.1.refs_4_), channel_id=1, source_target_pairs={{0,1},{1,0},{2,3},{3,2},{4,5},{5,4},{6,7},{7,6},{8,9},{9,8},{10,11... | collective-permute-start | bytes 294920 | tf_op jit(solution)/shard_map/ppermute | solution.py:309
  16.9 6.3 %collective-permute-start.11 = (bf16[16,3072]{1,0:T(8,128)(2,1)S(1)}, bf16[16,3072]{1,0:T(8,128)(2,1)S(1)}, u32[]{:S(2)}, u32[]{:S(2)}) collective-permute-start(bf16[16,3072]{1,0:T(8,128)(2,1)S(1)} %collective-permute-done.refs_2_), channel_id=1, source_target_pairs={{0,1},{1,0},{2,3},{3,2},{4,5},{5,4},{6,7},{7,6},{8,9},{9,8},{10,11... | collective-permute-start | bytes 294920 | tf_op jit(solution)/shard_map/ppermute | solution.py:309
  17.9 7.2 %copy-start = (bf16[16,3072]{1,0:T(8,128)(2,1)S(1)}, bf16[16,3072]{1,0:T(8,128)(2,1)}, u32[]{:S(2)}) copy-start(bf16[16,3072]{1,0:T(8,128)(2,1)} %refs_4_.1) | copy-start | bytes 294916
  25.0 18.0 %collective-permute-start.14 = (bf16[2,32,3072]{2,1,0:T(8,128)(2,1)S(1)}, bf16[2,32,3072]{2,1,0:T(8,128)(2,1)S(1)}, u32[]{:S(2)}, u32[]{:S(2)}) collective-permute-start(bf16[2,32,3072]{2,1,0:T(8,128)(2,1)S(1)} %get-tuple-element.70), channel_id=1, source_target_pairs={{0,8},{8,0},{16,24},{24,16},{1,9},{9,1},{17,25},{25,17},{2,10},{10... | collective-permute-start | bytes 1179656 | tf_op jit(solution)/shard_map/ppermute | solution.py:309
  25.1 9.4 %collective-permute-start.8 = (bf16[16,3072]{1,0:T(8,128)(2,1)S(1)}, bf16[16,3072]{1,0:T(8,128)(2,1)S(1)}, u32[]{:S(2)}, u32[]{:S(2)}) collective-permute-start(bf16[16,3072]{1,0:T(8,128)(2,1)S(1)} %copy-done), channel_id=1, source_target_pairs={{0,6},{1,7},{2,0},{3,1},{4,2},{5,3},{6,4},{7,5},{8,14},{9,15},{10,... | collective-permute-start | bytes 294920 | tf_op jit(solution)/shard_map/ppermute | solution.py:314
  31.2 9.7 %collective-permute-start.6 = (bf16[16,3072]{1,0:T(8,128)(2,1)S(1)}, bf16[16,3072]{1,0:T(8,128)(2,1)S(1)}, u32[]{:S(2)}, u32[]{:S(2)}) collective-permute-start(bf16[16,3072]{1,0:T(8,128)(2,1)S(1)} %copy-done), channel_id=1, source_target_pairs={{0,4},{1,5},{2,6},{3,7},{4,0},{5,1},{6,2},{7,3},{8,12},{9,13},{10,... | collective-permute-start | bytes 294920 | tf_op jit(solution)/shard_map/ppermute | solution.py:314
  31.3 10.0 %collective-permute-start.4 = (bf16[16,3072]{1,0:T(8,128)(2,1)S(1)}, bf16[16,3072]{1,0:T(8,128)(2,1)S(1)}, u32[]{:S(2)}, u32[]{:S(2)}) collective-permute-start(bf16[16,3072]{1,0:T(8,128)(2,1)S(1)} %copy-done), channel_id=1, source_target_pairs={{0,2},{1,3},{2,4},{3,5},{4,6},{5,7},{6,0},{7,1},{8,10},{9,11},{10,... | collective-permute-start | bytes 294920 | tf_op jit(solution)/shard_map/ppermute | solution.py:314
  31.9 13.3 %collective-permute-start.3 = (bf16[16,3072]{1,0:T(8,128)(2,1)S(1)}, bf16[16,3072]{1,0:T(8,128)(2,1)S(1)}, u32[]{:S(2)}, u32[]{:S(2)}) collective-permute-start(bf16[16,3072]{1,0:T(8,128)(2,1)S(1)} %copy-done), channel_id=1, source_target_pairs={{0,1},{1,0},{2,3},{3,2},{4,5},{5,4},{6,7},{7,6},{8,9},{9,8},{10,11... | collective-permute-start | bytes 294920 | tf_op jit(solution)/shard_map/ppermute | solution.py:309
  34.5 10.7 %collective-permute-start.9 = (bf16[16,3072]{1,0:T(8,128)(2,1)S(1)}, bf16[16,3072]{1,0:T(8,128)(2,1)S(1)}, u32[]{:S(2)}, u32[]{:S(2)}) collective-permute-start(bf16[16,3072]{1,0:T(8,128)(2,1)S(1)} %collective-permute-done.8.refs_6_.refs_10_), channel_id=1, source_target_pairs={{0,1},{1,0},{2,3},{3,2},{4,5},{5,4},{6,7},{7,6},{8,9},{9,8},{10,11... | collective-permute-start | bytes 294920 | tf_op jit(solution)/shard_map/ppermute | solution.py:309
  41.0 5.7 %collective-permute-start.7 = (bf16[16,3072]{1,0:T(8,128)(2,1)S(1)}, bf16[16,3072]{1,0:T(8,128)(2,1)S(1)}, u32[]{:S(2)}, u32[]{:S(2)}) collective-permute-start(bf16[16,3072]{1,0:T(8,128)(2,1)S(1)} %collective-permute-done.6.refs_4_.refs_8_), channel_id=1, source_target_pairs={{0,1},{1,0},{2,3},{3,2},{4,5},{5,4},{6,7},{7,6},{8,9},{9,8},{10,11... | collective-permute-start | bytes 294920 | tf_op jit(solution)/shard_map/ppermute | solution.py:309
  41.2 6.6 %collective-permute-start.5 = (bf16[16,3072]{1,0:T(8,128)(2,1)S(1)}, bf16[16,3072]{1,0:T(8,128)(2,1)S(1)}, u32[]{:S(2)}, u32[]{:S(2)}) collective-permute-start(bf16[16,3072]{1,0:T(8,128)(2,1)S(1)} %collective-permute-done.4.refs_2_.refs_6_), channel_id=1, source_target_pairs={{0,1},{1,0},{2,3},{3,2},{4,5},{5,4},{6,7},{7,6},{8,9},{9,8},{10,11... | collective-permute-start | bytes 294920 | tf_op jit(solution)/shard_map/ppermute | solution.py:309
  43.0 8.1 %collective-permute-start.15 = (bf16[32,3072]{1,0:T(8,128)(2,1)S(1)}, bf16[32,3072]{1,0:T(8,128)(2,1)S(1)}, u32[]{:S(2)}, u32[]{:S(2)}) collective-permute-start(bf16[32,3072]{1,0:T(8,128)(2,1)S(1)} %fusion.7), channel_id=1, source_target_pairs={{0,16},{8,24},{16,0},{24,8},{1,17},{9,25},{17,1},{25,9},{2,18},{10... | collective-permute-start | bytes 589832 | tf_op jit(solution)/shard_map/ppermute | solution.py:314
  51.0 1.8 %collective-permute-start.19 = (bf16[2,32,3072]{2,1,0:T(8,128)(2,1)S(1)}, bf16[2,32,3072]{2,1,0:T(8,128)(2,1)S(1)}, u32[]{:S(2)}, u32[]{:S(2)}) collective-permute-start(bf16[2,32,3072]{2,1,0:T(8,128)(2,1)S(1)} %get-tuple-element.84), channel_id=1, source_target_pairs={{0,8},{8,0},{16,24},{24,16},{1,9},{9,1},{17,25},{25,17},{2,10},{10... | collective-permute-start | bytes 1179656 | tf_op jit(solution)/shard_map/ppermute | solution.py:309
  51.4 9.0 %collective-permute-start.17 = (bf16[32,3072]{1,0:T(8,128)(2,1)S(1)}, bf16[32,3072]{1,0:T(8,128)(2,1)S(1)}, u32[]{:S(2)}, u32[]{:S(2)}) collective-permute-start(bf16[32,3072]{1,0:T(8,128)(2,1)S(1)} %multiply_convert_fusion.refs_0_), channel_id=1, source_target_pairs={{0,16},{8,24},{16,0},{24,8},{1,17},{9,25},{17,1},{25,9},{2,18},{10... | collective-permute-start | bytes 589832 | tf_op jit(solution)/shard_map/ppermute | solution.py:314
  52.9 10.0 %collective-permute-start.20 = (bf16[32,3072]{1,0:T(8,128)(2,1)S(1)}, bf16[32,3072]{1,0:T(8,128)(2,1)S(1)}, u32[]{:S(2)}, u32[]{:S(2)}) collective-permute-start(bf16[32,3072]{1,0:T(8,128)(2,1)S(1)} %fusion.8), channel_id=1, source_target_pairs={{0,16},{8,24},{16,0},{24,8},{1,17},{9,25},{17,1},{25,9},{2,18},{10... | collective-permute-start | bytes 589832 | tf_op jit(solution)/shard_map/ppermute | solution.py:314
  60.3 3.3 %collective-permute-start.16 = (bf16[32,3072]{1,0:T(8,128)(2,1)S(1)}, bf16[32,3072]{1,0:T(8,128)(2,1)S(1)}, u32[]{:S(2)}, u32[]{:S(2)}) collective-permute-start(bf16[32,3072]{1,0:T(8,128)(2,1)S(1)} %multiply_convert_fusion.refs_0_), channel_id=1, source_target_pairs={{0,8},{8,0},{16,24},{24,16},{1,9},{9,1},{17,25},{25,17},{2,10},{10... | collective-permute-start | bytes 589832 | tf_op jit(solution)/shard_map/ppermute | solution.py:309
  60.4 3.2 %collective-permute-start.18 = (bf16[32,3072]{1,0:T(8,128)(2,1)S(1)}, bf16[32,3072]{1,0:T(8,128)(2,1)S(1)}, u32[]{:S(2)}, u32[]{:S(2)}) collective-permute-start(bf16[32,3072]{1,0:T(8,128)(2,1)S(1)} %collective-permute-done.17.refs_2_), channel_id=1, source_target_pairs={{0,8},{8,0},{16,24},{24,16},{1,9},{9,1},{17,25},{25,17},{2,10},{10... | collective-permute-start | bytes 589832 | tf_op jit(solution)/shard_map/ppermute | solution.py:309
  63.3 6.4 %collective-permute-start.23 = (bf16[32,3072]{1,0:T(8,128)(2,1)S(1)}, bf16[32,3072]{1,0:T(8,128)(2,1)S(1)}, u32[]{:S(2)}, u32[]{:S(2)}) collective-permute-start(bf16[32,3072]{1,0:T(8,128)(2,1)S(1)} %fusion.6.refs_0_.refs_8_), channel_id=1, source_target_pairs={{0,16},{8,24},{16,0},{24,8},{1,17},{9,25},{17,1},{25,9},{2,18},{10... | collective-permute-start | bytes 589832 | tf_op jit(solution)/shard_map/ppermute | solution.py:314
  68.1 11.7 %collective-permute-start.21 = (bf16[4,16,3072]{2,1,0:T(8,128)(2,1)S(1)}, bf16[4,16,3072]{2,1,0:T(8,128)(2,1)S(1)}, u32[]{:S(2)}, u32[]{:S(2)}) collective-permute-start(bf16[4,16,3072]{2,1,0:T(8,128)(2,1)S(1)} %get-tuple-element.91), channel_id=1, source_target_pairs={{0,1},{1,0},{2,3},{3,2},{4,5},{5,4},{6,7},{7,6},{8,9},{9,8},{10,11... | collective-permute-start | bytes 1179656 | tf_op jit(solution)/shard_map/ppermute | solution.py:309
  69.5 1.5 %collective-permute-start.22 = (bf16[32,3072]{1,0:T(8,128)(2,1)S(1)}, bf16[32,3072]{1,0:T(8,128)(2,1)S(1)}, u32[]{:S(2)}, u32[]{:S(2)}) collective-permute-start(bf16[32,3072]{1,0:T(8,128)(2,1)S(1)} %fusion.6.refs_0_.refs_8_), channel_id=1, source_target_pairs={{0,8},{8,0},{16,24},{24,16},{1,9},{9,1},{17,25},{25,17},{2,10},{10... | collective-permute-start | bytes 589832 | tf_op jit(solution)/shard_map/ppermute | solution.py:309
  69.7 1.5 %collective-permute-start.24 = (bf16[32,3072]{1,0:T(8,128)(2,1)S(1)}, bf16[32,3072]{1,0:T(8,128)(2,1)S(1)}, u32[]{:S(2)}, u32[]{:S(2)}) collective-permute-start(bf16[32,3072]{1,0:T(8,128)(2,1)S(1)} %collective-permute-done.23.refs_2_.refs_10_), channel_id=1, source_target_pairs={{0,8},{8,0},{16,24},{24,16},{1,9},{9,1},{17,25},{25,17},{2,10},{10... | collective-permute-start | bytes 589832 | tf_op jit(solution)/shard_map/ppermute | solution.py:309
  73.1 21.5 %collective-permute-start.28 = (bf16[4,16,3072]{2,1,0:T(8,128)(2,1)S(1)}, bf16[4,16,3072]{2,1,0:T(8,128)(2,1)S(1)}, u32[]{:S(2)}, u32[]{:S(2)}) collective-permute-start(bf16[4,16,3072]{2,1,0:T(8,128)(2,1)S(1)} %get-tuple-element.100), channel_id=1, source_target_pairs={{0,1},{1,0},{2,3},{3,2},{4,5},{5,4},{6,7},{7,6},{8,9},{9,8},{10,11... | collective-permute-start | bytes 1179656 | tf_op jit(solution)/shard_map/ppermute | solution.py:309
  79.9 13.9 %collective-permute-start.25 = (bf16[16,3072]{1,0:T(8,128)(2,1)S(1)}, bf16[16,3072]{1,0:T(8,128)(2,1)S(1)}, u32[]{:S(2)}, u32[]{:S(2)}) collective-permute-start(bf16[16,3072]{1,0:T(8,128)(2,1)S(1)} %get-tuple-element.113), channel_id=1, source_target_pairs={{0,6},{1,7},{2,0},{3,1},{4,2},{5,3},{6,4},{7,5},{8,14},{9,15},{10,... | collective-permute-start | bytes 294920 | tf_op jit(solution)/shard_map/ppermute | solution.py:314
  81.7 12.1 %collective-permute-start.27 = (bf16[16,3072]{1,0:T(8,128)(2,1)S(1)}, bf16[16,3072]{1,0:T(8,128)(2,1)S(1)}, u32[]{:S(2)}, u32[]{:S(2)}) collective-permute-start(bf16[16,3072]{1,0:T(8,128)(2,1)S(1)} %get-tuple-element.114), channel_id=1, source_target_pairs={{0,2},{1,3},{2,4},{3,5},{4,6},{5,7},{6,0},{7,1},{8,10},{9,11},{10,... | collective-permute-start | bytes 294920 | tf_op jit(solution)/shard_map/ppermute | solution.py:314
  82.0 11.8 %collective-permute-start.26 = (bf16[16,3072]{1,0:T(8,128)(2,1)S(1)}, bf16[16,3072]{1,0:T(8,128)(2,1)S(1)}, u32[]{:S(2)}, u32[]{:S(2)}) collective-permute-start(bf16[16,3072]{1,0:T(8,128)(2,1)S(1)} %get-tuple-element.115), channel_id=1, source_target_pairs={{0,4},{1,5},{2,6},{3,7},{4,0},{5,1},{6,2},{7,3},{8,12},{9,13},{10,... | collective-permute-start | bytes 294920 | tf_op jit(solution)/shard_map/ppermute | solution.py:314
  94.6 11.3 %collective-permute-start.29 = (bf16[16,3072]{1,0:T(8,128)(2,1)S(1)}, bf16[16,3072]{1,0:T(8,128)(2,1)S(1)}, u32[]{:S(2)}, u32[]{:S(2)}) collective-permute-start(bf16[16,3072]{1,0:T(8,128)(2,1)S(1)} %get-tuple-element.110), channel_id=1, source_target_pairs={{0,6},{1,7},{2,0},{3,1},{4,2},{5,3},{6,4},{7,5},{8,14},{9,15},{10,... | collective-permute-start | bytes 294920 | tf_op jit(solution)/shard_map/ppermute | solution.py:314
  95.6 10.3 %collective-permute-start.31 = (bf16[16,3072]{1,0:T(8,128)(2,1)S(1)}, bf16[16,3072]{1,0:T(8,128)(2,1)S(1)}, u32[]{:S(2)}, u32[]{:S(2)}) collective-permute-start(bf16[16,3072]{1,0:T(8,128)(2,1)S(1)} %get-tuple-element.111), channel_id=1, source_target_pairs={{0,2},{1,3},{2,4},{3,5},{4,6},{5,7},{6,0},{7,1},{8,10},{9,11},{10,... | collective-permute-start | bytes 294920 | tf_op jit(solution)/shard_map/ppermute | solution.py:314
  96.7 9.3 %collective-permute-start.30 = (bf16[16,3072]{1,0:T(8,128)(2,1)S(1)}, bf16[16,3072]{1,0:T(8,128)(2,1)S(1)}, u32[]{:S(2)}, u32[]{:S(2)}) collective-permute-start(bf16[16,3072]{1,0:T(8,128)(2,1)S(1)} %get-tuple-element.112), channel_id=1, source_target_pairs={{0,4},{1,5},{2,6},{3,7},{4,0},{5,1},{6,2},{7,3},{8,12},{9,13},{10,... | collective-permute-start | bytes 294920 | tf_op jit(solution)/shard_map/ppermute | solution.py:314

commit v3 on v2

--- a/solution.py
+++ b/solution.py
@@ -42,7 +42,7 @@
 
 
 def pair_tables(jobs, weights=()):
-    cap = jobs[0][0].shape[0]
+    cap = jobs[0][0].shape[-1]
     specs = [job[1:] for job in jobs]
     n, m = len(jobs), len(weights)
     limits = [pair_limit(cap, rows if by_row else cols) for rows, cols, by_row in specs]
@@ -70,7 +70,7 @@
                 entries = []
                 for u in range(step):
                     k = g * step + u
-                    pos = slot_refs[t][k]
+                    pos = slot_refs[t][0, 0, k]
                     filled = pos >= 0
                     safe = jnp.maximum(pos, 0)
                     row = (safe * (-(-65536 // cols))) >> 16
@@ -216,24 +216,24 @@
     )(table, in_arr, out_arr, *pieces, blocks, *stage)
 
 
-def block_grads(left, left_rows, right, right_rows, rows, cols, cap):
-    width = 128
+def block_grads(left, left_rows, right, right_rows, slots, part=0, parts=1, base=None):
+    width, cap = 128, slots.shape[-1]
     n_left, n_right = left[0].shape[1] // width, right[0].shape[1] // width
     tokens = sum(piece.shape[0] for piece in left)
     chunk = largest_divisor(cap, 48)
     unroll = chunk
-    steps = cap // chunk
+    steps = cap // chunk // parts
+    skip = part * steps
     n_l, n_r = len(left), len(right)
     dims = (((1,), (0,)), ((), ()))
     zero_rows = jnp.zeros((1,), jnp.int32)
     left_arr = zero_rows if left_rows is None else left_rows
     right_arr = zero_rows if right_rows is None else right_rows
 
-    def body(row_s, col_s, left_s, right_s, *refs):
+    def body(slot_s, left_s, right_s, *refs):
         l_refs = refs[:n_l]
         r_refs = refs[n_l : n_l + n_r]
-        out = refs[n_l + n_r]
-        ls, lt, rs = refs[n_l + n_r + 1 :]
+        out, ls, lt, rs = refs[len(refs) - 4 :]
         step = pl.program_id(0)
 
         @pl.when(step == 0)
@@ -250,24 +250,31 @@
                 lt[b] = ls[b].T
 
         def some(g, carry):
-            base = g * unroll
+            at = g * unroll
             for u in range(unroll):
-                k = step * chunk + base + u
-                out[base + u] = lax.dot_general(
-                    lt[row_s[k]], rs[col_s[k]], dims, preferred_element_type=jnp.float32
+                k = (step + skip) * chunk + at + u
+                pos = slot_s[0, 0, k]
+                safe = jnp.maximum(pos, 0)
+                row = (safe * (-(-65536 // n_right))) >> 16
+                col = jnp.where(pos >= 0, safe - row * n_right, n_right)
+                out[at + u] = lax.dot_general(
+                    lt[row], rs[col], dims, preferred_element_type=jnp.float32
                 )
             return carry
 
         lax.fori_loop(0, chunk // unroll, some, 0)
 
+    extra = [] if base is None else [base]
     whole = lambda shape: pl.BlockSpec(shape, lambda i, *s: (0,) * len(shape))
     return pl.pallas_call(
         body,
         grid_spec=pltpu.PrefetchScalarGridSpec(
-            num_scalar_prefetch=4,
+            num_scalar_prefetch=3,
             grid=(steps,),
-            in_specs=[whole(piece.shape) for piece in left] + [whole(piece.shape) for piece in right],
-            out_specs=pl.BlockSpec((chunk, width, width), lambda i, *s: (i, 0, 0)),
+            in_specs=[whole(piece.shape) for piece in left]
+            + [whole(piece.shape) for piece in right]
+            + [pl.BlockSpec(memory_space=pltpu.HBM)] * len(extra),
+            out_specs=pl.BlockSpec((chunk, width, width), lambda i, *s: (i + skip, 0, 0)),
             scratch_shapes=[
                 pltpu.VMEM((n_left, tokens, width), jnp.bfloat16),
                 pltpu.VMEM((n_left, width, tokens), jnp.bfloat16),
@@ -283,8 +290,9 @@
             bytes_accessed=cap * width * width * 4 + tokens * width * 2 * (n_left + n_right),
             transcendentals=0,
         ),
+        input_output_aliases={3 + n_l + n_r: 0} if extra else {},
         name="block_grads",
-    )(rows, cols, left_arr, right_arr, *left, *right)
+    )(slots, left_arr, right_arr, *left, *right, *extra)
 
 
 def on_device(tokens, in_blocks, in_slots, out_blocks, out_slots, cotangent, *, hidden_total):
@@ -292,8 +300,8 @@
     w_out = out_blocks.reshape(out_blocks.shape[2:])
     w_in = pltpu.with_memory_space_constraint(w_in, pltpu.HBM)
     w_out = pltpu.with_memory_space_constraint(w_out, pltpu.HBM)
-    slots_in = in_slots.reshape(-1)
-    slots_out = out_slots.reshape(-1)
+    slots_in = in_slots
+    slots_out = out_slots.reshape(in_slots.shape)
     width = w_in.shape[-1]
     cap = w_in.shape[0]
     tensor_count = lax.axis_size("tensor")
@@ -319,14 +327,6 @@
     seq_part = (far_of * 2 + (me % 2 + shifts % 2) % 2) * seq_rows
     near_order = jnp.concatenate([seq_part[0::2], seq_part[1::2]])
 
-    def positions(slot_list, cols):
-        filled = slot_list >= 0
-        safe = jnp.where(filled, slot_list, 0)
-        return safe // cols, jnp.where(filled, safe % cols, cols)
-
-    in_row, in_col = positions(slots_in, hid_blocks)
-    out_row, out_col = positions(slots_out, feat_blocks)
-
     def gather_far(own):
         return [own] + [far_move(own, "tensor", tensor_count, k) for k in range(1, far_t)]
 
@@ -373,15 +373,15 @@
     token_rows = [(2 * k + flip) * tensor_rows for flip in range(2) for k in range(far_t)]
 
     tok_far = gather_far(tokens)
-    in_by_col, w_in_near = pair_tables([(slots_in, feat_blocks, hid_blocks, False)], [w_in])
+    in_by_col, out_by_row, w_in_near = pair_tables(
+        [(in_slots, feat_blocks, hid_blocks, False), (slots_out, hid_blocks, feat_blocks, True)],
+        [w_in],
+    )
     cot_far = gather_far(cotangent)
     tok = gather_near(tok_far)
     cot = gather_near(cot_far)
-    out_by_row, w_out_near = pair_tables(
-        [(after(slots_out, tok_far[1:]), hid_blocks, feat_blocks, True)], [w_out]
-    )
-    keep_h, send_h = block_product(
-        after(tok, out_by_row), None, w_in_near, in_by_col, hid_blocks, hidden_lengths, near_order, False
+    keep_h, send_h, w_out_near = block_product(
+        tok, None, w_in_near, in_by_col, hid_blocks, hidden_lengths, near_order, False, [w_out]
     )
     own_h, pairs_h = pair_hidden(keep_h, send_h)
     keep_g, send_g = block_product(
@@ -393,10 +393,10 @@
     )
     hidden = total_hidden(own_h, pairs_h)
     own_act = gelu_value(hidden).astype(jnp.bfloat16)
-    act_far = spread_far(own_act)
+    own_g, pairs_g = pair_hidden(keep_g, send_g)
+    act_far = spread_far(after(own_act, pairs_g))
     activated = spread_near(act_far)
-    own_g, pairs_g = pair_hidden(keep_g, send_g)
-    grad_act = total_hidden(own_g, pairs_g, own_act)
+    grad_act = total_hidden(own_g, pairs_g, own_act, out_by_col)
     own_gh = (grad_act * gelu_slope(hidden)).astype(jnp.bfloat16)
     gh_far = spread_far(own_gh)
     grad_hidden = spread_near(gh_far)
@@ -417,10 +417,16 @@
         after(grad_hidden, keep_o), seq_part, w_in_near, in_by_row, feat_blocks, token_lengths, token_rows, True
     )
     got_t = near_move(send_t, "tensor", tensor_count)
-    own_o, pairs_o = pair_out(keep_o, after(got_o, keep_t))
-    grad_out = block_grads(after(activated, pairs_o), seq_part, cot, None, out_row, out_col, cap)
+    parts = 2 if cap % 96 == 0 else 1
+    act_t = after(activated, keep_t)
+    grad_out = block_grads(act_t, seq_part, cot, None, slots_out, 0, parts)
+    own_o, pairs_o = pair_out(keep_o, after(got_o, grad_out))
+    for part in range(1, parts):
+        grad_out = block_grads(
+            after(act_t, pairs_o), seq_part, cot, None, slots_out, part, parts, grad_out
+        )
     own_t, pairs_t = pair_out(keep_t, after(got_t, grad_out))
-    grad_in = block_grads(tok, None, after(grad_hidden, pairs_t), seq_part, in_row, in_col, cap)
+    grad_in = block_grads(tok, None, after(grad_hidden, pairs_t), seq_part, slots_in)
     output = total_out(own_o, pairs_o)
     grad_tokens = total_out(own_t, pairs_t)
     return (

time: 107 us -> 115 us (1.075)
  the two profiles are of different devices: /device:TPU:0 before, /device:TPU:1 now
where the time goes in v3:
time: 115 us; the launch traced here: 114 us
  Pallas kernels  49.3 us (43%)
  starting transfers between devices  39.6 us (34%)
  waiting for transfers between devices  20.3 us (18%)
  other arithmetic  2.32 us (2%)
  local copies, waits for them, and re-layouts  1.57 us (1%)
    ppermute x16, starting transfers between devices, far_move(): return lax.ppermute(v, axis, pairs)  24 us
    pallas_call x3, Pallas kernels, block_grads(): pl.pallas_call(body, grid_spec=pltpu.PrefetchScalarGridSpec(num_scalar_pr...  19.8 us
    pallas_call x4, Pallas kernels, block_product(): pl.pallas_call(body, in_specs=[smem] * 3 + [vmem] * (n_in + 1) + [pl.Bloc...  16.1 us
    ppermute x16, starting transfers between devices, near_move(): return lax.ppermute(v, axis, [(i, i ^ 1) for i in range(count)])  15.6 us
    pallas_call x2, Pallas kernels, pair_tables(): pl.pallas_call(body, in_specs=[smem] * n + [pl.BlockSpec(memory_space=plt...  13.5 us
    ppermute x16, waiting for transfers between devices, far_move(): return lax.ppermute(v, axis, pairs)  12.4 us
    ppermute x16, waiting for transfers between devices, near_move(): return lax.ppermute(v, axis, [(i, i ^ 1) for i in range(count)])  7.89 us
  transfers between devices with their start and end apart: 32, of which 11 were waited for; matrix products, arithmetic and copies ran while one was open for 1% of the time, Pallas kernels for 40%

profile of v3, /device:TPU:1, one launch (start us, length us, event | category | flops | bytes accessed | tf_op | source)
XLA Modules:
  0.0 113.9 jit_solution(15625808922073508041)
XLA Ops:
  0.6 2.1 %collective-permute-start.7 = (bf16[16,3072]{1,0:T(8,128)(2,1)}, bf16[16,3072]{1,0:T(8,128)(2,1)S(1)}, u32[]{:S(2)}, u32[]{:S(2)}) collective-permute-start(bf16[16,3072]{1,0:T(8,128)(2,1)} %refs_0_.7), channel_id=1, source_target_pairs={{0,1},{1,0},{2,3},{3,2},{4,5},{5,4},{6,7},{7,6},{8,9},{9,8},{10,11... | collective-permute-start | bytes 294920 | tf_op jit(solution)/shard_map/ppermute | solution.py:317
  2.7 1.3 %collective-permute-start.8 = (bf16[16,3072]{1,0:T(8,128)(2,1)}, bf16[16,3072]{1,0:T(8,128)(2,1)S(1)}, u32[]{:S(2)}, u32[]{:S(2)}) collective-permute-start(bf16[16,3072]{1,0:T(8,128)(2,1)} %refs_0_.7), channel_id=1, source_target_pairs={{0,2},{1,3},{2,4},{3,5},{4,6},{5,7},{6,0},{7,1},{8,10},{9,11},{10,... | collective-permute-start | bytes 294920 | tf_op jit(solution)/shard_map/ppermute | solution.py:322
  4.0 2.3 %collective-permute-start.10 = (bf16[16,3072]{1,0:T(8,128)(2,1)}, bf16[16,3072]{1,0:T(8,128)(2,1)S(1)}, u32[]{:S(2)}, u32[]{:S(2)}) collective-permute-start(bf16[16,3072]{1,0:T(8,128)(2,1)} %refs_0_.7), channel_id=1, source_target_pairs={{0,4},{1,5},{2,6},{3,7},{4,0},{5,1},{6,2},{7,3},{8,12},{9,13},{10,... | collective-permute-start | bytes 294920 | tf_op jit(solution)/shard_map/ppermute | solution.py:322
  6.3 1.1 collective-permute-start.12
  7.6 0.7 copy-done.2
  8.3 0.7 copy-done.4
  9.0 6.8 %pair_tables.2 = (s32[521]{0:T(1024)S(1)}, s32[521]{0:T(1024)S(1)}, bf16[288,128,128]{2,1,0:T(8,128)(2,1)S(1)}) custom-call(s32[1,1,288]{2,1,0:T(1,128)S(1)} %copy-done.4, s32[1,1,288]{2,1,0:T(1,128)S(1)} %copy-done.2, bf16[288,128,128]{2,1,0:T(8,128)(2,1)} %bitcast.47), custom_call_target="tpu_custom_call" | custom-call | tf_op jit(solution)/shard_map/pair_tables/pallas_call | solution.py:113
  16.1 1.2 %collective-permute-start.11 = (bf16[16,3072]{1,0:T(8,128)(2,1)S(1)}, bf16[16,3072]{1,0:T(8,128)(2,1)S(1)}, u32[]{:S(2)}, u32[]{:S(2)}) collective-permute-start(bf16[16,3072]{1,0:T(8,128)(2,1)S(1)} %collective-permute-done.10.refs_4_), channel_id=1, source_target_pairs={{0,1},{1,0},{2,3},{3,2},{4,5},{5,4},{6,7},{7,6},{8,9},{9,8},{10,11... | collective-permute-start | bytes 294920 | tf_op jit(solution)/shard_map/ppermute | solution.py:317
  17.6 1.7 %collective-permute-done.9.refs_3_ = bf16[16,3072]{1,0:T(8,128)(2,1)S(1)} collective-permute-done((bf16[16,3072]{1,0:T(8,128)(2,1)S(1)}, bf16[16,3072]{1,0:T(8,128)(2,1)S(1)}, u32[]{:S(2)}, u32[]{:S(2)}) %collective-permute-start.9) | collective-permute-done | bytes 98336 | tf_op jit(solution)/shard_map/ppermute | solution.py:317
  19.3 1.1 collective-permute-done.11.refs_5_
  20.3 2.2 %collective-permute-done.13.refs_7_ = bf16[16,3072]{1,0:T(8,128)(2,1)S(1)} collective-permute-done((bf16[16,3072]{1,0:T(8,128)(2,1)S(1)}, bf16[16,3072]{1,0:T(8,128)(2,1)S(1)}, u32[]{:S(2)}, u32[]{:S(2)}) %collective-permute-start.13) | collective-permute-done | bytes 98336 | tf_op jit(solution)/shard_map/ppermute | solution.py:317
  22.6 4.3 %block_product.4 = (bf16[2,32,3072]{2,1,0:T(8,128)(2,1)S(1)}, bf16[2,32,3072]{2,1,0:T(8,128)(2,1)S(1)}, bf16[288,128,128]{2,1,0:T(8,128)(2,1)S(1)}) custom-call(s32[521]{0:T(1024)S(1)} %get-tuple-element.54.table_s, s32[1]{0:T(128)} %constant.62.clone.1.in_s.out_s.right_s.left_s, s32[4]{0:T(128)S(1)} %pad_add_fusion.out_s, bf16[16,3072]{1,0:T(8,128)(2,1)S(1)} %copy-done.1, ...), custom_call_target="tpu_custom_call" | custom-call | flops 1207959552 | bytes 11010048 | tf_op jit(solution)/shard_map/block_product/pallas_call | solution.py:198
  26.9 2.7 %collective-permute-start.14 = (bf16[2,32,3072]{2,1,0:T(8,128)(2,1)S(1)}, bf16[2,32,3072]{2,1,0:T(8,128)(2,1)S(1)}, u32[]{:S(2)}, u32[]{:S(2)}) collective-permute-start(bf16[2,32,3072]{2,1,0:T(8,128)(2,1)S(1)} %get-tuple-element.57), channel_id=1, source_target_pairs={{0,8},{8,0},{16,24},{24,16},{1,9},{9,1},{17,25},{25,17},{2,10},{10... | collective-permute-start | bytes 1179656 | tf_op jit(solution)/shard_map/ppermute | solution.py:317
  30.0 1.3 %collective-permute-start.3 = (bf16[16,3072]{1,0:T(8,128)(2,1)S(1)}, bf16[16,3072]{1,0:T(8,128)(2,1)S(1)}, u32[]{:S(2)}, u32[]{:S(2)}) collective-permute-start(bf16[16,3072]{1,0:T(8,128)(2,1)S(1)} %copy-done), channel_id=1, source_target_pairs={{0,4},{1,5},{2,6},{3,7},{4,0},{5,1},{6,2},{7,3},{8,12},{9,13},{10,... | collective-permute-start | bytes 294920 | tf_op jit(solution)/shard_map/ppermute | solution.py:322
  31.3 1.5 %collective-permute-start.5 = (bf16[16,3072]{1,0:T(8,128)(2,1)S(1)}, bf16[16,3072]{1,0:T(8,128)(2,1)S(1)}, u32[]{:S(2)}, u32[]{:S(2)}) collective-permute-start(bf16[16,3072]{1,0:T(8,128)(2,1)S(1)} %copy-done), channel_id=1, source_target_pairs={{0,6},{1,7},{2,0},{3,1},{4,2},{5,3},{6,4},{7,5},{8,14},{9,15},{10,... | collective-permute-start | bytes 294920 | tf_op jit(solution)/shard_map/ppermute | solution.py:322
  32.9 0.9 collective-permute-start
  33.8 2.0 %collective-permute-done.1.refs_2_.refs_6_ = bf16[16,3072]{1,0:T(8,128)(2,1)S(1)} collective-permute-done((bf16[16,3072]{1,0:T(8,128)(2,1)S(1)}, bf16[16,3072]{1,0:T(8,128)(2,1)S(1)}, u32[]{:S(2)}, u32[]{:S(2)}) %collective-permute-start.1) | collective-permute-done | bytes 98336 | tf_op jit(solution)/shard_map/ppermute | solution.py:322
  35.7 0.4 collective-permute-start.2
  36.2 3.2 %collective-permute-done.3.refs_4_.refs_8_ = bf16[16,3072]{1,0:T(8,128)(2,1)S(1)} collective-permute-done((bf16[16,3072]{1,0:T(8,128)(2,1)S(1)}, bf16[16,3072]{1,0:T(8,128)(2,1)S(1)}, u32[]{:S(2)}, u32[]{:S(2)}) %collective-permute-start.3) | collective-permute-done | bytes 98336 | tf_op jit(solution)/shard_map/ppermute | solution.py:322
  39.8 1.0 collective-permute-start.6
  40.9 2.3 %collective-permute-start.15 = (bf16[32,3072]{1,0:T(8,128)(2,1)S(1)}, bf16[32,3072]{1,0:T(8,128)(2,1)S(1)}, u32[]{:S(2)}, u32[]{:S(2)}) collective-permute-start(bf16[32,3072]{1,0:T(8,128)(2,1)S(1)} %fusion.7), channel_id=1, source_target_pairs={{0,16},{8,24},{16,0},{24,8},{1,17},{9,25},{17,1},{25,9},{2,18},{10... | collective-permute-start | bytes 589832 | tf_op jit(solution)/shard_map/ppermute | solution.py:322
  43.2 1.0 collective-permute-done.6.refs_7_.refs_11_
  44.2 4.1 %block_product.5 = (bf16[2,32,3072]{2,1,0:T(8,128)(2,1)S(1)}, bf16[2,32,3072]{2,1,0:T(8,128)(2,1)S(1)}) custom-call(s32[521]{0:T(1024)S(1)} %get-tuple-element.53.table_s, s32[1]{0:T(128)} %constant.62.clone.1.in_s.out_s.right_s.left_s, s32[4]{0:T(128)S(1)} %pad_add_fusion.out_s, bf16[16,3072]{1,0:T(8,128)(2,1)S(1)} %copy-done, ...), custom_call_target="tpu_custom_call" | custom-call | flops 1207959552 | bytes 11010048 | tf_op jit(solution)/shard_map/block_product/pallas_call | solution.py:198
  48.3 1.6 %collective-permute-start.16 = (bf16[2,32,3072]{2,1,0:T(8,128)(2,1)S(1)}, bf16[2,32,3072]{2,1,0:T(8,128)(2,1)S(1)}, u32[]{:S(2)}, u32[]{:S(2)}) collective-permute-start(bf16[2,32,3072]{2,1,0:T(8,128)(2,1)S(1)} %get-tuple-element.71), channel_id=1, source_target_pairs={{0,8},{8,0},{16,24},{24,16},{1,9},{9,1},{17,25},{25,17},{2,10},{10... | collective-permute-start | bytes 1179656 | tf_op jit(solution)/shard_map/ppermute | solution.py:317
  50.1 1.1 %collective-permute-done.16 = bf16[2,32,3072]{2,1,0:T(8,128)(2,1)S(1)} collective-permute-done((bf16[2,32,3072]{2,1,0:T(8,128)(2,1)S(1)}, bf16[2,32,3072]{2,1,0:T(8,128)(2,1)S(1)}, u32[]{:S(2)}, u32[]{:S(2)}) %collective-permute-start.16) | collective-permute-done | bytes 393248 | tf_op jit(solution)/shard_map/ppermute | solution.py:317
  51.3 1.0 collective-permute-start.20
  52.3 0.6 collective-permute-start.18
  52.9 6.7 %pair_tables.3 = (s32[521]{0:T(1024)S(1)}, s32[521]{0:T(1024)S(1)}) custom-call(s32[1,1,288]{2,1,0:T(1,128)S(1)} %copy-done.3, s32[1,1,288]{2,1,0:T(1,128)S(1)} %copy-done.5), custom_call_target="tpu_custom_call" | custom-call | tf_op jit(solution)/shard_map/pair_tables/pallas_call | solution.py:113
  59.6 1.0 collective-permute-start.17
  60.6 1.1 collective-permute-done.18.refs_2_
  61.7 1.2 %collective-permute-start.19 = (bf16[32,3072]{1,0:T(8,128)(2,1)S(1)}, bf16[32,3072]{1,0:T(8,128)(2,1)S(1)}, u32[]{:S(2)}, u32[]{:S(2)}) collective-permute-start(bf16[32,3072]{1,0:T(8,128)(2,1)S(1)} %collective-permute-done.18.refs_2_), channel_id=1, source_target_pairs={{0,8},{8,0},{16,24},{24,16},{1,9},{9,1},{17,25},{25,17},{2,10},{10... | collective-permute-start | bytes 589832 | tf_op jit(solution)/shard_map/ppermute | solution.py:317
  63.3 1.0 collective-permute-start.23
  64.6 5.3 %collective-permute-done.23.refs_2_.refs_10_ = bf16[32,3072]{1,0:T(8,128)(2,1)S(1)} collective-permute-done((bf16[32,3072]{1,0:T(8,128)(2,1)S(1)}, bf16[32,3072]{1,0:T(8,128)(2,1)S(1)}, u32[]{:S(2)}, u32[]{:S(2)}) %collective-permute-start.23) | collective-permute-done | bytes 196640 | tf_op jit(solution)/shard_map/ppermute | solution.py:322
  69.8 0.9 collective-permute-start.24
  70.7 4.5 %block_product.6 = (bf16[4,16,3072]{2,1,0:T(8,128)(2,1)S(1)}, bf16[4,16,3072]{2,1,0:T(8,128)(2,1)S(1)}, bf16[288,128,128]{2,1,0:T(8,128)(2,1)S(1)}) custom-call(s32[521]{0:T(1024)S(1)} %get-tuple-element.70.table_s, s32[4]{0:T(128)S(1)} %fusion.26.in_s.left_s.right_s, s32[1]{0:T(128)} %constant.62.clone.1.in_s.out_s.right_s.left_s, ...), custom_call_target="tpu_custom_call" | custom-call | flops 1207959552 | bytes 11010048 | tf_op jit(solution)/shard_map/block_product/pallas_call | solution.py:198
  75.2 1.1 collective-permute-start.21
  76.3 3.2 %block_product.7 = (bf16[4,16,3072]{2,1,0:T(8,128)(2,1)S(1)}, bf16[4,16,3072]{2,1,0:T(8,128)(2,1)S(1)}) custom-call(s32[521]{0:T(1024)S(1)} %get-tuple-element.80.table_s, s32[4]{0:T(128)S(1)} %fusion.26.in_s.left_s.right_s, s32[1]{0:T(128)} %constant.62.clone.1.in_s.out_s.right_s.left_s, bf16[32,3072]{1,0:T(8,128)(2,1)S(1)} %fusion.6.refs_0_.refs_8_, ...), custom_call_target="tpu_custom_call" | custom-call | flops 1207959552 | bytes 11010048 | tf_op jit(solution)/shard_map/block_product/pallas_call | solution.py:198
  79.6 5.6 %block_grads.3.refs_12_ = f32[288,128,128]{2,1,0:T(8,128)} custom-call(s32[1,1,288]{2,1,0:T(1,128)S(1)} %copy-done.3, s32[4]{0:T(128)S(1)} %fusion.26.in_s.left_s.right_s, s32[1]{0:T(128)} %constant.62.clone.1.in_s.out_s.right_s.left_s, bf16[32,3072]{1,0:T(8,128)(2,1)S(1)} %multiply_convert_fusion.refs_0_, ...), custom_call_target="tpu_custom_call" | custom-call | flops 1207959552 | bytes 20447232 | tf_op jit(solution)/shard_map/block_grads/pallas_call | solution.py:269
  85.2 0.8 collective-permute-done.21
  86.0 4.4 %collective-permute-start.27 = (bf16[16,3072]{1,0:T(8,128)(2,1)S(1)}, bf16[16,3072]{1,0:T(8,128)(2,1)S(1)}, u32[]{:S(2)}, u32[]{:S(2)}) collective-permute-start(bf16[16,3072]{1,0:T(8,128)(2,1)S(1)} %get-tuple-element.106), channel_id=1, source_target_pairs={{0,2},{1,3},{2,4},{3,5},{4,6},{5,7},{6,0},{7,1},{8,10},{9,11},{10,... | collective-permute-start | bytes 294920 | tf_op jit(solution)/shard_map/ppermute | solution.py:322
  90.5 2.2 %collective-permute-start.25 = (bf16[16,3072]{1,0:T(8,128)(2,1)S(1)}, bf16[16,3072]{1,0:T(8,128)(2,1)S(1)}, u32[]{:S(2)}, u32[]{:S(2)}) collective-permute-start(bf16[16,3072]{1,0:T(8,128)(2,1)S(1)} %get-tuple-element.105), channel_id=1, source_target_pairs={{0,6},{1,7},{2,0},{3,1},{4,2},{5,3},{6,4},{7,5},{8,14},{9,15},{10,... | collective-permute-start | bytes 294920 | tf_op jit(solution)/shard_map/ppermute | solution.py:322
  92.6 5.5 %block_grads.4 = f32[288,128,128]{2,1,0:T(8,128)} custom-call(s32[1,1,288]{2,1,0:T(1,128)S(1)} %copy-done.3, s32[4]{0:T(128)S(1)} %fusion.26.in_s.left_s.right_s, s32[1]{0:T(128)} %constant.62.clone.1.in_s.out_s.right_s.left_s, bf16[32,3072]{1,0:T(8,128)(2,1)S(1)} %multiply_convert_fusion.refs_0_, ...), custom_call_target="tpu_custom_call", output_to_operand_aliasing={{}: (15, {})} | custom-call | flops 1207959552 | bytes 20447232 | tf_op jit(solution)/shard_map/block_grads/pallas_call | solution.py:269
  98.2 0.9 collective-permute-done.26
  99.0 0.7 fusion.14
  99.8 2.5 %collective-permute-start.31 = (bf16[16,3072]{1,0:T(8,128)(2,1)S(1)}, bf16[16,3072]{1,0:T(8,128)(2,1)S(1)}, u32[]{:S(2)}, u32[]{:S(2)}) collective-permute-start(bf16[16,3072]{1,0:T(8,128)(2,1)S(1)} %get-tuple-element.103), channel_id=1, source_target_pairs={{0,2},{1,3},{2,4},{3,5},{4,6},{5,7},{6,0},{7,1},{8,10},{9,11},{10,... | collective-permute-start | bytes 294920 | tf_op jit(solution)/shard_map/ppermute | solution.py:322
  102.3 2.2 %collective-permute-start.29 = (bf16[16,3072]{1,0:T(8,128)(2,1)S(1)}, bf16[16,3072]{1,0:T(8,128)(2,1)S(1)}, u32[]{:S(2)}, u32[]{:S(2)}) collective-permute-start(bf16[16,3072]{1,0:T(8,128)(2,1)S(1)} %get-tuple-element.102), channel_id=1, source_target_pairs={{0,6},{1,7},{2,0},{3,1},{4,2},{5,3},{6,4},{7,5},{8,14},{9,15},{10,... | collective-permute-start | bytes 294920 | tf_op jit(solution)/shard_map/ppermute | solution.py:322
  104.5 8.7 %block_grads.5 = f32[288,128,128]{2,1,0:T(8,128)} custom-call(s32[1,1,288]{2,1,0:T(1,128)S(1)} %copy-done.5, s32[1]{0:T(128)} %constant.62.clone.1.in_s.out_s.right_s.left_s, s32[4]{0:T(128)S(1)} %fusion.26.in_s.left_s.right_s, bf16[16,3072]{1,0:T(8,128)(2,1)S(1)} %copy-done.1, bf16[16,3072]{1,0:T(8,128)(2,1)S(1)} %collective-permute-done.7.refs_1_, ...), custom_call_target="tpu_custom_call" | custom-call | flops 1207959552 | bytes 20447232 | tf_op jit(solution)/shard_map/block_grads/pallas_call | solution.py:269
  113.1 0.7 fusion.11
  (49 shorter events, 2.9 us)
Async XLA Ops:
  0.6 22.0 %copy-start.1 = (bf16[16,3072]{1,0:T(8,128)(2,1)S(1)}, bf16[16,3072]{1,0:T(8,128)(2,1)}, u32[]{:S(2)}) copy-start(bf16[16,3072]{1,0:T(8,128)(2,1)} %refs_0_.7) | copy-start | bytes 294916
  0.6 17.0 %collective-permute-start.7 = (bf16[16,3072]{1,0:T(8,128)(2,1)}, bf16[16,3072]{1,0:T(8,128)(2,1)S(1)}, u32[]{:S(2)}, u32[]{:S(2)}) collective-permute-start(bf16[16,3072]{1,0:T(8,128)(2,1)} %refs_0_.7), channel_id=1, source_target_pairs={{0,1},{1,0},{2,3},{3,2},{4,5},{5,4},{6,7},{7,6},{8,9},{9,8},{10,11... | collective-permute-start | bytes 294920 | tf_op jit(solution)/shard_map/ppermute | solution.py:317
  2.7 13.0 %collective-permute-start.8 = (bf16[16,3072]{1,0:T(8,128)(2,1)}, bf16[16,3072]{1,0:T(8,128)(2,1)S(1)}, u32[]{:S(2)}, u32[]{:S(2)}) collective-permute-start(bf16[16,3072]{1,0:T(8,128)(2,1)} %refs_0_.7), channel_id=1, source_target_pairs={{0,2},{1,3},{2,4},{3,5},{4,6},{5,7},{6,0},{7,1},{8,10},{9,11},{10,... | collective-permute-start | bytes 294920 | tf_op jit(solution)/shard_map/ppermute | solution.py:322
  4.0 12.1 %collective-permute-start.10 = (bf16[16,3072]{1,0:T(8,128)(2,1)}, bf16[16,3072]{1,0:T(8,128)(2,1)S(1)}, u32[]{:S(2)}, u32[]{:S(2)}) collective-permute-start(bf16[16,3072]{1,0:T(8,128)(2,1)} %refs_0_.7), channel_id=1, source_target_pairs={{0,4},{1,5},{2,6},{3,7},{4,0},{5,1},{6,2},{7,3},{8,12},{9,13},{10,... | collective-permute-start | bytes 294920 | tf_op jit(solution)/shard_map/ppermute | solution.py:322
  6.3 11.0 %collective-permute-start.12 = (bf16[16,3072]{1,0:T(8,128)(2,1)}, bf16[16,3072]{1,0:T(8,128)(2,1)S(1)}, u32[]{:S(2)}, u32[]{:S(2)}) collective-permute-start(bf16[16,3072]{1,0:T(8,128)(2,1)} %refs_0_.7), channel_id=1, source_target_pairs={{0,6},{1,7},{2,0},{3,1},{4,2},{5,3},{6,4},{7,5},{8,14},{9,15},{10,... | collective-permute-start | bytes 294920 | tf_op jit(solution)/shard_map/ppermute | solution.py:322
  7.6 0.7 copy-start.2
  8.3 0.7 copy-start.4
  15.8 3.5 %collective-permute-start.9 = (bf16[16,3072]{1,0:T(8,128)(2,1)S(1)}, bf16[16,3072]{1,0:T(8,128)(2,1)S(1)}, u32[]{:S(2)}, u32[]{:S(2)}) collective-permute-start(bf16[16,3072]{1,0:T(8,128)(2,1)S(1)} %collective-permute-done.8.refs_2_), channel_id=1, source_target_pairs={{0,1},{1,0},{2,3},{3,2},{4,5},{5,4},{6,7},{7,6},{8,9},{9,8},{10,11... | collective-permute-start | bytes 294920 | tf_op jit(solution)/shard_map/ppermute | solution.py:317
  16.1 4.3 %collective-permute-start.11 = (bf16[16,3072]{1,0:T(8,128)(2,1)S(1)}, bf16[16,3072]{1,0:T(8,128)(2,1)S(1)}, u32[]{:S(2)}, u32[]{:S(2)}) collective-permute-start(bf16[16,3072]{1,0:T(8,128)(2,1)S(1)} %collective-permute-done.10.refs_4_), channel_id=1, source_target_pairs={{0,1},{1,0},{2,3},{3,2},{4,5},{5,4},{6,7},{7,6},{8,9},{9,8},{10,11... | collective-permute-start | bytes 294920 | tf_op jit(solution)/shard_map/ppermute | solution.py:317
  17.3 5.3 %collective-permute-start.13 = (bf16[16,3072]{1,0:T(8,128)(2,1)S(1)}, bf16[16,3072]{1,0:T(8,128)(2,1)S(1)}, u32[]{:S(2)}, u32[]{:S(2)}) collective-permute-start(bf16[16,3072]{1,0:T(8,128)(2,1)S(1)} %collective-permute-done.12.refs_6_), channel_id=1, source_target_pairs={{0,1},{1,0},{2,3},{3,2},{4,5},{5,4},{6,7},{7,6},{8,9},{9,8},{10,11... | collective-permute-start | bytes 294920 | tf_op jit(solution)/shard_map/ppermute | solution.py:317
  22.6 7.0 %copy-start = (bf16[16,3072]{1,0:T(8,128)(2,1)S(1)}, bf16[16,3072]{1,0:T(8,128)(2,1)}, u32[]{:S(2)}) copy-start(bf16[16,3072]{1,0:T(8,128)(2,1)} %refs_4_.3) | copy-start | bytes 294916
  26.9 26.0 %copy-start.3 = (s32[1,1,288]{2,1,0:T(1,128)S(1)}, s32[1,1,288]{2,1,0:T(1,128)}, u32[]{:S(2)}) copy-start(s32[1,1,288]{2,1,0:T(1,128)} %slot_s.4) | copy-start | bytes 3460
  26.9 26.0 %copy-start.5 = (s32[1,1,288]{2,1,0:T(1,128)S(1)}, s32[1,1,288]{2,1,0:T(1,128)}, u32[]{:S(2)}) copy-start(s32[1,1,288]{2,1,0:T(1,128)} %slot_s.5) | copy-start | bytes 3460
  26.9 13.9 %collective-permute-start.14 = (bf16[2,32,3072]{2,1,0:T(8,128)(2,1)S(1)}, bf16[2,32,3072]{2,1,0:T(8,128)(2,1)S(1)}, u32[]{:S(2)}, u32[]{:S(2)}) collective-permute-start(bf16[2,32,3072]{2,1,0:T(8,128)(2,1)S(1)} %get-tuple-element.57), channel_id=1, source_target_pairs={{0,8},{8,0},{16,24},{24,16},{1,9},{9,1},{17,25},{25,17},{2,10},{10... | collective-permute-start | bytes 1179656 | tf_op jit(solution)/shard_map/ppermute | solution.py:317
  29.6 6.1 %collective-permute-start.1 = (bf16[16,3072]{1,0:T(8,128)(2,1)S(1)}, bf16[16,3072]{1,0:T(8,128)(2,1)S(1)}, u32[]{:S(2)}, u32[]{:S(2)}) collective-permute-start(bf16[16,3072]{1,0:T(8,128)(2,1)S(1)} %copy-done), channel_id=1, source_target_pairs={{0,2},{1,3},{2,4},{3,5},{4,6},{5,7},{6,0},{7,1},{8,10},{9,11},{10,... | collective-permute-start | bytes 294920 | tf_op jit(solution)/shard_map/ppermute | solution.py:322
  30.0 9.3 %collective-permute-start.3 = (bf16[16,3072]{1,0:T(8,128)(2,1)S(1)}, bf16[16,3072]{1,0:T(8,128)(2,1)S(1)}, u32[]{:S(2)}, u32[]{:S(2)}) collective-permute-start(bf16[16,3072]{1,0:T(8,128)(2,1)S(1)} %copy-done), channel_id=1, source_target_pairs={{0,4},{1,5},{2,6},{3,7},{4,0},{5,1},{6,2},{7,3},{8,12},{9,13},{10,... | collective-permute-start | bytes 294920 | tf_op jit(solution)/shard_map/ppermute | solution.py:322
  31.3 8.4 %collective-permute-start.5 = (bf16[16,3072]{1,0:T(8,128)(2,1)S(1)}, bf16[16,3072]{1,0:T(8,128)(2,1)S(1)}, u32[]{:S(2)}, u32[]{:S(2)}) collective-permute-start(bf16[16,3072]{1,0:T(8,128)(2,1)S(1)} %copy-done), channel_id=1, source_target_pairs={{0,6},{1,7},{2,0},{3,1},{4,2},{5,3},{6,4},{7,5},{8,14},{9,15},{10,... | collective-permute-start | bytes 294920 | tf_op jit(solution)/shard_map/ppermute | solution.py:322
  32.9 10.3 %collective-permute-start = (bf16[16,3072]{1,0:T(8,128)(2,1)S(1)}, bf16[16,3072]{1,0:T(8,128)(2,1)S(1)}, u32[]{:S(2)}, u32[]{:S(2)}) collective-permute-start(bf16[16,3072]{1,0:T(8,128)(2,1)S(1)} %copy-done), channel_id=1, source_target_pairs={{0,1},{1,0},{2,3},{3,2},{4,5},{5,4},{6,7},{7,6},{8,9},{9,8},{10,11... | collective-permute-start | bytes 294920 | tf_op jit(solution)/shard_map/ppermute | solution.py:317
  35.7 7.5 %collective-permute-start.2 = (bf16[16,3072]{1,0:T(8,128)(2,1)S(1)}, bf16[16,3072]{1,0:T(8,128)(2,1)S(1)}, u32[]{:S(2)}, u32[]{:S(2)}) collective-permute-start(bf16[16,3072]{1,0:T(8,128)(2,1)S(1)} %collective-permute-done.1.refs_2_.refs_6_), channel_id=1, source_target_pairs={{0,1},{1,0},{2,3},{3,2},{4,5},{5,4},{6,7},{7,6},{8,9},{9,8},{10,11... | collective-permute-start | bytes 294920 | tf_op jit(solution)/shard_map/ppermute | solution.py:317
  39.3 3.9 %collective-permute-start.4 = (bf16[16,3072]{1,0:T(8,128)(2,1)S(1)}, bf16[16,3072]{1,0:T(8,128)(2,1)S(1)}, u32[]{:S(2)}, u32[]{:S(2)}) collective-permute-start(bf16[16,3072]{1,0:T(8,128)(2,1)S(1)} %collective-permute-done.3.refs_4_.refs_8_), channel_id=1, source_target_pairs={{0,1},{1,0},{2,3},{3,2},{4,5},{5,4},{6,7},{7,6},{8,9},{9,8},{10,11... | collective-permute-start | bytes 294920 | tf_op jit(solution)/shard_map/ppermute | solution.py:317
  39.8 4.4 %collective-permute-start.6 = (bf16[16,3072]{1,0:T(8,128)(2,1)S(1)}, bf16[16,3072]{1,0:T(8,128)(2,1)S(1)}, u32[]{:S(2)}, u32[]{:S(2)}) collective-permute-start(bf16[16,3072]{1,0:T(8,128)(2,1)S(1)} %collective-permute-done.5.refs_6_.refs_10_), channel_id=1, source_target_pairs={{0,1},{1,0},{2,3},{3,2},{4,5},{5,4},{6,7},{7,6},{8,9},{9,8},{10,11... | collective-permute-start | bytes 294920 | tf_op jit(solution)/shard_map/ppermute | solution.py:317
  40.9 9.1 %collective-permute-start.15 = (bf16[32,3072]{1,0:T(8,128)(2,1)S(1)}, bf16[32,3072]{1,0:T(8,128)(2,1)S(1)}, u32[]{:S(2)}, u32[]{:S(2)}) collective-permute-start(bf16[32,3072]{1,0:T(8,128)(2,1)S(1)} %fusion.7), channel_id=1, source_target_pairs={{0,16},{8,24},{16,0},{24,8},{1,17},{9,25},{17,1},{25,9},{2,18},{10... | collective-permute-start | bytes 589832 | tf_op jit(solution)/shard_map/ppermute | solution.py:322
  48.3 3.0 %collective-permute-start.16 = (bf16[2,32,3072]{2,1,0:T(8,128)(2,1)S(1)}, bf16[2,32,3072]{2,1,0:T(8,128)(2,1)S(1)}, u32[]{:S(2)}, u32[]{:S(2)}) collective-permute-start(bf16[2,32,3072]{2,1,0:T(8,128)(2,1)S(1)} %get-tuple-element.71), channel_id=1, source_target_pairs={{0,8},{8,0},{16,24},{24,16},{1,9},{9,1},{17,25},{25,17},{2,10},{10... | collective-permute-start | bytes 1179656 | tf_op jit(solution)/shard_map/ppermute | solution.py:317
  51.3 9.3 %collective-permute-start.20 = (bf16[32,3072]{1,0:T(8,128)(2,1)S(1)}, bf16[32,3072]{1,0:T(8,128)(2,1)S(1)}, u32[]{:S(2)}, u32[]{:S(2)}) collective-permute-start(bf16[32,3072]{1,0:T(8,128)(2,1)S(1)} %fusion.8), channel_id=1, source_target_pairs={{0,16},{8,24},{16,0},{24,8},{1,17},{9,25},{17,1},{25,9},{2,18},{10... | collective-permute-start | bytes 589832 | tf_op jit(solution)/shard_map/ppermute | solution.py:322
  52.3 9.4 %collective-permute-start.18 = (bf16[32,3072]{1,0:T(8,128)(2,1)S(1)}, bf16[32,3072]{1,0:T(8,128)(2,1)S(1)}, u32[]{:S(2)}, u32[]{:S(2)}) collective-permute-start(bf16[32,3072]{1,0:T(8,128)(2,1)S(1)} %multiply_convert_fusion.refs_0_), channel_id=1, source_target_pairs={{0,16},{8,24},{16,0},{24,8},{1,17},{9,25},{17,1},{25,9},{2,18},{10... | collective-permute-start | bytes 589832 | tf_op jit(solution)/shard_map/ppermute | solution.py:322
  59.6 5.0 %collective-permute-start.17 = (bf16[32,3072]{1,0:T(8,128)(2,1)S(1)}, bf16[32,3072]{1,0:T(8,128)(2,1)S(1)}, u32[]{:S(2)}, u32[]{:S(2)}) collective-permute-start(bf16[32,3072]{1,0:T(8,128)(2,1)S(1)} %multiply_convert_fusion.refs_0_), channel_id=1, source_target_pairs={{0,8},{8,0},{16,24},{24,16},{1,9},{9,1},{17,25},{25,17},{2,10},{10... | collective-permute-start | bytes 589832 | tf_op jit(solution)/shard_map/ppermute | solution.py:317
  61.7 2.9 %collective-permute-start.19 = (bf16[32,3072]{1,0:T(8,128)(2,1)S(1)}, bf16[32,3072]{1,0:T(8,128)(2,1)S(1)}, u32[]{:S(2)}, u32[]{:S(2)}) collective-permute-start(bf16[32,3072]{1,0:T(8,128)(2,1)S(1)} %collective-permute-done.18.refs_2_), channel_id=1, source_target_pairs={{0,8},{8,0},{16,24},{24,16},{1,9},{9,1},{17,25},{25,17},{2,10},{10... | collective-permute-start | bytes 589832 | tf_op jit(solution)/shard_map/ppermute | solution.py:317
  63.3 6.5 %collective-permute-start.23 = (bf16[32,3072]{1,0:T(8,128)(2,1)S(1)}, bf16[32,3072]{1,0:T(8,128)(2,1)S(1)}, u32[]{:S(2)}, u32[]{:S(2)}) collective-permute-start(bf16[32,3072]{1,0:T(8,128)(2,1)S(1)} %fusion.6.refs_0_.refs_8_), channel_id=1, source_target_pairs={{0,16},{8,24},{16,0},{24,8},{1,17},{9,25},{17,1},{25,9},{2,18},{10... | collective-permute-start | bytes 589832 | tf_op jit(solution)/shard_map/ppermute | solution.py:322
  64.3 12.0 %collective-permute-start.22 = (bf16[32,3072]{1,0:T(8,128)(2,1)S(1)}, bf16[32,3072]{1,0:T(8,128)(2,1)S(1)}, u32[]{:S(2)}, u32[]{:S(2)}) collective-permute-start(bf16[32,3072]{1,0:T(8,128)(2,1)S(1)} %fusion.6.refs_0_.refs_8_), channel_id=1, source_target_pairs={{0,8},{8,0},{16,24},{24,16},{1,9},{9,1},{17,25},{25,17},{2,10},{10... | collective-permute-start | bytes 589832 | tf_op jit(solution)/shard_map/ppermute | solution.py:317
  69.8 6.5 %collective-permute-start.24 = (bf16[32,3072]{1,0:T(8,128)(2,1)S(1)}, bf16[32,3072]{1,0:T(8,128)(2,1)S(1)}, u32[]{:S(2)}, u32[]{:S(2)}) collective-permute-start(bf16[32,3072]{1,0:T(8,128)(2,1)S(1)} %collective-permute-done.23.refs_2_.refs_10_), channel_id=1, source_target_pairs={{0,8},{8,0},{16,24},{24,16},{1,9},{9,1},{17,25},{25,17},{2,10},{10... | collective-permute-start | bytes 589832 | tf_op jit(solution)/shard_map/ppermute | solution.py:317
  75.2 10.7 %collective-permute-start.21 = (bf16[4,16,3072]{2,1,0:T(8,128)(2,1)S(1)}, bf16[4,16,3072]{2,1,0:T(8,128)(2,1)S(1)}, u32[]{:S(2)}, u32[]{:S(2)}) collective-permute-start(bf16[4,16,3072]{2,1,0:T(8,128)(2,1)S(1)} %get-tuple-element.79), channel_id=1, source_target_pairs={{0,1},{1,0},{2,3},{3,2},{4,5},{5,4},{6,7},{7,6},{8,9},{9,8},{10,11... | collective-permute-start | bytes 1179656 | tf_op jit(solution)/shard_map/ppermute | solution.py:317
  79.5 20.2 %collective-permute-start.28 = (bf16[4,16,3072]{2,1,0:T(8,128)(2,1)S(1)}, bf16[4,16,3072]{2,1,0:T(8,128)(2,1)S(1)}, u32[]{:S(2)}, u32[]{:S(2)}) collective-permute-start(bf16[4,16,3072]{2,1,0:T(8,128)(2,1)S(1)} %get-tuple-element.92), channel_id=1, source_target_pairs={{0,1},{1,0},{2,3},{3,2},{4,5},{5,4},{6,7},{7,6},{8,9},{9,8},{10,11... | collective-permute-start | bytes 1179656 | tf_op jit(solution)/shard_map/ppermute | solution.py:317
  86.0 12.1 %collective-permute-start.27 = (bf16[16,3072]{1,0:T(8,128)(2,1)S(1)}, bf16[16,3072]{1,0:T(8,128)(2,1)S(1)}, u32[]{:S(2)}, u32[]{:S(2)}) collective-permute-start(bf16[16,3072]{1,0:T(8,128)(2,1)S(1)} %get-tuple-element.106), channel_id=1, source_target_pairs={{0,2},{1,3},{2,4},{3,5},{4,6},{5,7},{6,0},{7,1},{8,10},{9,11},{10,... | collective-permute-start | bytes 294920 | tf_op jit(solution)/shard_map/ppermute | solution.py:322
  90.5 8.6 %collective-permute-start.26 = (bf16[16,3072]{1,0:T(8,128)(2,1)S(1)}, bf16[16,3072]{1,0:T(8,128)(2,1)S(1)}, u32[]{:S(2)}, u32[]{:S(2)}) collective-permute-start(bf16[16,3072]{1,0:T(8,128)(2,1)S(1)} %get-tuple-element.107), channel_id=1, source_target_pairs={{0,4},{1,5},{2,6},{3,7},{4,0},{5,1},{6,2},{7,3},{8,12},{9,13},{10,... | collective-permute-start | bytes 294920 | tf_op jit(solution)/shard_map/ppermute | solution.py:322
  90.5 8.6 %collective-permute-start.25 = (bf16[16,3072]{1,0:T(8,128)(2,1)S(1)}, bf16[16,3072]{1,0:T(8,128)(2,1)S(1)}, u32[]{:S(2)}, u32[]{:S(2)}) collective-permute-start(bf16[16,3072]{1,0:T(8,128)(2,1)S(1)} %get-tuple-element.105), channel_id=1, source_target_pairs={{0,6},{1,7},{2,0},{3,1},{4,2},{5,3},{6,4},{7,5},{8,14},{9,15},{10,... | collective-permute-start | bytes 294920 | tf_op jit(solution)/shard_map/ppermute | solution.py:322
  99.8 13.3 %collective-permute-start.31 = (bf16[16,3072]{1,0:T(8,128)(2,1)S(1)}, bf16[16,3072]{1,0:T(8,128)(2,1)S(1)}, u32[]{:S(2)}, u32[]{:S(2)}) collective-permute-start(bf16[16,3072]{1,0:T(8,128)(2,1)S(1)} %get-tuple-element.103), channel_id=1, source_target_pairs={{0,2},{1,3},{2,4},{3,5},{4,6},{5,7},{6,0},{7,1},{8,10},{9,11},{10,... | collective-permute-start | bytes 294920 | tf_op jit(solution)/shard_map/ppermute | solution.py:322
  102.3 10.8 %collective-permute-start.30 = (bf16[16,3072]{1,0:T(8,128)(2,1)S(1)}, bf16[16,3072]{1,0:T(8,128)(2,1)S(1)}, u32[]{:S(2)}, u32[]{:S(2)}) collective-permute-start(bf16[16,3072]{1,0:T(8,128)(2,1)S(1)} %get-tuple-element.104), channel_id=1, source_target_pairs={{0,4},{1,5},{2,6},{3,7},{4,0},{5,1},{6,2},{7,3},{8,12},{9,13},{10,... | collective-permute-start | bytes 294920 | tf_op jit(solution)/shard_map/ppermute | solution.py:322
  102.3 10.8 %collective-permute-start.29 = (bf16[16,3072]{1,0:T(8,128)(2,1)S(1)}, bf16[16,3072]{1,0:T(8,128)(2,1)S(1)}, u32[]{:S(2)}, u32[]{:S(2)}) collective-permute-start(bf16[16,3072]{1,0:T(8,128)(2,1)S(1)} %get-tuple-element.102), channel_id=1, source_target_pairs={{0,6},{1,7},{2,0},{3,1},{4,2},{5,3},{6,4},{7,5},{8,14},{9,15},{10,... | collective-permute-start | bytes 294920 | tf_op jit(solution)/shard_map/ppermute | solution.py:322

commit v4 on v3

--- a/solution.py
+++ b/solution.py
@@ -373,13 +373,13 @@
     token_rows = [(2 * k + flip) * tensor_rows for flip in range(2) for k in range(far_t)]
 
     tok_far = gather_far(tokens)
-    in_by_col, out_by_row, w_in_near = pair_tables(
-        [(in_slots, feat_blocks, hid_blocks, False), (slots_out, hid_blocks, feat_blocks, True)],
-        [w_in],
-    )
     cot_far = gather_far(cotangent)
     tok = gather_near(tok_far)
     cot = gather_near(cot_far)
+    first_in, first_out = after((slots_in, slots_out), tok_far[1:])
+    in_by_col, out_by_row, w_in_near = pair_tables(
+        [(first_in, feat_blocks, hid_blocks, False), (first_out, hid_blocks, feat_blocks, True)], [w_in]
+    )
     keep_h, send_h, w_out_near = block_product(
         tok, None, w_in_near, in_by_col, hid_blocks, hidden_lengths, near_order, False, [w_out]
     )
@@ -395,9 +395,9 @@
     own_act = gelu_value(hidden).astype(jnp.bfloat16)
     own_g, pairs_g = pair_hidden(keep_g, send_g)
     act_far = spread_far(after(own_act, pairs_g))
-    activated = spread_near(act_far)
     grad_act = total_hidden(own_g, pairs_g, own_act, out_by_col)
     own_gh = (grad_act * gelu_slope(hidden)).astype(jnp.bfloat16)
+    activated = spread_near([act_far[0]] + after(act_far[1:], own_gh))
     gh_far = spread_far(own_gh)
     grad_hidden = spread_near(gh_far)
 

time: 115 us -> 122 us (1.061)
  waiting for transfers between devices: 20.3 us -> 27.9 us
  starting transfers between devices: 39.6 us -> 37.8 us
    ppermute x16, waiting for transfers between devices: 12.4 us -> 22.4 us  [far_move(): return lax.ppermute(v, axis, pairs)]
    ppermute x16, starting transfers between devices: 15.6 us -> 12.3 us  [near_move(): return lax.ppermute(v, axis, [(i, i ^ 1) for i in range(count)])]
    ppermute x16, waiting for transfers between devices: 7.89 us -> 5.46 us  [near_move(): return lax.ppermute(v, axis, [(i, i ^ 1) for i in range(count)])]
    ppermute x16, starting transfers between devices: 24 us -> 25.5 us  [far_move(): return lax.ppermute(v, axis, pairs)]
  transfers between devices with their start and end apart: 32 -> 32, of which waited for: 11 -> 10; matrix products, arithmetic and copies ran while one was open for 1% -> 1% of each run, Pallas kernels for 40% -> 34%
where the time goes in v4:
time: 122 us; the launch traced here: 120 us
  Pallas kernels  49.4 us (40%)
  starting transfers between devices  37.8 us (31%)
  waiting for transfers between devices  27.9 us (23%)
  other arithmetic  2.33 us (2%)
  local copies, waits for them, and re-layouts  1.57 us (1%)
    ppermute x16, starting transfers between devices, far_move(): return lax.ppermute(v, axis, pairs)  25.5 us
    ppermute x16, waiting for transfers between devices, far_move(): return lax.ppermute(v, axis, pairs)  22.4 us
    pallas_call x3, Pallas kernels, block_grads(): pl.pallas_call(body, grid_spec=pltpu.PrefetchScalarGridSpec(num_scalar_pr...  19.8 us
    pallas_call x4, Pallas kernels, block_product(): pl.pallas_call(body, in_specs=[smem] * 3 + [vmem] * (n_in + 1) + [pl.Bloc...  16.1 us
    pallas_call x2, Pallas kernels, pair_tables(): pl.pallas_call(body, in_specs=[smem] * n + [pl.BlockSpec(memory_space=plt...  13.5 us
    ppermute x16, starting transfers between devices, near_move(): return lax.ppermute(v, axis, [(i, i ^ 1) for i in range(count)])  12.3 us
    ppermute x16, waiting for transfers between devices, near_move(): return lax.ppermute(v, axis, [(i, i ^ 1) for i in range(count)])  5.46 us
  transfers between devices with their start and end apart: 32, of which 10 were waited for; matrix products, arithmetic and copies ran while one was open for 1% of the time, Pallas kernels for 34%

profile of v4, /device:TPU:1, one launch (start us, length us, event | category | flops | bytes accessed | tf_op | source)
XLA Modules:
  0.0 119.8 jit_solution(9850974904336298395)
XLA Ops:
  0.6 2.2 %collective-permute-start = (bf16[16,3072]{1,0:T(8,128)(2,1)}, bf16[16,3072]{1,0:T(8,128)(2,1)S(1)}, u32[]{:S(2)}, u32[]{:S(2)}) collective-permute-start(bf16[16,3072]{1,0:T(8,128)(2,1)} %refs_0_.6), channel_id=1, source_target_pairs={{0,2},{1,3},{2,4},{3,5},{4,6},{5,7},{6,0},{7,1},{8,10},{9,11},{10,... | collective-permute-start | bytes 294920 | tf_op jit(solution)/shard_map/ppermute | solution.py:322
  2.8 2.3 %collective-permute-start.1 = (bf16[16,3072]{1,0:T(8,128)(2,1)}, bf16[16,3072]{1,0:T(8,128)(2,1)S(1)}, u32[]{:S(2)}, u32[]{:S(2)}) collective-permute-start(bf16[16,3072]{1,0:T(8,128)(2,1)} %refs_0_.6), channel_id=1, source_target_pairs={{0,4},{1,5},{2,6},{3,7},{4,0},{5,1},{6,2},{7,3},{8,12},{9,13},{10,... | collective-permute-start | bytes 294920 | tf_op jit(solution)/shard_map/ppermute | solution.py:322
  5.1 1.1 collective-permute-start.2
  6.2 1.2 %collective-permute-start.10 = (bf16[16,3072]{1,0:T(8,128)(2,1)}, bf16[16,3072]{1,0:T(8,128)(2,1)S(1)}, u32[]{:S(2)}, u32[]{:S(2)}) collective-permute-start(bf16[16,3072]{1,0:T(8,128)(2,1)} %refs_0_.6), channel_id=1, source_target_pairs={{0,1},{1,0},{2,3},{3,2},{4,5},{5,4},{6,7},{7,6},{8,9},{9,8},{10,11... | collective-permute-start | bytes 294920 | tf_op jit(solution)/shard_map/ppermute | solution.py:317
  7.6 0.7 collective-permute-start.11
  8.3 4.2 %collective-permute-done.1.refs_4_ = bf16[16,3072]{1,0:T(8,128)(2,1)S(1)} collective-permute-done((bf16[16,3072]{1,0:T(8,128)(2,1)}, bf16[16,3072]{1,0:T(8,128)(2,1)S(1)}, u32[]{:S(2)}, u32[]{:S(2)}) %collective-permute-start.1) | collective-permute-done | bytes 98336 | tf_op jit(solution)/shard_map/ppermute | solution.py:322
  12.6 1.2 %collective-permute-start.12 = (bf16[16,3072]{1,0:T(8,128)(2,1)S(1)}, bf16[16,3072]{1,0:T(8,128)(2,1)S(1)}, u32[]{:S(2)}, u32[]{:S(2)}) collective-permute-start(bf16[16,3072]{1,0:T(8,128)(2,1)S(1)} %collective-permute-done.1.refs_4_), channel_id=1, source_target_pairs={{0,1},{1,0},{2,3},{3,2},{4,5},{5,4},{6,7},{7,6},{8,9},{9,8},{10,11... | collective-permute-start | bytes 294920 | tf_op jit(solution)/shard_map/ppermute | solution.py:317
  14.1 0.7 copy-done.2
  14.8 0.7 copy-done.4
  15.5 6.8 %pair_tables.2 = (s32[521]{0:T(1024)S(1)}, s32[521]{0:T(1024)S(1)}, bf16[288,128,128]{2,1,0:T(8,128)(2,1)S(1)}) custom-call(s32[1,1,288]{2,1,0:T(1,128)S(1)} %copy-done.4, s32[1,1,288]{2,1,0:T(1,128)S(1)} %copy-done.2, bf16[288,128,128]{2,1,0:T(8,128)(2,1)} %bitcast.47), custom_call_target="tpu_custom_call" | custom-call | tf_op jit(solution)/shard_map/pair_tables/pallas_call | solution.py:113
  22.3 4.3 %block_product.4 = (bf16[2,32,3072]{2,1,0:T(8,128)(2,1)S(1)}, bf16[2,32,3072]{2,1,0:T(8,128)(2,1)S(1)}, bf16[288,128,128]{2,1,0:T(8,128)(2,1)S(1)}) custom-call(s32[521]{0:T(1024)S(1)} %get-tuple-element.59.table_s, s32[1]{0:T(128)} %constant.62.clone.1.in_s.out_s.right_s.left_s, s32[4]{0:T(128)S(1)} %pad_add_fusion.out_s, bf16[16,3072]{1,0:T(8,128)(2,1)S(1)} %copy-done.1, ...), custom_call_target="tpu_custom_call" | custom-call | flops 1207959552 | bytes 11010048 | tf_op jit(solution)/shard_map/block_product/pallas_call | solution.py:198
  26.6 1.2 %collective-permute-start.14 = (bf16[2,32,3072]{2,1,0:T(8,128)(2,1)S(1)}, bf16[2,32,3072]{2,1,0:T(8,128)(2,1)S(1)}, u32[]{:S(2)}, u32[]{:S(2)}) collective-permute-start(bf16[2,32,3072]{2,1,0:T(8,128)(2,1)S(1)} %get-tuple-element.62), channel_id=1, source_target_pairs={{0,8},{8,0},{16,24},{24,16},{1,9},{9,1},{17,25},{25,17},{2,10},{10... | collective-permute-start | bytes 1179656 | tf_op jit(solution)/shard_map/ppermute | solution.py:317
  27.8 1.9 %collective-permute-start.4 = (bf16[16,3072]{1,0:T(8,128)(2,1)S(1)}, bf16[16,3072]{1,0:T(8,128)(2,1)S(1)}, u32[]{:S(2)}, u32[]{:S(2)}) collective-permute-start(bf16[16,3072]{1,0:T(8,128)(2,1)S(1)} %copy-done), channel_id=1, source_target_pairs={{0,2},{1,3},{2,4},{3,5},{4,6},{5,7},{6,0},{7,1},{8,10},{9,11},{10,... | collective-permute-start | bytes 294920 | tf_op jit(solution)/shard_map/ppermute | solution.py:322
  29.7 3.0 %collective-permute-start.6 = (bf16[16,3072]{1,0:T(8,128)(2,1)S(1)}, bf16[16,3072]{1,0:T(8,128)(2,1)S(1)}, u32[]{:S(2)}, u32[]{:S(2)}) collective-permute-start(bf16[16,3072]{1,0:T(8,128)(2,1)S(1)} %copy-done), channel_id=1, source_target_pairs={{0,4},{1,5},{2,6},{3,7},{4,0},{5,1},{6,2},{7,3},{8,12},{9,13},{10,... | collective-permute-start | bytes 294920 | tf_op jit(solution)/shard_map/ppermute | solution.py:322
  32.7 0.4 collective-permute-start.8
  33.1 1.5 %collective-permute-start.3 = (bf16[16,3072]{1,0:T(8,128)(2,1)S(1)}, bf16[16,3072]{1,0:T(8,128)(2,1)S(1)}, u32[]{:S(2)}, u32[]{:S(2)}) collective-permute-start(bf16[16,3072]{1,0:T(8,128)(2,1)S(1)} %copy-done), channel_id=1, source_target_pairs={{0,1},{1,0},{2,3},{3,2},{4,5},{5,4},{6,7},{7,6},{8,9},{9,8},{10,11... | collective-permute-start | bytes 294920 | tf_op jit(solution)/shard_map/ppermute | solution.py:317
  34.6 0.9 collective-permute-done.4.refs_2_.refs_6_
  35.5 4.4 %collective-permute-done.6.refs_4_.refs_8_ = bf16[16,3072]{1,0:T(8,128)(2,1)S(1)} collective-permute-done((bf16[16,3072]{1,0:T(8,128)(2,1)S(1)}, bf16[16,3072]{1,0:T(8,128)(2,1)S(1)}, u32[]{:S(2)}, u32[]{:S(2)}) %collective-permute-start.6) | collective-permute-done | bytes 98336 | tf_op jit(solution)/shard_map/ppermute | solution.py:322
  40.0 1.5 %collective-permute-start.9 = (bf16[16,3072]{1,0:T(8,128)(2,1)S(1)}, bf16[16,3072]{1,0:T(8,128)(2,1)S(1)}, u32[]{:S(2)}, u32[]{:S(2)}) collective-permute-start(bf16[16,3072]{1,0:T(8,128)(2,1)S(1)} %collective-permute-done.8.refs_6_.refs_10_), channel_id=1, source_target_pairs={{0,1},{1,0},{2,3},{3,2},{4,5},{5,4},{6,7},{7,6},{8,9},{9,8},{10,11... | collective-permute-start | bytes 294920 | tf_op jit(solution)/shard_map/ppermute | solution.py:317
  41.5 2.3 %collective-permute-done.7.refs_5_.refs_9_ = bf16[16,3072]{1,0:T(8,128)(2,1)S(1)} collective-permute-done((bf16[16,3072]{1,0:T(8,128)(2,1)S(1)}, bf16[16,3072]{1,0:T(8,128)(2,1)S(1)}, u32[]{:S(2)}, u32[]{:S(2)}) %collective-permute-start.7) | collective-permute-done | bytes 98336 | tf_op jit(solution)/shard_map/ppermute | solution.py:317
  43.8 2.1 %collective-permute-done.9.refs_7_.refs_11_ = bf16[16,3072]{1,0:T(8,128)(2,1)S(1)} collective-permute-done((bf16[16,3072]{1,0:T(8,128)(2,1)S(1)}, bf16[16,3072]{1,0:T(8,128)(2,1)S(1)}, u32[]{:S(2)}, u32[]{:S(2)}) %collective-permute-start.9) | collective-permute-done | bytes 98336 | tf_op jit(solution)/shard_map/ppermute | solution.py:317
  45.9 4.1 %block_product.5 = (bf16[2,32,3072]{2,1,0:T(8,128)(2,1)S(1)}, bf16[2,32,3072]{2,1,0:T(8,128)(2,1)S(1)}) custom-call(s32[521]{0:T(1024)S(1)} %get-tuple-element.58.table_s, s32[1]{0:T(128)} %constant.62.clone.1.in_s.out_s.right_s.left_s, s32[4]{0:T(128)S(1)} %pad_add_fusion.out_s, bf16[16,3072]{1,0:T(8,128)(2,1)S(1)} %copy-done, ...), custom_call_target="tpu_custom_call" | custom-call | flops 1207959552 | bytes 11010048 | tf_op jit(solution)/shard_map/block_product/pallas_call | solution.py:198
  50.0 0.5 collective-permute-start.16
  50.6 6.7 %pair_tables.3 = (s32[521]{0:T(1024)S(1)}, s32[521]{0:T(1024)S(1)}) custom-call(s32[1,1,288]{2,1,0:T(1,128)S(1)} %copy-done.3, s32[1,1,288]{2,1,0:T(1,128)S(1)} %copy-done.5), custom_call_target="tpu_custom_call" | custom-call | tf_op jit(solution)/shard_map/pair_tables/pallas_call | solution.py:113
  57.4 1.5 %collective-permute-start.19 = (bf16[32,3072]{1,0:T(8,128)(2,1)S(1)}, bf16[32,3072]{1,0:T(8,128)(2,1)S(1)}, u32[]{:S(2)}, u32[]{:S(2)}) collective-permute-start(bf16[32,3072]{1,0:T(8,128)(2,1)S(1)} %fusion.8), channel_id=1, source_target_pairs={{0,16},{8,24},{16,0},{24,8},{1,17},{9,25},{17,1},{25,9},{2,18},{10... | collective-permute-start | bytes 589832 | tf_op jit(solution)/shard_map/ppermute | solution.py:322
  59.1 0.7 collective-permute-start.17
  60.0 3.4 %collective-permute-done.19 = bf16[32,3072]{1,0:T(8,128)(2,1)S(1)} collective-permute-done((bf16[32,3072]{1,0:T(8,128)(2,1)S(1)}, bf16[32,3072]{1,0:T(8,128)(2,1)S(1)}, u32[]{:S(2)}, u32[]{:S(2)}) %collective-permute-start.19) | collective-permute-done | bytes 196640 | tf_op jit(solution)/shard_map/ppermute | solution.py:322
  63.4 0.4 fusion.6.refs_0_.refs_8_
  63.8 3.8 %collective-permute-done.18.refs_2_ = bf16[32,3072]{1,0:T(8,128)(2,1)S(1)} collective-permute-done((bf16[32,3072]{1,0:T(8,128)(2,1)S(1)}, bf16[32,3072]{1,0:T(8,128)(2,1)S(1)}, u32[]{:S(2)}, u32[]{:S(2)}) %collective-permute-start.18) | collective-permute-done | bytes 196640 | tf_op jit(solution)/shard_map/ppermute | solution.py:322
  67.6 1.4 %collective-permute-start.20 = (bf16[32,3072]{1,0:T(8,128)(2,1)S(1)}, bf16[32,3072]{1,0:T(8,128)(2,1)S(1)}, u32[]{:S(2)}, u32[]{:S(2)}) collective-permute-start(bf16[32,3072]{1,0:T(8,128)(2,1)S(1)} %collective-permute-done.18.refs_2_), channel_id=1, source_target_pairs={{0,8},{8,0},{16,24},{24,16},{1,9},{9,1},{17,25},{25,17},{2,10},{10... | collective-permute-start | bytes 589832 | tf_op jit(solution)/shard_map/ppermute | solution.py:317
  69.0 1.5 %collective-permute-start.23 = (bf16[32,3072]{1,0:T(8,128)(2,1)S(1)}, bf16[32,3072]{1,0:T(8,128)(2,1)S(1)}, u32[]{:S(2)}, u32[]{:S(2)}) collective-permute-start(bf16[32,3072]{1,0:T(8,128)(2,1)S(1)} %fusion.6.refs_0_.refs_8_), channel_id=1, source_target_pairs={{0,16},{8,24},{16,0},{24,8},{1,17},{9,25},{17,1},{25,9},{2,18},{10... | collective-permute-start | bytes 589832 | tf_op jit(solution)/shard_map/ppermute | solution.py:322
  70.7 4.7 %collective-permute-done.23.refs_2_.refs_10_ = bf16[32,3072]{1,0:T(8,128)(2,1)S(1)} collective-permute-done((bf16[32,3072]{1,0:T(8,128)(2,1)S(1)}, bf16[32,3072]{1,0:T(8,128)(2,1)S(1)}, u32[]{:S(2)}, u32[]{:S(2)}) %collective-permute-start.23) | collective-permute-done | bytes 196640 | tf_op jit(solution)/shard_map/ppermute | solution.py:322
  75.4 0.9 collective-permute-start.24
  76.3 4.5 %block_product.6 = (bf16[4,16,3072]{2,1,0:T(8,128)(2,1)S(1)}, bf16[4,16,3072]{2,1,0:T(8,128)(2,1)S(1)}, bf16[288,128,128]{2,1,0:T(8,128)(2,1)S(1)}) custom-call(s32[521]{0:T(1024)S(1)} %get-tuple-element.75.table_s, s32[4]{0:T(128)S(1)} %fusion.26.in_s.left_s.right_s, s32[1]{0:T(128)} %constant.62.clone.1.in_s.out_s.right_s.left_s, ...), custom_call_target="tpu_custom_call" | custom-call | flops 1207959552 | bytes 11010048 | tf_op jit(solution)/shard_map/block_product/pallas_call | solution.py:198
  80.8 0.9 collective-permute-start.21
  81.7 3.2 %block_product.7 = (bf16[4,16,3072]{2,1,0:T(8,128)(2,1)S(1)}, bf16[4,16,3072]{2,1,0:T(8,128)(2,1)S(1)}) custom-call(s32[521]{0:T(1024)S(1)} %get-tuple-element.86.table_s, s32[4]{0:T(128)S(1)} %fusion.26.in_s.left_s.right_s, s32[1]{0:T(128)} %constant.62.clone.1.in_s.out_s.right_s.left_s, bf16[32,3072]{1,0:T(8,128)(2,1)S(1)} %fusion.6.refs_0_.refs_8_, ...), custom_call_target="tpu_custom_call" | custom-call | flops 1207959552 | bytes 11010048 | tf_op jit(solution)/shard_map/block_product/pallas_call | solution.py:198
  85.0 5.6 %block_grads.3.refs_12_ = f32[288,128,128]{2,1,0:T(8,128)} custom-call(s32[1,1,288]{2,1,0:T(1,128)S(1)} %copy-done.3, s32[4]{0:T(128)S(1)} %fusion.26.in_s.left_s.right_s, s32[1]{0:T(128)} %constant.62.clone.1.in_s.out_s.right_s.left_s, bf16[32,3072]{1,0:T(8,128)(2,1)S(1)} %multiply_convert_fusion.refs_0_, ...), custom_call_target="tpu_custom_call" | custom-call | flops 1207959552 | bytes 20447232 | tf_op jit(solution)/shard_map/block_grads/pallas_call | solution.py:269
  90.5 1.0 collective-permute-done.21
  91.6 4.7 %collective-permute-start.27 = (bf16[16,3072]{1,0:T(8,128)(2,1)S(1)}, bf16[16,3072]{1,0:T(8,128)(2,1)S(1)}, u32[]{:S(2)}, u32[]{:S(2)}) collective-permute-start(bf16[16,3072]{1,0:T(8,128)(2,1)S(1)} %get-tuple-element.112), channel_id=1, source_target_pairs={{0,2},{1,3},{2,4},{3,5},{4,6},{5,7},{6,0},{7,1},{8,10},{9,11},{10,... | collective-permute-start | bytes 294920 | tf_op jit(solution)/shard_map/ppermute | solution.py:322
  96.3 0.7 collective-permute-start.26
  97.0 1.5 %collective-permute-start.25 = (bf16[16,3072]{1,0:T(8,128)(2,1)S(1)}, bf16[16,3072]{1,0:T(8,128)(2,1)S(1)}, u32[]{:S(2)}, u32[]{:S(2)}) collective-permute-start(bf16[16,3072]{1,0:T(8,128)(2,1)S(1)} %get-tuple-element.111), channel_id=1, source_target_pairs={{0,6},{1,7},{2,0},{3,1},{4,2},{5,3},{6,4},{7,5},{8,14},{9,15},{10,... | collective-permute-start | bytes 294920 | tf_op jit(solution)/shard_map/ppermute | solution.py:322
  98.5 5.5 %block_grads.4 = f32[288,128,128]{2,1,0:T(8,128)} custom-call(s32[1,1,288]{2,1,0:T(1,128)S(1)} %copy-done.3, s32[4]{0:T(128)S(1)} %fusion.26.in_s.left_s.right_s, s32[1]{0:T(128)} %constant.62.clone.1.in_s.out_s.right_s.left_s, bf16[32,3072]{1,0:T(8,128)(2,1)S(1)} %multiply_convert_fusion.refs_0_, ...), custom_call_target="tpu_custom_call", output_to_operand_aliasing={{}: (15, {})} | custom-call | flops 1207959552 | bytes 20447232 | tf_op jit(solution)/shard_map/block_grads/pallas_call | solution.py:269
  104.0 0.9 collective-permute-done.26
  105.0 0.7 fusion.14
  105.7 2.4 %collective-permute-start.31 = (bf16[16,3072]{1,0:T(8,128)(2,1)S(1)}, bf16[16,3072]{1,0:T(8,128)(2,1)S(1)}, u32[]{:S(2)}, u32[]{:S(2)}) collective-permute-start(bf16[16,3072]{1,0:T(8,128)(2,1)S(1)} %get-tuple-element.109), channel_id=1, source_target_pairs={{0,2},{1,3},{2,4},{3,5},{4,6},{5,7},{6,0},{7,1},{8,10},{9,11},{10,... | collective-permute-start | bytes 294920 | tf_op jit(solution)/shard_map/ppermute | solution.py:322
  108.2 2.2 %collective-permute-start.29 = (bf16[16,3072]{1,0:T(8,128)(2,1)S(1)}, bf16[16,3072]{1,0:T(8,128)(2,1)S(1)}, u32[]{:S(2)}, u32[]{:S(2)}) collective-permute-start(bf16[16,3072]{1,0:T(8,128)(2,1)S(1)} %get-tuple-element.108), channel_id=1, source_target_pairs={{0,6},{1,7},{2,0},{3,1},{4,2},{5,3},{6,4},{7,5},{8,14},{9,15},{10,... | collective-permute-start | bytes 294920 | tf_op jit(solution)/shard_map/ppermute | solution.py:322
  110.3 8.7 %block_grads.5 = f32[288,128,128]{2,1,0:T(8,128)} custom-call(s32[1,1,288]{2,1,0:T(1,128)S(1)} %copy-done.5, s32[1]{0:T(128)} %constant.62.clone.1.in_s.out_s.right_s.left_s, s32[4]{0:T(128)S(1)} %fusion.26.in_s.left_s.right_s, bf16[16,3072]{1,0:T(8,128)(2,1)S(1)} %copy-done.1, bf16[16,3072]{1,0:T(8,128)(2,1)S(1)} %collective-permute-done.10.refs_1_, ...), custom_call_target="tpu_custom_call" | custom-call | flops 1207959552 | bytes 20447232 | tf_op jit(solution)/shard_map/block_grads/pallas_call | solution.py:269
  119.1 0.7 fusion.11
  (49 shorter events, 1.6 us)
Async XLA Ops:
  0.6 21.7 %copy-start.1 = (bf16[16,3072]{1,0:T(8,128)(2,1)S(1)}, bf16[16,3072]{1,0:T(8,128)(2,1)}, u32[]{:S(2)}) copy-start(bf16[16,3072]{1,0:T(8,128)(2,1)} %refs_0_.6) | copy-start | bytes 294916
  0.6 7.0 %collective-permute-start = (bf16[16,3072]{1,0:T(8,128)(2,1)}, bf16[16,3072]{1,0:T(8,128)(2,1)S(1)}, u32[]{:S(2)}, u32[]{:S(2)}) collective-permute-start(bf16[16,3072]{1,0:T(8,128)(2,1)} %refs_0_.6), channel_id=1, source_target_pairs={{0,2},{1,3},{2,4},{3,5},{4,6},{5,7},{6,0},{7,1},{8,10},{9,11},{10,... | collective-permute-start | bytes 294920 | tf_op jit(solution)/shard_map/ppermute | solution.py:322
  2.8 9.8 %collective-permute-start.1 = (bf16[16,3072]{1,0:T(8,128)(2,1)}, bf16[16,3072]{1,0:T(8,128)(2,1)S(1)}, u32[]{:S(2)}, u32[]{:S(2)}) collective-permute-start(bf16[16,3072]{1,0:T(8,128)(2,1)} %refs_0_.6), channel_id=1, source_target_pairs={{0,4},{1,5},{2,6},{3,7},{4,0},{5,1},{6,2},{7,3},{8,12},{9,13},{10,... | collective-permute-start | bytes 294920 | tf_op jit(solution)/shard_map/ppermute | solution.py:322
  5.1 8.7 %collective-permute-start.2 = (bf16[16,3072]{1,0:T(8,128)(2,1)}, bf16[16,3072]{1,0:T(8,128)(2,1)S(1)}, u32[]{:S(2)}, u32[]{:S(2)}) collective-permute-start(bf16[16,3072]{1,0:T(8,128)(2,1)} %refs_0_.6), channel_id=1, source_target_pairs={{0,6},{1,7},{2,0},{3,1},{4,2},{5,3},{6,4},{7,5},{8,14},{9,15},{10,... | collective-permute-start | bytes 294920 | tf_op jit(solution)/shard_map/ppermute | solution.py:322
  6.2 16.1 %collective-permute-start.10 = (bf16[16,3072]{1,0:T(8,128)(2,1)}, bf16[16,3072]{1,0:T(8,128)(2,1)S(1)}, u32[]{:S(2)}, u32[]{:S(2)}) collective-permute-start(bf16[16,3072]{1,0:T(8,128)(2,1)} %refs_0_.6), channel_id=1, source_target_pairs={{0,1},{1,0},{2,3},{3,2},{4,5},{5,4},{6,7},{7,6},{8,9},{9,8},{10,11... | collective-permute-start | bytes 294920 | tf_op jit(solution)/shard_map/ppermute | solution.py:317
  7.6 14.7 %collective-permute-start.11 = (bf16[16,3072]{1,0:T(8,128)(2,1)S(1)}, bf16[16,3072]{1,0:T(8,128)(2,1)S(1)}, u32[]{:S(2)}, u32[]{:S(2)}) collective-permute-start(bf16[16,3072]{1,0:T(8,128)(2,1)S(1)} %collective-permute-done.refs_2_), channel_id=1, source_target_pairs={{0,1},{1,0},{2,3},{3,2},{4,5},{5,4},{6,7},{7,6},{8,9},{9,8},{10,11... | collective-permute-start | bytes 294920 | tf_op jit(solution)/shard_map/ppermute | solution.py:317
  12.6 9.7 %collective-permute-start.12 = (bf16[16,3072]{1,0:T(8,128)(2,1)S(1)}, bf16[16,3072]{1,0:T(8,128)(2,1)S(1)}, u32[]{:S(2)}, u32[]{:S(2)}) collective-permute-start(bf16[16,3072]{1,0:T(8,128)(2,1)S(1)} %collective-permute-done.1.refs_4_), channel_id=1, source_target_pairs={{0,1},{1,0},{2,3},{3,2},{4,5},{5,4},{6,7},{7,6},{8,9},{9,8},{10,11... | collective-permute-start | bytes 294920 | tf_op jit(solution)/shard_map/ppermute | solution.py:317
  13.8 8.5 %collective-permute-start.13 = (bf16[16,3072]{1,0:T(8,128)(2,1)S(1)}, bf16[16,3072]{1,0:T(8,128)(2,1)S(1)}, u32[]{:S(2)}, u32[]{:S(2)}) collective-permute-start(bf16[16,3072]{1,0:T(8,128)(2,1)S(1)} %collective-permute-done.2.refs_6_), channel_id=1, source_target_pairs={{0,1},{1,0},{2,3},{3,2},{4,5},{5,4},{6,7},{7,6},{8,9},{9,8},{10,11... | collective-permute-start | bytes 294920 | tf_op jit(solution)/shard_map/ppermute | solution.py:317
  14.1 0.7 copy-start.2
  14.8 0.7 copy-start.4
  22.3 5.5 %copy-start = (bf16[16,3072]{1,0:T(8,128)(2,1)S(1)}, bf16[16,3072]{1,0:T(8,128)(2,1)}, u32[]{:S(2)}) copy-start(bf16[16,3072]{1,0:T(8,128)(2,1)} %refs_4_.3) | copy-start | bytes 294916
  26.6 24.0 %copy-start.3 = (s32[1,1,288]{2,1,0:T(1,128)S(1)}, s32[1,1,288]{2,1,0:T(1,128)}, u32[]{:S(2)}) copy-start(s32[1,1,288]{2,1,0:T(1,128)} %slot_s.4) | copy-start | bytes 3460
  26.6 24.0 %copy-start.5 = (s32[1,1,288]{2,1,0:T(1,128)S(1)}, s32[1,1,288]{2,1,0:T(1,128)}, u32[]{:S(2)}) copy-start(s32[1,1,288]{2,1,0:T(1,128)} %slot_s.5) | copy-start | bytes 3460
  26.6 14.8 %collective-permute-start.14 = (bf16[2,32,3072]{2,1,0:T(8,128)(2,1)S(1)}, bf16[2,32,3072]{2,1,0:T(8,128)(2,1)S(1)}, u32[]{:S(2)}, u32[]{:S(2)}) collective-permute-start(bf16[2,32,3072]{2,1,0:T(8,128)(2,1)S(1)} %get-tuple-element.62), channel_id=1, source_target_pairs={{0,8},{8,0},{16,24},{24,16},{1,9},{9,1},{17,25},{25,17},{2,10},{10... | collective-permute-start | bytes 1179656 | tf_op jit(solution)/shard_map/ppermute | solution.py:317
  27.8 7.7 %collective-permute-start.4 = (bf16[16,3072]{1,0:T(8,128)(2,1)S(1)}, bf16[16,3072]{1,0:T(8,128)(2,1)S(1)}, u32[]{:S(2)}, u32[]{:S(2)}) collective-permute-start(bf16[16,3072]{1,0:T(8,128)(2,1)S(1)} %copy-done), channel_id=1, source_target_pairs={{0,2},{1,3},{2,4},{3,5},{4,6},{5,7},{6,0},{7,1},{8,10},{9,11},{10,... | collective-permute-start | bytes 294920 | tf_op jit(solution)/shard_map/ppermute | solution.py:322
  29.7 10.3 %collective-permute-start.6 = (bf16[16,3072]{1,0:T(8,128)(2,1)S(1)}, bf16[16,3072]{1,0:T(8,128)(2,1)S(1)}, u32[]{:S(2)}, u32[]{:S(2)}) collective-permute-start(bf16[16,3072]{1,0:T(8,128)(2,1)S(1)} %copy-done), channel_id=1, source_target_pairs={{0,4},{1,5},{2,6},{3,7},{4,0},{5,1},{6,2},{7,3},{8,12},{9,13},{10,... | collective-permute-start | bytes 294920 | tf_op jit(solution)/shard_map/ppermute | solution.py:322
  32.7 7.2 %collective-permute-start.8 = (bf16[16,3072]{1,0:T(8,128)(2,1)S(1)}, bf16[16,3072]{1,0:T(8,128)(2,1)S(1)}, u32[]{:S(2)}, u32[]{:S(2)}) collective-permute-start(bf16[16,3072]{1,0:T(8,128)(2,1)S(1)} %copy-done), channel_id=1, source_target_pairs={{0,6},{1,7},{2,0},{3,1},{4,2},{5,3},{6,4},{7,5},{8,14},{9,15},{10,... | collective-permute-start | bytes 294920 | tf_op jit(solution)/shard_map/ppermute | solution.py:322
  33.1 8.4 %collective-permute-start.3 = (bf16[16,3072]{1,0:T(8,128)(2,1)S(1)}, bf16[16,3072]{1,0:T(8,128)(2,1)S(1)}, u32[]{:S(2)}, u32[]{:S(2)}) collective-permute-start(bf16[16,3072]{1,0:T(8,128)(2,1)S(1)} %copy-done), channel_id=1, source_target_pairs={{0,1},{1,0},{2,3},{3,2},{4,5},{5,4},{6,7},{7,6},{8,9},{9,8},{10,11... | collective-permute-start | bytes 294920 | tf_op jit(solution)/shard_map/ppermute | solution.py:317
  35.5 6.0 %collective-permute-start.5 = (bf16[16,3072]{1,0:T(8,128)(2,1)S(1)}, bf16[16,3072]{1,0:T(8,128)(2,1)S(1)}, u32[]{:S(2)}, u32[]{:S(2)}) collective-permute-start(bf16[16,3072]{1,0:T(8,128)(2,1)S(1)} %collective-permute-done.4.refs_2_.refs_6_), channel_id=1, source_target_pairs={{0,1},{1,0},{2,3},{3,2},{4,5},{5,4},{6,7},{7,6},{8,9},{9,8},{10,11... | collective-permute-start | bytes 294920 | tf_op jit(solution)/shard_map/ppermute | solution.py:317
  40.0 3.9 %collective-permute-start.7 = (bf16[16,3072]{1,0:T(8,128)(2,1)S(1)}, bf16[16,3072]{1,0:T(8,128)(2,1)S(1)}, u32[]{:S(2)}, u32[]{:S(2)}) collective-permute-start(bf16[16,3072]{1,0:T(8,128)(2,1)S(1)} %collective-permute-done.6.refs_4_.refs_8_), channel_id=1, source_target_pairs={{0,1},{1,0},{2,3},{3,2},{4,5},{5,4},{6,7},{7,6},{8,9},{9,8},{10,11... | collective-permute-start | bytes 294920 | tf_op jit(solution)/shard_map/ppermute | solution.py:317
  40.0 6.0 %collective-permute-start.9 = (bf16[16,3072]{1,0:T(8,128)(2,1)S(1)}, bf16[16,3072]{1,0:T(8,128)(2,1)S(1)}, u32[]{:S(2)}, u32[]{:S(2)}) collective-permute-start(bf16[16,3072]{1,0:T(8,128)(2,1)S(1)} %collective-permute-done.8.refs_6_.refs_10_), channel_id=1, source_target_pairs={{0,1},{1,0},{2,3},{3,2},{4,5},{5,4},{6,7},{7,6},{8,9},{9,8},{10,11... | collective-permute-start | bytes 294920 | tf_op jit(solution)/shard_map/ppermute | solution.py:317
  50.0 7.3 %collective-permute-start.16 = (bf16[2,32,3072]{2,1,0:T(8,128)(2,1)S(1)}, bf16[2,32,3072]{2,1,0:T(8,128)(2,1)S(1)}, u32[]{:S(2)}, u32[]{:S(2)}) collective-permute-start(bf16[2,32,3072]{2,1,0:T(8,128)(2,1)S(1)} %get-tuple-element.76), channel_id=1, source_target_pairs={{0,8},{8,0},{16,24},{24,16},{1,9},{9,1},{17,25},{25,17},{2,10},{10... | collective-permute-start | bytes 1179656 | tf_op jit(solution)/shard_map/ppermute | solution.py:317
  50.5 6.8 %collective-permute-start.15 = (bf16[32,3072]{1,0:T(8,128)(2,1)S(1)}, bf16[32,3072]{1,0:T(8,128)(2,1)S(1)}, u32[]{:S(2)}, u32[]{:S(2)}) collective-permute-start(bf16[32,3072]{1,0:T(8,128)(2,1)S(1)} %fusion.7), channel_id=1, source_target_pairs={{0,16},{8,24},{16,0},{24,8},{1,17},{9,25},{17,1},{25,9},{2,18},{10... | collective-permute-start | bytes 589832 | tf_op jit(solution)/shard_map/ppermute | solution.py:322
  57.4 6.0 %collective-permute-start.19 = (bf16[32,3072]{1,0:T(8,128)(2,1)S(1)}, bf16[32,3072]{1,0:T(8,128)(2,1)S(1)}, u32[]{:S(2)}, u32[]{:S(2)}) collective-permute-start(bf16[32,3072]{1,0:T(8,128)(2,1)S(1)} %fusion.8), channel_id=1, source_target_pairs={{0,16},{8,24},{16,0},{24,8},{1,17},{9,25},{17,1},{25,9},{2,18},{10... | collective-permute-start | bytes 589832 | tf_op jit(solution)/shard_map/ppermute | solution.py:322
  59.1 11.6 %collective-permute-start.17 = (bf16[32,3072]{1,0:T(8,128)(2,1)S(1)}, bf16[32,3072]{1,0:T(8,128)(2,1)S(1)}, u32[]{:S(2)}, u32[]{:S(2)}) collective-permute-start(bf16[32,3072]{1,0:T(8,128)(2,1)S(1)} %multiply_convert_fusion.refs_0_), channel_id=1, source_target_pairs={{0,8},{8,0},{16,24},{24,16},{1,9},{9,1},{17,25},{25,17},{2,10},{10... | collective-permute-start | bytes 589832 | tf_op jit(solution)/shard_map/ppermute | solution.py:317
  59.8 7.8 %collective-permute-start.18 = (bf16[32,3072]{1,0:T(8,128)(2,1)S(1)}, bf16[32,3072]{1,0:T(8,128)(2,1)S(1)}, u32[]{:S(2)}, u32[]{:S(2)}) collective-permute-start(bf16[32,3072]{1,0:T(8,128)(2,1)S(1)} %multiply_convert_fusion.refs_0_), channel_id=1, source_target_pairs={{0,16},{8,24},{16,0},{24,8},{1,17},{9,25},{17,1},{25,9},{2,18},{10... | collective-permute-start | bytes 589832 | tf_op jit(solution)/shard_map/ppermute | solution.py:322
  67.6 3.1 %collective-permute-start.20 = (bf16[32,3072]{1,0:T(8,128)(2,1)S(1)}, bf16[32,3072]{1,0:T(8,128)(2,1)S(1)}, u32[]{:S(2)}, u32[]{:S(2)}) collective-permute-start(bf16[32,3072]{1,0:T(8,128)(2,1)S(1)} %collective-permute-done.18.refs_2_), channel_id=1, source_target_pairs={{0,8},{8,0},{16,24},{24,16},{1,9},{9,1},{17,25},{25,17},{2,10},{10... | collective-permute-start | bytes 589832 | tf_op jit(solution)/shard_map/ppermute | solution.py:317
  69.0 6.5 %collective-permute-start.23 = (bf16[32,3072]{1,0:T(8,128)(2,1)S(1)}, bf16[32,3072]{1,0:T(8,128)(2,1)S(1)}, u32[]{:S(2)}, u32[]{:S(2)}) collective-permute-start(bf16[32,3072]{1,0:T(8,128)(2,1)S(1)} %fusion.6.refs_0_.refs_8_), channel_id=1, source_target_pairs={{0,16},{8,24},{16,0},{24,8},{1,17},{9,25},{17,1},{25,9},{2,18},{10... | collective-permute-start | bytes 589832 | tf_op jit(solution)/shard_map/ppermute | solution.py:322
  70.4 11.2 %collective-permute-start.22 = (bf16[32,3072]{1,0:T(8,128)(2,1)S(1)}, bf16[32,3072]{1,0:T(8,128)(2,1)S(1)}, u32[]{:S(2)}, u32[]{:S(2)}) collective-permute-start(bf16[32,3072]{1,0:T(8,128)(2,1)S(1)} %fusion.6.refs_0_.refs_8_), channel_id=1, source_target_pairs={{0,8},{8,0},{16,24},{24,16},{1,9},{9,1},{17,25},{25,17},{2,10},{10... | collective-permute-start | bytes 589832 | tf_op jit(solution)/shard_map/ppermute | solution.py:317
  75.4 6.3 %collective-permute-start.24 = (bf16[32,3072]{1,0:T(8,128)(2,1)S(1)}, bf16[32,3072]{1,0:T(8,128)(2,1)S(1)}, u32[]{:S(2)}, u32[]{:S(2)}) collective-permute-start(bf16[32,3072]{1,0:T(8,128)(2,1)S(1)} %collective-permute-done.23.refs_2_.refs_10_), channel_id=1, source_target_pairs={{0,8},{8,0},{16,24},{24,16},{1,9},{9,1},{17,25},{25,17},{2,10},{10... | collective-permute-start | bytes 589832 | tf_op jit(solution)/shard_map/ppermute | solution.py:317
  80.8 10.7 %collective-permute-start.21 = (bf16[4,16,3072]{2,1,0:T(8,128)(2,1)S(1)}, bf16[4,16,3072]{2,1,0:T(8,128)(2,1)S(1)}, u32[]{:S(2)}, u32[]{:S(2)}) collective-permute-start(bf16[4,16,3072]{2,1,0:T(8,128)(2,1)S(1)} %get-tuple-element.85), channel_id=1, source_target_pairs={{0,1},{1,0},{2,3},{3,2},{4,5},{5,4},{6,7},{7,6},{8,9},{9,8},{10,11... | collective-permute-start | bytes 1179656 | tf_op jit(solution)/shard_map/ppermute | solution.py:317
  84.9 20.8 %collective-permute-start.28 = (bf16[4,16,3072]{2,1,0:T(8,128)(2,1)S(1)}, bf16[4,16,3072]{2,1,0:T(8,128)(2,1)S(1)}, u32[]{:S(2)}, u32[]{:S(2)}) collective-permute-start(bf16[4,16,3072]{2,1,0:T(8,128)(2,1)S(1)} %get-tuple-element.98), channel_id=1, source_target_pairs={{0,1},{1,0},{2,3},{3,2},{4,5},{5,4},{6,7},{7,6},{8,9},{9,8},{10,11... | collective-permute-start | bytes 1179656 | tf_op jit(solution)/shard_map/ppermute | solution.py:317
  91.6 12.4 %collective-permute-start.27 = (bf16[16,3072]{1,0:T(8,128)(2,1)S(1)}, bf16[16,3072]{1,0:T(8,128)(2,1)S(1)}, u32[]{:S(2)}, u32[]{:S(2)}) collective-permute-start(bf16[16,3072]{1,0:T(8,128)(2,1)S(1)} %get-tuple-element.112), channel_id=1, source_target_pairs={{0,2},{1,3},{2,4},{3,5},{4,6},{5,7},{6,0},{7,1},{8,10},{9,11},{10,... | collective-permute-start | bytes 294920 | tf_op jit(solution)/shard_map/ppermute | solution.py:322
  96.3 8.6 %collective-permute-start.26 = (bf16[16,3072]{1,0:T(8,128)(2,1)S(1)}, bf16[16,3072]{1,0:T(8,128)(2,1)S(1)}, u32[]{:S(2)}, u32[]{:S(2)}) collective-permute-start(bf16[16,3072]{1,0:T(8,128)(2,1)S(1)} %get-tuple-element.113), channel_id=1, source_target_pairs={{0,4},{1,5},{2,6},{3,7},{4,0},{5,1},{6,2},{7,3},{8,12},{9,13},{10,... | collective-permute-start | bytes 294920 | tf_op jit(solution)/shard_map/ppermute | solution.py:322
  97.0 7.9 %collective-permute-start.25 = (bf16[16,3072]{1,0:T(8,128)(2,1)S(1)}, bf16[16,3072]{1,0:T(8,128)(2,1)S(1)}, u32[]{:S(2)}, u32[]{:S(2)}) collective-permute-start(bf16[16,3072]{1,0:T(8,128)(2,1)S(1)} %get-tuple-element.111), channel_id=1, source_target_pairs={{0,6},{1,7},{2,0},{3,1},{4,2},{5,3},{6,4},{7,5},{8,14},{9,15},{10,... | collective-permute-start | bytes 294920 | tf_op jit(solution)/shard_map/ppermute | solution.py:322
  105.7 13.3 %collective-permute-start.31 = (bf16[16,3072]{1,0:T(8,128)(2,1)S(1)}, bf16[16,3072]{1,0:T(8,128)(2,1)S(1)}, u32[]{:S(2)}, u32[]{:S(2)}) collective-permute-start(bf16[16,3072]{1,0:T(8,128)(2,1)S(1)} %get-tuple-element.109), channel_id=1, source_target_pairs={{0,2},{1,3},{2,4},{3,5},{4,6},{5,7},{6,0},{7,1},{8,10},{9,11},{10,... | collective-permute-start | bytes 294920 | tf_op jit(solution)/shard_map/ppermute | solution.py:322
  108.2 10.9 %collective-permute-start.30 = (bf16[16,3072]{1,0:T(8,128)(2,1)S(1)}, bf16[16,3072]{1,0:T(8,128)(2,1)S(1)}, u32[]{:S(2)}, u32[]{:S(2)}) collective-permute-start(bf16[16,3072]{1,0:T(8,128)(2,1)S(1)} %get-tuple-element.110), channel_id=1, source_target_pairs={{0,4},{1,5},{2,6},{3,7},{4,0},{5,1},{6,2},{7,3},{8,12},{9,13},{10,... | collective-permute-start | bytes 294920 | tf_op jit(solution)/shard_map/ppermute | solution.py:322
  108.2 10.9 %collective-permute-start.29 = (bf16[16,3072]{1,0:T(8,128)(2,1)S(1)}, bf16[16,3072]{1,0:T(8,128)(2,1)S(1)}, u32[]{:S(2)}, u32[]{:S(2)}) collective-permute-start(bf16[16,3072]{1,0:T(8,128)(2,1)S(1)} %get-tuple-element.108), channel_id=1, source_target_pairs={{0,6},{1,7},{2,0},{3,1},{4,2},{5,3},{6,4},{7,5},{8,14},{9,15},{10,... | collective-permute-start | bytes 294920 | tf_op jit(solution)/shard_map/ppermute | solution.py:322

commit v5 on v4

--- a/solution.py
+++ b/solution.py
@@ -41,84 +41,78 @@
             store[b, pl.ds(start, length), :] = piece[:, b * width : (b + 1) * width]
 
 
-def pair_tables(jobs, weights=()):
+def pair_tables(jobs, weights):
     cap = jobs[0][0].shape[-1]
+    lanes = -(-cap // 128) * 128
     specs = [job[1:] for job in jobs]
     n, m = len(jobs), len(weights)
     limits = [pair_limit(cap, rows if by_row else cols) for rows, cols, by_row in specs]
 
     def body(*refs):
         slot_refs, far, tables, near = refs[:n], refs[n : n + m], refs[n + m : 2 * n + m], refs[2 * n + m : 2 * n + 2 * m]
-        pending, sems = refs[2 * n + 2 * m : 3 * n + 2 * m], refs[3 * n + 2 * m :]
+        padded, sems = refs[2 * n + 2 * m], refs[2 * n + 2 * m + 1 :]
         copies = [pltpu.make_async_copy(*copy) for copy in zip(far, near, sems)]
         for copy in copies:
             copy.start()
-        for (rows, cols, by_row), pend in zip(specs, pending):
-
-            def clear(i, carry, pend=pend):
-                pend[i] = -1
-                return carry
-
-            lax.fori_loop(0, (rows if by_row else cols) + 1, clear, 0)
-
-        step = largest_divisor(cap, 8)
-
-        def some(g, counts):
-            counts = list(counts)
-            for t, (rows, cols, by_row) in enumerate(specs):
-                table, pend, limit = tables[t], pending[t], limits[t]
-                entries = []
-                for u in range(step):
-                    k = g * step + u
-                    pos = slot_refs[t][0, 0, k]
-                    filled = pos >= 0
-                    safe = jnp.maximum(pos, 0)
-                    row = (safe * (-(-65536 // cols))) >> 16
-                    col = safe - row * cols
-                    key, src, end = (row, col, rows) if by_row else (col, row, cols)
-                    entries.append((jnp.where(filled, key, end), k + src * 4096, filled))
-                for key, word, filled in entries:
-                    first = pend[key]
-                    at = counts[t]
-                    table[at] = first
-                    table[limit + at] = word
-                    table[2 * limit + at] = key
-                    pend[key] = jnp.where(first >= 0, -1, word)
-                    counts[t] = at + jnp.logical_and(first >= 0, filled).astype(jnp.int32)
-            return tuple(counts)
-
-        counts = lax.fori_loop(0, cap // step, some, (jnp.int32(0),) * n)
+        iota = lambda shape, dim: lax.broadcasted_iota(jnp.int32, shape, dim)
+        matmul = lambda x, y, dim: lax.dot_general(
+            x.astype(jnp.bfloat16),
+            y.astype(jnp.bfloat16),
+            (((1,), (dim,)), ((), ())),
+            preferred_element_type=jnp.float32,
+        )
+        flag = lambda x: jnp.where(x, 1.0, 0.0)
+        upto = flag(iota((lanes, lanes), 0) <= iota((lanes, lanes), 1))
+        index = iota((1, lanes), 1)
         for t, (rows, cols, by_row) in enumerate(specs):
-            table, pend, limit = tables[t], pending[t], limits[t]
             n_dst, n_src = (rows, cols) if by_row else (cols, rows)
-
-            def rest(d, at, table=table, pend=pend, limit=limit, n_src=n_src):
-                first = pend[d]
-                table[at] = first
-                table[limit + at] = n_src * 4096
-                table[2 * limit + at] = d
-                return at + (first >= 0).astype(jnp.int32)
-
-            at = lax.fori_loop(0, n_dst, rest, counts[t])
-            for u in range(PAIR_UNROLL):
-                table[at + u] = n_src * 4096
-                table[limit + at + u] = n_src * 4096
-                table[2 * limit + at + u] = n_dst
-            table[3 * limit] = counts[t]
-            table[3 * limit + 1] = (at + (PAIR_UNROLL - 1)) >> PAIR_SHIFT
+            dst_pad, limit = -(-n_dst // 16) * 16, limits[t]
+            padded[...] = jnp.full((1, lanes), -1, jnp.int32)
+            padded[:, :cap] = slot_refs[t][0]
+            pos = padded[...]
+            filled = pos >= 0
+            safe = jnp.maximum(pos, 0)
+            row = (safe * (-(-65536 // cols))) >> 16
+            col = safe - row * cols
+            key, src = (row, col) if by_row else (col, row)
+            key = jnp.where(filled, key, -1)
+            hot = flag(iota((dst_pad, lanes), 0) == key)
+            running = matmul(hot, upto, 0)
+            rank = jnp.sum(hot * running, axis=0, keepdims=True).astype(jnp.int32) - 1
+            count = running[:, lanes - 1 :].astype(jnp.int32)
+            pairs = ((count + 1) >> 1).astype(jnp.float32)
+            below = flag(iota((dst_pad, dst_pad), 1) < iota((dst_pad, dst_pad), 0))
+            start = matmul(below, jnp.broadcast_to(pairs, (dst_pad, 128)), 0)[:, :1]
+            first = jnp.sum(hot * start, axis=0, keepdims=True).astype(jnp.int32)
+            place = jnp.where(filled, first + (rank >> 1), -1)
+            line = iota((16, lanes), 0)
+            facts = jnp.where(line == 0, index >> 4, jnp.where(line == 1, index & 15, jnp.where(line == 2, src + 1, key + 1)))
+            facts = facts.astype(jnp.float32)
+            got = []
+            for side in range(2):
+                goes = flag(iota((limit, lanes), 0) == jnp.where((rank & 1) == side, place, -1))
+                got.append(matmul(facts, goes, 1).astype(jnp.int32))
+            for side in range(2):
+                words = got[side]
+                there = words[2:3] > 0
+                word = words[0:1] * 16 + words[1:2] + (words[2:3] - 1) * 4096
+                tables[t][side : side + 1] = jnp.where(there, word, n_src * 4096)
+            keys = got[0][3:4]
+            tables[t][2:3] = jnp.where(keys > 0, keys - 1, n_dst)
+            total = jnp.sum(pairs, axis=0, keepdims=True).astype(jnp.int32)
+            tables[t][3:4] = jnp.broadcast_to((total + (PAIR_UNROLL - 1)) >> PAIR_SHIFT, (1, limit))
         for copy in copies:
             copy.wait()
 
-    smem = pl.BlockSpec(memory_space=pltpu.SMEM)
+    vmem = pl.BlockSpec(memory_space=pltpu.VMEM)
     return pl.pallas_call(
         body,
-        in_specs=[smem] * n + [pl.BlockSpec(memory_space=pltpu.HBM)] * m,
-        out_specs=[smem] * n + [pl.BlockSpec(memory_space=pltpu.VMEM)] * m,
-        out_shape=[jax.ShapeDtypeStruct((3 * limit + 2,), jnp.int32) for limit in limits]
+        in_specs=[vmem] * n + [pl.BlockSpec(memory_space=pltpu.HBM)] * m,
+        out_specs=[vmem] * (n + m),
+        out_shape=[jax.ShapeDtypeStruct((4, limit), jnp.int32) for limit in limits]
         + [jax.ShapeDtypeStruct(weight.shape, weight.dtype) for weight in weights],
-        scratch_shapes=[pltpu.SMEM(((rows if by_row else cols) + 1,), jnp.int32) for rows, cols, by_row in specs]
-        + [pltpu.SemaphoreType.DMA] * m,
-        compiler_params=pltpu.CompilerParams(vmem_limit_bytes=1024 * 1024),
+        scratch_shapes=[pltpu.VMEM((1, lanes), jnp.int32)] + [pltpu.SemaphoreType.DMA] * m,
+        compiler_params=pltpu.CompilerParams(vmem_limit_bytes=8 * 1024 * 1024),
         name="pair_tables",
     )(*[job[0] for job in jobs], *weights)
 
@@ -128,14 +122,13 @@
 
 
 def pair_limit(cap, n_dst):
-    return (cap + n_dst) // 2 + PAIR_UNROLL + 1
+    return -(-((cap + n_dst) // 2 + PAIR_UNROLL) // 128) * 128
 
 
 def block_product(pieces, in_rows, blocks, table, n_dst, out_lengths, out_rows, transposed, stage=()):
     cap, width = blocks.shape[0], blocks.shape[1]
     n_src = pieces[0].shape[1] // width
     tokens = sum(piece.shape[0] for piece in pieces)
-    limit = pair_limit(cap, n_dst)
     dims = (((1,), (1 if transposed else 0,)), ((), ()))
     zero_rows = jnp.zeros((1,), jnp.int32)
     in_arr = zero_rows if in_rows is None else in_rows
@@ -165,17 +158,17 @@
             terms = []
             for u in range(PAIR_UNROLL):
                 n = g * PAIR_UNROLL + u
-                one, two = table_s[n], table_s[limit + n]
+                one, two = table_s[0, n], table_s[1, n]
                 left = jnp.concatenate([xs[one >> 12], xs[two >> 12]], axis=1)
                 right = jnp.concatenate(
                     [w_ref[one & 4095], w_ref[two & 4095]], axis=1 if transposed else 0
                 )
                 terms.append(lax.dot_general(left, right, dims, preferred_element_type=jnp.float32))
             for u in range(PAIR_UNROLL):
-                acc[table_s[2 * limit + g * PAIR_UNROLL + u]] += terms[u]
+                acc[table_s[2, g * PAIR_UNROLL + u]] += terms[u]
             return carry
 
-        lax.fori_loop(0, table_s[3 * limit + 1], some, 0)
+        lax.fori_loop(0, table_s[3, 0], some, 0)
         at = 0
         for ref in out_refs:
             lead = ref.shape[:-2]
@@ -377,8 +370,14 @@
     tok = gather_near(tok_far)
     cot = gather_near(cot_far)
     first_in, first_out = after((slots_in, slots_out), tok_far[1:])
-    in_by_col, out_by_row, w_in_near = pair_tables(
-        [(first_in, feat_blocks, hid_blocks, False), (first_out, hid_blocks, feat_blocks, True)], [w_in]
+    in_by_col, out_by_row, out_by_col, in_by_row, w_in_near = pair_tables(
+        [
+            (first_in, feat_blocks, hid_blocks, False),
+            (first_out, hid_blocks, feat_blocks, True),
+            (first_out, hid_blocks, feat_blocks, False),
+            (first_in, feat_blocks, hid_blocks, True),
+        ],
+        [w_in],
     )
     keep_h, send_h, w_out_near = block_product(
         tok, None, w_in_near, in_by_col, hid_blocks, hidden_lengths, near_order, False, [w_out]
@@ -386,16 +385,12 @@
     own_h, pairs_h = pair_hidden(keep_h, send_h)
     keep_g, send_g = block_product(
         after(cot, pairs_h), None, w_out_near, out_by_row, hid_blocks, hidden_lengths, near_order, True
-    )
-    later_in, later_out = after((slots_in, slots_out), keep_g)
-    out_by_col, in_by_row = pair_tables(
-        [(later_out, hid_blocks, feat_blocks, False), (later_in, feat_blocks, hid_blocks, True)]
     )
     hidden = total_hidden(own_h, pairs_h)
     own_act = gelu_value(hidden).astype(jnp.bfloat16)
     own_g, pairs_g = pair_hidden(keep_g, send_g)
     act_far = spread_far(after(own_act, pairs_g))
-    grad_act = total_hidden(own_g, pairs_g, own_act, out_by_col)
+    grad_act = total_hidden(own_g, pairs_g, own_act)
     own_gh = (grad_act * gelu_slope(hidden)).astype(jnp.bfloat16)
     activated = spread_near([act_far[0]] + after(act_far[1:], own_gh))
     gh_far = spread_far(own_gh)

time: 122 us -> 118 us (0.967)
  Pallas kernels: 49.4 us -> 39.7 us
  waiting for transfers between devices: 27.9 us -> 34.8 us
    pallas_call x2 -> x1, Pallas kernels: 13.5 us -> 3.69 us  [pair_tables(): pl.pallas_call(body, in_specs=[vmem] * n + [pl.BlockSpec(memory_space=plt...]
    ppermute x16, waiting for transfers between devices: 22.4 us -> 28.6 us  [far_move(): return lax.ppermute(v, axis, pairs)]
  transfers between devices with their start and end apart: 32 -> 32, of which waited for: 10 -> 12; matrix products, arithmetic and copies ran while one was open for 1% -> 1% of each run, Pallas kernels for 34% -> 27%
where the time goes in v5:
time: 118 us; the launch traced here: 116 us
  Pallas kernels  39.7 us (34%)
  starting transfers between devices  37.2 us (32%)
  waiting for transfers between devices  34.8 us (29%)
  other arithmetic  2.32 us (2%)
  local copies, waits for them, and re-layouts  1.57 us (1%)
    ppermute x16, waiting for transfers between devices, far_move(): return lax.ppermute(v, axis, pairs)  28.6 us
    ppermute x16, starting transfers between devices, far_move(): return lax.ppermute(v, axis, pairs)  24.5 us
    pallas_call x3, Pallas kernels, block_grads(): pl.pallas_call(body, grid_spec=pltpu.PrefetchScalarGridSpec(num_scalar_pr...  19.7 us
    pallas_call x4, Pallas kernels, block_product(): pl.pallas_call(body, in_specs=[smem] * 3 + [vmem] * (n_in + 1) + [pl.Bloc...  16.3 us
    ppermute x16, starting transfers between devices, near_move(): return lax.ppermute(v, axis, [(i, i ^ 1) for i in range(count)])  12.7 us
    ppermute x16, waiting for transfers between devices, near_move(): return lax.ppermute(v, axis, [(i, i ^ 1) for i in range(count)])  6.21 us
    pallas_call x1, Pallas kernels, pair_tables(): pl.pallas_call(body, in_specs=[vmem] * n + [pl.BlockSpec(memory_space=plt...  3.69 us
  transfers between devices with their start and end apart: 32, of which 12 were waited for; matrix products, arithmetic and copies ran while one was open for 1% of the time, Pallas kernels for 27%

profile of v5, /device:TPU:1, one launch (start us, length us, event | category | flops | bytes accessed | tf_op | source)
XLA Modules:
  0.0 116.5 jit_solution(11937012892131144850)
XLA Ops:
  0.6 2.2 %collective-permute-start = (bf16[16,3072]{1,0:T(8,128)(2,1)}, bf16[16,3072]{1,0:T(8,128)(2,1)S(1)}, u32[]{:S(2)}, u32[]{:S(2)}) collective-permute-start(bf16[16,3072]{1,0:T(8,128)(2,1)} %refs_0_.5), channel_id=1, source_target_pairs={{0,2},{1,3},{2,4},{3,5},{4,6},{5,7},{6,0},{7,1},{8,10},{9,11},{10,... | collective-permute-start | bytes 294920 | tf_op jit(solution)/shard_map/ppermute | solution.py:315
  2.8 2.3 %collective-permute-start.1 = (bf16[16,3072]{1,0:T(8,128)(2,1)}, bf16[16,3072]{1,0:T(8,128)(2,1)S(1)}, u32[]{:S(2)}, u32[]{:S(2)}) collective-permute-start(bf16[16,3072]{1,0:T(8,128)(2,1)} %refs_0_.5), channel_id=1, source_target_pairs={{0,4},{1,5},{2,6},{3,7},{4,0},{5,1},{6,2},{7,3},{8,12},{9,13},{10,... | collective-permute-start | bytes 294920 | tf_op jit(solution)/shard_map/ppermute | solution.py:315
  5.1 1.1 collective-permute-start.2
  6.2 1.2 %collective-permute-start.3 = (bf16[16,3072]{1,0:T(8,128)(2,1)}, bf16[16,3072]{1,0:T(8,128)(2,1)S(1)}, u32[]{:S(2)}, u32[]{:S(2)}) collective-permute-start(bf16[16,3072]{1,0:T(8,128)(2,1)} %refs_0_.5), channel_id=1, source_target_pairs={{0,1},{1,0},{2,3},{3,2},{4,5},{5,4},{6,7},{7,6},{8,9},{9,8},{10,11... | collective-permute-start | bytes 294920 | tf_op jit(solution)/shard_map/ppermute | solution.py:310
  7.6 0.7 collective-permute-start.4
  8.3 4.2 %collective-permute-done.1.refs_4_ = bf16[16,3072]{1,0:T(8,128)(2,1)S(1)} collective-permute-done((bf16[16,3072]{1,0:T(8,128)(2,1)}, bf16[16,3072]{1,0:T(8,128)(2,1)S(1)}, u32[]{:S(2)}, u32[]{:S(2)}) %collective-permute-start.1) | collective-permute-done | bytes 98336 | tf_op jit(solution)/shard_map/ppermute | solution.py:315
  12.6 1.2 %collective-permute-start.5 = (bf16[16,3072]{1,0:T(8,128)(2,1)S(1)}, bf16[16,3072]{1,0:T(8,128)(2,1)S(1)}, u32[]{:S(2)}, u32[]{:S(2)}) collective-permute-start(bf16[16,3072]{1,0:T(8,128)(2,1)S(1)} %collective-permute-done.1.refs_4_), channel_id=1, source_target_pairs={{0,1},{1,0},{2,3},{3,2},{4,5},{5,4},{6,7},{7,6},{8,9},{9,8},{10,11... | collective-permute-start | bytes 294920 | tf_op jit(solution)/shard_map/ppermute | solution.py:310
  14.1 0.7 copy-done.2
  14.8 0.7 copy-done.4
  15.5 3.7 %pair_tables.1 = (s32[4,256]{1,0:T(4,128)S(1)}, s32[4,256]{1,0:T(4,128)S(1)}, s32[4,256]{1,0:T(4,128)S(1)}, s32[4,256]{1,0:T(4,128)S(1)}, bf16[288,128,128]{2,1,0:T(8,128)(2,1)S(1)}) custom-call(s32[1,1,288]{2,1,0:T(1,128)S(1)} %copy-done.4, s32[1,1,288]{2,1,0:T(1,128)S(1)} %copy-done.2, s32[1,1,288]{2,1,0:T(1,128)S(1)} %copy-done.2, ...), custom_call_target="tpu_custom_call" | custom-call | tf_op jit(solution)/shard_map/pair_tables/pallas_call | solution.py:108
  19.2 4.3 %block_product.4 = (bf16[2,32,3072]{2,1,0:T(8,128)(2,1)S(1)}, bf16[2,32,3072]{2,1,0:T(8,128)(2,1)S(1)}, bf16[288,128,128]{2,1,0:T(8,128)(2,1)S(1)}) custom-call(s32[4,256]{1,0:T(4,128)S(1)} %get-tuple-element.57.table_s, s32[1]{0:T(128)} %constant.68.clone.1.in_s.out_s.right_s.left_s, s32[4]{0:T(128)S(1)} %pad_add_fusion.out_s, ...), custom_call_target="tpu_custom_call" | custom-call | flops 1207959552 | bytes 11010048 | tf_op jit(solution)/shard_map/block_product/pallas_call | solution.py:191
  23.5 1.2 %collective-permute-start.7 = (bf16[2,32,3072]{2,1,0:T(8,128)(2,1)S(1)}, bf16[2,32,3072]{2,1,0:T(8,128)(2,1)S(1)}, u32[]{:S(2)}, u32[]{:S(2)}) collective-permute-start(bf16[2,32,3072]{2,1,0:T(8,128)(2,1)S(1)} %get-tuple-element.60), channel_id=1, source_target_pairs={{0,8},{8,0},{16,24},{24,16},{1,9},{9,1},{17,25},{25,17},{2,10},{10... | collective-permute-start | bytes 1179656 | tf_op jit(solution)/shard_map/ppermute | solution.py:310
  24.8 1.9 %collective-permute-start.10 = (bf16[16,3072]{1,0:T(8,128)(2,1)S(1)}, bf16[16,3072]{1,0:T(8,128)(2,1)S(1)}, u32[]{:S(2)}, u32[]{:S(2)}) collective-permute-start(bf16[16,3072]{1,0:T(8,128)(2,1)S(1)} %copy-done), channel_id=1, source_target_pairs={{0,2},{1,3},{2,4},{3,5},{4,6},{5,7},{6,0},{7,1},{8,10},{9,11},{10,... | collective-permute-start | bytes 294920 | tf_op jit(solution)/shard_map/ppermute | solution.py:315
  26.6 3.0 %collective-permute-start.12 = (bf16[16,3072]{1,0:T(8,128)(2,1)S(1)}, bf16[16,3072]{1,0:T(8,128)(2,1)S(1)}, u32[]{:S(2)}, u32[]{:S(2)}) collective-permute-start(bf16[16,3072]{1,0:T(8,128)(2,1)S(1)} %copy-done), channel_id=1, source_target_pairs={{0,4},{1,5},{2,6},{3,7},{4,0},{5,1},{6,2},{7,3},{8,12},{9,13},{10,... | collective-permute-start | bytes 294920 | tf_op jit(solution)/shard_map/ppermute | solution.py:315
  29.6 0.4 collective-permute-start.14
  30.0 1.5 %collective-permute-start.9 = (bf16[16,3072]{1,0:T(8,128)(2,1)S(1)}, bf16[16,3072]{1,0:T(8,128)(2,1)S(1)}, u32[]{:S(2)}, u32[]{:S(2)}) collective-permute-start(bf16[16,3072]{1,0:T(8,128)(2,1)S(1)} %copy-done), channel_id=1, source_target_pairs={{0,1},{1,0},{2,3},{3,2},{4,5},{5,4},{6,7},{7,6},{8,9},{9,8},{10,11... | collective-permute-start | bytes 294920 | tf_op jit(solution)/shard_map/ppermute | solution.py:310
  31.5 0.9 collective-permute-done.10.refs_2_.refs_6_
  32.5 4.4 %collective-permute-done.12.refs_4_.refs_8_ = bf16[16,3072]{1,0:T(8,128)(2,1)S(1)} collective-permute-done((bf16[16,3072]{1,0:T(8,128)(2,1)S(1)}, bf16[16,3072]{1,0:T(8,128)(2,1)S(1)}, u32[]{:S(2)}, u32[]{:S(2)}) %collective-permute-start.12) | collective-permute-done | bytes 98336 | tf_op jit(solution)/shard_map/ppermute | solution.py:315
  36.9 1.5 %collective-permute-start.15 = (bf16[16,3072]{1,0:T(8,128)(2,1)S(1)}, bf16[16,3072]{1,0:T(8,128)(2,1)S(1)}, u32[]{:S(2)}, u32[]{:S(2)}) collective-permute-start(bf16[16,3072]{1,0:T(8,128)(2,1)S(1)} %collective-permute-done.14.refs_6_.refs_10_), channel_id=1, source_target_pairs={{0,1},{1,0},{2,3},{3,2},{4,5},{5,4},{6,7},{7,6},{8,9},{9,8},{10,11... | collective-permute-start | bytes 294920 | tf_op jit(solution)/shard_map/ppermute | solution.py:310
  38.4 2.3 %collective-permute-done.13.refs_5_.refs_9_ = bf16[16,3072]{1,0:T(8,128)(2,1)S(1)} collective-permute-done((bf16[16,3072]{1,0:T(8,128)(2,1)S(1)}, bf16[16,3072]{1,0:T(8,128)(2,1)S(1)}, u32[]{:S(2)}, u32[]{:S(2)}) %collective-permute-start.13) | collective-permute-done | bytes 98336 | tf_op jit(solution)/shard_map/ppermute | solution.py:310
  40.7 2.1 %collective-permute-done.15.refs_7_.refs_11_ = bf16[16,3072]{1,0:T(8,128)(2,1)S(1)} collective-permute-done((bf16[16,3072]{1,0:T(8,128)(2,1)S(1)}, bf16[16,3072]{1,0:T(8,128)(2,1)S(1)}, u32[]{:S(2)}, u32[]{:S(2)}) %collective-permute-start.15) | collective-permute-done | bytes 98336 | tf_op jit(solution)/shard_map/ppermute | solution.py:310
  42.8 4.2 %block_product.5 = (bf16[2,32,3072]{2,1,0:T(8,128)(2,1)S(1)}, bf16[2,32,3072]{2,1,0:T(8,128)(2,1)S(1)}) custom-call(s32[4,256]{1,0:T(4,128)S(1)} %get-tuple-element.61.table_s, s32[1]{0:T(128)} %constant.68.clone.1.in_s.out_s.right_s.left_s, s32[4]{0:T(128)S(1)} %pad_add_fusion.out_s, bf16[16,3072]{1,0:T(8,128)(2,1)S(1)} %copy-done, ...), custom_call_target="tpu_custom_call" | custom-call | flops 1207959552 | bytes 11010048 | tf_op jit(solution)/shard_map/block_product/pallas_call | solution.py:191
  47.0 0.5 collective-permute-start.16
  47.5 6.4 %collective-permute-done.8 = bf16[32,3072]{1,0:T(8,128)(2,1)S(1)} collective-permute-done((bf16[32,3072]{1,0:T(8,128)(2,1)S(1)}, bf16[32,3072]{1,0:T(8,128)(2,1)S(1)}, u32[]{:S(2)}, u32[]{:S(2)}) %collective-permute-start.8) | collective-permute-done | bytes 196640 | tf_op jit(solution)/shard_map/ppermute | solution.py:315
  53.9 0.3 collective-permute-start.19
  54.5 1.0 collective-permute-start.17
  55.5 1.5 %collective-permute-start.18 = (bf16[32,3072]{1,0:T(8,128)(2,1)S(1)}, bf16[32,3072]{1,0:T(8,128)(2,1)S(1)}, u32[]{:S(2)}, u32[]{:S(2)}) collective-permute-start(bf16[32,3072]{1,0:T(8,128)(2,1)S(1)} %multiply_convert_fusion.refs_0_), channel_id=1, source_target_pairs={{0,16},{8,24},{16,0},{24,8},{1,17},{9,25},{17,1},{25,9},{2,18},{10... | collective-permute-start | bytes 589832 | tf_op jit(solution)/shard_map/ppermute | solution.py:315
  57.0 2.5 %collective-permute-done.19 = bf16[32,3072]{1,0:T(8,128)(2,1)S(1)} collective-permute-done((bf16[32,3072]{1,0:T(8,128)(2,1)S(1)}, bf16[32,3072]{1,0:T(8,128)(2,1)S(1)}, u32[]{:S(2)}, u32[]{:S(2)}) %collective-permute-start.19) | collective-permute-done | bytes 196640 | tf_op jit(solution)/shard_map/ppermute | solution.py:315
  59.5 0.4 fusion.6.refs_0_.refs_8_
  59.9 3.8 %collective-permute-done.18.refs_2_ = bf16[32,3072]{1,0:T(8,128)(2,1)S(1)} collective-permute-done((bf16[32,3072]{1,0:T(8,128)(2,1)S(1)}, bf16[32,3072]{1,0:T(8,128)(2,1)S(1)}, u32[]{:S(2)}, u32[]{:S(2)}) %collective-permute-start.18) | collective-permute-done | bytes 196640 | tf_op jit(solution)/shard_map/ppermute | solution.py:315
  63.7 1.8 %collective-permute-start.20 = (bf16[32,3072]{1,0:T(8,128)(2,1)S(1)}, bf16[32,3072]{1,0:T(8,128)(2,1)S(1)}, u32[]{:S(2)}, u32[]{:S(2)}) collective-permute-start(bf16[32,3072]{1,0:T(8,128)(2,1)S(1)} %collective-permute-done.18.refs_2_), channel_id=1, source_target_pairs={{0,8},{8,0},{16,24},{24,16},{1,9},{9,1},{17,25},{25,17},{2,10},{10... | collective-permute-start | bytes 589832 | tf_op jit(solution)/shard_map/ppermute | solution.py:310
  66.1 0.5 collective-permute-done.20.refs_3_
  66.6 5.4 %collective-permute-done.23.refs_2_.refs_10_ = bf16[32,3072]{1,0:T(8,128)(2,1)S(1)} collective-permute-done((bf16[32,3072]{1,0:T(8,128)(2,1)S(1)}, bf16[32,3072]{1,0:T(8,128)(2,1)S(1)}, u32[]{:S(2)}, u32[]{:S(2)}) %collective-permute-start.23) | collective-permute-done | bytes 196640 | tf_op jit(solution)/shard_map/ppermute | solution.py:315
  72.0 0.9 collective-permute-start.24
  72.9 4.5 %block_product.6 = (bf16[4,16,3072]{2,1,0:T(8,128)(2,1)S(1)}, bf16[4,16,3072]{2,1,0:T(8,128)(2,1)S(1)}, bf16[288,128,128]{2,1,0:T(8,128)(2,1)S(1)}) custom-call(s32[4,256]{1,0:T(4,128)S(1)} %get-tuple-element.56.table_s, s32[4]{0:T(128)S(1)} %fusion.26.in_s.left_s.right_s, s32[1]{0:T(128)} %constant.68.clone.1.in_s.out_s.right_s.left_s, ...), custom_call_target="tpu_custom_call" | custom-call | flops 1207959552 | bytes 11010048 | tf_op jit(solution)/shard_map/block_product/pallas_call | solution.py:191
  77.5 3.3 %block_product.7 = (bf16[4,16,3072]{2,1,0:T(8,128)(2,1)S(1)}, bf16[4,16,3072]{2,1,0:T(8,128)(2,1)S(1)}) custom-call(s32[4,256]{1,0:T(4,128)S(1)} %get-tuple-element.82.table_s, s32[4]{0:T(128)S(1)} %fusion.26.in_s.left_s.right_s, s32[1]{0:T(128)} %constant.68.clone.1.in_s.out_s.right_s.left_s, bf16[32,3072]{1,0:T(8,128)(2,1)S(1)} %fusion.6.refs_0_.refs_8_, ...), custom_call_target="tpu_custom_call" | custom-call | flops 1207959552 | bytes 11010048 | tf_op jit(solution)/shard_map/block_product/pallas_call | solution.py:191
  80.8 0.6 collective-permute-start.28
  81.3 5.5 %block_grads.3.refs_12_ = f32[288,128,128]{2,1,0:T(8,128)} custom-call(s32[1,1,288]{2,1,0:T(1,128)S(1)} %copy-done.3, s32[4]{0:T(128)S(1)} %fusion.26.in_s.left_s.right_s, s32[1]{0:T(128)} %constant.68.clone.1.in_s.out_s.right_s.left_s, bf16[32,3072]{1,0:T(8,128)(2,1)S(1)} %multiply_convert_fusion.refs_0_, ...), custom_call_target="tpu_custom_call" | custom-call | flops 1207959552 | bytes 20447232 | tf_op jit(solution)/shard_map/block_grads/pallas_call | solution.py:262
  86.9 1.3 %collective-permute-done.21 = bf16[4,16,3072]{2,1,0:T(8,128)(2,1)S(1)} collective-permute-done((bf16[4,16,3072]{2,1,0:T(8,128)(2,1)S(1)}, bf16[4,16,3072]{2,1,0:T(8,128)(2,1)S(1)}, u32[]{:S(2)}, u32[]{:S(2)}) %collective-permute-start.21) | collective-permute-done | bytes 393248 | tf_op jit(solution)/shard_map/ppermute | solution.py:310
  88.2 4.9 %collective-permute-start.27 = (bf16[16,3072]{1,0:T(8,128)(2,1)S(1)}, bf16[16,3072]{1,0:T(8,128)(2,1)S(1)}, u32[]{:S(2)}, u32[]{:S(2)}) collective-permute-start(bf16[16,3072]{1,0:T(8,128)(2,1)S(1)} %get-tuple-element.108), channel_id=1, source_target_pairs={{0,2},{1,3},{2,4},{3,5},{4,6},{5,7},{6,0},{7,1},{8,10},{9,11},{10,... | collective-permute-start | bytes 294920 | tf_op jit(solution)/shard_map/ppermute | solution.py:315
  93.1 2.2 %collective-permute-start.25 = (bf16[16,3072]{1,0:T(8,128)(2,1)S(1)}, bf16[16,3072]{1,0:T(8,128)(2,1)S(1)}, u32[]{:S(2)}, u32[]{:S(2)}) collective-permute-start(bf16[16,3072]{1,0:T(8,128)(2,1)S(1)} %get-tuple-element.107), channel_id=1, source_target_pairs={{0,6},{1,7},{2,0},{3,1},{4,2},{5,3},{6,4},{7,5},{8,14},{9,15},{10,... | collective-permute-start | bytes 294920 | tf_op jit(solution)/shard_map/ppermute | solution.py:315
  95.3 5.5 %block_grads.4 = f32[288,128,128]{2,1,0:T(8,128)} custom-call(s32[1,1,288]{2,1,0:T(1,128)S(1)} %copy-done.3, s32[4]{0:T(128)S(1)} %fusion.26.in_s.left_s.right_s, s32[1]{0:T(128)} %constant.68.clone.1.in_s.out_s.right_s.left_s, bf16[32,3072]{1,0:T(8,128)(2,1)S(1)} %multiply_convert_fusion.refs_0_, ...), custom_call_target="tpu_custom_call", output_to_operand_aliasing={{}: (15, {})} | custom-call | flops 1207959552 | bytes 20447232 | tf_op jit(solution)/shard_map/block_grads/pallas_call | solution.py:262
  100.8 0.9 collective-permute-done.26
  101.7 0.7 fusion.14
  102.5 2.4 %collective-permute-start.31 = (bf16[16,3072]{1,0:T(8,128)(2,1)S(1)}, bf16[16,3072]{1,0:T(8,128)(2,1)S(1)}, u32[]{:S(2)}, u32[]{:S(2)}) collective-permute-start(bf16[16,3072]{1,0:T(8,128)(2,1)S(1)} %get-tuple-element.105), channel_id=1, source_target_pairs={{0,2},{1,3},{2,4},{3,5},{4,6},{5,7},{6,0},{7,1},{8,10},{9,11},{10,... | collective-permute-start | bytes 294920 | tf_op jit(solution)/shard_map/ppermute | solution.py:315
  104.9 2.2 %collective-permute-start.29 = (bf16[16,3072]{1,0:T(8,128)(2,1)S(1)}, bf16[16,3072]{1,0:T(8,128)(2,1)S(1)}, u32[]{:S(2)}, u32[]{:S(2)}) collective-permute-start(bf16[16,3072]{1,0:T(8,128)(2,1)S(1)} %get-tuple-element.104), channel_id=1, source_target_pairs={{0,6},{1,7},{2,0},{3,1},{4,2},{5,3},{6,4},{7,5},{8,14},{9,15},{10,... | collective-permute-start | bytes 294920 | tf_op jit(solution)/shard_map/ppermute | solution.py:315
  107.1 8.7 %block_grads.5 = f32[288,128,128]{2,1,0:T(8,128)} custom-call(s32[1,1,288]{2,1,0:T(1,128)S(1)} %copy-done.5, s32[1]{0:T(128)} %constant.68.clone.1.in_s.out_s.right_s.left_s, s32[4]{0:T(128)S(1)} %fusion.26.in_s.left_s.right_s, bf16[16,3072]{1,0:T(8,128)(2,1)S(1)} %copy-done.1, bf16[16,3072]{1,0:T(8,128)(2,1)S(1)} %collective-permute-done.3.refs_1_, ...), custom_call_target="tpu_custom_call" | custom-call | flops 1207959552 | bytes 20447232 | tf_op jit(solution)/shard_map/block_grads/pallas_call | solution.py:262
  115.8 0.7 fusion.11
  (48 shorter events, 1.7 us)
Async XLA Ops:
  0.6 18.6 %copy-start.1 = (bf16[16,3072]{1,0:T(8,128)(2,1)S(1)}, bf16[16,3072]{1,0:T(8,128)(2,1)}, u32[]{:S(2)}) copy-start(bf16[16,3072]{1,0:T(8,128)(2,1)} %refs_0_.5) | copy-start | bytes 294916
  0.6 7.0 %collective-permute-start = (bf16[16,3072]{1,0:T(8,128)(2,1)}, bf16[16,3072]{1,0:T(8,128)(2,1)S(1)}, u32[]{:S(2)}, u32[]{:S(2)}) collective-permute-start(bf16[16,3072]{1,0:T(8,128)(2,1)} %refs_0_.5), channel_id=1, source_target_pairs={{0,2},{1,3},{2,4},{3,5},{4,6},{5,7},{6,0},{7,1},{8,10},{9,11},{10,... | collective-permute-start | bytes 294920 | tf_op jit(solution)/shard_map/ppermute | solution.py:315
  2.8 9.8 %collective-permute-start.1 = (bf16[16,3072]{1,0:T(8,128)(2,1)}, bf16[16,3072]{1,0:T(8,128)(2,1)S(1)}, u32[]{:S(2)}, u32[]{:S(2)}) collective-permute-start(bf16[16,3072]{1,0:T(8,128)(2,1)} %refs_0_.5), channel_id=1, source_target_pairs={{0,4},{1,5},{2,6},{3,7},{4,0},{5,1},{6,2},{7,3},{8,12},{9,13},{10,... | collective-permute-start | bytes 294920 | tf_op jit(solution)/shard_map/ppermute | solution.py:315
  5.1 8.7 %collective-permute-start.2 = (bf16[16,3072]{1,0:T(8,128)(2,1)}, bf16[16,3072]{1,0:T(8,128)(2,1)S(1)}, u32[]{:S(2)}, u32[]{:S(2)}) collective-permute-start(bf16[16,3072]{1,0:T(8,128)(2,1)} %refs_0_.5), channel_id=1, source_target_pairs={{0,6},{1,7},{2,0},{3,1},{4,2},{5,3},{6,4},{7,5},{8,14},{9,15},{10,... | collective-permute-start | bytes 294920 | tf_op jit(solution)/shard_map/ppermute | solution.py:315
  6.2 13.0 %collective-permute-start.3 = (bf16[16,3072]{1,0:T(8,128)(2,1)}, bf16[16,3072]{1,0:T(8,128)(2,1)S(1)}, u32[]{:S(2)}, u32[]{:S(2)}) collective-permute-start(bf16[16,3072]{1,0:T(8,128)(2,1)} %refs_0_.5), channel_id=1, source_target_pairs={{0,1},{1,0},{2,3},{3,2},{4,5},{5,4},{6,7},{7,6},{8,9},{9,8},{10,11... | collective-permute-start | bytes 294920 | tf_op jit(solution)/shard_map/ppermute | solution.py:310
  7.6 11.6 %collective-permute-start.4 = (bf16[16,3072]{1,0:T(8,128)(2,1)S(1)}, bf16[16,3072]{1,0:T(8,128)(2,1)S(1)}, u32[]{:S(2)}, u32[]{:S(2)}) collective-permute-start(bf16[16,3072]{1,0:T(8,128)(2,1)S(1)} %collective-permute-done.refs_2_), channel_id=1, source_target_pairs={{0,1},{1,0},{2,3},{3,2},{4,5},{5,4},{6,7},{7,6},{8,9},{9,8},{10,11... | collective-permute-start | bytes 294920 | tf_op jit(solution)/shard_map/ppermute | solution.py:310
  12.6 6.6 %collective-permute-start.5 = (bf16[16,3072]{1,0:T(8,128)(2,1)S(1)}, bf16[16,3072]{1,0:T(8,128)(2,1)S(1)}, u32[]{:S(2)}, u32[]{:S(2)}) collective-permute-start(bf16[16,3072]{1,0:T(8,128)(2,1)S(1)} %collective-permute-done.1.refs_4_), channel_id=1, source_target_pairs={{0,1},{1,0},{2,3},{3,2},{4,5},{5,4},{6,7},{7,6},{8,9},{9,8},{10,11... | collective-permute-start | bytes 294920 | tf_op jit(solution)/shard_map/ppermute | solution.py:310
  13.8 5.4 %collective-permute-start.6 = (bf16[16,3072]{1,0:T(8,128)(2,1)S(1)}, bf16[16,3072]{1,0:T(8,128)(2,1)S(1)}, u32[]{:S(2)}, u32[]{:S(2)}) collective-permute-start(bf16[16,3072]{1,0:T(8,128)(2,1)S(1)} %collective-permute-done.2.refs_6_), channel_id=1, source_target_pairs={{0,1},{1,0},{2,3},{3,2},{4,5},{5,4},{6,7},{7,6},{8,9},{9,8},{10,11... | collective-permute-start | bytes 294920 | tf_op jit(solution)/shard_map/ppermute | solution.py:310
  14.1 0.7 copy-start.2
  14.8 0.7 copy-start.4
  19.2 5.5 %copy-start = (bf16[16,3072]{1,0:T(8,128)(2,1)S(1)}, bf16[16,3072]{1,0:T(8,128)(2,1)}, u32[]{:S(2)}) copy-start(bf16[16,3072]{1,0:T(8,128)(2,1)} %refs_4_.3) | copy-start | bytes 294916
  23.5 14.8 %collective-permute-start.7 = (bf16[2,32,3072]{2,1,0:T(8,128)(2,1)S(1)}, bf16[2,32,3072]{2,1,0:T(8,128)(2,1)S(1)}, u32[]{:S(2)}, u32[]{:S(2)}) collective-permute-start(bf16[2,32,3072]{2,1,0:T(8,128)(2,1)S(1)} %get-tuple-element.60), channel_id=1, source_target_pairs={{0,8},{8,0},{16,24},{24,16},{1,9},{9,1},{17,25},{25,17},{2,10},{10... | collective-permute-start | bytes 1179656 | tf_op jit(solution)/shard_map/ppermute | solution.py:310
  24.8 7.7 %collective-permute-start.10 = (bf16[16,3072]{1,0:T(8,128)(2,1)S(1)}, bf16[16,3072]{1,0:T(8,128)(2,1)S(1)}, u32[]{:S(2)}, u32[]{:S(2)}) collective-permute-start(bf16[16,3072]{1,0:T(8,128)(2,1)S(1)} %copy-done), channel_id=1, source_target_pairs={{0,2},{1,3},{2,4},{3,5},{4,6},{5,7},{6,0},{7,1},{8,10},{9,11},{10,... | collective-permute-start | bytes 294920 | tf_op jit(solution)/shard_map/ppermute | solution.py:315
  26.6 10.3 %collective-permute-start.12 = (bf16[16,3072]{1,0:T(8,128)(2,1)S(1)}, bf16[16,3072]{1,0:T(8,128)(2,1)S(1)}, u32[]{:S(2)}, u32[]{:S(2)}) collective-permute-start(bf16[16,3072]{1,0:T(8,128)(2,1)S(1)} %copy-done), channel_id=1, source_target_pairs={{0,4},{1,5},{2,6},{3,7},{4,0},{5,1},{6,2},{7,3},{8,12},{9,13},{10,... | collective-permute-start | bytes 294920 | tf_op jit(solution)/shard_map/ppermute | solution.py:315
  29.6 7.2 %collective-permute-start.14 = (bf16[16,3072]{1,0:T(8,128)(2,1)S(1)}, bf16[16,3072]{1,0:T(8,128)(2,1)S(1)}, u32[]{:S(2)}, u32[]{:S(2)}) collective-permute-start(bf16[16,3072]{1,0:T(8,128)(2,1)S(1)} %copy-done), channel_id=1, source_target_pairs={{0,6},{1,7},{2,0},{3,1},{4,2},{5,3},{6,4},{7,5},{8,14},{9,15},{10,... | collective-permute-start | bytes 294920 | tf_op jit(solution)/shard_map/ppermute | solution.py:315
  30.0 8.4 %collective-permute-start.9 = (bf16[16,3072]{1,0:T(8,128)(2,1)S(1)}, bf16[16,3072]{1,0:T(8,128)(2,1)S(1)}, u32[]{:S(2)}, u32[]{:S(2)}) collective-permute-start(bf16[16,3072]{1,0:T(8,128)(2,1)S(1)} %copy-done), channel_id=1, source_target_pairs={{0,1},{1,0},{2,3},{3,2},{4,5},{5,4},{6,7},{7,6},{8,9},{9,8},{10,11... | collective-permute-start | bytes 294920 | tf_op jit(solution)/shard_map/ppermute | solution.py:310
  32.5 6.0 %collective-permute-start.11 = (bf16[16,3072]{1,0:T(8,128)(2,1)S(1)}, bf16[16,3072]{1,0:T(8,128)(2,1)S(1)}, u32[]{:S(2)}, u32[]{:S(2)}) collective-permute-start(bf16[16,3072]{1,0:T(8,128)(2,1)S(1)} %collective-permute-done.10.refs_2_.refs_6_), channel_id=1, source_target_pairs={{0,1},{1,0},{2,3},{3,2},{4,5},{5,4},{6,7},{7,6},{8,9},{9,8},{10,11... | collective-permute-start | bytes 294920 | tf_op jit(solution)/shard_map/ppermute | solution.py:310
  36.9 3.9 %collective-permute-start.13 = (bf16[16,3072]{1,0:T(8,128)(2,1)S(1)}, bf16[16,3072]{1,0:T(8,128)(2,1)S(1)}, u32[]{:S(2)}, u32[]{:S(2)}) collective-permute-start(bf16[16,3072]{1,0:T(8,128)(2,1)S(1)} %collective-permute-done.12.refs_4_.refs_8_), channel_id=1, source_target_pairs={{0,1},{1,0},{2,3},{3,2},{4,5},{5,4},{6,7},{7,6},{8,9},{9,8},{10,11... | collective-permute-start | bytes 294920 | tf_op jit(solution)/shard_map/ppermute | solution.py:310
  36.9 6.0 %collective-permute-start.15 = (bf16[16,3072]{1,0:T(8,128)(2,1)S(1)}, bf16[16,3072]{1,0:T(8,128)(2,1)S(1)}, u32[]{:S(2)}, u32[]{:S(2)}) collective-permute-start(bf16[16,3072]{1,0:T(8,128)(2,1)S(1)} %collective-permute-done.14.refs_6_.refs_10_), channel_id=1, source_target_pairs={{0,1},{1,0},{2,3},{3,2},{4,5},{5,4},{6,7},{7,6},{8,9},{9,8},{10,11... | collective-permute-start | bytes 294920 | tf_op jit(solution)/shard_map/ppermute | solution.py:310
  47.0 6.8 %collective-permute-start.16 = (bf16[2,32,3072]{2,1,0:T(8,128)(2,1)S(1)}, bf16[2,32,3072]{2,1,0:T(8,128)(2,1)S(1)}, u32[]{:S(2)}, u32[]{:S(2)}) collective-permute-start(bf16[2,32,3072]{2,1,0:T(8,128)(2,1)S(1)} %get-tuple-element.72), channel_id=1, source_target_pairs={{0,8},{8,0},{16,24},{24,16},{1,9},{9,1},{17,25},{25,17},{2,10},{10... | collective-permute-start | bytes 1179656 | tf_op jit(solution)/shard_map/ppermute | solution.py:310
  47.5 6.4 %collective-permute-start.8 = (bf16[32,3072]{1,0:T(8,128)(2,1)S(1)}, bf16[32,3072]{1,0:T(8,128)(2,1)S(1)}, u32[]{:S(2)}, u32[]{:S(2)}) collective-permute-start(bf16[32,3072]{1,0:T(8,128)(2,1)S(1)} %fusion.7), channel_id=1, source_target_pairs={{0,16},{8,24},{16,0},{24,8},{1,17},{9,25},{17,1},{25,9},{2,18},{10... | collective-permute-start | bytes 589832 | tf_op jit(solution)/shard_map/ppermute | solution.py:315
  53.9 5.6 %collective-permute-start.19 = (bf16[32,3072]{1,0:T(8,128)(2,1)S(1)}, bf16[32,3072]{1,0:T(8,128)(2,1)S(1)}, u32[]{:S(2)}, u32[]{:S(2)}) collective-permute-start(bf16[32,3072]{1,0:T(8,128)(2,1)S(1)} %fusion.8), channel_id=1, source_target_pairs={{0,16},{8,24},{16,0},{24,8},{1,17},{9,25},{17,1},{25,9},{2,18},{10... | collective-permute-start | bytes 589832 | tf_op jit(solution)/shard_map/ppermute | solution.py:315
  54.5 11.6 %collective-permute-start.17 = (bf16[32,3072]{1,0:T(8,128)(2,1)S(1)}, bf16[32,3072]{1,0:T(8,128)(2,1)S(1)}, u32[]{:S(2)}, u32[]{:S(2)}) collective-permute-start(bf16[32,3072]{1,0:T(8,128)(2,1)S(1)} %multiply_convert_fusion.refs_0_), channel_id=1, source_target_pairs={{0,8},{8,0},{16,24},{24,16},{1,9},{9,1},{17,25},{25,17},{2,10},{10... | collective-permute-start | bytes 589832 | tf_op jit(solution)/shard_map/ppermute | solution.py:310
  55.5 8.2 %collective-permute-start.18 = (bf16[32,3072]{1,0:T(8,128)(2,1)S(1)}, bf16[32,3072]{1,0:T(8,128)(2,1)S(1)}, u32[]{:S(2)}, u32[]{:S(2)}) collective-permute-start(bf16[32,3072]{1,0:T(8,128)(2,1)S(1)} %multiply_convert_fusion.refs_0_), channel_id=1, source_target_pairs={{0,16},{8,24},{16,0},{24,8},{1,17},{9,25},{17,1},{25,9},{2,18},{10... | collective-permute-start | bytes 589832 | tf_op jit(solution)/shard_map/ppermute | solution.py:315
  63.7 2.9 %collective-permute-start.20 = (bf16[32,3072]{1,0:T(8,128)(2,1)S(1)}, bf16[32,3072]{1,0:T(8,128)(2,1)S(1)}, u32[]{:S(2)}, u32[]{:S(2)}) collective-permute-start(bf16[32,3072]{1,0:T(8,128)(2,1)S(1)} %collective-permute-done.18.refs_2_), channel_id=1, source_target_pairs={{0,8},{8,0},{16,24},{24,16},{1,9},{9,1},{17,25},{25,17},{2,10},{10... | collective-permute-start | bytes 589832 | tf_op jit(solution)/shard_map/ppermute | solution.py:310
  65.5 6.5 %collective-permute-start.23 = (bf16[32,3072]{1,0:T(8,128)(2,1)S(1)}, bf16[32,3072]{1,0:T(8,128)(2,1)S(1)}, u32[]{:S(2)}, u32[]{:S(2)}) collective-permute-start(bf16[32,3072]{1,0:T(8,128)(2,1)S(1)} %fusion.6.refs_0_.refs_8_), channel_id=1, source_target_pairs={{0,16},{8,24},{16,0},{24,8},{1,17},{9,25},{17,1},{25,9},{2,18},{10... | collective-permute-start | bytes 589832 | tf_op jit(solution)/shard_map/ppermute | solution.py:315
  65.8 11.7 %collective-permute-start.22 = (bf16[32,3072]{1,0:T(8,128)(2,1)S(1)}, bf16[32,3072]{1,0:T(8,128)(2,1)S(1)}, u32[]{:S(2)}, u32[]{:S(2)}) collective-permute-start(bf16[32,3072]{1,0:T(8,128)(2,1)S(1)} %fusion.6.refs_0_.refs_8_), channel_id=1, source_target_pairs={{0,8},{8,0},{16,24},{24,16},{1,9},{9,1},{17,25},{25,17},{2,10},{10... | collective-permute-start | bytes 589832 | tf_op jit(solution)/shard_map/ppermute | solution.py:310
  72.0 5.5 %collective-permute-start.24 = (bf16[32,3072]{1,0:T(8,128)(2,1)S(1)}, bf16[32,3072]{1,0:T(8,128)(2,1)S(1)}, u32[]{:S(2)}, u32[]{:S(2)}) collective-permute-start(bf16[32,3072]{1,0:T(8,128)(2,1)S(1)} %collective-permute-done.23.refs_2_.refs_10_), channel_id=1, source_target_pairs={{0,8},{8,0},{16,24},{24,16},{1,9},{9,1},{17,25},{25,17},{2,10},{10... | collective-permute-start | bytes 589832 | tf_op jit(solution)/shard_map/ppermute | solution.py:310
  77.4 4.0 %copy-start.3 = (s32[1,1,288]{2,1,0:T(1,128)S(1)}, s32[1,1,288]{2,1,0:T(1,128)}, u32[]{:S(2)}) copy-start(s32[1,1,288]{2,1,0:T(1,128)} %slot_s.4) | copy-start | bytes 3460
  77.4 10.7 %collective-permute-start.21 = (bf16[4,16,3072]{2,1,0:T(8,128)(2,1)S(1)}, bf16[4,16,3072]{2,1,0:T(8,128)(2,1)S(1)}, u32[]{:S(2)}, u32[]{:S(2)}) collective-permute-start(bf16[4,16,3072]{2,1,0:T(8,128)(2,1)S(1)} %get-tuple-element.81), channel_id=1, source_target_pairs={{0,1},{1,0},{2,3},{3,2},{4,5},{5,4},{6,7},{7,6},{8,9},{9,8},{10,11... | collective-permute-start | bytes 1179656 | tf_op jit(solution)/shard_map/ppermute | solution.py:310
  80.8 21.6 %collective-permute-start.28 = (bf16[4,16,3072]{2,1,0:T(8,128)(2,1)S(1)}, bf16[4,16,3072]{2,1,0:T(8,128)(2,1)S(1)}, u32[]{:S(2)}, u32[]{:S(2)}) collective-permute-start(bf16[4,16,3072]{2,1,0:T(8,128)(2,1)S(1)} %get-tuple-element.94), channel_id=1, source_target_pairs={{0,1},{1,0},{2,3},{3,2},{4,5},{5,4},{6,7},{7,6},{8,9},{9,8},{10,11... | collective-permute-start | bytes 1179656 | tf_op jit(solution)/shard_map/ppermute | solution.py:310
  88.2 12.6 %collective-permute-start.27 = (bf16[16,3072]{1,0:T(8,128)(2,1)S(1)}, bf16[16,3072]{1,0:T(8,128)(2,1)S(1)}, u32[]{:S(2)}, u32[]{:S(2)}) collective-permute-start(bf16[16,3072]{1,0:T(8,128)(2,1)S(1)} %get-tuple-element.108), channel_id=1, source_target_pairs={{0,2},{1,3},{2,4},{3,5},{4,6},{5,7},{6,0},{7,1},{8,10},{9,11},{10,... | collective-permute-start | bytes 294920 | tf_op jit(solution)/shard_map/ppermute | solution.py:315
  93.1 8.6 %collective-permute-start.26 = (bf16[16,3072]{1,0:T(8,128)(2,1)S(1)}, bf16[16,3072]{1,0:T(8,128)(2,1)S(1)}, u32[]{:S(2)}, u32[]{:S(2)}) collective-permute-start(bf16[16,3072]{1,0:T(8,128)(2,1)S(1)} %get-tuple-element.109), channel_id=1, source_target_pairs={{0,4},{1,5},{2,6},{3,7},{4,0},{5,1},{6,2},{7,3},{8,12},{9,13},{10,... | collective-permute-start | bytes 294920 | tf_op jit(solution)/shard_map/ppermute | solution.py:315
  93.1 14.0 %copy-start.5 = (s32[1,1,288]{2,1,0:T(1,128)S(1)}, s32[1,1,288]{2,1,0:T(1,128)}, u32[]{:S(2)}) copy-start(s32[1,1,288]{2,1,0:T(1,128)} %slot_s.5) | copy-start | bytes 3460
  93.1 8.6 %collective-permute-start.25 = (bf16[16,3072]{1,0:T(8,128)(2,1)S(1)}, bf16[16,3072]{1,0:T(8,128)(2,1)S(1)}, u32[]{:S(2)}, u32[]{:S(2)}) collective-permute-start(bf16[16,3072]{1,0:T(8,128)(2,1)S(1)} %get-tuple-element.107), channel_id=1, source_target_pairs={{0,6},{1,7},{2,0},{3,1},{4,2},{5,3},{6,4},{7,5},{8,14},{9,15},{10,... | collective-permute-start | bytes 294920 | tf_op jit(solution)/shard_map/ppermute | solution.py:315
  102.5 13.3 %collective-permute-start.31 = (bf16[16,3072]{1,0:T(8,128)(2,1)S(1)}, bf16[16,3072]{1,0:T(8,128)(2,1)S(1)}, u32[]{:S(2)}, u32[]{:S(2)}) collective-permute-start(bf16[16,3072]{1,0:T(8,128)(2,1)S(1)} %get-tuple-element.105), channel_id=1, source_target_pairs={{0,2},{1,3},{2,4},{3,5},{4,6},{5,7},{6,0},{7,1},{8,10},{9,11},{10,... | collective-permute-start | bytes 294920 | tf_op jit(solution)/shard_map/ppermute | solution.py:315
  104.9 10.9 %collective-permute-start.30 = (bf16[16,3072]{1,0:T(8,128)(2,1)S(1)}, bf16[16,3072]{1,0:T(8,128)(2,1)S(1)}, u32[]{:S(2)}, u32[]{:S(2)}) collective-permute-start(bf16[16,3072]{1,0:T(8,128)(2,1)S(1)} %get-tuple-element.106), channel_id=1, source_target_pairs={{0,4},{1,5},{2,6},{3,7},{4,0},{5,1},{6,2},{7,3},{8,12},{9,13},{10,... | collective-permute-start | bytes 294920 | tf_op jit(solution)/shard_map/ppermute | solution.py:315
  104.9 10.9 %collective-permute-start.29 = (bf16[16,3072]{1,0:T(8,128)(2,1)S(1)}, bf16[16,3072]{1,0:T(8,128)(2,1)S(1)}, u32[]{:S(2)}, u32[]{:S(2)}) collective-permute-start(bf16[16,3072]{1,0:T(8,128)(2,1)S(1)} %get-tuple-element.104), channel_id=1, source_target_pairs={{0,6},{1,7},{2,0},{3,1},{4,2},{5,3},{6,4},{7,5},{8,14},{9,15},{10,... | collective-permute-start | bytes 294920 | tf_op jit(solution)/shard_map/ppermute | solution.py:315

commit v6 on v5

--- a/solution.py
+++ b/solution.py
@@ -50,9 +50,11 @@
 
     def body(*refs):
         slot_refs, far, tables, near = refs[:n], refs[n : n + m], refs[n + m : 2 * n + m], refs[2 * n + m : 2 * n + 2 * m]
-        padded, sems = refs[2 * n + 2 * m], refs[2 * n + 2 * m + 1 :]
+        padded, listed = refs[2 * n + 2 * m : 2 * n + 2 * m + 2]
+        sems, list_sems = refs[2 * n + 2 * m + 2 : 2 * n + 3 * m + 2], refs[2 * n + 3 * m + 2 :]
+        lists = [pltpu.make_async_copy(slot_refs[t], listed.at[t], list_sems[t]) for t in range(n)]
         copies = [pltpu.make_async_copy(*copy) for copy in zip(far, near, sems)]
-        for copy in copies:
+        for copy in lists + copies:
             copy.start()
         iota = lambda shape, dim: lax.broadcasted_iota(jnp.int32, shape, dim)
         matmul = lambda x, y, dim: lax.dot_general(
@@ -68,7 +70,8 @@
             n_dst, n_src = (rows, cols) if by_row else (cols, rows)
             dst_pad, limit = -(-n_dst // 16) * 16, limits[t]
             padded[...] = jnp.full((1, lanes), -1, jnp.int32)
-            padded[:, :cap] = slot_refs[t][0]
+            lists[t].wait()
+            padded[:, :cap] = listed[t, 0]
             pos = padded[...]
             filled = pos >= 0
             safe = jnp.maximum(pos, 0)
@@ -107,14 +110,15 @@
     vmem = pl.BlockSpec(memory_space=pltpu.VMEM)
     return pl.pallas_call(
         body,
-        in_specs=[vmem] * n + [pl.BlockSpec(memory_space=pltpu.HBM)] * m,
+        in_specs=[pl.BlockSpec(memory_space=pltpu.HBM)] * (n + m),
         out_specs=[vmem] * (n + m),
         out_shape=[jax.ShapeDtypeStruct((4, limit), jnp.int32) for limit in limits]
         + [jax.ShapeDtypeStruct(weight.shape, weight.dtype) for weight in weights],
-        scratch_shapes=[pltpu.VMEM((1, lanes), jnp.int32)] + [pltpu.SemaphoreType.DMA] * m,
+        scratch_shapes=[pltpu.VMEM((1, lanes), jnp.int32), pltpu.VMEM((n, 1, 1, cap), jnp.int32)]
+        + [pltpu.SemaphoreType.DMA] * (m + n),
         compiler_params=pltpu.CompilerParams(vmem_limit_bytes=8 * 1024 * 1024),
         name="pair_tables",
-    )(*[job[0] for job in jobs], *weights)
+    )(*[pltpu.with_memory_space_constraint(job[0], pltpu.HBM) for job in jobs], *weights)
 
 
 PAIR_SHIFT = 4
@@ -340,6 +344,15 @@
             total = total + value.astype(jnp.float32)
         return total.astype(jnp.bfloat16)
 
+    def total_out_halving(own, pairs):
+        parts = [own] + [value.astype(jnp.float32) for value in pairs]
+        while len(parts) > 1:
+            half = len(parts) // 2
+            sent = jnp.stack([value.astype(jnp.bfloat16) for value in parts[half:]])
+            moved = far_move(sent, "tensor", tensor_count, far_t - half)
+            parts = [parts[k] + moved[k].astype(jnp.float32) for k in range(half)]
+        return parts[0].astype(jnp.bfloat16)
+
     def pair_hidden(keep, send):
         got = near_move(send, "seq", seq_count)
         pair = [keep[k].astype(jnp.float32) + got[k].astype(jnp.float32) for k in range(far_s)]
@@ -422,7 +435,7 @@
         )
     own_t, pairs_t = pair_out(keep_t, after(got_t, grad_out))
     grad_in = block_grads(tok, None, after(grad_hidden, pairs_t), seq_part, slots_in)
-    output = total_out(own_o, pairs_o)
+    output = total_out_halving(own_o, pairs_o)
     grad_tokens = total_out(own_t, pairs_t)
     return (
         output,

time: 118 us -> 117 us (level)
  starting transfers between devices: 37.2 us -> 25.7 us
  waiting for transfers between devices: 34.8 us -> 45.6 us
  local copies, waits for them, and re-layouts: 1.57 us -> 0.21 us
    ppermute x16 -> x15, starting transfers between devices: 24.5 us -> 11.5 us  [far_move(): return lax.ppermute(v, axis, pairs)]
    ppermute x16 -> x15, waiting for transfers between devices: 28.6 us -> 38.8 us  [far_move(): return lax.ppermute(v, axis, pairs)]
    ppermute x16, starting transfers between devices: 12.7 us -> 14.3 us  [near_move(): return lax.ppermute(v, axis, [(i, i ^ 1) for i in range(count)])]
    unnamed x12 -> x8, local copies, waits for them, and re-layouts: 1.38 us -> 0.02 us
  transfers between devices with their start and end apart: 32 -> 31, of which waited for: 12 -> 13; matrix products, arithmetic and copies ran while one was open for 1% -> 1% of each run, Pallas kernels for 27% -> 27%
where the time goes in v6:
time: 117 us; the launch traced here: 115 us
  waiting for transfers between devices  45.6 us (39%)
  Pallas kernels  39.8 us (34%)
  starting transfers between devices  25.7 us (22%)
  other arithmetic  2.35 us (2%)
    ppermute x15, waiting for transfers between devices, far_move(): return lax.ppermute(v, axis, pairs)  38.8 us
    pallas_call x3, Pallas kernels, block_grads(): pl.pallas_call(body, grid_spec=pltpu.PrefetchScalarGridSpec(num_scalar_pr...  19.8 us
    pallas_call x4, Pallas kernels, block_product(): pl.pallas_call(body, in_specs=[smem] * 3 + [vmem] * (n_in + 1) + [pl.Bloc...  16.3 us
    ppermute x16, starting transfers between devices, near_move(): return lax.ppermute(v, axis, [(i, i ^ 1) for i in range(count)])  14.3 us
    ppermute x15, starting transfers between devices, far_move(): return lax.ppermute(v, axis, pairs)  11.5 us
    ppermute x16, waiting for transfers between devices, near_move(): return lax.ppermute(v, axis, [(i, i ^ 1) for i in range(count)])  6.81 us
    pallas_call x1, Pallas kernels, pair_tables(): pl.pallas_call(body, in_specs=[pl.BlockSpec(memory_space=pltpu.HBM)] * (n...  3.79 us
  transfers between devices with their start and end apart: 31, of which 13 were waited for; matrix products, arithmetic and copies ran while one was open for 1% of the time, Pallas kernels for 27%

profile of v6, /device:TPU:1, one launch (start us, length us, event | category | flops | bytes accessed | tf_op | source)
XLA Modules:
  0.0 114.6 jit_solution(11669752637583067293)
XLA Ops:
  0.6 2.1 %collective-permute-start.3 = (bf16[16,3072]{1,0:T(8,128)(2,1)}, bf16[16,3072]{1,0:T(8,128)(2,1)S(1)}, u32[]{:S(2)}, u32[]{:S(2)}) collective-permute-start(bf16[16,3072]{1,0:T(8,128)(2,1)} %refs_0_.5), channel_id=1, source_target_pairs={{0,1},{1,0},{2,3},{3,2},{4,5},{5,4},{6,7},{7,6},{8,9},{9,8},{10,11... | collective-permute-start | bytes 294920 | tf_op jit(solution)/shard_map/ppermute | solution.py:314
  2.7 3.3 %collective-permute-start.2 = (bf16[16,3072]{1,0:T(8,128)(2,1)}, bf16[16,3072]{1,0:T(8,128)(2,1)S(1)}, u32[]{:S(2)}, u32[]{:S(2)}) collective-permute-start(bf16[16,3072]{1,0:T(8,128)(2,1)} %refs_0_.5), channel_id=1, source_target_pairs={{0,6},{1,7},{2,0},{3,1},{4,2},{5,3},{6,4},{7,5},{8,14},{9,15},{10,... | collective-permute-start | bytes 294920 | tf_op jit(solution)/shard_map/ppermute | solution.py:319
  6.1 0.5 collective-permute-start
  6.7 1.3 %collective-permute-done.2.refs_6_ = bf16[16,3072]{1,0:T(8,128)(2,1)S(1)} collective-permute-done((bf16[16,3072]{1,0:T(8,128)(2,1)}, bf16[16,3072]{1,0:T(8,128)(2,1)S(1)}, u32[]{:S(2)}, u32[]{:S(2)}) %collective-permute-start.2) | collective-permute-done | bytes 98336 | tf_op jit(solution)/shard_map/ppermute | solution.py:319
  8.0 0.3 collective-permute-start.6
  8.3 6.5 %collective-permute-done.1.refs_4_ = bf16[16,3072]{1,0:T(8,128)(2,1)S(1)} collective-permute-done((bf16[16,3072]{1,0:T(8,128)(2,1)}, bf16[16,3072]{1,0:T(8,128)(2,1)S(1)}, u32[]{:S(2)}, u32[]{:S(2)}) %collective-permute-start.1) | collective-permute-done | bytes 98336 | tf_op jit(solution)/shard_map/ppermute | solution.py:319
  14.8 0.3 collective-permute-start.5
  15.1 1.2 %collective-permute-start.4 = (bf16[16,3072]{1,0:T(8,128)(2,1)S(1)}, bf16[16,3072]{1,0:T(8,128)(2,1)S(1)}, u32[]{:S(2)}, u32[]{:S(2)}) collective-permute-start(bf16[16,3072]{1,0:T(8,128)(2,1)S(1)} %collective-permute-done.refs_2_), channel_id=1, source_target_pairs={{0,1},{1,0},{2,3},{3,2},{4,5},{5,4},{6,7},{7,6},{8,9},{9,8},{10,11... | collective-permute-start | bytes 294920 | tf_op jit(solution)/shard_map/ppermute | solution.py:314
  16.3 3.8 %pair_tables.1 = (s32[4,256]{1,0:T(4,128)S(1)}, s32[4,256]{1,0:T(4,128)S(1)}, s32[4,256]{1,0:T(4,128)S(1)}, s32[4,256]{1,0:T(4,128)S(1)}, bf16[288,128,128]{2,1,0:T(8,128)(2,1)S(1)}) custom-call(s32[1,1,288]{2,1,0:T(1,128)} %slot_s.5, s32[1,1,288]{2,1,0:T(1,128)} %slot_s.4, s32[1,1,288]{2,1,0:T(1,128)} %slot_s.4, s32[1,1,288]{2,1,0:T(1,128)} %slot_s.5, ...), custom_call_target="tpu_custom_call" | custom-call | tf_op jit(solution)/shard_map/pair_tables/pallas_call | solution.py:111
  20.2 4.3 %block_product.4 = (bf16[2,32,3072]{2,1,0:T(8,128)(2,1)S(1)}, bf16[2,32,3072]{2,1,0:T(8,128)(2,1)S(1)}, bf16[288,128,128]{2,1,0:T(8,128)(2,1)S(1)}) custom-call(s32[4,256]{1,0:T(4,128)S(1)} %get-tuple-element.57.table_s, s32[1]{0:T(128)} %constant.68.clone.1.in_s.out_s.right_s.left_s, s32[4]{0:T(128)S(1)} %pad_add_fusion.out_s, ...), custom_call_target="tpu_custom_call" | custom-call | flops 1207959552 | bytes 11010048 | tf_op jit(solution)/shard_map/block_product/pallas_call | solution.py:195
  24.5 2.0 %collective-permute-start.7 = (bf16[2,32,3072]{2,1,0:T(8,128)(2,1)S(1)}, bf16[2,32,3072]{2,1,0:T(8,128)(2,1)S(1)}, u32[]{:S(2)}, u32[]{:S(2)}) collective-permute-start(bf16[2,32,3072]{2,1,0:T(8,128)(2,1)S(1)} %get-tuple-element.60), channel_id=1, source_target_pairs={{0,8},{8,0},{16,24},{24,16},{1,9},{9,1},{17,25},{25,17},{2,10},{10... | collective-permute-start | bytes 1179656 | tf_op jit(solution)/shard_map/ppermute | solution.py:314
  26.5 2.7 %collective-permute-start.14 = (bf16[16,3072]{1,0:T(8,128)(2,1)S(1)}, bf16[16,3072]{1,0:T(8,128)(2,1)S(1)}, u32[]{:S(2)}, u32[]{:S(2)}) collective-permute-start(bf16[16,3072]{1,0:T(8,128)(2,1)S(1)} %copy-done), channel_id=1, source_target_pairs={{0,6},{1,7},{2,0},{3,1},{4,2},{5,3},{6,4},{7,5},{8,14},{9,15},{10,... | collective-permute-start | bytes 294920 | tf_op jit(solution)/shard_map/ppermute | solution.py:319
  29.2 0.3 collective-permute-start.10
  29.5 1.3 %collective-permute-start.9 = (bf16[16,3072]{1,0:T(8,128)(2,1)S(1)}, bf16[16,3072]{1,0:T(8,128)(2,1)S(1)}, u32[]{:S(2)}, u32[]{:S(2)}) collective-permute-start(bf16[16,3072]{1,0:T(8,128)(2,1)S(1)} %copy-done), channel_id=1, source_target_pairs={{0,1},{1,0},{2,3},{3,2},{4,5},{5,4},{6,7},{7,6},{8,9},{9,8},{10,11... | collective-permute-start | bytes 294920 | tf_op jit(solution)/shard_map/ppermute | solution.py:314
  30.7 0.6 collective-permute-done.14.refs_6_.refs_10_
  31.3 7.5 %collective-permute-done.12.refs_4_.refs_8_ = bf16[16,3072]{1,0:T(8,128)(2,1)S(1)} collective-permute-done((bf16[16,3072]{1,0:T(8,128)(2,1)S(1)}, bf16[16,3072]{1,0:T(8,128)(2,1)S(1)}, u32[]{:S(2)}, u32[]{:S(2)}) %collective-permute-start.12) | collective-permute-done | bytes 98336 | tf_op jit(solution)/shard_map/ppermute | solution.py:319
  38.8 1.5 %collective-permute-start.11 = (bf16[16,3072]{1,0:T(8,128)(2,1)S(1)}, bf16[16,3072]{1,0:T(8,128)(2,1)S(1)}, u32[]{:S(2)}, u32[]{:S(2)}) collective-permute-start(bf16[16,3072]{1,0:T(8,128)(2,1)S(1)} %collective-permute-done.10.refs_2_.refs_6_), channel_id=1, source_target_pairs={{0,1},{1,0},{2,3},{3,2},{4,5},{5,4},{6,7},{7,6},{8,9},{9,8},{10,11... | collective-permute-start | bytes 294920 | tf_op jit(solution)/shard_map/ppermute | solution.py:314
  40.3 2.3 %collective-permute-done.13.refs_5_.refs_9_ = bf16[16,3072]{1,0:T(8,128)(2,1)S(1)} collective-permute-done((bf16[16,3072]{1,0:T(8,128)(2,1)S(1)}, bf16[16,3072]{1,0:T(8,128)(2,1)S(1)}, u32[]{:S(2)}, u32[]{:S(2)}) %collective-permute-start.13) | collective-permute-done | bytes 98336 | tf_op jit(solution)/shard_map/ppermute | solution.py:314
  42.7 2.1 %collective-permute-done.11.refs_3_.refs_7_ = bf16[16,3072]{1,0:T(8,128)(2,1)S(1)} collective-permute-done((bf16[16,3072]{1,0:T(8,128)(2,1)S(1)}, bf16[16,3072]{1,0:T(8,128)(2,1)S(1)}, u32[]{:S(2)}, u32[]{:S(2)}) %collective-permute-start.11) | collective-permute-done | bytes 98336 | tf_op jit(solution)/shard_map/ppermute | solution.py:314
  44.8 4.2 %block_product.5 = (bf16[2,32,3072]{2,1,0:T(8,128)(2,1)S(1)}, bf16[2,32,3072]{2,1,0:T(8,128)(2,1)S(1)}) custom-call(s32[4,256]{1,0:T(4,128)S(1)} %get-tuple-element.61.table_s, s32[1]{0:T(128)} %constant.68.clone.1.in_s.out_s.right_s.left_s, s32[4]{0:T(128)S(1)} %pad_add_fusion.out_s, bf16[16,3072]{1,0:T(8,128)(2,1)S(1)} %copy-done, ...), custom_call_target="tpu_custom_call" | custom-call | flops 1207959552 | bytes 11010048 | tf_op jit(solution)/shard_map/block_product/pallas_call | solution.py:195
  49.0 0.5 collective-permute-start.16
  49.4 6.3 %collective-permute-done.8 = bf16[32,3072]{1,0:T(8,128)(2,1)S(1)} collective-permute-done((bf16[32,3072]{1,0:T(8,128)(2,1)S(1)}, bf16[32,3072]{1,0:T(8,128)(2,1)S(1)}, u32[]{:S(2)}, u32[]{:S(2)}) %collective-permute-start.8) | collective-permute-done | bytes 196640 | tf_op jit(solution)/shard_map/ppermute | solution.py:319
  55.8 0.3 collective-permute-start.19
  56.4 1.2 %collective-permute-start.18 = (bf16[32,3072]{1,0:T(8,128)(2,1)S(1)}, bf16[32,3072]{1,0:T(8,128)(2,1)S(1)}, u32[]{:S(2)}, u32[]{:S(2)}) collective-permute-start(bf16[32,3072]{1,0:T(8,128)(2,1)S(1)} %multiply_convert_fusion.refs_0_), channel_id=1, source_target_pairs={{0,16},{8,24},{16,0},{24,8},{1,17},{9,25},{17,1},{25,9},{2,18},{10... | collective-permute-start | bytes 589832 | tf_op jit(solution)/shard_map/ppermute | solution.py:319
  57.6 1.5 %collective-permute-start.17 = (bf16[32,3072]{1,0:T(8,128)(2,1)S(1)}, bf16[32,3072]{1,0:T(8,128)(2,1)S(1)}, u32[]{:S(2)}, u32[]{:S(2)}) collective-permute-start(bf16[32,3072]{1,0:T(8,128)(2,1)S(1)} %multiply_convert_fusion.refs_0_), channel_id=1, source_target_pairs={{0,8},{8,0},{16,24},{24,16},{1,9},{9,1},{17,25},{25,17},{2,10},{10... | collective-permute-start | bytes 589832 | tf_op jit(solution)/shard_map/ppermute | solution.py:314
  59.2 2.2 %collective-permute-done.19 = bf16[32,3072]{1,0:T(8,128)(2,1)S(1)} collective-permute-done((bf16[32,3072]{1,0:T(8,128)(2,1)S(1)}, bf16[32,3072]{1,0:T(8,128)(2,1)S(1)}, u32[]{:S(2)}, u32[]{:S(2)}) %collective-permute-start.19) | collective-permute-done | bytes 196640 | tf_op jit(solution)/shard_map/ppermute | solution.py:319
  61.4 0.4 fusion.6.refs_0_.refs_8_
  61.8 3.8 %collective-permute-done.18.refs_2_ = bf16[32,3072]{1,0:T(8,128)(2,1)S(1)} collective-permute-done((bf16[32,3072]{1,0:T(8,128)(2,1)S(1)}, bf16[32,3072]{1,0:T(8,128)(2,1)S(1)}, u32[]{:S(2)}, u32[]{:S(2)}) %collective-permute-start.18) | collective-permute-done | bytes 196640 | tf_op jit(solution)/shard_map/ppermute | solution.py:319
  65.6 1.8 %collective-permute-start.20 = (bf16[32,3072]{1,0:T(8,128)(2,1)S(1)}, bf16[32,3072]{1,0:T(8,128)(2,1)S(1)}, u32[]{:S(2)}, u32[]{:S(2)}) collective-permute-start(bf16[32,3072]{1,0:T(8,128)(2,1)S(1)} %collective-permute-done.18.refs_2_), channel_id=1, source_target_pairs={{0,8},{8,0},{16,24},{24,16},{1,9},{9,1},{17,25},{25,17},{2,10},{10... | collective-permute-start | bytes 589832 | tf_op jit(solution)/shard_map/ppermute | solution.py:314
  67.4 0.3 collective-permute-start.23
  67.7 0.3 collective-permute-start.22
  68.0 0.5 collective-permute-done.20.refs_3_
  68.5 5.4 %collective-permute-done.23.refs_2_.refs_10_ = bf16[32,3072]{1,0:T(8,128)(2,1)S(1)} collective-permute-done((bf16[32,3072]{1,0:T(8,128)(2,1)S(1)}, bf16[32,3072]{1,0:T(8,128)(2,1)S(1)}, u32[]{:S(2)}, u32[]{:S(2)}) %collective-permute-start.23) | collective-permute-done | bytes 196640 | tf_op jit(solution)/shard_map/ppermute | solution.py:319
  73.9 0.9 collective-permute-start.24
  74.7 4.5 %block_product.6 = (bf16[4,16,3072]{2,1,0:T(8,128)(2,1)S(1)}, bf16[4,16,3072]{2,1,0:T(8,128)(2,1)S(1)}, bf16[288,128,128]{2,1,0:T(8,128)(2,1)S(1)}) custom-call(s32[4,256]{1,0:T(4,128)S(1)} %get-tuple-element.56.table_s, s32[4]{0:T(128)S(1)} %fusion.21.in_s.left_s.right_s, s32[1]{0:T(128)} %constant.68.clone.1.in_s.out_s.right_s.left_s, ...), custom_call_target="tpu_custom_call" | custom-call | flops 1207959552 | bytes 11010048 | tf_op jit(solution)/shard_map/block_product/pallas_call | solution.py:195
  79.4 3.3 %block_product.7 = (bf16[4,16,3072]{2,1,0:T(8,128)(2,1)S(1)}, bf16[4,16,3072]{2,1,0:T(8,128)(2,1)S(1)}) custom-call(s32[4,256]{1,0:T(4,128)S(1)} %get-tuple-element.82.table_s, s32[4]{0:T(128)S(1)} %fusion.21.in_s.left_s.right_s, s32[1]{0:T(128)} %constant.68.clone.1.in_s.out_s.right_s.left_s, bf16[32,3072]{1,0:T(8,128)(2,1)S(1)} %fusion.6.refs_0_.refs_8_, ...), custom_call_target="tpu_custom_call" | custom-call | flops 1207959552 | bytes 11010048 | tf_op jit(solution)/shard_map/block_product/pallas_call | solution.py:195
  82.7 5.5 %block_grads.3.refs_12_ = f32[288,128,128]{2,1,0:T(8,128)} custom-call(s32[1,1,288]{2,1,0:T(1,128)S(1)} %copy-done.2, s32[4]{0:T(128)S(1)} %fusion.21.in_s.left_s.right_s, s32[1]{0:T(128)} %constant.68.clone.1.in_s.out_s.right_s.left_s, bf16[32,3072]{1,0:T(8,128)(2,1)S(1)} %multiply_convert_fusion.refs_0_, ...), custom_call_target="tpu_custom_call" | custom-call | flops 1207959552 | bytes 20447232 | tf_op jit(solution)/shard_map/block_grads/pallas_call | solution.py:266
  88.2 1.8 %collective-permute-done.21 = bf16[4,16,3072]{2,1,0:T(8,128)(2,1)S(1)} collective-permute-done((bf16[4,16,3072]{2,1,0:T(8,128)(2,1)S(1)}, bf16[4,16,3072]{2,1,0:T(8,128)(2,1)S(1)}, u32[]{:S(2)}, u32[]{:S(2)}) %collective-permute-start.21) | collective-permute-done | bytes 393248 | tf_op jit(solution)/shard_map/ppermute | solution.py:314
  90.2 0.7 collective-permute-start.27
  90.9 5.5 %block_grads.4 = f32[288,128,128]{2,1,0:T(8,128)} custom-call(s32[1,1,288]{2,1,0:T(1,128)S(1)} %copy-done.2, s32[4]{0:T(128)S(1)} %fusion.21.in_s.left_s.right_s, s32[1]{0:T(128)} %constant.68.clone.1.in_s.out_s.right_s.left_s, bf16[32,3072]{1,0:T(8,128)(2,1)S(1)} %multiply_convert_fusion.refs_0_, ...), custom_call_target="tpu_custom_call", output_to_operand_aliasing={{}: (15, {})} | custom-call | flops 1207959552 | bytes 20447232 | tf_op jit(solution)/shard_map/block_grads/pallas_call | solution.py:266
  96.4 5.2 %collective-permute-done.25 = bf16[2,16,3072]{2,1,0:T(8,128)(2,1)S(1)} collective-permute-done((bf16[2,16,3072]{2,1,0:T(8,128)(2,1)S(1)}, bf16[2,16,3072]{2,1,0:T(8,128)(2,1)S(1)}, u32[]{:S(2)}, u32[]{:S(2)}) %collective-permute-start.25) | collective-permute-done | bytes 196640 | tf_op jit(solution)/shard_map/ppermute | solution.py:319
  101.6 0.7 collective-permute-start.26
  102.4 0.6 collective-permute-start.28
  103.0 0.9 collective-permute-start.30
  103.9 0.5 collective-permute-start.29
  104.5 8.7 %block_grads.5 = f32[288,128,128]{2,1,0:T(8,128)} custom-call(s32[1,1,288]{2,1,0:T(1,128)S(1)} %copy-done.3, s32[1]{0:T(128)} %constant.68.clone.1.in_s.out_s.right_s.left_s, s32[4]{0:T(128)S(1)} %fusion.21.in_s.left_s.right_s, bf16[16,3072]{1,0:T(8,128)(2,1)S(1)} %copy-done.1, bf16[16,3072]{1,0:T(8,128)(2,1)S(1)} %collective-permute-done.3.refs_1_, ...), custom_call_target="tpu_custom_call" | custom-call | flops 1207959552 | bytes 20447232 | tf_op jit(solution)/shard_map/block_grads/pallas_call | solution.py:266
  113.2 0.7 fusion.12
  113.9 0.7 fusion.11
  (44 shorter events, 1.0 us)
Async XLA Ops:
  0.6 19.6 %copy-start.1 = (bf16[16,3072]{1,0:T(8,128)(2,1)S(1)}, bf16[16,3072]{1,0:T(8,128)(2,1)}, u32[]{:S(2)}) copy-start(bf16[16,3072]{1,0:T(8,128)(2,1)} %refs_0_.5) | copy-start | bytes 294916
  0.6 19.5 %collective-permute-start.3 = (bf16[16,3072]{1,0:T(8,128)(2,1)}, bf16[16,3072]{1,0:T(8,128)(2,1)S(1)}, u32[]{:S(2)}, u32[]{:S(2)}) collective-permute-start(bf16[16,3072]{1,0:T(8,128)(2,1)} %refs_0_.5), channel_id=1, source_target_pairs={{0,1},{1,0},{2,3},{3,2},{4,5},{5,4},{6,7},{7,6},{8,9},{9,8},{10,11... | collective-permute-start | bytes 294920 | tf_op jit(solution)/shard_map/ppermute | solution.py:314
  2.7 5.3 %collective-permute-start.2 = (bf16[16,3072]{1,0:T(8,128)(2,1)}, bf16[16,3072]{1,0:T(8,128)(2,1)S(1)}, u32[]{:S(2)}, u32[]{:S(2)}) collective-permute-start(bf16[16,3072]{1,0:T(8,128)(2,1)} %refs_0_.5), channel_id=1, source_target_pairs={{0,6},{1,7},{2,0},{3,1},{4,2},{5,3},{6,4},{7,5},{8,14},{9,15},{10,... | collective-permute-start | bytes 294920 | tf_op jit(solution)/shard_map/ppermute | solution.py:319
  6.1 8.7 %collective-permute-start.1 = (bf16[16,3072]{1,0:T(8,128)(2,1)}, bf16[16,3072]{1,0:T(8,128)(2,1)S(1)}, u32[]{:S(2)}, u32[]{:S(2)}) collective-permute-start(bf16[16,3072]{1,0:T(8,128)(2,1)} %refs_0_.5), channel_id=1, source_target_pairs={{0,4},{1,5},{2,6},{3,7},{4,0},{5,1},{6,2},{7,3},{8,12},{9,13},{10,... | collective-permute-start | bytes 294920 | tf_op jit(solution)/shard_map/ppermute | solution.py:319
  6.1 9.0 %collective-permute-start = (bf16[16,3072]{1,0:T(8,128)(2,1)}, bf16[16,3072]{1,0:T(8,128)(2,1)S(1)}, u32[]{:S(2)}, u32[]{:S(2)}) collective-permute-start(bf16[16,3072]{1,0:T(8,128)(2,1)} %refs_0_.5), channel_id=1, source_target_pairs={{0,2},{1,3},{2,4},{3,5},{4,6},{5,7},{6,0},{7,1},{8,10},{9,11},{10,... | collective-permute-start | bytes 294920 | tf_op jit(solution)/shard_map/ppermute | solution.py:319
  8.0 12.1 %collective-permute-start.6 = (bf16[16,3072]{1,0:T(8,128)(2,1)S(1)}, bf16[16,3072]{1,0:T(8,128)(2,1)S(1)}, u32[]{:S(2)}, u32[]{:S(2)}) collective-permute-start(bf16[16,3072]{1,0:T(8,128)(2,1)S(1)} %collective-permute-done.2.refs_6_), channel_id=1, source_target_pairs={{0,1},{1,0},{2,3},{3,2},{4,5},{5,4},{6,7},{7,6},{8,9},{9,8},{10,11... | collective-permute-start | bytes 294920 | tf_op jit(solution)/shard_map/ppermute | solution.py:314
  14.8 5.4 %collective-permute-start.5 = (bf16[16,3072]{1,0:T(8,128)(2,1)S(1)}, bf16[16,3072]{1,0:T(8,128)(2,1)S(1)}, u32[]{:S(2)}, u32[]{:S(2)}) collective-permute-start(bf16[16,3072]{1,0:T(8,128)(2,1)S(1)} %collective-permute-done.1.refs_4_), channel_id=1, source_target_pairs={{0,1},{1,0},{2,3},{3,2},{4,5},{5,4},{6,7},{7,6},{8,9},{9,8},{10,11... | collective-permute-start | bytes 294920 | tf_op jit(solution)/shard_map/ppermute | solution.py:314
  15.1 5.2 %collective-permute-start.4 = (bf16[16,3072]{1,0:T(8,128)(2,1)S(1)}, bf16[16,3072]{1,0:T(8,128)(2,1)S(1)}, u32[]{:S(2)}, u32[]{:S(2)}) collective-permute-start(bf16[16,3072]{1,0:T(8,128)(2,1)S(1)} %collective-permute-done.refs_2_), channel_id=1, source_target_pairs={{0,1},{1,0},{2,3},{3,2},{4,5},{5,4},{6,7},{7,6},{8,9},{9,8},{10,11... | collective-permute-start | bytes 294920 | tf_op jit(solution)/shard_map/ppermute | solution.py:314
  20.2 6.3 %copy-start = (bf16[16,3072]{1,0:T(8,128)(2,1)S(1)}, bf16[16,3072]{1,0:T(8,128)(2,1)}, u32[]{:S(2)}) copy-start(bf16[16,3072]{1,0:T(8,128)(2,1)} %refs_4_.3) | copy-start | bytes 294916
  24.5 15.7 %collective-permute-start.7 = (bf16[2,32,3072]{2,1,0:T(8,128)(2,1)S(1)}, bf16[2,32,3072]{2,1,0:T(8,128)(2,1)S(1)}, u32[]{:S(2)}, u32[]{:S(2)}) collective-permute-start(bf16[2,32,3072]{2,1,0:T(8,128)(2,1)S(1)} %get-tuple-element.60), channel_id=1, source_target_pairs={{0,8},{8,0},{16,24},{24,16},{1,9},{9,1},{17,25},{25,17},{2,10},{10... | collective-permute-start | bytes 1179656 | tf_op jit(solution)/shard_map/ppermute | solution.py:314
  26.5 4.8 %collective-permute-start.14 = (bf16[16,3072]{1,0:T(8,128)(2,1)S(1)}, bf16[16,3072]{1,0:T(8,128)(2,1)S(1)}, u32[]{:S(2)}, u32[]{:S(2)}) collective-permute-start(bf16[16,3072]{1,0:T(8,128)(2,1)S(1)} %copy-done), channel_id=1, source_target_pairs={{0,6},{1,7},{2,0},{3,1},{4,2},{5,3},{6,4},{7,5},{8,14},{9,15},{10,... | collective-permute-start | bytes 294920 | tf_op jit(solution)/shard_map/ppermute | solution.py:319
  29.2 9.6 %collective-permute-start.12 = (bf16[16,3072]{1,0:T(8,128)(2,1)S(1)}, bf16[16,3072]{1,0:T(8,128)(2,1)S(1)}, u32[]{:S(2)}, u32[]{:S(2)}) collective-permute-start(bf16[16,3072]{1,0:T(8,128)(2,1)S(1)} %copy-done), channel_id=1, source_target_pairs={{0,4},{1,5},{2,6},{3,7},{4,0},{5,1},{6,2},{7,3},{8,12},{9,13},{10,... | collective-permute-start | bytes 294920 | tf_op jit(solution)/shard_map/ppermute | solution.py:319
  29.2 9.6 %collective-permute-start.10 = (bf16[16,3072]{1,0:T(8,128)(2,1)S(1)}, bf16[16,3072]{1,0:T(8,128)(2,1)S(1)}, u32[]{:S(2)}, u32[]{:S(2)}) collective-permute-start(bf16[16,3072]{1,0:T(8,128)(2,1)S(1)} %copy-done), channel_id=1, source_target_pairs={{0,2},{1,3},{2,4},{3,5},{4,6},{5,7},{6,0},{7,1},{8,10},{9,11},{10,... | collective-permute-start | bytes 294920 | tf_op jit(solution)/shard_map/ppermute | solution.py:319
  29.5 10.8 %collective-permute-start.9 = (bf16[16,3072]{1,0:T(8,128)(2,1)S(1)}, bf16[16,3072]{1,0:T(8,128)(2,1)S(1)}, u32[]{:S(2)}, u32[]{:S(2)}) collective-permute-start(bf16[16,3072]{1,0:T(8,128)(2,1)S(1)} %copy-done), channel_id=1, source_target_pairs={{0,1},{1,0},{2,3},{3,2},{4,5},{5,4},{6,7},{7,6},{8,9},{9,8},{10,11... | collective-permute-start | bytes 294920 | tf_op jit(solution)/shard_map/ppermute | solution.py:314
  31.3 9.0 %collective-permute-start.15 = (bf16[16,3072]{1,0:T(8,128)(2,1)S(1)}, bf16[16,3072]{1,0:T(8,128)(2,1)S(1)}, u32[]{:S(2)}, u32[]{:S(2)}) collective-permute-start(bf16[16,3072]{1,0:T(8,128)(2,1)S(1)} %collective-permute-done.14.refs_6_.refs_10_), channel_id=1, source_target_pairs={{0,1},{1,0},{2,3},{3,2},{4,5},{5,4},{6,7},{7,6},{8,9},{9,8},{10,11... | collective-permute-start | bytes 294920 | tf_op jit(solution)/shard_map/ppermute | solution.py:314
  38.8 3.9 %collective-permute-start.13 = (bf16[16,3072]{1,0:T(8,128)(2,1)S(1)}, bf16[16,3072]{1,0:T(8,128)(2,1)S(1)}, u32[]{:S(2)}, u32[]{:S(2)}) collective-permute-start(bf16[16,3072]{1,0:T(8,128)(2,1)S(1)} %collective-permute-done.12.refs_4_.refs_8_), channel_id=1, source_target_pairs={{0,1},{1,0},{2,3},{3,2},{4,5},{5,4},{6,7},{7,6},{8,9},{9,8},{10,11... | collective-permute-start | bytes 294920 | tf_op jit(solution)/shard_map/ppermute | solution.py:314
  38.8 6.0 %collective-permute-start.11 = (bf16[16,3072]{1,0:T(8,128)(2,1)S(1)}, bf16[16,3072]{1,0:T(8,128)(2,1)S(1)}, u32[]{:S(2)}, u32[]{:S(2)}) collective-permute-start(bf16[16,3072]{1,0:T(8,128)(2,1)S(1)} %collective-permute-done.10.refs_2_.refs_6_), channel_id=1, source_target_pairs={{0,1},{1,0},{2,3},{3,2},{4,5},{5,4},{6,7},{7,6},{8,9},{9,8},{10,11... | collective-permute-start | bytes 294920 | tf_op jit(solution)/shard_map/ppermute | solution.py:314
  49.0 6.8 %collective-permute-start.16 = (bf16[2,32,3072]{2,1,0:T(8,128)(2,1)S(1)}, bf16[2,32,3072]{2,1,0:T(8,128)(2,1)S(1)}, u32[]{:S(2)}, u32[]{:S(2)}) collective-permute-start(bf16[2,32,3072]{2,1,0:T(8,128)(2,1)S(1)} %get-tuple-element.72), channel_id=1, source_target_pairs={{0,8},{8,0},{16,24},{24,16},{1,9},{9,1},{17,25},{25,17},{2,10},{10... | collective-permute-start | bytes 1179656 | tf_op jit(solution)/shard_map/ppermute | solution.py:314
  49.4 6.3 %collective-permute-start.8 = (bf16[32,3072]{1,0:T(8,128)(2,1)S(1)}, bf16[32,3072]{1,0:T(8,128)(2,1)S(1)}, u32[]{:S(2)}, u32[]{:S(2)}) collective-permute-start(bf16[32,3072]{1,0:T(8,128)(2,1)S(1)} %fusion.7), channel_id=1, source_target_pairs={{0,16},{8,24},{16,0},{24,8},{1,17},{9,25},{17,1},{25,9},{2,18},{10... | collective-permute-start | bytes 589832 | tf_op jit(solution)/shard_map/ppermute | solution.py:319
  55.8 5.6 %collective-permute-start.19 = (bf16[32,3072]{1,0:T(8,128)(2,1)S(1)}, bf16[32,3072]{1,0:T(8,128)(2,1)S(1)}, u32[]{:S(2)}, u32[]{:S(2)}) collective-permute-start(bf16[32,3072]{1,0:T(8,128)(2,1)S(1)} %fusion.8), channel_id=1, source_target_pairs={{0,16},{8,24},{16,0},{24,8},{1,17},{9,25},{17,1},{25,9},{2,18},{10... | collective-permute-start | bytes 589832 | tf_op jit(solution)/shard_map/ppermute | solution.py:319
  56.4 9.2 %collective-permute-start.18 = (bf16[32,3072]{1,0:T(8,128)(2,1)S(1)}, bf16[32,3072]{1,0:T(8,128)(2,1)S(1)}, u32[]{:S(2)}, u32[]{:S(2)}) collective-permute-start(bf16[32,3072]{1,0:T(8,128)(2,1)S(1)} %multiply_convert_fusion.refs_0_), channel_id=1, source_target_pairs={{0,16},{8,24},{16,0},{24,8},{1,17},{9,25},{17,1},{25,9},{2,18},{10... | collective-permute-start | bytes 589832 | tf_op jit(solution)/shard_map/ppermute | solution.py:319
  57.6 10.4 %collective-permute-start.17 = (bf16[32,3072]{1,0:T(8,128)(2,1)S(1)}, bf16[32,3072]{1,0:T(8,128)(2,1)S(1)}, u32[]{:S(2)}, u32[]{:S(2)}) collective-permute-start(bf16[32,3072]{1,0:T(8,128)(2,1)S(1)} %multiply_convert_fusion.refs_0_), channel_id=1, source_target_pairs={{0,8},{8,0},{16,24},{24,16},{1,9},{9,1},{17,25},{25,17},{2,10},{10... | collective-permute-start | bytes 589832 | tf_op jit(solution)/shard_map/ppermute | solution.py:314
  65.6 2.9 %collective-permute-start.20 = (bf16[32,3072]{1,0:T(8,128)(2,1)S(1)}, bf16[32,3072]{1,0:T(8,128)(2,1)S(1)}, u32[]{:S(2)}, u32[]{:S(2)}) collective-permute-start(bf16[32,3072]{1,0:T(8,128)(2,1)S(1)} %collective-permute-done.18.refs_2_), channel_id=1, source_target_pairs={{0,8},{8,0},{16,24},{24,16},{1,9},{9,1},{17,25},{25,17},{2,10},{10... | collective-permute-start | bytes 589832 | tf_op jit(solution)/shard_map/ppermute | solution.py:314
  67.4 6.5 %collective-permute-start.23 = (bf16[32,3072]{1,0:T(8,128)(2,1)S(1)}, bf16[32,3072]{1,0:T(8,128)(2,1)S(1)}, u32[]{:S(2)}, u32[]{:S(2)}) collective-permute-start(bf16[32,3072]{1,0:T(8,128)(2,1)S(1)} %fusion.6.refs_0_.refs_8_), channel_id=1, source_target_pairs={{0,16},{8,24},{16,0},{24,8},{1,17},{9,25},{17,1},{25,9},{2,18},{10... | collective-permute-start | bytes 589832 | tf_op jit(solution)/shard_map/ppermute | solution.py:319
  67.7 11.7 %collective-permute-start.22 = (bf16[32,3072]{1,0:T(8,128)(2,1)S(1)}, bf16[32,3072]{1,0:T(8,128)(2,1)S(1)}, u32[]{:S(2)}, u32[]{:S(2)}) collective-permute-start(bf16[32,3072]{1,0:T(8,128)(2,1)S(1)} %fusion.6.refs_0_.refs_8_), channel_id=1, source_target_pairs={{0,8},{8,0},{16,24},{24,16},{1,9},{9,1},{17,25},{25,17},{2,10},{10... | collective-permute-start | bytes 589832 | tf_op jit(solution)/shard_map/ppermute | solution.py:314
  73.9 5.5 %collective-permute-start.24 = (bf16[32,3072]{1,0:T(8,128)(2,1)S(1)}, bf16[32,3072]{1,0:T(8,128)(2,1)S(1)}, u32[]{:S(2)}, u32[]{:S(2)}) collective-permute-start(bf16[32,3072]{1,0:T(8,128)(2,1)S(1)} %collective-permute-done.23.refs_2_.refs_10_), channel_id=1, source_target_pairs={{0,8},{8,0},{16,24},{24,16},{1,9},{9,1},{17,25},{25,17},{2,10},{10... | collective-permute-start | bytes 589832 | tf_op jit(solution)/shard_map/ppermute | solution.py:314
  79.3 3.4 %copy-start.2 = (s32[1,1,288]{2,1,0:T(1,128)S(1)}, s32[1,1,288]{2,1,0:T(1,128)}, u32[]{:S(2)}) copy-start(s32[1,1,288]{2,1,0:T(1,128)} %slot_s.4) | copy-start | bytes 3460
  79.3 10.7 %collective-permute-start.21 = (bf16[4,16,3072]{2,1,0:T(8,128)(2,1)S(1)}, bf16[4,16,3072]{2,1,0:T(8,128)(2,1)S(1)}, u32[]{:S(2)}, u32[]{:S(2)}) collective-permute-start(bf16[4,16,3072]{2,1,0:T(8,128)(2,1)S(1)} %get-tuple-element.81), channel_id=1, source_target_pairs={{0,1},{1,0},{2,3},{3,2},{4,5},{5,4},{6,7},{7,6},{8,9},{9,8},{10,11... | collective-permute-start | bytes 1179656 | tf_op jit(solution)/shard_map/ppermute | solution.py:314
  90.1 11.5 %collective-permute-start.25 = (bf16[2,16,3072]{2,1,0:T(8,128)(2,1)S(1)}, bf16[2,16,3072]{2,1,0:T(8,128)(2,1)S(1)}, u32[]{:S(2)}, u32[]{:S(2)}) collective-permute-start(bf16[2,16,3072]{2,1,0:T(8,128)(2,1)S(1)} %pad_maximum_fusion), channel_id=1, source_target_pairs={{0,4},{1,5},{2,6},{3,7},{4,0},{5,1},{6,2},{7,3},{8,12},{9,13},{10,... | collective-permute-start | bytes 589832 | tf_op jit(solution)/shard_map/ppermute | solution.py:319
  90.2 14.3 %copy-start.3 = (s32[1,1,288]{2,1,0:T(1,128)S(1)}, s32[1,1,288]{2,1,0:T(1,128)}, u32[]{:S(2)}) copy-start(s32[1,1,288]{2,1,0:T(1,128)} %slot_s.5) | copy-start | bytes 3460
  90.2 12.1 %collective-permute-start.27 = (bf16[4,16,3072]{2,1,0:T(8,128)(2,1)S(1)}, bf16[4,16,3072]{2,1,0:T(8,128)(2,1)S(1)}, u32[]{:S(2)}, u32[]{:S(2)}) collective-permute-start(bf16[4,16,3072]{2,1,0:T(8,128)(2,1)S(1)} %get-tuple-element.94), channel_id=1, source_target_pairs={{0,1},{1,0},{2,3},{3,2},{4,5},{5,4},{6,7},{7,6},{8,9},{9,8},{10,11... | collective-permute-start | bytes 1179656 | tf_op jit(solution)/shard_map/ppermute | solution.py:314
  101.6 11.5 %collective-permute-start.26 = (bf16[1,16,3072]{2,1,0:T(8,128)(2,1)S(1)}, bf16[1,16,3072]{2,1,0:T(8,128)(2,1)S(1)}, u32[]{:S(2)}, u32[]{:S(2)}) collective-permute-start(bf16[1,16,3072]{2,1,0:T(8,128)(2,1)S(1)} %add_convert_fusion.6), channel_id=1, source_target_pairs={{0,6},{1,7},{2,0},{3,1},{4,2},{5,3},{6,4},{7,5},{8,14},{9,15},{10,... | collective-permute-start | bytes 294920 | tf_op jit(solution)/shard_map/ppermute | solution.py:319
  102.4 11.4 %collective-permute-start.28 = (bf16[16,3072]{1,0:T(8,128)(2,1)S(1)}, bf16[16,3072]{1,0:T(8,128)(2,1)S(1)}, u32[]{:S(2)}, u32[]{:S(2)}) collective-permute-start(bf16[16,3072]{1,0:T(8,128)(2,1)S(1)} %get-tuple-element.104), channel_id=1, source_target_pairs={{0,6},{1,7},{2,0},{3,1},{4,2},{5,3},{6,4},{7,5},{8,14},{9,15},{10,... | collective-permute-start | bytes 294920 | tf_op jit(solution)/shard_map/ppermute | solution.py:319
  103.0 10.8 %collective-permute-start.30 = (bf16[16,3072]{1,0:T(8,128)(2,1)S(1)}, bf16[16,3072]{1,0:T(8,128)(2,1)S(1)}, u32[]{:S(2)}, u32[]{:S(2)}) collective-permute-start(bf16[16,3072]{1,0:T(8,128)(2,1)S(1)} %get-tuple-element.105), channel_id=1, source_target_pairs={{0,2},{1,3},{2,4},{3,5},{4,6},{5,7},{6,0},{7,1},{8,10},{9,11},{10,... | collective-permute-start | bytes 294920 | tf_op jit(solution)/shard_map/ppermute | solution.py:319
  103.9 9.9 %collective-permute-start.29 = (bf16[16,3072]{1,0:T(8,128)(2,1)S(1)}, bf16[16,3072]{1,0:T(8,128)(2,1)S(1)}, u32[]{:S(2)}, u32[]{:S(2)}) collective-permute-start(bf16[16,3072]{1,0:T(8,128)(2,1)S(1)} %get-tuple-element.106), channel_id=1, source_target_pairs={{0,4},{1,5},{2,6},{3,7},{4,0},{5,1},{6,2},{7,3},{8,12},{9,13},{10,... | collective-permute-start | bytes 294920 | tf_op jit(solution)/shard_map/ppermute | solution.py:319

commit v7 on v6

--- a/solution.py
+++ b/solution.py
@@ -345,6 +345,15 @@
         return total.astype(jnp.bfloat16)
 
     def total_out_halving(own, pairs):
+        if far_t == 4:
+            sent = jnp.stack([pairs[0], pairs[2]])
+            pairing = [(o * 2 + c, (o ^ 1) * 2 + c) for o in range(far_t) for c in range(2)]
+            moved = lax.ppermute(sent, "tensor", pairing).astype(jnp.float32)
+            odd = (lax.axis_index("tensor") // 2) % 2 == 1
+            own = own + jnp.where(odd, moved[1], moved[0])
+            rest = pairs[1].astype(jnp.float32) + jnp.where(odd, moved[0], moved[1])
+            moved = far_move(rest.astype(jnp.bfloat16), "tensor", tensor_count, 2)
+            return (own + moved.astype(jnp.float32)).astype(jnp.bfloat16)
         parts = [own] + [value.astype(jnp.float32) for value in pairs]
         while len(parts) > 1:
             half = len(parts) // 2

time: 117 us -> 124 us (1.060)
  starting transfers between devices: 25.7 us -> 35.5 us
  waiting for transfers between devices: 45.6 us -> 39.2 us
  other arithmetic: 2.35 us -> 5.94 us
    ppermute x15 -> x14, waiting for transfers between devices: 38.8 us -> 27.3 us  [far_move(): return lax.ppermute(v, axis, pairs)]
    ppermute x0 -> x1, starting transfers between devices: none -> 5.64 us  [total_out_halving(): moved = lax.ppermute(sent, 'tensor', pairing).astype(jnp.float32)]
    ppermute x15 -> x14, starting transfers between devices: 11.5 us -> 17 us  [far_move(): return lax.ppermute(v, axis, pairs)]
    ppermute x0 -> x1, waiting for transfers between devices: none -> 5.17 us  [total_out_halving(): moved = lax.ppermute(sent, 'tensor', pairing).astype(jnp.float32)]
    convert_element_type x1 -> x3, other arithmetic: 0.04 us -> 3.58 us  [the longest x1 1.64 us: total_out_halving(): return (own + moved.astype(jnp.float32)).astype(jnp.bfloat16)]
    ppermute x16, starting transfers between devices: 14.3 us -> 12.9 us  [near_move(): return lax.ppermute(v, axis, [(i, i ^ 1) for i in range(count)])]
  transfers between devices with their start and end apart: 31 -> 31, of which waited for: 13 -> 13; matrix products, arithmetic and copies ran while one was open for 1% -> 4% of each run, Pallas kernels for 27% -> 26%
where the time goes in v7:
time: 124 us; the launch traced here: 122 us
  Pallas kernels  39.8 us (32%)
  waiting for transfers between devices  39.2 us (32%)
  starting transfers between devices  35.5 us (29%)
  other arithmetic  5.94 us (5%)
    ppermute x14, waiting for transfers between devices, far_move(): return lax.ppermute(v, axis, pairs)  27.3 us
    pallas_call x3, Pallas kernels, block_grads(): pl.pallas_call(body, grid_spec=pltpu.PrefetchScalarGridSpec(num_scalar_pr...  19.8 us
    ppermute x14, starting transfers between devices, far_move(): return lax.ppermute(v, axis, pairs)  17 us
    pallas_call x4, Pallas kernels, block_product(): pl.pallas_call(body, in_specs=[smem] * 3 + [vmem] * (n_in + 1) + [pl.Bloc...  16.3 us
    ppermute x16, starting transfers between devices, near_move(): return lax.ppermute(v, axis, [(i, i ^ 1) for i in range(count)])  12.9 us
    ppermute x16, waiting for transfers between devices, near_move(): return lax.ppermute(v, axis, [(i, i ^ 1) for i in range(count)])  6.68 us
    ppermute x1, starting transfers between devices, total_out_halving(): moved = lax.ppermute(sent, 'tensor', pairing).astype(jnp.float32)  5.64 us
    ppermute x1, waiting for transfers between devices, total_out_halving(): moved = lax.ppermute(sent, 'tensor', pairing).astype(jnp.float32)  5.17 us
  transfers between devices with their start and end apart: 31, of which 13 were waited for; matrix products, arithmetic and copies ran while one was open for 4% of the time, Pallas kernels for 26%

profile of v7, /device:TPU:1, one launch (start us, length us, event | category | flops | bytes accessed | tf_op | source)
XLA Modules:
  0.0 122.2 jit_solution(1617961173396209898)
XLA Ops:
  0.6 2.2 %collective-permute-start = (bf16[16,3072]{1,0:T(8,128)(2,1)}, bf16[16,3072]{1,0:T(8,128)(2,1)S(1)}, u32[]{:S(2)}, u32[]{:S(2)}) collective-permute-start(bf16[16,3072]{1,0:T(8,128)(2,1)} %refs_0_.5), channel_id=1, source_target_pairs={{0,2},{1,3},{2,4},{3,5},{4,6},{5,7},{6,0},{7,1},{8,10},{9,11},{10,... | collective-permute-start | bytes 294920 | tf_op jit(solution)/shard_map/ppermute | solution.py:319
  2.8 2.3 %collective-permute-start.1 = (bf16[16,3072]{1,0:T(8,128)(2,1)}, bf16[16,3072]{1,0:T(8,128)(2,1)S(1)}, u32[]{:S(2)}, u32[]{:S(2)}) collective-permute-start(bf16[16,3072]{1,0:T(8,128)(2,1)} %refs_0_.5), channel_id=1, source_target_pairs={{0,4},{1,5},{2,6},{3,7},{4,0},{5,1},{6,2},{7,3},{8,12},{9,13},{10,... | collective-permute-start | bytes 294920 | tf_op jit(solution)/shard_map/ppermute | solution.py:319
  5.1 1.1 collective-permute-start.2
  6.2 1.2 collective-permute-start.3
  7.6 0.7 collective-permute-start.4
  8.3 4.2 %collective-permute-done.1.refs_4_ = bf16[16,3072]{1,0:T(8,128)(2,1)S(1)} collective-permute-done((bf16[16,3072]{1,0:T(8,128)(2,1)}, bf16[16,3072]{1,0:T(8,128)(2,1)S(1)}, u32[]{:S(2)}, u32[]{:S(2)}) %collective-permute-start.1) | collective-permute-done | bytes 98336 | tf_op jit(solution)/shard_map/ppermute | solution.py:319
  12.6 1.2 collective-permute-start.5
  14.1 3.8 %pair_tables.1 = (s32[4,256]{1,0:T(4,128)S(1)}, s32[4,256]{1,0:T(4,128)S(1)}, s32[4,256]{1,0:T(4,128)S(1)}, s32[4,256]{1,0:T(4,128)S(1)}, bf16[288,128,128]{2,1,0:T(8,128)(2,1)S(1)}) custom-call(s32[1,1,288]{2,1,0:T(1,128)} %slot_s.5, s32[1,1,288]{2,1,0:T(1,128)} %slot_s.4, s32[1,1,288]{2,1,0:T(1,128)} %slot_s.4, s32[1,1,288]{2,1,0:T(1,128)} %slot_s.5, ...), custom_call_target="tpu_custom_call" | custom-call | tf_op jit(solution)/shard_map/pair_tables/pallas_call | solution.py:111
  17.9 0.7 collective-permute-done.6.refs_7_
  18.6 4.3 %block_product.4 = (bf16[2,32,3072]{2,1,0:T(8,128)(2,1)S(1)}, bf16[2,32,3072]{2,1,0:T(8,128)(2,1)S(1)}, bf16[288,128,128]{2,1,0:T(8,128)(2,1)S(1)}) custom-call(s32[4,256]{1,0:T(4,128)S(1)} %get-tuple-element.57.table_s, s32[1]{0:T(128)} %constant.82.clone.1.in_s.out_s.right_s.left_s, s32[4]{0:T(128)S(1)} %pad_add_fusion.out_s, ...), custom_call_target="tpu_custom_call" | custom-call | flops 1207959552 | bytes 11010048 | tf_op jit(solution)/shard_map/block_product/pallas_call | solution.py:195
  22.9 1.4 %collective-permute-start.7 = (bf16[2,32,3072]{2,1,0:T(8,128)(2,1)S(1)}, bf16[2,32,3072]{2,1,0:T(8,128)(2,1)S(1)}, u32[]{:S(2)}, u32[]{:S(2)}) collective-permute-start(bf16[2,32,3072]{2,1,0:T(8,128)(2,1)S(1)} %get-tuple-element.60), channel_id=1, source_target_pairs={{0,8},{8,0},{16,24},{24,16},{1,9},{9,1},{17,25},{25,17},{2,10},{10... | collective-permute-start | bytes 1179656 | tf_op jit(solution)/shard_map/ppermute | solution.py:314
  24.3 1.1 collective-permute-start.10
  25.3 3.2 %collective-permute-start.12 = (bf16[16,3072]{1,0:T(8,128)(2,1)S(1)}, bf16[16,3072]{1,0:T(8,128)(2,1)S(1)}, u32[]{:S(2)}, u32[]{:S(2)}) collective-permute-start(bf16[16,3072]{1,0:T(8,128)(2,1)S(1)} %copy-done), channel_id=1, source_target_pairs={{0,4},{1,5},{2,6},{3,7},{4,0},{5,1},{6,2},{7,3},{8,12},{9,13},{10,... | collective-permute-start | bytes 294920 | tf_op jit(solution)/shard_map/ppermute | solution.py:319
  28.7 1.8 %collective-permute-start.9 = (bf16[16,3072]{1,0:T(8,128)(2,1)S(1)}, bf16[16,3072]{1,0:T(8,128)(2,1)S(1)}, u32[]{:S(2)}, u32[]{:S(2)}) collective-permute-start(bf16[16,3072]{1,0:T(8,128)(2,1)S(1)} %copy-done), channel_id=1, source_target_pairs={{0,1},{1,0},{2,3},{3,2},{4,5},{5,4},{6,7},{7,6},{8,9},{9,8},{10,11... | collective-permute-start | bytes 294920 | tf_op jit(solution)/shard_map/ppermute | solution.py:314
  30.6 0.8 collective-permute-done.10.refs_2_.refs_6_
  31.6 4.2 %collective-permute-done.12.refs_4_.refs_8_ = bf16[16,3072]{1,0:T(8,128)(2,1)S(1)} collective-permute-done((bf16[16,3072]{1,0:T(8,128)(2,1)S(1)}, bf16[16,3072]{1,0:T(8,128)(2,1)S(1)}, u32[]{:S(2)}, u32[]{:S(2)}) %collective-permute-start.12) | collective-permute-done | bytes 98336 | tf_op jit(solution)/shard_map/ppermute | solution.py:319
  36.0 1.3 %collective-permute-start.15 = (bf16[16,3072]{1,0:T(8,128)(2,1)S(1)}, bf16[16,3072]{1,0:T(8,128)(2,1)S(1)}, u32[]{:S(2)}, u32[]{:S(2)}) collective-permute-start(bf16[16,3072]{1,0:T(8,128)(2,1)S(1)} %collective-permute-done.14.refs_6_.refs_10_), channel_id=1, source_target_pairs={{0,1},{1,0},{2,3},{3,2},{4,5},{5,4},{6,7},{7,6},{8,9},{9,8},{10,11... | collective-permute-start | bytes 294920 | tf_op jit(solution)/shard_map/ppermute | solution.py:314
  37.3 2.3 %collective-permute-done.13.refs_5_.refs_9_ = bf16[16,3072]{1,0:T(8,128)(2,1)S(1)} collective-permute-done((bf16[16,3072]{1,0:T(8,128)(2,1)S(1)}, bf16[16,3072]{1,0:T(8,128)(2,1)S(1)}, u32[]{:S(2)}, u32[]{:S(2)}) %collective-permute-start.13) | collective-permute-done | bytes 98336 | tf_op jit(solution)/shard_map/ppermute | solution.py:314
  39.6 2.1 %collective-permute-done.15.refs_7_.refs_11_ = bf16[16,3072]{1,0:T(8,128)(2,1)S(1)} collective-permute-done((bf16[16,3072]{1,0:T(8,128)(2,1)S(1)}, bf16[16,3072]{1,0:T(8,128)(2,1)S(1)}, u32[]{:S(2)}, u32[]{:S(2)}) %collective-permute-start.15) | collective-permute-done | bytes 98336 | tf_op jit(solution)/shard_map/ppermute | solution.py:314
  41.7 4.2 %block_product.5 = (bf16[2,32,3072]{2,1,0:T(8,128)(2,1)S(1)}, bf16[2,32,3072]{2,1,0:T(8,128)(2,1)S(1)}) custom-call(s32[4,256]{1,0:T(4,128)S(1)} %get-tuple-element.61.table_s, s32[1]{0:T(128)} %constant.82.clone.1.in_s.out_s.right_s.left_s, s32[4]{0:T(128)S(1)} %pad_add_fusion.out_s, bf16[16,3072]{1,0:T(8,128)(2,1)S(1)} %copy-done, ...), custom_call_target="tpu_custom_call" | custom-call | flops 1207959552 | bytes 11010048 | tf_op jit(solution)/shard_map/block_product/pallas_call | solution.py:195
  45.9 0.5 collective-permute-start.16
  46.4 6.4 %collective-permute-done.8 = bf16[32,3072]{1,0:T(8,128)(2,1)S(1)} collective-permute-done((bf16[32,3072]{1,0:T(8,128)(2,1)S(1)}, bf16[32,3072]{1,0:T(8,128)(2,1)S(1)}, u32[]{:S(2)}, u32[]{:S(2)}) %collective-permute-start.8) | collective-permute-done | bytes 196640 | tf_op jit(solution)/shard_map/ppermute | solution.py:319
  53.4 1.0 collective-permute-start.17
  54.4 1.5 %collective-permute-start.18 = (bf16[32,3072]{1,0:T(8,128)(2,1)S(1)}, bf16[32,3072]{1,0:T(8,128)(2,1)S(1)}, u32[]{:S(2)}, u32[]{:S(2)}) collective-permute-start(bf16[32,3072]{1,0:T(8,128)(2,1)S(1)} %multiply_convert_fusion.refs_0_), channel_id=1, source_target_pairs={{0,16},{8,24},{16,0},{24,8},{1,17},{9,25},{17,1},{25,9},{2,18},{10... | collective-permute-start | bytes 589832 | tf_op jit(solution)/shard_map/ppermute | solution.py:319
  55.9 2.6 %collective-permute-done.19 = bf16[32,3072]{1,0:T(8,128)(2,1)S(1)} collective-permute-done((bf16[32,3072]{1,0:T(8,128)(2,1)S(1)}, bf16[32,3072]{1,0:T(8,128)(2,1)S(1)}, u32[]{:S(2)}, u32[]{:S(2)}) %collective-permute-start.19) | collective-permute-done | bytes 196640 | tf_op jit(solution)/shard_map/ppermute | solution.py:319
  58.4 0.4 fusion.6.refs_0_.refs_8_
  58.8 3.8 %collective-permute-done.18.refs_2_ = bf16[32,3072]{1,0:T(8,128)(2,1)S(1)} collective-permute-done((bf16[32,3072]{1,0:T(8,128)(2,1)S(1)}, bf16[32,3072]{1,0:T(8,128)(2,1)S(1)}, u32[]{:S(2)}, u32[]{:S(2)}) %collective-permute-start.18) | collective-permute-done | bytes 196640 | tf_op jit(solution)/shard_map/ppermute | solution.py:319
  62.6 1.8 %collective-permute-start.20 = (bf16[32,3072]{1,0:T(8,128)(2,1)S(1)}, bf16[32,3072]{1,0:T(8,128)(2,1)S(1)}, u32[]{:S(2)}, u32[]{:S(2)}) collective-permute-start(bf16[32,3072]{1,0:T(8,128)(2,1)S(1)} %collective-permute-done.18.refs_2_), channel_id=1, source_target_pairs={{0,8},{8,0},{16,24},{24,16},{1,9},{9,1},{17,25},{25,17},{2,10},{10... | collective-permute-start | bytes 589832 | tf_op jit(solution)/shard_map/ppermute | solution.py:314
  65.0 0.5 collective-permute-done.20.refs_3_
  65.5 5.4 %collective-permute-done.23.refs_2_.refs_10_ = bf16[32,3072]{1,0:T(8,128)(2,1)S(1)} collective-permute-done((bf16[32,3072]{1,0:T(8,128)(2,1)S(1)}, bf16[32,3072]{1,0:T(8,128)(2,1)S(1)}, u32[]{:S(2)}, u32[]{:S(2)}) %collective-permute-start.23) | collective-permute-done | bytes 196640 | tf_op jit(solution)/shard_map/ppermute | solution.py:319
  70.9 0.9 collective-permute-start.24
  71.8 4.5 %block_product.6 = (bf16[4,16,3072]{2,1,0:T(8,128)(2,1)S(1)}, bf16[4,16,3072]{2,1,0:T(8,128)(2,1)S(1)}, bf16[288,128,128]{2,1,0:T(8,128)(2,1)S(1)}) custom-call(s32[4,256]{1,0:T(4,128)S(1)} %get-tuple-element.56.table_s, s32[4]{0:T(128)S(1)} %fusion.23.in_s.left_s.right_s, s32[1]{0:T(128)} %constant.82.clone.1.in_s.out_s.right_s.left_s, ...), custom_call_target="tpu_custom_call" | custom-call | flops 1207959552 | bytes 11010048 | tf_op jit(solution)/shard_map/block_product/pallas_call | solution.py:195
  76.4 3.3 %block_product.7 = (bf16[4,16,3072]{2,1,0:T(8,128)(2,1)S(1)}, bf16[4,16,3072]{2,1,0:T(8,128)(2,1)S(1)}) custom-call(s32[4,256]{1,0:T(4,128)S(1)} %get-tuple-element.82.table_s, s32[4]{0:T(128)S(1)} %fusion.23.in_s.left_s.right_s, s32[1]{0:T(128)} %constant.82.clone.1.in_s.out_s.right_s.left_s, bf16[32,3072]{1,0:T(8,128)(2,1)S(1)} %fusion.6.refs_0_.refs_8_, ...), custom_call_target="tpu_custom_call" | custom-call | flops 1207959552 | bytes 11010048 | tf_op jit(solution)/shard_map/block_product/pallas_call | solution.py:195
  79.7 0.7 copy-done.5
  80.4 5.5 %block_grads.3.refs_12_ = f32[288,128,128]{2,1,0:T(8,128)} custom-call(s32[1,1,288]{2,1,0:T(1,128)S(1)} %copy-done.3, s32[4]{0:T(128)S(1)} %fusion.23.in_s.left_s.right_s, s32[1]{0:T(128)} %constant.82.clone.1.in_s.out_s.right_s.left_s, bf16[32,3072]{1,0:T(8,128)(2,1)S(1)} %multiply_convert_fusion.refs_0_, ...), custom_call_target="tpu_custom_call" | custom-call | flops 1207959552 | bytes 20447232 | tf_op jit(solution)/shard_map/block_grads/pallas_call | solution.py:266
  86.0 1.1 collective-permute-done.21
  87.1 0.8 pad_maximum_fusion
  87.9 5.6 %collective-permute-start.25 = (bf16[2,16,3072]{2,1,0:T(8,128)(2,1)}, bf16[2,16,3072]{2,1,0:T(8,128)(2,1)}, u32[]{:S(2)}, u32[]{:S(2)}) collective-permute-start(bf16[2,16,3072]{2,1,0:T(8,128)(2,1)} %pad_maximum_fusion), channel_id=1, source_target_pairs={{0,2},{1,3},{2,0},{3,1},{4,6},{5,7},{6,4},{7,5},{8,10},{9,11},{10,... | collective-permute-start | bytes 589832 | tf_op jit(solution)/shard_map/ppermute | solution.py:351
  93.5 5.2 %collective-permute-done.25 = bf16[2,16,3072]{2,1,0:T(8,128)(2,1)} collective-permute-done((bf16[2,16,3072]{2,1,0:T(8,128)(2,1)}, bf16[2,16,3072]{2,1,0:T(8,128)(2,1)}, u32[]{:S(2)}, u32[]{:S(2)}) %collective-permute-start.25) | collective-permute-done | bytes 196640 | tf_op jit(solution)/shard_map/ppermute | solution.py:351
  98.7 1.0 convert_element_type.203
  99.7 1.0 fusion.12
  100.7 5.5 %block_grads.4 = f32[288,128,128]{2,1,0:T(8,128)} custom-call(s32[1,1,288]{2,1,0:T(1,128)S(1)} %copy-done.3, s32[4]{0:T(128)S(1)} %fusion.23.in_s.left_s.right_s, s32[1]{0:T(128)} %constant.82.clone.1.in_s.out_s.right_s.left_s, bf16[32,3072]{1,0:T(8,128)(2,1)S(1)} %multiply_convert_fusion.refs_0_, ...), custom_call_target="tpu_custom_call", output_to_operand_aliasing={{}: (15, {})} | custom-call | flops 1207959552 | bytes 20447232 | tf_op jit(solution)/shard_map/block_grads/pallas_call | solution.py:266
  106.4 1.8 %collective-permute-start.30 = (bf16[16,3072]{1,0:T(8,128)(2,1)S(1)}, bf16[16,3072]{1,0:T(8,128)(2,1)S(1)}, u32[]{:S(2)}, u32[]{:S(2)}) collective-permute-start(bf16[16,3072]{1,0:T(8,128)(2,1)S(1)} %get-tuple-element.107), channel_id=1, source_target_pairs={{0,2},{1,3},{2,4},{3,5},{4,6},{5,7},{6,0},{7,1},{8,10},{9,11},{10,... | collective-permute-start | bytes 294920 | tf_op jit(solution)/shard_map/ppermute | solution.py:319
  108.2 2.3 %collective-permute-start.29 = (bf16[16,3072]{1,0:T(8,128)(2,1)S(1)}, bf16[16,3072]{1,0:T(8,128)(2,1)S(1)}, u32[]{:S(2)}, u32[]{:S(2)}) collective-permute-start(bf16[16,3072]{1,0:T(8,128)(2,1)S(1)} %get-tuple-element.108), channel_id=1, source_target_pairs={{0,4},{1,5},{2,6},{3,7},{4,0},{5,1},{6,2},{7,3},{8,12},{9,13},{10,... | collective-permute-start | bytes 294920 | tf_op jit(solution)/shard_map/ppermute | solution.py:319
  110.5 0.6 collective-permute-start.28
  111.1 8.7 %block_grads.5 = f32[288,128,128]{2,1,0:T(8,128)} custom-call(s32[1,1,288]{2,1,0:T(1,128)S(1)} %copy-done.4, s32[1]{0:T(128)} %constant.82.clone.1.in_s.out_s.right_s.left_s, s32[4]{0:T(128)S(1)} %fusion.23.in_s.left_s.right_s, bf16[16,3072]{1,0:T(8,128)(2,1)S(1)} %copy-done.1, bf16[16,3072]{1,0:T(8,128)(2,1)S(1)} %collective-permute-done.3.refs_1_, ...), custom_call_target="tpu_custom_call" | custom-call | flops 1207959552 | bytes 20447232 | tf_op jit(solution)/shard_map/block_grads/pallas_call | solution.py:266
  119.8 1.6 %fusion.13 = bf16[16,3072]{1,0:T(8,128)(2,1)} fusion(bf16[16,3072]{1,0:T(8,128)(2,1)S(1)} %collective-permute-done.26, f32[2,16,3072]{2,1,0:T(8,128)S(1)} %convert_element_type.203, bf16[4,16,3072]{2,1,0:T(8,128)(2,1)} %copy-done.6, bf16[4,16,3072]{2,1,0:T(8,128)(2,1)} %copy-done.2, pred[]{:T(512)S(6)} %eq.10), kind=kLoop, calls=%fused_computation.24 | loop fusion | flops 393216 | bytes 786433 | tf_op jit(solution)/shard_map/convert_element_type | solution.py:356
  121.5 0.7 fusion.11
  (51 shorter events, 2.8 us)
Async XLA Ops:
  0.6 18.0 %copy-start.1 = (bf16[16,3072]{1,0:T(8,128)(2,1)S(1)}, bf16[16,3072]{1,0:T(8,128)(2,1)}, u32[]{:S(2)}) copy-start(bf16[16,3072]{1,0:T(8,128)(2,1)} %refs_0_.5) | copy-start | bytes 294916
  0.6 7.0 %collective-permute-start = (bf16[16,3072]{1,0:T(8,128)(2,1)}, bf16[16,3072]{1,0:T(8,128)(2,1)S(1)}, u32[]{:S(2)}, u32[]{:S(2)}) collective-permute-start(bf16[16,3072]{1,0:T(8,128)(2,1)} %refs_0_.5), channel_id=1, source_target_pairs={{0,2},{1,3},{2,4},{3,5},{4,6},{5,7},{6,0},{7,1},{8,10},{9,11},{10,... | collective-permute-start | bytes 294920 | tf_op jit(solution)/shard_map/ppermute | solution.py:319
  2.8 9.8 %collective-permute-start.1 = (bf16[16,3072]{1,0:T(8,128)(2,1)}, bf16[16,3072]{1,0:T(8,128)(2,1)S(1)}, u32[]{:S(2)}, u32[]{:S(2)}) collective-permute-start(bf16[16,3072]{1,0:T(8,128)(2,1)} %refs_0_.5), channel_id=1, source_target_pairs={{0,4},{1,5},{2,6},{3,7},{4,0},{5,1},{6,2},{7,3},{8,12},{9,13},{10,... | collective-permute-start | bytes 294920 | tf_op jit(solution)/shard_map/ppermute | solution.py:319
  5.1 8.7 %collective-permute-start.2 = (bf16[16,3072]{1,0:T(8,128)(2,1)}, bf16[16,3072]{1,0:T(8,128)(2,1)S(1)}, u32[]{:S(2)}, u32[]{:S(2)}) collective-permute-start(bf16[16,3072]{1,0:T(8,128)(2,1)} %refs_0_.5), channel_id=1, source_target_pairs={{0,6},{1,7},{2,0},{3,1},{4,2},{5,3},{6,4},{7,5},{8,14},{9,15},{10,... | collective-permute-start | bytes 294920 | tf_op jit(solution)/shard_map/ppermute | solution.py:319
  6.2 11.7 %collective-permute-start.3 = (bf16[16,3072]{1,0:T(8,128)(2,1)}, bf16[16,3072]{1,0:T(8,128)(2,1)S(1)}, u32[]{:S(2)}, u32[]{:S(2)}) collective-permute-start(bf16[16,3072]{1,0:T(8,128)(2,1)} %refs_0_.5), channel_id=1, source_target_pairs={{0,1},{1,0},{2,3},{3,2},{4,5},{5,4},{6,7},{7,6},{8,9},{9,8},{10,11... | collective-permute-start | bytes 294920 | tf_op jit(solution)/shard_map/ppermute | solution.py:314
  7.6 10.3 %collective-permute-start.4 = (bf16[16,3072]{1,0:T(8,128)(2,1)S(1)}, bf16[16,3072]{1,0:T(8,128)(2,1)S(1)}, u32[]{:S(2)}, u32[]{:S(2)}) collective-permute-start(bf16[16,3072]{1,0:T(8,128)(2,1)S(1)} %collective-permute-done.refs_2_), channel_id=1, source_target_pairs={{0,1},{1,0},{2,3},{3,2},{4,5},{5,4},{6,7},{7,6},{8,9},{9,8},{10,11... | collective-permute-start | bytes 294920 | tf_op jit(solution)/shard_map/ppermute | solution.py:314
  12.6 5.4 %collective-permute-start.5 = (bf16[16,3072]{1,0:T(8,128)(2,1)S(1)}, bf16[16,3072]{1,0:T(8,128)(2,1)S(1)}, u32[]{:S(2)}, u32[]{:S(2)}) collective-permute-start(bf16[16,3072]{1,0:T(8,128)(2,1)S(1)} %collective-permute-done.1.refs_4_), channel_id=1, source_target_pairs={{0,1},{1,0},{2,3},{3,2},{4,5},{5,4},{6,7},{7,6},{8,9},{9,8},{10,11... | collective-permute-start | bytes 294920 | tf_op jit(solution)/shard_map/ppermute | solution.py:314
  13.8 4.8 %collective-permute-start.6 = (bf16[16,3072]{1,0:T(8,128)(2,1)S(1)}, bf16[16,3072]{1,0:T(8,128)(2,1)S(1)}, u32[]{:S(2)}, u32[]{:S(2)}) collective-permute-start(bf16[16,3072]{1,0:T(8,128)(2,1)S(1)} %collective-permute-done.2.refs_6_), channel_id=1, source_target_pairs={{0,1},{1,0},{2,3},{3,2},{4,5},{5,4},{6,7},{7,6},{8,9},{9,8},{10,11... | collective-permute-start | bytes 294920 | tf_op jit(solution)/shard_map/ppermute | solution.py:314
  18.6 5.7 %copy-start = (bf16[16,3072]{1,0:T(8,128)(2,1)S(1)}, bf16[16,3072]{1,0:T(8,128)(2,1)}, u32[]{:S(2)}) copy-start(bf16[16,3072]{1,0:T(8,128)(2,1)} %refs_4_.3) | copy-start | bytes 294916
  22.9 14.3 %collective-permute-start.7 = (bf16[2,32,3072]{2,1,0:T(8,128)(2,1)S(1)}, bf16[2,32,3072]{2,1,0:T(8,128)(2,1)S(1)}, u32[]{:S(2)}, u32[]{:S(2)}) collective-permute-start(bf16[2,32,3072]{2,1,0:T(8,128)(2,1)S(1)} %get-tuple-element.60), channel_id=1, source_target_pairs={{0,8},{8,0},{16,24},{24,16},{1,9},{9,1},{17,25},{25,17},{2,10},{10... | collective-permute-start | bytes 1179656 | tf_op jit(solution)/shard_map/ppermute | solution.py:314
  24.3 7.1 %collective-permute-start.10 = (bf16[16,3072]{1,0:T(8,128)(2,1)S(1)}, bf16[16,3072]{1,0:T(8,128)(2,1)S(1)}, u32[]{:S(2)}, u32[]{:S(2)}) collective-permute-start(bf16[16,3072]{1,0:T(8,128)(2,1)S(1)} %copy-done), channel_id=1, source_target_pairs={{0,2},{1,3},{2,4},{3,5},{4,6},{5,7},{6,0},{7,1},{8,10},{9,11},{10,... | collective-permute-start | bytes 294920 | tf_op jit(solution)/shard_map/ppermute | solution.py:319
  25.3 10.4 %collective-permute-start.12 = (bf16[16,3072]{1,0:T(8,128)(2,1)S(1)}, bf16[16,3072]{1,0:T(8,128)(2,1)S(1)}, u32[]{:S(2)}, u32[]{:S(2)}) collective-permute-start(bf16[16,3072]{1,0:T(8,128)(2,1)S(1)} %copy-done), channel_id=1, source_target_pairs={{0,4},{1,5},{2,6},{3,7},{4,0},{5,1},{6,2},{7,3},{8,12},{9,13},{10,... | collective-permute-start | bytes 294920 | tf_op jit(solution)/shard_map/ppermute | solution.py:319
  28.5 7.4 %collective-permute-start.14 = (bf16[16,3072]{1,0:T(8,128)(2,1)S(1)}, bf16[16,3072]{1,0:T(8,128)(2,1)S(1)}, u32[]{:S(2)}, u32[]{:S(2)}) collective-permute-start(bf16[16,3072]{1,0:T(8,128)(2,1)S(1)} %copy-done), channel_id=1, source_target_pairs={{0,6},{1,7},{2,0},{3,1},{4,2},{5,3},{6,4},{7,5},{8,14},{9,15},{10,... | collective-permute-start | bytes 294920 | tf_op jit(solution)/shard_map/ppermute | solution.py:319
  28.7 8.5 %collective-permute-start.9 = (bf16[16,3072]{1,0:T(8,128)(2,1)S(1)}, bf16[16,3072]{1,0:T(8,128)(2,1)S(1)}, u32[]{:S(2)}, u32[]{:S(2)}) collective-permute-start(bf16[16,3072]{1,0:T(8,128)(2,1)S(1)} %copy-done), channel_id=1, source_target_pairs={{0,1},{1,0},{2,3},{3,2},{4,5},{5,4},{6,7},{7,6},{8,9},{9,8},{10,11... | collective-permute-start | bytes 294920 | tf_op jit(solution)/shard_map/ppermute | solution.py:314
  31.3 6.0 %collective-permute-start.11 = (bf16[16,3072]{1,0:T(8,128)(2,1)S(1)}, bf16[16,3072]{1,0:T(8,128)(2,1)S(1)}, u32[]{:S(2)}, u32[]{:S(2)}) collective-permute-start(bf16[16,3072]{1,0:T(8,128)(2,1)S(1)} %collective-permute-done.10.refs_2_.refs_6_), channel_id=1, source_target_pairs={{0,1},{1,0},{2,3},{3,2},{4,5},{5,4},{6,7},{7,6},{8,9},{9,8},{10,11... | collective-permute-start | bytes 294920 | tf_op jit(solution)/shard_map/ppermute | solution.py:314
  35.8 3.9 %collective-permute-start.13 = (bf16[16,3072]{1,0:T(8,128)(2,1)S(1)}, bf16[16,3072]{1,0:T(8,128)(2,1)S(1)}, u32[]{:S(2)}, u32[]{:S(2)}) collective-permute-start(bf16[16,3072]{1,0:T(8,128)(2,1)S(1)} %collective-permute-done.12.refs_4_.refs_8_), channel_id=1, source_target_pairs={{0,1},{1,0},{2,3},{3,2},{4,5},{5,4},{6,7},{7,6},{8,9},{9,8},{10,11... | collective-permute-start | bytes 294920 | tf_op jit(solution)/shard_map/ppermute | solution.py:314
  36.0 5.8 %collective-permute-start.15 = (bf16[16,3072]{1,0:T(8,128)(2,1)S(1)}, bf16[16,3072]{1,0:T(8,128)(2,1)S(1)}, u32[]{:S(2)}, u32[]{:S(2)}) collective-permute-start(bf16[16,3072]{1,0:T(8,128)(2,1)S(1)} %collective-permute-done.14.refs_6_.refs_10_), channel_id=1, source_target_pairs={{0,1},{1,0},{2,3},{3,2},{4,5},{5,4},{6,7},{7,6},{8,9},{9,8},{10,11... | collective-permute-start | bytes 294920 | tf_op jit(solution)/shard_map/ppermute | solution.py:314
  45.9 6.9 %collective-permute-start.16 = (bf16[2,32,3072]{2,1,0:T(8,128)(2,1)S(1)}, bf16[2,32,3072]{2,1,0:T(8,128)(2,1)S(1)}, u32[]{:S(2)}, u32[]{:S(2)}) collective-permute-start(bf16[2,32,3072]{2,1,0:T(8,128)(2,1)S(1)} %get-tuple-element.72), channel_id=1, source_target_pairs={{0,8},{8,0},{16,24},{24,16},{1,9},{9,1},{17,25},{25,17},{2,10},{10... | collective-permute-start | bytes 1179656 | tf_op jit(solution)/shard_map/ppermute | solution.py:314
  46.4 6.4 %collective-permute-start.8 = (bf16[32,3072]{1,0:T(8,128)(2,1)S(1)}, bf16[32,3072]{1,0:T(8,128)(2,1)S(1)}, u32[]{:S(2)}, u32[]{:S(2)}) collective-permute-start(bf16[32,3072]{1,0:T(8,128)(2,1)S(1)} %fusion.7), channel_id=1, source_target_pairs={{0,16},{8,24},{16,0},{24,8},{1,17},{9,25},{17,1},{25,9},{2,18},{10... | collective-permute-start | bytes 589832 | tf_op jit(solution)/shard_map/ppermute | solution.py:319
  52.8 5.6 %collective-permute-start.19 = (bf16[32,3072]{1,0:T(8,128)(2,1)S(1)}, bf16[32,3072]{1,0:T(8,128)(2,1)S(1)}, u32[]{:S(2)}, u32[]{:S(2)}) collective-permute-start(bf16[32,3072]{1,0:T(8,128)(2,1)S(1)} %fusion.8), channel_id=1, source_target_pairs={{0,16},{8,24},{16,0},{24,8},{1,17},{9,25},{17,1},{25,9},{2,18},{10... | collective-permute-start | bytes 589832 | tf_op jit(solution)/shard_map/ppermute | solution.py:319
  53.4 11.6 %collective-permute-start.17 = (bf16[32,3072]{1,0:T(8,128)(2,1)S(1)}, bf16[32,3072]{1,0:T(8,128)(2,1)S(1)}, u32[]{:S(2)}, u32[]{:S(2)}) collective-permute-start(bf16[32,3072]{1,0:T(8,128)(2,1)S(1)} %multiply_convert_fusion.refs_0_), channel_id=1, source_target_pairs={{0,8},{8,0},{16,24},{24,16},{1,9},{9,1},{17,25},{25,17},{2,10},{10... | collective-permute-start | bytes 589832 | tf_op jit(solution)/shard_map/ppermute | solution.py:314
  54.4 8.2 %collective-permute-start.18 = (bf16[32,3072]{1,0:T(8,128)(2,1)S(1)}, bf16[32,3072]{1,0:T(8,128)(2,1)S(1)}, u32[]{:S(2)}, u32[]{:S(2)}) collective-permute-start(bf16[32,3072]{1,0:T(8,128)(2,1)S(1)} %multiply_convert_fusion.refs_0_), channel_id=1, source_target_pairs={{0,16},{8,24},{16,0},{24,8},{1,17},{9,25},{17,1},{25,9},{2,18},{10... | collective-permute-start | bytes 589832 | tf_op jit(solution)/shard_map/ppermute | solution.py:319
  62.6 2.9 %collective-permute-start.20 = (bf16[32,3072]{1,0:T(8,128)(2,1)S(1)}, bf16[32,3072]{1,0:T(8,128)(2,1)S(1)}, u32[]{:S(2)}, u32[]{:S(2)}) collective-permute-start(bf16[32,3072]{1,0:T(8,128)(2,1)S(1)} %collective-permute-done.18.refs_2_), channel_id=1, source_target_pairs={{0,8},{8,0},{16,24},{24,16},{1,9},{9,1},{17,25},{25,17},{2,10},{10... | collective-permute-start | bytes 589832 | tf_op jit(solution)/shard_map/ppermute | solution.py:314
  64.4 6.5 %collective-permute-start.23 = (bf16[32,3072]{1,0:T(8,128)(2,1)S(1)}, bf16[32,3072]{1,0:T(8,128)(2,1)S(1)}, u32[]{:S(2)}, u32[]{:S(2)}) collective-permute-start(bf16[32,3072]{1,0:T(8,128)(2,1)S(1)} %fusion.6.refs_0_.refs_8_), channel_id=1, source_target_pairs={{0,16},{8,24},{16,0},{24,8},{1,17},{9,25},{17,1},{25,9},{2,18},{10... | collective-permute-start | bytes 589832 | tf_op jit(solution)/shard_map/ppermute | solution.py:319
  64.7 11.7 %collective-permute-start.22 = (bf16[32,3072]{1,0:T(8,128)(2,1)S(1)}, bf16[32,3072]{1,0:T(8,128)(2,1)S(1)}, u32[]{:S(2)}, u32[]{:S(2)}) collective-permute-start(bf16[32,3072]{1,0:T(8,128)(2,1)S(1)} %fusion.6.refs_0_.refs_8_), channel_id=1, source_target_pairs={{0,8},{8,0},{16,24},{24,16},{1,9},{9,1},{17,25},{25,17},{2,10},{10... | collective-permute-start | bytes 589832 | tf_op jit(solution)/shard_map/ppermute | solution.py:314
  70.9 5.5 %collective-permute-start.24 = (bf16[32,3072]{1,0:T(8,128)(2,1)S(1)}, bf16[32,3072]{1,0:T(8,128)(2,1)S(1)}, u32[]{:S(2)}, u32[]{:S(2)}) collective-permute-start(bf16[32,3072]{1,0:T(8,128)(2,1)S(1)} %collective-permute-done.23.refs_2_.refs_10_), channel_id=1, source_target_pairs={{0,8},{8,0},{16,24},{24,16},{1,9},{9,1},{17,25},{25,17},{2,10},{10... | collective-permute-start | bytes 589832 | tf_op jit(solution)/shard_map/ppermute | solution.py:314
  76.3 10.8 %copy-start.2 = (bf16[4,16,3072]{2,1,0:T(8,128)(2,1)}, bf16[4,16,3072]{2,1,0:T(8,128)(2,1)S(1)}, u32[]{:S(2)}) copy-start(bf16[4,16,3072]{2,1,0:T(8,128)(2,1)S(1)} %get-tuple-element.80) | copy-start | bytes 1179652
  76.3 4.1 %copy-start.3 = (s32[1,1,288]{2,1,0:T(1,128)S(1)}, s32[1,1,288]{2,1,0:T(1,128)}, u32[]{:S(2)}) copy-start(s32[1,1,288]{2,1,0:T(1,128)} %slot_s.4) | copy-start | bytes 3460
  76.3 10.7 %collective-permute-start.21 = (bf16[4,16,3072]{2,1,0:T(8,128)(2,1)S(1)}, bf16[4,16,3072]{2,1,0:T(8,128)(2,1)S(1)}, u32[]{:S(2)}, u32[]{:S(2)}) collective-permute-start(bf16[4,16,3072]{2,1,0:T(8,128)(2,1)S(1)} %get-tuple-element.81), channel_id=1, source_target_pairs={{0,1},{1,0},{2,3},{3,2},{4,5},{5,4},{6,7},{7,6},{8,9},{9,8},{10,11... | collective-permute-start | bytes 1179656 | tf_op jit(solution)/shard_map/ppermute | solution.py:314
  79.7 0.7 copy-start.5
  87.0 0.8 copy-start.6
  87.9 10.9 %collective-permute-start.25 = (bf16[2,16,3072]{2,1,0:T(8,128)(2,1)}, bf16[2,16,3072]{2,1,0:T(8,128)(2,1)}, u32[]{:S(2)}, u32[]{:S(2)}) collective-permute-start(bf16[2,16,3072]{2,1,0:T(8,128)(2,1)} %pad_maximum_fusion), channel_id=1, source_target_pairs={{0,2},{1,3},{2,0},{3,1},{4,6},{5,7},{6,4},{7,5},{8,10},{9,11},{10,... | collective-permute-start | bytes 589832 | tf_op jit(solution)/shard_map/ppermute | solution.py:351
  93.5 12.8 %collective-permute-start.27 = (bf16[4,16,3072]{2,1,0:T(8,128)(2,1)}, bf16[4,16,3072]{2,1,0:T(8,128)(2,1)S(1)}, u32[]{:S(2)}, u32[]{:S(2)}) collective-permute-start(bf16[4,16,3072]{2,1,0:T(8,128)(2,1)} %copy-done.5), channel_id=1, source_target_pairs={{0,1},{1,0},{2,3},{3,2},{4,5},{5,4},{6,7},{7,6},{8,9},{9,8},{10,11... | collective-permute-start | bytes 1179656 | tf_op jit(solution)/shard_map/ppermute | solution.py:314
  100.7 10.5 %copy-start.4 = (s32[1,1,288]{2,1,0:T(1,128)S(1)}, s32[1,1,288]{2,1,0:T(1,128)}, u32[]{:S(2)}) copy-start(s32[1,1,288]{2,1,0:T(1,128)} %slot_s.5) | copy-start | bytes 3460
  100.7 19.1 %collective-permute-start.26 = (bf16[16,3072]{1,0:T(8,128)(2,1)S(1)}, bf16[16,3072]{1,0:T(8,128)(2,1)S(1)}, u32[]{:S(2)}, u32[]{:S(2)}) collective-permute-start(bf16[16,3072]{1,0:T(8,128)(2,1)S(1)} %fusion.12), channel_id=1, source_target_pairs={{0,4},{1,5},{2,6},{3,7},{4,0},{5,1},{6,2},{7,3},{8,12},{9,13},{10,... | collective-permute-start | bytes 294920 | tf_op jit(solution)/shard_map/ppermute | solution.py:319
  106.4 15.1 %collective-permute-start.30 = (bf16[16,3072]{1,0:T(8,128)(2,1)S(1)}, bf16[16,3072]{1,0:T(8,128)(2,1)S(1)}, u32[]{:S(2)}, u32[]{:S(2)}) collective-permute-start(bf16[16,3072]{1,0:T(8,128)(2,1)S(1)} %get-tuple-element.107), channel_id=1, source_target_pairs={{0,2},{1,3},{2,4},{3,5},{4,6},{5,7},{6,0},{7,1},{8,10},{9,11},{10,... | collective-permute-start | bytes 294920 | tf_op jit(solution)/shard_map/ppermute | solution.py:319
  108.2 13.3 %collective-permute-start.29 = (bf16[16,3072]{1,0:T(8,128)(2,1)S(1)}, bf16[16,3072]{1,0:T(8,128)(2,1)S(1)}, u32[]{:S(2)}, u32[]{:S(2)}) collective-permute-start(bf16[16,3072]{1,0:T(8,128)(2,1)S(1)} %get-tuple-element.108), channel_id=1, source_target_pairs={{0,4},{1,5},{2,6},{3,7},{4,0},{5,1},{6,2},{7,3},{8,12},{9,13},{10,... | collective-permute-start | bytes 294920 | tf_op jit(solution)/shard_map/ppermute | solution.py:319
  110.5 11.0 %collective-permute-start.28 = (bf16[16,3072]{1,0:T(8,128)(2,1)S(1)}, bf16[16,3072]{1,0:T(8,128)(2,1)S(1)}, u32[]{:S(2)}, u32[]{:S(2)}) collective-permute-start(bf16[16,3072]{1,0:T(8,128)(2,1)S(1)} %get-tuple-element.106), channel_id=1, source_target_pairs={{0,6},{1,7},{2,0},{3,1},{4,2},{5,3},{6,4},{7,5},{8,14},{9,15},{10,... | collective-permute-start | bytes 294920 | tf_op jit(solution)/shard_map/ppermute | solution.py:319

commit v8 on v6

--- a/solution.py
+++ b/solution.py
@@ -300,7 +300,6 @@
     slots_in = in_slots
     slots_out = out_slots.reshape(in_slots.shape)
     width = w_in.shape[-1]
-    cap = w_in.shape[0]
     tensor_count = lax.axis_size("tensor")
     seq_count = lax.axis_size("seq")
     feat_blocks = tokens.shape[1] // width
@@ -325,7 +324,10 @@
     near_order = jnp.concatenate([seq_part[0::2], seq_part[1::2]])
 
     def gather_far(own):
-        return [own] + [far_move(own, "tensor", tensor_count, k) for k in range(1, far_t)]
+        pieces = [own]
+        for k in range(1, far_t):
+            pieces.append(far_move(own, "tensor", tensor_count, k))
+        return pieces
 
     def gather_near(far):
         pieces = []
@@ -343,15 +345,6 @@
         for value in moved:
             total = total + value.astype(jnp.float32)
         return total.astype(jnp.bfloat16)
-
-    def total_out_halving(own, pairs):
-        parts = [own] + [value.astype(jnp.float32) for value in pairs]
-        while len(parts) > 1:
-            half = len(parts) // 2
-            sent = jnp.stack([value.astype(jnp.bfloat16) for value in parts[half:]])
-            moved = far_move(sent, "tensor", tensor_count, far_t - half)
-            parts = [parts[k] + moved[k].astype(jnp.float32) for k in range(half)]
-        return parts[0].astype(jnp.bfloat16)
 
     def pair_hidden(keep, send):
         got = near_move(send, "seq", seq_count)
@@ -402,15 +395,15 @@
     hidden = total_hidden(own_h, pairs_h)
     own_act = gelu_value(hidden).astype(jnp.bfloat16)
     own_g, pairs_g = pair_hidden(keep_g, send_g)
-    act_far = spread_far(after(own_act, pairs_g))
+    act_far = spread_far(own_act)
     grad_act = total_hidden(own_g, pairs_g, own_act)
     own_gh = (grad_act * gelu_slope(hidden)).astype(jnp.bfloat16)
-    activated = spread_near([act_far[0]] + after(act_far[1:], own_gh))
+    activated = spread_near(act_far)
     gh_far = spread_far(own_gh)
     grad_hidden = spread_near(gh_far)
 
     keep_o, send_o, w_in_near = block_product(
-        after(activated, own_gh),
+        activated,
         seq_part,
         w_out_near,
         out_by_col,
@@ -421,21 +414,15 @@
         [w_in],
     )
     got_o = near_move(send_o, "tensor", tensor_count)
+    grad_out = block_grads(after(activated, keep_o), seq_part, cot, None, slots_out)
     keep_t, send_t = block_product(
-        after(grad_hidden, keep_o), seq_part, w_in_near, in_by_row, feat_blocks, token_lengths, token_rows, True
+        after(grad_hidden, grad_out), seq_part, w_in_near, in_by_row, feat_blocks, token_lengths, token_rows, True
     )
     got_t = near_move(send_t, "tensor", tensor_count)
-    parts = 2 if cap % 96 == 0 else 1
-    act_t = after(activated, keep_t)
-    grad_out = block_grads(act_t, seq_part, cot, None, slots_out, 0, parts)
-    own_o, pairs_o = pair_out(keep_o, after(got_o, grad_out))
-    for part in range(1, parts):
-        grad_out = block_grads(
-            after(act_t, pairs_o), seq_part, cot, None, slots_out, part, parts, grad_out
-        )
-    own_t, pairs_t = pair_out(keep_t, after(got_t, grad_out))
+    own_o, pairs_o = pair_out(keep_o, after(got_o, keep_t))
+    own_t, pairs_t = pair_out(keep_t, after(got_t, pairs_o))
     grad_in = block_grads(tok, None, after(grad_hidden, pairs_t), seq_part, slots_in)
-    output = total_out_halving(own_o, pairs_o)
+    output = total_out(own_o, pairs_o)
     grad_tokens = total_out(own_t, pairs_t)
     return (
         output,

time: 117 us -> 109 us (0.932)
  the two profiles are of different devices: /device:TPU:1 before, /device:TPU:8 now
where the time goes in v8:
time: 109 us
  Pallas kernels  40.9 us (38%)
  starting transfers between devices  33.8 us (31%)
  waiting for transfers between devices  30.6 us (28%)
  other arithmetic  2.33 us (2%)
    ppermute x16, starting transfers between devices, far_move(): return lax.ppermute(v, axis, pairs)  27.3 us
    ppermute x16, waiting for transfers between devices, far_move(): return lax.ppermute(v, axis, pairs)  22.2 us
    pallas_call x4, Pallas kernels, block_product(): pl.pallas_call(body, in_specs=[smem] * 3 + [vmem] * (n_in + 1) + [pl.Bloc...  19.6 us
    pallas_call x2, Pallas kernels, block_grads(): pl.pallas_call(body, grid_spec=pltpu.PrefetchScalarGridSpec(num_scalar_pr...  17.5 us
    ppermute x16, waiting for transfers between devices, near_move(): return lax.ppermute(v, axis, [(i, i ^ 1) for i in range(count)])  8.43 us
    ppermute x16, starting transfers between devices, near_move(): return lax.ppermute(v, axis, [(i, i ^ 1) for i in range(count)])  6.43 us
    pallas_call x1, Pallas kernels, pair_tables(): pl.pallas_call(body, in_specs=[pl.BlockSpec(memory_space=pltpu.HBM)] * (n...  3.79 us
  transfers between devices with their start and end apart: 32, of which 15 were waited for; matrix products, arithmetic and copies ran while one was open for 2% of the time, Pallas kernels for 34%

profile of v8, /device:TPU:8, one launch (start us, length us, event | category | flops | bytes accessed | tf_op | source)
XLA Modules:
  0.0 108.7 jit_solution(9431317591333968712)
XLA Ops:
  0.6 1.6 %collective-permute-start.3 = (bf16[16,3072]{1,0:T(8,128)(2,1)}, bf16[16,3072]{1,0:T(8,128)(2,1)S(1)}, u32[]{:S(2)}, u32[]{:S(2)}) collective-permute-start(bf16[16,3072]{1,0:T(8,128)(2,1)} %refs_0_.5), channel_id=1, source_target_pairs={{0,1},{1,0},{2,3},{3,2},{4,5},{5,4},{6,7},{7,6},{8,9},{9,8},{10,11... | collective-permute-start | bytes 294920 | tf_op jit(solution)/shard_map/ppermute | solution.py:313
  2.2 0.4 collective-permute-start.2
  2.6 2.6 %collective-permute-start.1 = (bf16[16,3072]{1,0:T(8,128)(2,1)}, bf16[16,3072]{1,0:T(8,128)(2,1)S(1)}, u32[]{:S(2)}, u32[]{:S(2)}) collective-permute-start(bf16[16,3072]{1,0:T(8,128)(2,1)} %refs_0_.5), channel_id=1, source_target_pairs={{0,4},{1,5},{2,6},{3,7},{4,0},{5,1},{6,2},{7,3},{8,12},{9,13},{10,... | collective-permute-start | bytes 294920 | tf_op jit(solution)/shard_map/ppermute | solution.py:318
  5.2 2.5 %collective-permute-start = (bf16[16,3072]{1,0:T(8,128)(2,1)}, bf16[16,3072]{1,0:T(8,128)(2,1)S(1)}, u32[]{:S(2)}, u32[]{:S(2)}) collective-permute-start(bf16[16,3072]{1,0:T(8,128)(2,1)} %refs_0_.5), channel_id=1, source_target_pairs={{0,2},{1,3},{2,4},{3,5},{4,6},{5,7},{6,0},{7,1},{8,10},{9,11},{10,... | collective-permute-start | bytes 294920 | tf_op jit(solution)/shard_map/ppermute | solution.py:318
  7.7 0.1 slice.79
  7.8 0.1 slice.78
  7.9 0.5 collective-permute-start.6
  8.5 3.6 %collective-permute-done.1.refs_4_ = bf16[16,3072]{1,0:T(8,128)(2,1)S(1)} collective-permute-done((bf16[16,3072]{1,0:T(8,128)(2,1)}, bf16[16,3072]{1,0:T(8,128)(2,1)S(1)}, u32[]{:S(2)}, u32[]{:S(2)}) %collective-permute-start.1) | collective-permute-done | bytes 98336 | tf_op jit(solution)/shard_map/ppermute | solution.py:318
  12.1 0.5 collective-permute-start.5
  12.6 0.7 collective-permute-done.refs_2_
  13.4 0.7 collective-permute-start.4
  14.2 3.8 %pair_tables.1 = (s32[4,256]{1,0:T(4,128)S(1)}, s32[4,256]{1,0:T(4,128)S(1)}, s32[4,256]{1,0:T(4,128)S(1)}, s32[4,256]{1,0:T(4,128)S(1)}, bf16[288,128,128]{2,1,0:T(8,128)(2,1)S(1)}) custom-call(s32[1,1,288]{2,1,0:T(1,128)} %slot_s.3, s32[1,1,288]{2,1,0:T(1,128)} %slot_s.2, s32[1,1,288]{2,1,0:T(1,128)} %slot_s.2, s32[1,1,288]{2,1,0:T(1,128)} %slot_s.3, ...), custom_call_target="tpu_custom_call" | custom-call | tf_op jit(solution)/shard_map/pair_tables/pallas_call | solution.py:111
  18.0 0.4 collective-permute-done.4.refs_3_
  18.4 4.3 %block_product.4 = (bf16[2,32,3072]{2,1,0:T(8,128)(2,1)S(1)}, bf16[2,32,3072]{2,1,0:T(8,128)(2,1)S(1)}, bf16[288,128,128]{2,1,0:T(8,128)(2,1)S(1)}) custom-call(s32[4,256]{1,0:T(4,128)S(1)} %get-tuple-element.47.table_s, s32[1]{0:T(128)} %constant.68.clone.1.in_s.out_s.right_s.left_s, s32[4]{0:T(128)S(1)} %pad_add_fusion.out_s, ...), custom_call_target="tpu_custom_call" | custom-call | flops 1207959552 | bytes 11010048 | tf_op jit(solution)/shard_map/block_product/pallas_call | solution.py:195
  22.8 2.7 %collective-permute-start.18 = (bf16[16,3072]{1,0:T(8,128)(2,1)S(1)}, bf16[16,3072]{1,0:T(8,128)(2,1)S(1)}, u32[]{:S(2)}, u32[]{:S(2)}) collective-permute-start(bf16[16,3072]{1,0:T(8,128)(2,1)S(1)} %copy-done), channel_id=1, source_target_pairs={{0,6},{1,7},{2,0},{3,1},{4,2},{5,3},{6,4},{7,5},{8,14},{9,15},{10,... | collective-permute-start | bytes 294920 | tf_op jit(solution)/shard_map/ppermute | solution.py:318
  25.5 1.6 %collective-permute-start.16 = (bf16[16,3072]{1,0:T(8,128)(2,1)S(1)}, bf16[16,3072]{1,0:T(8,128)(2,1)S(1)}, u32[]{:S(2)}, u32[]{:S(2)}) collective-permute-start(bf16[16,3072]{1,0:T(8,128)(2,1)S(1)} %copy-done), channel_id=1, source_target_pairs={{0,4},{1,5},{2,6},{3,7},{4,0},{5,1},{6,2},{7,3},{8,12},{9,13},{10,... | collective-permute-start | bytes 294920 | tf_op jit(solution)/shard_map/ppermute | solution.py:318
  27.1 2.8 %collective-permute-start.14 = (bf16[16,3072]{1,0:T(8,128)(2,1)S(1)}, bf16[16,3072]{1,0:T(8,128)(2,1)S(1)}, u32[]{:S(2)}, u32[]{:S(2)}) collective-permute-start(bf16[16,3072]{1,0:T(8,128)(2,1)S(1)} %copy-done), channel_id=1, source_target_pairs={{0,2},{1,3},{2,4},{3,5},{4,6},{5,7},{6,0},{7,1},{8,10},{9,11},{10,... | collective-permute-start | bytes 294920 | tf_op jit(solution)/shard_map/ppermute | solution.py:318
  30.0 2.0 %collective-permute-start.19 = (bf16[16,3072]{1,0:T(8,128)(2,1)S(1)}, bf16[16,3072]{1,0:T(8,128)(2,1)S(1)}, u32[]{:S(2)}, u32[]{:S(2)}) collective-permute-start(bf16[16,3072]{1,0:T(8,128)(2,1)S(1)} %collective-permute-done.18.refs_6_.refs_10_), channel_id=1, source_target_pairs={{0,1},{1,0},{2,3},{3,2},{4,5},{5,4},{6,7},{7,6},{8,9},{9,8},{10,11... | collective-permute-start | bytes 294920 | tf_op jit(solution)/shard_map/ppermute | solution.py:313
  32.0 2.5 %collective-permute-done.16.refs_4_.refs_8_ = bf16[16,3072]{1,0:T(8,128)(2,1)S(1)} collective-permute-done((bf16[16,3072]{1,0:T(8,128)(2,1)S(1)}, bf16[16,3072]{1,0:T(8,128)(2,1)S(1)}, u32[]{:S(2)}, u32[]{:S(2)}) %collective-permute-start.16) | collective-permute-done | bytes 98336 | tf_op jit(solution)/shard_map/ppermute | solution.py:318
  34.5 0.2 collective-permute-start.17
  34.7 1.3 %collective-permute-done.14.refs_2_.refs_6_ = bf16[16,3072]{1,0:T(8,128)(2,1)S(1)} collective-permute-done((bf16[16,3072]{1,0:T(8,128)(2,1)S(1)}, bf16[16,3072]{1,0:T(8,128)(2,1)S(1)}, u32[]{:S(2)}, u32[]{:S(2)}) %collective-permute-start.14) | collective-permute-done | bytes 98336 | tf_op jit(solution)/shard_map/ppermute | solution.py:318
  36.0 0.5 collective-permute-start.15
  36.6 1.4 %collective-permute-start.8 = (bf16[32,3072]{1,0:T(8,128)(2,1)S(1)}, bf16[32,3072]{1,0:T(8,128)(2,1)S(1)}, u32[]{:S(2)}, u32[]{:S(2)}) collective-permute-start(bf16[32,3072]{1,0:T(8,128)(2,1)S(1)} %fusion.7), channel_id=1, source_target_pairs={{0,16},{8,24},{16,0},{24,8},{1,17},{9,25},{17,1},{25,9},{2,18},{10... | collective-permute-start | bytes 589832 | tf_op jit(solution)/shard_map/ppermute | solution.py:318
  38.0 2.2 %collective-permute-done.17.refs_5_.refs_9_ = bf16[16,3072]{1,0:T(8,128)(2,1)S(1)} collective-permute-done((bf16[16,3072]{1,0:T(8,128)(2,1)S(1)}, bf16[16,3072]{1,0:T(8,128)(2,1)S(1)}, u32[]{:S(2)}, u32[]{:S(2)}) %collective-permute-start.17) | collective-permute-done | bytes 98336 | tf_op jit(solution)/shard_map/ppermute | solution.py:313
  40.1 1.1 %collective-permute-done.15.refs_3_.refs_7_ = bf16[16,3072]{1,0:T(8,128)(2,1)S(1)} collective-permute-done((bf16[16,3072]{1,0:T(8,128)(2,1)S(1)}, bf16[16,3072]{1,0:T(8,128)(2,1)S(1)}, u32[]{:S(2)}, u32[]{:S(2)}) %collective-permute-start.15) | collective-permute-done | bytes 98336 | tf_op jit(solution)/shard_map/ppermute | solution.py:313
  41.2 5.6 %block_product.6 = (bf16[2,32,3072]{2,1,0:T(8,128)(2,1)S(1)}, bf16[2,32,3072]{2,1,0:T(8,128)(2,1)S(1)}) custom-call(s32[4,256]{1,0:T(4,128)S(1)} %get-tuple-element.55.table_s, s32[1]{0:T(128)} %constant.68.clone.1.in_s.out_s.right_s.left_s, s32[4]{0:T(128)S(1)} %pad_add_fusion.out_s, bf16[16,3072]{1,0:T(8,128)(2,1)S(1)} %copy-done, ...), custom_call_target="tpu_custom_call" | custom-call | flops 1207959552 | bytes 11010048 | tf_op jit(solution)/shard_map/block_product/pallas_call | solution.py:195
  46.9 0.2 multiply_convert_fusion.refs_0_
  47.2 1.4 %collective-permute-done.20 = bf16[2,32,3072]{2,1,0:T(8,128)(2,1)S(1)} collective-permute-done((bf16[2,32,3072]{2,1,0:T(8,128)(2,1)S(1)}, bf16[2,32,3072]{2,1,0:T(8,128)(2,1)S(1)}, u32[]{:S(2)}, u32[]{:S(2)}) %collective-permute-start.20) | collective-permute-done | bytes 393248 | tf_op jit(solution)/shard_map/ppermute | solution.py:313
  48.7 0.7 collective-permute-start.21
  49.3 5.6 %collective-permute-done.10.refs_2_ = bf16[32,3072]{1,0:T(8,128)(2,1)S(1)} collective-permute-done((bf16[32,3072]{1,0:T(8,128)(2,1)S(1)}, bf16[32,3072]{1,0:T(8,128)(2,1)S(1)}, u32[]{:S(2)}, u32[]{:S(2)}) %collective-permute-start.10) | collective-permute-done | bytes 196640 | tf_op jit(solution)/shard_map/ppermute | solution.py:318
  55.0 3.7 %collective-permute-done.21 = bf16[32,3072]{1,0:T(8,128)(2,1)S(1)} collective-permute-done((bf16[32,3072]{1,0:T(8,128)(2,1)S(1)}, bf16[32,3072]{1,0:T(8,128)(2,1)S(1)}, u32[]{:S(2)}, u32[]{:S(2)}) %collective-permute-start.21) | collective-permute-done | bytes 196640 | tf_op jit(solution)/shard_map/ppermute | solution.py:318
  58.7 0.4 fusion.6.refs_0_.refs_8_
  59.1 0.4 collective-permute-start.23
  59.4 5.1 %block_product.5 = (bf16[4,16,3072]{2,1,0:T(8,128)(2,1)S(1)}, bf16[4,16,3072]{2,1,0:T(8,128)(2,1)S(1)}, bf16[288,128,128]{2,1,0:T(8,128)(2,1)S(1)}) custom-call(s32[4,256]{1,0:T(4,128)S(1)} %get-tuple-element.46.table_s, s32[4]{0:T(128)S(1)} %fusion.26.in_s.left_s.right_s, s32[1]{0:T(128)} %constant.68.clone.1.in_s.out_s.right_s.left_s, ...), custom_call_target="tpu_custom_call" | custom-call | flops 1207959552 | bytes 11010048 | tf_op jit(solution)/shard_map/block_product/pallas_call | solution.py:195
  64.7 0.9 collective-permute-done.23.refs_2_.refs_10_
  65.6 8.8 %block_grads.2 = f32[288,128,128]{2,1,0:T(8,128)} custom-call(s32[1,1,288]{2,1,0:T(1,128)S(1)} %copy-done.2, s32[4]{0:T(128)S(1)} %fusion.26.in_s.left_s.right_s, s32[1]{0:T(128)} %constant.68.clone.1.in_s.out_s.right_s.left_s, bf16[32,3072]{1,0:T(8,128)(2,1)S(1)} %multiply_convert_fusion.refs_0_, bf16[32,3072]{1,0:T(8,128)(2,1)S(1)} %collective-permute-done.9.refs_1_, ...), custom_call_target="tpu_custom_call" | custom-call | flops 1207959552 | bytes 20447232 | tf_op jit(solution)/shard_map/block_grads/pallas_call | solution.py:266
  74.4 4.7 %block_product.7 = (bf16[4,16,3072]{2,1,0:T(8,128)(2,1)S(1)}, bf16[4,16,3072]{2,1,0:T(8,128)(2,1)S(1)}) custom-call(s32[4,256]{1,0:T(4,128)S(1)} %get-tuple-element.54.table_s, s32[4]{0:T(128)S(1)} %fusion.26.in_s.left_s.right_s, s32[1]{0:T(128)} %constant.68.clone.1.in_s.out_s.right_s.left_s, bf16[32,3072]{1,0:T(8,128)(2,1)S(1)} %fusion.6.refs_0_.refs_8_, ...), custom_call_target="tpu_custom_call" | custom-call | flops 1207959552 | bytes 11010048 | tf_op jit(solution)/shard_map/block_product/pallas_call | solution.py:195
  79.2 2.0 %collective-permute-start.27 = (bf16[16,3072]{1,0:T(8,128)(2,1)S(1)}, bf16[16,3072]{1,0:T(8,128)(2,1)S(1)}, u32[]{:S(2)}, u32[]{:S(2)}) collective-permute-start(bf16[16,3072]{1,0:T(8,128)(2,1)S(1)} %get-tuple-element.88), channel_id=1, source_target_pairs={{0,2},{1,3},{2,4},{3,5},{4,6},{5,7},{6,0},{7,1},{8,10},{9,11},{10,... | collective-permute-start | bytes 294920 | tf_op jit(solution)/shard_map/ppermute | solution.py:318
  81.2 5.3 %collective-permute-start.26 = (bf16[16,3072]{1,0:T(8,128)(2,1)S(1)}, bf16[16,3072]{1,0:T(8,128)(2,1)S(1)}, u32[]{:S(2)}, u32[]{:S(2)}) collective-permute-start(bf16[16,3072]{1,0:T(8,128)(2,1)S(1)} %get-tuple-element.89), channel_id=1, source_target_pairs={{0,4},{1,5},{2,6},{3,7},{4,0},{5,1},{6,2},{7,3},{8,12},{9,13},{10,... | collective-permute-start | bytes 294920 | tf_op jit(solution)/shard_map/ppermute | solution.py:318
  86.5 0.5 collective-permute-done.25
  87.0 0.8 collective-permute-done.27
  87.8 2.4 %collective-permute-done.26 = bf16[16,3072]{1,0:T(8,128)(2,1)S(1)} collective-permute-done((bf16[16,3072]{1,0:T(8,128)(2,1)S(1)}, bf16[16,3072]{1,0:T(8,128)(2,1)S(1)}, u32[]{:S(2)}, u32[]{:S(2)}) %collective-permute-start.26) | collective-permute-done | bytes 98336 | tf_op jit(solution)/shard_map/ppermute | solution.py:318
  90.2 0.7 fusion.14
  90.9 3.3 %collective-permute-done.28 = bf16[4,16,3072]{2,1,0:T(8,128)(2,1)S(1)} collective-permute-done((bf16[4,16,3072]{2,1,0:T(8,128)(2,1)S(1)}, bf16[4,16,3072]{2,1,0:T(8,128)(2,1)S(1)}, u32[]{:S(2)}, u32[]{:S(2)}) %collective-permute-start.28) | collective-permute-done | bytes 393248 | tf_op jit(solution)/shard_map/ppermute | solution.py:313
  94.4 2.0 %collective-permute-start.31 = (bf16[16,3072]{1,0:T(8,128)(2,1)S(1)}, bf16[16,3072]{1,0:T(8,128)(2,1)S(1)}, u32[]{:S(2)}, u32[]{:S(2)}) collective-permute-start(bf16[16,3072]{1,0:T(8,128)(2,1)S(1)} %get-tuple-element.85), channel_id=1, source_target_pairs={{0,2},{1,3},{2,4},{3,5},{4,6},{5,7},{6,0},{7,1},{8,10},{9,11},{10,... | collective-permute-start | bytes 294920 | tf_op jit(solution)/shard_map/ppermute | solution.py:318
  96.4 2.8 %collective-permute-start.30 = (bf16[16,3072]{1,0:T(8,128)(2,1)S(1)}, bf16[16,3072]{1,0:T(8,128)(2,1)S(1)}, u32[]{:S(2)}, u32[]{:S(2)}) collective-permute-start(bf16[16,3072]{1,0:T(8,128)(2,1)S(1)} %get-tuple-element.86), channel_id=1, source_target_pairs={{0,4},{1,5},{2,6},{3,7},{4,0},{5,1},{6,2},{7,3},{8,12},{9,13},{10,... | collective-permute-start | bytes 294920 | tf_op jit(solution)/shard_map/ppermute | solution.py:318
  99.2 8.7 %block_grads.3 = f32[288,128,128]{2,1,0:T(8,128)} custom-call(s32[1,1,288]{2,1,0:T(1,128)S(1)} %copy-done.3, s32[1]{0:T(128)} %constant.68.clone.1.in_s.out_s.right_s.left_s, s32[4]{0:T(128)S(1)} %fusion.26.in_s.left_s.right_s, bf16[16,3072]{1,0:T(8,128)(2,1)S(1)} %copy-done.1, bf16[16,3072]{1,0:T(8,128)(2,1)S(1)} %collective-permute-done.3.refs_1_, ...), custom_call_target="tpu_custom_call" | custom-call | flops 1207959552 | bytes 20447232 | tf_op jit(solution)/shard_map/block_grads/pallas_call | solution.py:266
  107.9 0.7 fusion.11
  (43 shorter events, 0.9 us)
Async XLA Ops:
  0.6 17.8 %copy-start.1 = (bf16[16,3072]{1,0:T(8,128)(2,1)S(1)}, bf16[16,3072]{1,0:T(8,128)(2,1)}, u32[]{:S(2)}) copy-start(bf16[16,3072]{1,0:T(8,128)(2,1)} %refs_0_.5) | copy-start | bytes 294916
  0.6 17.3 %collective-permute-start.3 = (bf16[16,3072]{1,0:T(8,128)(2,1)}, bf16[16,3072]{1,0:T(8,128)(2,1)S(1)}, u32[]{:S(2)}, u32[]{:S(2)}) collective-permute-start(bf16[16,3072]{1,0:T(8,128)(2,1)} %refs_0_.5), channel_id=1, source_target_pairs={{0,1},{1,0},{2,3},{3,2},{4,5},{5,4},{6,7},{7,6},{8,9},{9,8},{10,11... | collective-permute-start | bytes 294920 | tf_op jit(solution)/shard_map/ppermute | solution.py:313
  2.2 5.7 %collective-permute-start.2 = (bf16[16,3072]{1,0:T(8,128)(2,1)}, bf16[16,3072]{1,0:T(8,128)(2,1)S(1)}, u32[]{:S(2)}, u32[]{:S(2)}) collective-permute-start(bf16[16,3072]{1,0:T(8,128)(2,1)} %refs_0_.5), channel_id=1, source_target_pairs={{0,6},{1,7},{2,0},{3,1},{4,2},{5,3},{6,4},{7,5},{8,14},{9,15},{10,... | collective-permute-start | bytes 294920 | tf_op jit(solution)/shard_map/ppermute | solution.py:318
  2.6 9.4 %collective-permute-start.1 = (bf16[16,3072]{1,0:T(8,128)(2,1)}, bf16[16,3072]{1,0:T(8,128)(2,1)S(1)}, u32[]{:S(2)}, u32[]{:S(2)}) collective-permute-start(bf16[16,3072]{1,0:T(8,128)(2,1)} %refs_0_.5), channel_id=1, source_target_pairs={{0,4},{1,5},{2,6},{3,7},{4,0},{5,1},{6,2},{7,3},{8,12},{9,13},{10,... | collective-permute-start | bytes 294920 | tf_op jit(solution)/shard_map/ppermute | solution.py:318
  5.2 8.1 %collective-permute-start = (bf16[16,3072]{1,0:T(8,128)(2,1)}, bf16[16,3072]{1,0:T(8,128)(2,1)S(1)}, u32[]{:S(2)}, u32[]{:S(2)}) collective-permute-start(bf16[16,3072]{1,0:T(8,128)(2,1)} %refs_0_.5), channel_id=1, source_target_pairs={{0,2},{1,3},{2,4},{3,5},{4,6},{5,7},{6,0},{7,1},{8,10},{9,11},{10,... | collective-permute-start | bytes 294920 | tf_op jit(solution)/shard_map/ppermute | solution.py:318
  7.9 10.1 %collective-permute-start.6 = (bf16[16,3072]{1,0:T(8,128)(2,1)S(1)}, bf16[16,3072]{1,0:T(8,128)(2,1)S(1)}, u32[]{:S(2)}, u32[]{:S(2)}) collective-permute-start(bf16[16,3072]{1,0:T(8,128)(2,1)S(1)} %collective-permute-done.2.refs_6_), channel_id=1, source_target_pairs={{0,1},{1,0},{2,3},{3,2},{4,5},{5,4},{6,7},{7,6},{8,9},{9,8},{10,11... | collective-permute-start | bytes 294920 | tf_op jit(solution)/shard_map/ppermute | solution.py:313
  12.1 5.9 %collective-permute-start.5 = (bf16[16,3072]{1,0:T(8,128)(2,1)S(1)}, bf16[16,3072]{1,0:T(8,128)(2,1)S(1)}, u32[]{:S(2)}, u32[]{:S(2)}) collective-permute-start(bf16[16,3072]{1,0:T(8,128)(2,1)S(1)} %collective-permute-done.1.refs_4_), channel_id=1, source_target_pairs={{0,1},{1,0},{2,3},{3,2},{4,5},{5,4},{6,7},{7,6},{8,9},{9,8},{10,11... | collective-permute-start | bytes 294920 | tf_op jit(solution)/shard_map/ppermute | solution.py:313
  13.4 5.0 %collective-permute-start.4 = (bf16[16,3072]{1,0:T(8,128)(2,1)S(1)}, bf16[16,3072]{1,0:T(8,128)(2,1)S(1)}, u32[]{:S(2)}, u32[]{:S(2)}) collective-permute-start(bf16[16,3072]{1,0:T(8,128)(2,1)S(1)} %collective-permute-done.refs_2_), channel_id=1, source_target_pairs={{0,1},{1,0},{2,3},{3,2},{4,5},{5,4},{6,7},{7,6},{8,9},{9,8},{10,11... | collective-permute-start | bytes 294920 | tf_op jit(solution)/shard_map/ppermute | solution.py:313
  18.4 4.4 %copy-start = (bf16[16,3072]{1,0:T(8,128)(2,1)S(1)}, bf16[16,3072]{1,0:T(8,128)(2,1)}, u32[]{:S(2)}) copy-start(bf16[16,3072]{1,0:T(8,128)(2,1)} %refs_4_.1) | copy-start | bytes 294916
  22.7 13.8 %collective-permute-start.7 = (bf16[2,32,3072]{2,1,0:T(8,128)(2,1)S(1)}, bf16[2,32,3072]{2,1,0:T(8,128)(2,1)S(1)}, u32[]{:S(2)}, u32[]{:S(2)}) collective-permute-start(bf16[2,32,3072]{2,1,0:T(8,128)(2,1)S(1)} %get-tuple-element.50), channel_id=1, source_target_pairs={{0,8},{8,0},{16,24},{24,16},{1,9},{9,1},{17,25},{25,17},{2,10},{10... | collective-permute-start | bytes 1179656 | tf_op jit(solution)/shard_map/ppermute | solution.py:313
  22.8 7.2 %collective-permute-start.18 = (bf16[16,3072]{1,0:T(8,128)(2,1)S(1)}, bf16[16,3072]{1,0:T(8,128)(2,1)S(1)}, u32[]{:S(2)}, u32[]{:S(2)}) collective-permute-start(bf16[16,3072]{1,0:T(8,128)(2,1)S(1)} %copy-done), channel_id=1, source_target_pairs={{0,6},{1,7},{2,0},{3,1},{4,2},{5,3},{6,4},{7,5},{8,14},{9,15},{10,... | collective-permute-start | bytes 294920 | tf_op jit(solution)/shard_map/ppermute | solution.py:318
  25.5 9.0 %collective-permute-start.16 = (bf16[16,3072]{1,0:T(8,128)(2,1)S(1)}, bf16[16,3072]{1,0:T(8,128)(2,1)S(1)}, u32[]{:S(2)}, u32[]{:S(2)}) collective-permute-start(bf16[16,3072]{1,0:T(8,128)(2,1)S(1)} %copy-done), channel_id=1, source_target_pairs={{0,4},{1,5},{2,6},{3,7},{4,0},{5,1},{6,2},{7,3},{8,12},{9,13},{10,... | collective-permute-start | bytes 294920 | tf_op jit(solution)/shard_map/ppermute | solution.py:318
  27.1 8.9 %collective-permute-start.14 = (bf16[16,3072]{1,0:T(8,128)(2,1)S(1)}, bf16[16,3072]{1,0:T(8,128)(2,1)S(1)}, u32[]{:S(2)}, u32[]{:S(2)}) collective-permute-start(bf16[16,3072]{1,0:T(8,128)(2,1)S(1)} %copy-done), channel_id=1, source_target_pairs={{0,2},{1,3},{2,4},{3,5},{4,6},{5,7},{6,0},{7,1},{8,10},{9,11},{10,... | collective-permute-start | bytes 294920 | tf_op jit(solution)/shard_map/ppermute | solution.py:318
  30.0 8.0 %collective-permute-start.13 = (bf16[16,3072]{1,0:T(8,128)(2,1)S(1)}, bf16[16,3072]{1,0:T(8,128)(2,1)S(1)}, u32[]{:S(2)}, u32[]{:S(2)}) collective-permute-start(bf16[16,3072]{1,0:T(8,128)(2,1)S(1)} %copy-done), channel_id=1, source_target_pairs={{0,1},{1,0},{2,3},{3,2},{4,5},{5,4},{6,7},{7,6},{8,9},{9,8},{10,11... | collective-permute-start | bytes 294920 | tf_op jit(solution)/shard_map/ppermute | solution.py:313
  30.0 8.0 %collective-permute-start.19 = (bf16[16,3072]{1,0:T(8,128)(2,1)S(1)}, bf16[16,3072]{1,0:T(8,128)(2,1)S(1)}, u32[]{:S(2)}, u32[]{:S(2)}) collective-permute-start(bf16[16,3072]{1,0:T(8,128)(2,1)S(1)} %collective-permute-done.18.refs_6_.refs_10_), channel_id=1, source_target_pairs={{0,1},{1,0},{2,3},{3,2},{4,5},{5,4},{6,7},{7,6},{8,9},{9,8},{10,11... | collective-permute-start | bytes 294920 | tf_op jit(solution)/shard_map/ppermute | solution.py:313
  34.5 5.6 %collective-permute-start.17 = (bf16[16,3072]{1,0:T(8,128)(2,1)S(1)}, bf16[16,3072]{1,0:T(8,128)(2,1)S(1)}, u32[]{:S(2)}, u32[]{:S(2)}) collective-permute-start(bf16[16,3072]{1,0:T(8,128)(2,1)S(1)} %collective-permute-done.16.refs_4_.refs_8_), channel_id=1, source_target_pairs={{0,1},{1,0},{2,3},{3,2},{4,5},{5,4},{6,7},{7,6},{8,9},{9,8},{10,11... | collective-permute-start | bytes 294920 | tf_op jit(solution)/shard_map/ppermute | solution.py:313
  36.0 5.2 %collective-permute-start.15 = (bf16[16,3072]{1,0:T(8,128)(2,1)S(1)}, bf16[16,3072]{1,0:T(8,128)(2,1)S(1)}, u32[]{:S(2)}, u32[]{:S(2)}) collective-permute-start(bf16[16,3072]{1,0:T(8,128)(2,1)S(1)} %collective-permute-done.14.refs_2_.refs_6_), channel_id=1, source_target_pairs={{0,1},{1,0},{2,3},{3,2},{4,5},{5,4},{6,7},{7,6},{8,9},{9,8},{10,11... | collective-permute-start | bytes 294920 | tf_op jit(solution)/shard_map/ppermute | solution.py:313
  36.6 10.3 %collective-permute-start.8 = (bf16[32,3072]{1,0:T(8,128)(2,1)S(1)}, bf16[32,3072]{1,0:T(8,128)(2,1)S(1)}, u32[]{:S(2)}, u32[]{:S(2)}) collective-permute-start(bf16[32,3072]{1,0:T(8,128)(2,1)S(1)} %fusion.7), channel_id=1, source_target_pairs={{0,16},{8,24},{16,0},{24,8},{1,17},{9,25},{17,1},{25,9},{2,18},{10... | collective-permute-start | bytes 589832 | tf_op jit(solution)/shard_map/ppermute | solution.py:318
  46.8 1.8 %collective-permute-start.20 = (bf16[2,32,3072]{2,1,0:T(8,128)(2,1)S(1)}, bf16[2,32,3072]{2,1,0:T(8,128)(2,1)S(1)}, u32[]{:S(2)}, u32[]{:S(2)}) collective-permute-start(bf16[2,32,3072]{2,1,0:T(8,128)(2,1)S(1)} %get-tuple-element.65), channel_id=1, source_target_pairs={{0,8},{8,0},{16,24},{24,16},{1,9},{9,1},{17,25},{25,17},{2,10},{10... | collective-permute-start | bytes 1179656 | tf_op jit(solution)/shard_map/ppermute | solution.py:313
  47.1 7.8 %collective-permute-start.10 = (bf16[32,3072]{1,0:T(8,128)(2,1)S(1)}, bf16[32,3072]{1,0:T(8,128)(2,1)S(1)}, u32[]{:S(2)}, u32[]{:S(2)}) collective-permute-start(bf16[32,3072]{1,0:T(8,128)(2,1)S(1)} %multiply_convert_fusion.refs_0_), channel_id=1, source_target_pairs={{0,16},{8,24},{16,0},{24,8},{1,17},{9,25},{17,1},{25,9},{2,18},{10... | collective-permute-start | bytes 589832 | tf_op jit(solution)/shard_map/ppermute | solution.py:318
  48.7 10.0 %collective-permute-start.21 = (bf16[32,3072]{1,0:T(8,128)(2,1)S(1)}, bf16[32,3072]{1,0:T(8,128)(2,1)S(1)}, u32[]{:S(2)}, u32[]{:S(2)}) collective-permute-start(bf16[32,3072]{1,0:T(8,128)(2,1)S(1)} %fusion.8), channel_id=1, source_target_pairs={{0,16},{8,24},{16,0},{24,8},{1,17},{9,25},{17,1},{25,9},{2,18},{10... | collective-permute-start | bytes 589832 | tf_op jit(solution)/shard_map/ppermute | solution.py:318
  49.3 10.1 %collective-permute-start.9 = (bf16[32,3072]{1,0:T(8,128)(2,1)S(1)}, bf16[32,3072]{1,0:T(8,128)(2,1)S(1)}, u32[]{:S(2)}, u32[]{:S(2)}) collective-permute-start(bf16[32,3072]{1,0:T(8,128)(2,1)S(1)} %multiply_convert_fusion.refs_0_), channel_id=1, source_target_pairs={{0,8},{8,0},{16,24},{24,16},{1,9},{9,1},{17,25},{25,17},{2,10},{10... | collective-permute-start | bytes 589832 | tf_op jit(solution)/shard_map/ppermute | solution.py:313
  55.0 4.5 %collective-permute-start.11 = (bf16[32,3072]{1,0:T(8,128)(2,1)S(1)}, bf16[32,3072]{1,0:T(8,128)(2,1)S(1)}, u32[]{:S(2)}, u32[]{:S(2)}) collective-permute-start(bf16[32,3072]{1,0:T(8,128)(2,1)S(1)} %collective-permute-done.10.refs_2_), channel_id=1, source_target_pairs={{0,8},{8,0},{16,24},{24,16},{1,9},{9,1},{17,25},{25,17},{2,10},{10... | collective-permute-start | bytes 589832 | tf_op jit(solution)/shard_map/ppermute | solution.py:313
  59.1 6.5 %collective-permute-start.23 = (bf16[32,3072]{1,0:T(8,128)(2,1)S(1)}, bf16[32,3072]{1,0:T(8,128)(2,1)S(1)}, u32[]{:S(2)}, u32[]{:S(2)}) collective-permute-start(bf16[32,3072]{1,0:T(8,128)(2,1)S(1)} %fusion.6.refs_0_.refs_8_), channel_id=1, source_target_pairs={{0,16},{8,24},{16,0},{24,8},{1,17},{9,25},{17,1},{25,9},{2,18},{10... | collective-permute-start | bytes 589832 | tf_op jit(solution)/shard_map/ppermute | solution.py:318
  59.4 6.1 %copy-start.2 = (s32[1,1,288]{2,1,0:T(1,128)S(1)}, s32[1,1,288]{2,1,0:T(1,128)}, u32[]{:S(2)}) copy-start(s32[1,1,288]{2,1,0:T(1,128)} %slot_s.2) | copy-start | bytes 3460
  64.5 14.5 %collective-permute-start.12 = (bf16[4,16,3072]{2,1,0:T(8,128)(2,1)S(1)}, bf16[4,16,3072]{2,1,0:T(8,128)(2,1)S(1)}, u32[]{:S(2)}, u32[]{:S(2)}) collective-permute-start(bf16[4,16,3072]{2,1,0:T(8,128)(2,1)S(1)} %get-tuple-element.53), channel_id=1, source_target_pairs={{0,1},{1,0},{2,3},{3,2},{4,5},{5,4},{6,7},{7,6},{8,9},{9,8},{10,11... | collective-permute-start | bytes 1179656 | tf_op jit(solution)/shard_map/ppermute | solution.py:313
  64.6 9.8 %collective-permute-start.22 = (bf16[32,3072]{1,0:T(8,128)(2,1)S(1)}, bf16[32,3072]{1,0:T(8,128)(2,1)S(1)}, u32[]{:S(2)}, u32[]{:S(2)}) collective-permute-start(bf16[32,3072]{1,0:T(8,128)(2,1)S(1)} %fusion.6.refs_0_.refs_8_), channel_id=1, source_target_pairs={{0,8},{8,0},{16,24},{24,16},{1,9},{9,1},{17,25},{25,17},{2,10},{10... | collective-permute-start | bytes 589832 | tf_op jit(solution)/shard_map/ppermute | solution.py:313
  65.6 8.8 %collective-permute-start.24 = (bf16[32,3072]{1,0:T(8,128)(2,1)S(1)}, bf16[32,3072]{1,0:T(8,128)(2,1)S(1)}, u32[]{:S(2)}, u32[]{:S(2)}) collective-permute-start(bf16[32,3072]{1,0:T(8,128)(2,1)S(1)} %collective-permute-done.23.refs_2_.refs_10_), channel_id=1, source_target_pairs={{0,8},{8,0},{16,24},{24,16},{1,9},{9,1},{17,25},{25,17},{2,10},{10... | collective-permute-start | bytes 589832 | tf_op jit(solution)/shard_map/ppermute | solution.py:313
  74.4 24.9 %copy-start.3 = (s32[1,1,288]{2,1,0:T(1,128)S(1)}, s32[1,1,288]{2,1,0:T(1,128)}, u32[]{:S(2)}) copy-start(s32[1,1,288]{2,1,0:T(1,128)} %slot_s.3) | copy-start | bytes 3460
  79.1 7.8 %collective-permute-start.25 = (bf16[16,3072]{1,0:T(8,128)(2,1)S(1)}, bf16[16,3072]{1,0:T(8,128)(2,1)S(1)}, u32[]{:S(2)}, u32[]{:S(2)}) collective-permute-start(bf16[16,3072]{1,0:T(8,128)(2,1)S(1)} %get-tuple-element.87), channel_id=1, source_target_pairs={{0,6},{1,7},{2,0},{3,1},{4,2},{5,3},{6,4},{7,5},{8,14},{9,15},{10,... | collective-permute-start | bytes 294920 | tf_op jit(solution)/shard_map/ppermute | solution.py:318
  79.2 8.6 %collective-permute-start.27 = (bf16[16,3072]{1,0:T(8,128)(2,1)S(1)}, bf16[16,3072]{1,0:T(8,128)(2,1)S(1)}, u32[]{:S(2)}, u32[]{:S(2)}) collective-permute-start(bf16[16,3072]{1,0:T(8,128)(2,1)S(1)} %get-tuple-element.88), channel_id=1, source_target_pairs={{0,2},{1,3},{2,4},{3,5},{4,6},{5,7},{6,0},{7,1},{8,10},{9,11},{10,... | collective-permute-start | bytes 294920 | tf_op jit(solution)/shard_map/ppermute | solution.py:318
  81.2 9.0 %collective-permute-start.26 = (bf16[16,3072]{1,0:T(8,128)(2,1)S(1)}, bf16[16,3072]{1,0:T(8,128)(2,1)S(1)}, u32[]{:S(2)}, u32[]{:S(2)}) collective-permute-start(bf16[16,3072]{1,0:T(8,128)(2,1)S(1)} %get-tuple-element.89), channel_id=1, source_target_pairs={{0,4},{1,5},{2,6},{3,7},{4,0},{5,1},{6,2},{7,3},{8,12},{9,13},{10,... | collective-permute-start | bytes 294920 | tf_op jit(solution)/shard_map/ppermute | solution.py:318
  86.5 7.8 %collective-permute-start.28 = (bf16[4,16,3072]{2,1,0:T(8,128)(2,1)S(1)}, bf16[4,16,3072]{2,1,0:T(8,128)(2,1)S(1)}, u32[]{:S(2)}, u32[]{:S(2)}) collective-permute-start(bf16[4,16,3072]{2,1,0:T(8,128)(2,1)S(1)} %get-tuple-element.78), channel_id=1, source_target_pairs={{0,1},{1,0},{2,3},{3,2},{4,5},{5,4},{6,7},{7,6},{8,9},{9,8},{10,11... | collective-permute-start | bytes 1179656 | tf_op jit(solution)/shard_map/ppermute | solution.py:313
  94.3 13.6 %collective-permute-start.29 = (bf16[16,3072]{1,0:T(8,128)(2,1)S(1)}, bf16[16,3072]{1,0:T(8,128)(2,1)S(1)}, u32[]{:S(2)}, u32[]{:S(2)}) collective-permute-start(bf16[16,3072]{1,0:T(8,128)(2,1)S(1)} %get-tuple-element.84), channel_id=1, source_target_pairs={{0,6},{1,7},{2,0},{3,1},{4,2},{5,3},{6,4},{7,5},{8,14},{9,15},{10,... | collective-permute-start | bytes 294920 | tf_op jit(solution)/shard_map/ppermute | solution.py:318
  94.4 13.5 %collective-permute-start.31 = (bf16[16,3072]{1,0:T(8,128)(2,1)S(1)}, bf16[16,3072]{1,0:T(8,128)(2,1)S(1)}, u32[]{:S(2)}, u32[]{:S(2)}) collective-permute-start(bf16[16,3072]{1,0:T(8,128)(2,1)S(1)} %get-tuple-element.85), channel_id=1, source_target_pairs={{0,2},{1,3},{2,4},{3,5},{4,6},{5,7},{6,0},{7,1},{8,10},{9,11},{10,... | collective-permute-start | bytes 294920 | tf_op jit(solution)/shard_map/ppermute | solution.py:318
  96.4 11.5 %collective-permute-start.30 = (bf16[16,3072]{1,0:T(8,128)(2,1)S(1)}, bf16[16,3072]{1,0:T(8,128)(2,1)S(1)}, u32[]{:S(2)}, u32[]{:S(2)}) collective-permute-start(bf16[16,3072]{1,0:T(8,128)(2,1)S(1)} %get-tuple-element.86), channel_id=1, source_target_pairs={{0,4},{1,5},{2,6},{3,7},{4,0},{5,1},{6,2},{7,3},{8,12},{9,13},{10,... | collective-permute-start | bytes 294920 | tf_op jit(solution)/shard_map/ppermute | solution.py:318

commit v9 on v8

--- a/solution.py
+++ b/solution.py
@@ -398,12 +398,12 @@
     act_far = spread_far(own_act)
     grad_act = total_hidden(own_g, pairs_g, own_act)
     own_gh = (grad_act * gelu_slope(hidden)).astype(jnp.bfloat16)
-    activated = spread_near(act_far)
+    activated = spread_near([act_far[0]] + after(act_far[1:], own_gh))
     gh_far = spread_far(own_gh)
     grad_hidden = spread_near(gh_far)
 
     keep_o, send_o, w_in_near = block_product(
-        activated,
+        after(activated, own_gh),
         seq_part,
         w_out_near,
         out_by_col,
@@ -414,12 +414,18 @@
         [w_in],
     )
     got_o = near_move(send_o, "tensor", tensor_count)
-    grad_out = block_grads(after(activated, keep_o), seq_part, cot, None, slots_out)
     keep_t, send_t = block_product(
-        after(grad_hidden, grad_out), seq_part, w_in_near, in_by_row, feat_blocks, token_lengths, token_rows, True
+        after(grad_hidden, keep_o), seq_part, w_in_near, in_by_row, feat_blocks, token_lengths, token_rows, True
     )
     got_t = near_move(send_t, "tensor", tensor_count)
-    own_o, pairs_o = pair_out(keep_o, after(got_o, keep_t))
+    parts = 1
+    act_t = after(activated, keep_t)
+    grad_out = block_grads(act_t, seq_part, cot, None, slots_out, 0, parts)
+    own_o, pairs_o = pair_out(keep_o, after(got_o, grad_out))
+    for part in range(1, parts):
+        grad_out = block_grads(
+            after(act_t, pairs_o), seq_part, cot, None, slots_out, part, parts, grad_out
+        )
     own_t, pairs_t = pair_out(keep_t, after(got_t, pairs_o))
     grad_in = block_grads(tok, None, after(grad_hidden, pairs_t), seq_part, slots_in)
     output = total_out(own_o, pairs_o)

time: 109 us -> 121 us (1.11)
  the two profiles are of different devices: /device:TPU:8 before, /device:TPU:0 now
where the time goes in v9:
time: 121 us; the launch traced here: 120 us
  waiting for transfers between devices  48.5 us (40%)
  Pallas kernels  35.3 us (29%)
  starting transfers between devices  33.3 us (28%)
  other arithmetic  2.33 us (2%)
    ppermute x16, waiting for transfers between devices, far_move(): return lax.ppermute(v, axis, pairs)  41.2 us
    ppermute x16, starting transfers between devices, far_move(): return lax.ppermute(v, axis, pairs)  22 us
    pallas_call x2, Pallas kernels, block_grads(): pl.pallas_call(body, grid_spec=pltpu.PrefetchScalarGridSpec(num_scalar_pr...  17.5 us
    pallas_call x4, Pallas kernels, block_product(): pl.pallas_call(body, in_specs=[smem] * 3 + [vmem] * (n_in + 1) + [pl.Bloc...  14 us
    ppermute x16, starting transfers between devices, near_move(): return lax.ppermute(v, axis, [(i, i ^ 1) for i in range(count)])  11.3 us
    ppermute x16, waiting for transfers between devices, near_move(): return lax.ppermute(v, axis, [(i, i ^ 1) for i in range(count)])  7.28 us
    pallas_call x1, Pallas kernels, pair_tables(): pl.pallas_call(body, in_specs=[pl.BlockSpec(memory_space=pltpu.HBM)] * (n...  3.79 us
  transfers between devices with their start and end apart: 32, of which 17 were waited for; matrix products, arithmetic and copies ran while one was open for 1% of the time, Pallas kernels for 23%

profile of v9, /device:TPU:0, one launch (start us, length us, event | category | flops | bytes accessed | tf_op | source)
XLA Modules:
  0.0 120.5 jit_solution(9276492879544616057)
XLA Ops:
  0.6 3.0 %collective-permute-start.3 = (bf16[16,3072]{1,0:T(8,128)(2,1)}, bf16[16,3072]{1,0:T(8,128)(2,1)S(1)}, u32[]{:S(2)}, u32[]{:S(2)}) collective-permute-start(bf16[16,3072]{1,0:T(8,128)(2,1)} %refs_0_.5), channel_id=1, source_target_pairs={{0,1},{1,0},{2,3},{3,2},{4,5},{5,4},{6,7},{7,6},{8,9},{9,8},{10,11... | collective-permute-start | bytes 294920 | tf_op jit(solution)/shard_map/ppermute | solution.py:313
  3.7 3.6 %collective-permute-start.2 = (bf16[16,3072]{1,0:T(8,128)(2,1)}, bf16[16,3072]{1,0:T(8,128)(2,1)S(1)}, u32[]{:S(2)}, u32[]{:S(2)}) collective-permute-start(bf16[16,3072]{1,0:T(8,128)(2,1)} %refs_0_.5), channel_id=1, source_target_pairs={{0,6},{1,7},{2,0},{3,1},{4,2},{5,3},{6,4},{7,5},{8,14},{9,15},{10,... | collective-permute-start | bytes 294920 | tf_op jit(solution)/shard_map/ppermute | solution.py:318
  7.3 1.0 collective-permute-start
  8.5 2.3 %collective-permute-done.2.refs_6_ = bf16[16,3072]{1,0:T(8,128)(2,1)S(1)} collective-permute-done((bf16[16,3072]{1,0:T(8,128)(2,1)}, bf16[16,3072]{1,0:T(8,128)(2,1)S(1)}, u32[]{:S(2)}, u32[]{:S(2)}) %collective-permute-start.2) | collective-permute-done | bytes 98336 | tf_op jit(solution)/shard_map/ppermute | solution.py:318
  10.8 0.5 collective-permute-start.6
  11.3 4.5 %collective-permute-done.1.refs_4_ = bf16[16,3072]{1,0:T(8,128)(2,1)S(1)} collective-permute-done((bf16[16,3072]{1,0:T(8,128)(2,1)}, bf16[16,3072]{1,0:T(8,128)(2,1)S(1)}, u32[]{:S(2)}, u32[]{:S(2)}) %collective-permute-start.1) | collective-permute-done | bytes 98336 | tf_op jit(solution)/shard_map/ppermute | solution.py:318
  15.8 0.5 collective-permute-start.5
  16.4 1.5 %collective-permute-start.4 = (bf16[16,3072]{1,0:T(8,128)(2,1)S(1)}, bf16[16,3072]{1,0:T(8,128)(2,1)S(1)}, u32[]{:S(2)}, u32[]{:S(2)}) collective-permute-start(bf16[16,3072]{1,0:T(8,128)(2,1)S(1)} %collective-permute-done.refs_2_), channel_id=1, source_target_pairs={{0,1},{1,0},{2,3},{3,2},{4,5},{5,4},{6,7},{7,6},{8,9},{9,8},{10,11... | collective-permute-start | bytes 294920 | tf_op jit(solution)/shard_map/ppermute | solution.py:313
  17.9 3.8 %pair_tables.1 = (s32[4,256]{1,0:T(4,128)S(1)}, s32[4,256]{1,0:T(4,128)S(1)}, s32[4,256]{1,0:T(4,128)S(1)}, s32[4,256]{1,0:T(4,128)S(1)}, bf16[288,128,128]{2,1,0:T(8,128)(2,1)S(1)}) custom-call(s32[1,1,288]{2,1,0:T(1,128)} %slot_s.3, s32[1,1,288]{2,1,0:T(1,128)} %slot_s.2, s32[1,1,288]{2,1,0:T(1,128)} %slot_s.2, s32[1,1,288]{2,1,0:T(1,128)} %slot_s.3, ...), custom_call_target="tpu_custom_call" | custom-call | tf_op jit(solution)/shard_map/pair_tables/pallas_call | solution.py:111
  21.8 0.3 collective-permute-done.4.refs_3_
  22.1 4.3 %block_product.4 = (bf16[2,32,3072]{2,1,0:T(8,128)(2,1)S(1)}, bf16[2,32,3072]{2,1,0:T(8,128)(2,1)S(1)}, bf16[288,128,128]{2,1,0:T(8,128)(2,1)S(1)}) custom-call(s32[4,256]{1,0:T(4,128)S(1)} %get-tuple-element.52.table_s, s32[1]{0:T(128)} %constant.68.clone.1.in_s.out_s.right_s.left_s, s32[4]{0:T(128)S(1)} %pad_add_fusion.out_s, ...), custom_call_target="tpu_custom_call" | custom-call | flops 1207959552 | bytes 11010048 | tf_op jit(solution)/shard_map/block_product/pallas_call | solution.py:195
  26.5 3.0 %collective-permute-start.16 = (bf16[16,3072]{1,0:T(8,128)(2,1)S(1)}, bf16[16,3072]{1,0:T(8,128)(2,1)S(1)}, u32[]{:S(2)}, u32[]{:S(2)}) collective-permute-start(bf16[16,3072]{1,0:T(8,128)(2,1)S(1)} %copy-done), channel_id=1, source_target_pairs={{0,6},{1,7},{2,0},{3,1},{4,2},{5,3},{6,4},{7,5},{8,14},{9,15},{10,... | collective-permute-start | bytes 294920 | tf_op jit(solution)/shard_map/ppermute | solution.py:318
  29.5 0.6 collective-permute-start.12
  30.2 1.8 %collective-permute-start.11 = (bf16[16,3072]{1,0:T(8,128)(2,1)S(1)}, bf16[16,3072]{1,0:T(8,128)(2,1)S(1)}, u32[]{:S(2)}, u32[]{:S(2)}) collective-permute-start(bf16[16,3072]{1,0:T(8,128)(2,1)S(1)} %copy-done), channel_id=1, source_target_pairs={{0,1},{1,0},{2,3},{3,2},{4,5},{5,4},{6,7},{7,6},{8,9},{9,8},{10,11... | collective-permute-start | bytes 294920 | tf_op jit(solution)/shard_map/ppermute | solution.py:313
  31.9 0.8 collective-permute-done.16.refs_6_.refs_10_
  32.8 6.5 %collective-permute-done.14.refs_4_.refs_8_ = bf16[16,3072]{1,0:T(8,128)(2,1)S(1)} collective-permute-done((bf16[16,3072]{1,0:T(8,128)(2,1)S(1)}, bf16[16,3072]{1,0:T(8,128)(2,1)S(1)}, u32[]{:S(2)}, u32[]{:S(2)}) %collective-permute-start.14) | collective-permute-done | bytes 98336 | tf_op jit(solution)/shard_map/ppermute | solution.py:318
  39.2 0.4 collective-permute-start.15
  39.6 1.6 %collective-permute-start.13 = (bf16[16,3072]{1,0:T(8,128)(2,1)S(1)}, bf16[16,3072]{1,0:T(8,128)(2,1)S(1)}, u32[]{:S(2)}, u32[]{:S(2)}) collective-permute-start(bf16[16,3072]{1,0:T(8,128)(2,1)S(1)} %collective-permute-done.12.refs_2_.refs_6_), channel_id=1, source_target_pairs={{0,1},{1,0},{2,3},{3,2},{4,5},{5,4},{6,7},{7,6},{8,9},{9,8},{10,11... | collective-permute-start | bytes 294920 | tf_op jit(solution)/shard_map/ppermute | solution.py:313
  41.3 3.6 %collective-permute-done.15.refs_5_.refs_9_ = bf16[16,3072]{1,0:T(8,128)(2,1)S(1)} collective-permute-done((bf16[16,3072]{1,0:T(8,128)(2,1)S(1)}, bf16[16,3072]{1,0:T(8,128)(2,1)S(1)}, u32[]{:S(2)}, u32[]{:S(2)}) %collective-permute-start.15) | collective-permute-done | bytes 98336 | tf_op jit(solution)/shard_map/ppermute | solution.py:313
  44.9 1.2 collective-permute-done.13.refs_3_.refs_7_
  46.1 3.3 %block_product.5 = (bf16[2,32,3072]{2,1,0:T(8,128)(2,1)S(1)}, bf16[2,32,3072]{2,1,0:T(8,128)(2,1)S(1)}) custom-call(s32[4,256]{1,0:T(4,128)S(1)} %get-tuple-element.56.table_s, s32[1]{0:T(128)} %constant.68.clone.1.in_s.out_s.right_s.left_s, s32[4]{0:T(128)S(1)} %pad_add_fusion.out_s, bf16[16,3072]{1,0:T(8,128)(2,1)S(1)} %copy-done, ...), custom_call_target="tpu_custom_call" | custom-call | flops 1207959552 | bytes 11010048 | tf_op jit(solution)/shard_map/block_product/pallas_call | solution.py:195
  49.5 7.2 %collective-permute-done.8 = bf16[32,3072]{1,0:T(8,128)(2,1)S(1)} collective-permute-done((bf16[32,3072]{1,0:T(8,128)(2,1)S(1)}, bf16[32,3072]{1,0:T(8,128)(2,1)S(1)}, u32[]{:S(2)}, u32[]{:S(2)}) %collective-permute-start.8) | collective-permute-done | bytes 196640 | tf_op jit(solution)/shard_map/ppermute | solution.py:318
  56.8 0.3 collective-permute-start.19
  57.1 0.2 multiply_convert_fusion.refs_0_
  57.3 1.8 %collective-permute-start.10 = (bf16[32,3072]{1,0:T(8,128)(2,1)S(1)}, bf16[32,3072]{1,0:T(8,128)(2,1)S(1)}, u32[]{:S(2)}, u32[]{:S(2)}) collective-permute-start(bf16[32,3072]{1,0:T(8,128)(2,1)S(1)} %multiply_convert_fusion.refs_0_), channel_id=1, source_target_pairs={{0,16},{8,24},{16,0},{24,8},{1,17},{9,25},{17,1},{25,9},{2,18},{10... | collective-permute-start | bytes 589832 | tf_op jit(solution)/shard_map/ppermute | solution.py:318
  59.1 5.5 %collective-permute-done.19 = bf16[32,3072]{1,0:T(8,128)(2,1)S(1)} collective-permute-done((bf16[32,3072]{1,0:T(8,128)(2,1)S(1)}, bf16[32,3072]{1,0:T(8,128)(2,1)S(1)}, u32[]{:S(2)}, u32[]{:S(2)}) %collective-permute-start.19) | collective-permute-done | bytes 196640 | tf_op jit(solution)/shard_map/ppermute | solution.py:318
  64.6 0.4 fusion.6.refs_0_.refs_8_
  65.0 2.4 %collective-permute-done.10.refs_2_ = bf16[32,3072]{1,0:T(8,128)(2,1)S(1)} collective-permute-done((bf16[32,3072]{1,0:T(8,128)(2,1)S(1)}, bf16[32,3072]{1,0:T(8,128)(2,1)S(1)}, u32[]{:S(2)}, u32[]{:S(2)}) %collective-permute-start.10) | collective-permute-done | bytes 196640 | tf_op jit(solution)/shard_map/ppermute | solution.py:318
  67.4 0.6 collective-permute-start.23
  68.0 0.2 collective-permute-start.22
  68.2 0.6 collective-permute-done.20.refs_3_
  68.9 5.9 %collective-permute-done.23.refs_2_.refs_10_ = bf16[32,3072]{1,0:T(8,128)(2,1)S(1)} collective-permute-done((bf16[32,3072]{1,0:T(8,128)(2,1)S(1)}, bf16[32,3072]{1,0:T(8,128)(2,1)S(1)}, u32[]{:S(2)}, u32[]{:S(2)}) %collective-permute-start.23) | collective-permute-done | bytes 196640 | tf_op jit(solution)/shard_map/ppermute | solution.py:318
  74.7 4.5 %block_product.6 = (bf16[4,16,3072]{2,1,0:T(8,128)(2,1)S(1)}, bf16[4,16,3072]{2,1,0:T(8,128)(2,1)S(1)}, bf16[288,128,128]{2,1,0:T(8,128)(2,1)S(1)}) custom-call(s32[4,256]{1,0:T(4,128)S(1)} %get-tuple-element.51.table_s, s32[4]{0:T(128)S(1)} %fusion.26.in_s.left_s.right_s, s32[1]{0:T(128)} %constant.68.clone.1.in_s.out_s.right_s.left_s, ...), custom_call_target="tpu_custom_call" | custom-call | flops 1207959552 | bytes 11010048 | tf_op jit(solution)/shard_map/block_product/pallas_call | solution.py:195
  79.4 1.9 %block_product.7 = (bf16[4,16,3072]{2,1,0:T(8,128)(2,1)S(1)}, bf16[4,16,3072]{2,1,0:T(8,128)(2,1)S(1)}) custom-call(s32[4,256]{1,0:T(4,128)S(1)} %get-tuple-element.76.table_s, s32[4]{0:T(128)S(1)} %fusion.26.in_s.left_s.right_s, s32[1]{0:T(128)} %constant.68.clone.1.in_s.out_s.right_s.left_s, bf16[32,3072]{1,0:T(8,128)(2,1)S(1)} %fusion.6.refs_0_.refs_8_, ...), custom_call_target="tpu_custom_call" | custom-call | flops 1207959552 | bytes 11010048 | tf_op jit(solution)/shard_map/block_product/pallas_call | solution.py:195
  81.3 8.8 %block_grads.2 = f32[288,128,128]{2,1,0:T(8,128)} custom-call(s32[1,1,288]{2,1,0:T(1,128)S(1)} %copy-done.2, s32[4]{0:T(128)S(1)} %fusion.26.in_s.left_s.right_s, s32[1]{0:T(128)} %constant.68.clone.1.in_s.out_s.right_s.left_s, bf16[32,3072]{1,0:T(8,128)(2,1)S(1)} %multiply_convert_fusion.refs_0_, bf16[32,3072]{1,0:T(8,128)(2,1)S(1)} %collective-permute-done.9.refs_1_, ...), custom_call_target="tpu_custom_call" | custom-call | flops 1207959552 | bytes 20447232 | tf_op jit(solution)/shard_map/block_grads/pallas_call | solution.py:266
  90.1 0.8 collective-permute-done.21
  90.9 6.3 %collective-permute-start.25 = (bf16[16,3072]{1,0:T(8,128)(2,1)S(1)}, bf16[16,3072]{1,0:T(8,128)(2,1)S(1)}, u32[]{:S(2)}, u32[]{:S(2)}) collective-permute-start(bf16[16,3072]{1,0:T(8,128)(2,1)S(1)} %get-tuple-element.97), channel_id=1, source_target_pairs={{0,6},{1,7},{2,0},{3,1},{4,2},{5,3},{6,4},{7,5},{8,14},{9,15},{10,... | collective-permute-start | bytes 294920 | tf_op jit(solution)/shard_map/ppermute | solution.py:318
  97.3 0.6 collective-permute-start.26
  97.9 1.4 %collective-permute-start.28 = (bf16[4,16,3072]{2,1,0:T(8,128)(2,1)S(1)}, bf16[4,16,3072]{2,1,0:T(8,128)(2,1)S(1)}, u32[]{:S(2)}, u32[]{:S(2)}) collective-permute-start(bf16[4,16,3072]{2,1,0:T(8,128)(2,1)S(1)} %get-tuple-element.88), channel_id=1, source_target_pairs={{0,1},{1,0},{2,3},{3,2},{4,5},{5,4},{6,7},{7,6},{8,9},{9,8},{10,11... | collective-permute-start | bytes 1179656 | tf_op jit(solution)/shard_map/ppermute | solution.py:313
  99.3 0.2 collective-permute-done.25
  99.5 4.3 %collective-permute-done.27 = bf16[16,3072]{1,0:T(8,128)(2,1)S(1)} collective-permute-done((bf16[16,3072]{1,0:T(8,128)(2,1)S(1)}, bf16[16,3072]{1,0:T(8,128)(2,1)S(1)}, u32[]{:S(2)}, u32[]{:S(2)}) %collective-permute-start.27) | collective-permute-done | bytes 98336 | tf_op jit(solution)/shard_map/ppermute | solution.py:318
  103.8 1.6 %collective-permute-done.26 = bf16[16,3072]{1,0:T(8,128)(2,1)S(1)} collective-permute-done((bf16[16,3072]{1,0:T(8,128)(2,1)S(1)}, bf16[16,3072]{1,0:T(8,128)(2,1)S(1)}, u32[]{:S(2)}, u32[]{:S(2)}) %collective-permute-start.26) | collective-permute-done | bytes 98336 | tf_op jit(solution)/shard_map/ppermute | solution.py:318
  105.4 0.7 fusion.14
  106.2 0.8 collective-permute-done.28
  107.0 2.7 %collective-permute-start.29 = (bf16[16,3072]{1,0:T(8,128)(2,1)S(1)}, bf16[16,3072]{1,0:T(8,128)(2,1)S(1)}, u32[]{:S(2)}, u32[]{:S(2)}) collective-permute-start(bf16[16,3072]{1,0:T(8,128)(2,1)S(1)} %get-tuple-element.94), channel_id=1, source_target_pairs={{0,6},{1,7},{2,0},{3,1},{4,2},{5,3},{6,4},{7,5},{8,14},{9,15},{10,... | collective-permute-start | bytes 294920 | tf_op jit(solution)/shard_map/ppermute | solution.py:318
  109.7 1.4 %collective-permute-start.30 = (bf16[16,3072]{1,0:T(8,128)(2,1)S(1)}, bf16[16,3072]{1,0:T(8,128)(2,1)S(1)}, u32[]{:S(2)}, u32[]{:S(2)}) collective-permute-start(bf16[16,3072]{1,0:T(8,128)(2,1)S(1)} %get-tuple-element.96), channel_id=1, source_target_pairs={{0,4},{1,5},{2,6},{3,7},{4,0},{5,1},{6,2},{7,3},{8,12},{9,13},{10,... | collective-permute-start | bytes 294920 | tf_op jit(solution)/shard_map/ppermute | solution.py:318
  111.0 8.7 %block_grads.3 = f32[288,128,128]{2,1,0:T(8,128)} custom-call(s32[1,1,288]{2,1,0:T(1,128)S(1)} %copy-done.3, s32[1]{0:T(128)} %constant.68.clone.1.in_s.out_s.right_s.left_s, s32[4]{0:T(128)S(1)} %fusion.26.in_s.left_s.right_s, bf16[16,3072]{1,0:T(8,128)(2,1)S(1)} %copy-done.1, bf16[16,3072]{1,0:T(8,128)(2,1)S(1)} %collective-permute-done.3.refs_1_, ...), custom_call_target="tpu_custom_call" | custom-call | flops 1207959552 | bytes 20447232 | tf_op jit(solution)/shard_map/block_grads/pallas_call | solution.py:266
  119.8 0.7 fusion.11
  (43 shorter events, 0.9 us)
Async XLA Ops:
  0.6 21.5 %copy-start.1 = (bf16[16,3072]{1,0:T(8,128)(2,1)S(1)}, bf16[16,3072]{1,0:T(8,128)(2,1)}, u32[]{:S(2)}) copy-start(bf16[16,3072]{1,0:T(8,128)(2,1)} %refs_0_.5) | copy-start | bytes 294916
  0.6 21.1 %collective-permute-start.3 = (bf16[16,3072]{1,0:T(8,128)(2,1)}, bf16[16,3072]{1,0:T(8,128)(2,1)S(1)}, u32[]{:S(2)}, u32[]{:S(2)}) collective-permute-start(bf16[16,3072]{1,0:T(8,128)(2,1)} %refs_0_.5), channel_id=1, source_target_pairs={{0,1},{1,0},{2,3},{3,2},{4,5},{5,4},{6,7},{7,6},{8,9},{9,8},{10,11... | collective-permute-start | bytes 294920 | tf_op jit(solution)/shard_map/ppermute | solution.py:313
  3.7 7.1 %collective-permute-start.2 = (bf16[16,3072]{1,0:T(8,128)(2,1)}, bf16[16,3072]{1,0:T(8,128)(2,1)S(1)}, u32[]{:S(2)}, u32[]{:S(2)}) collective-permute-start(bf16[16,3072]{1,0:T(8,128)(2,1)} %refs_0_.5), channel_id=1, source_target_pairs={{0,6},{1,7},{2,0},{3,1},{4,2},{5,3},{6,4},{7,5},{8,14},{9,15},{10,... | collective-permute-start | bytes 294920 | tf_op jit(solution)/shard_map/ppermute | solution.py:318
  7.3 8.6 %collective-permute-start.1 = (bf16[16,3072]{1,0:T(8,128)(2,1)}, bf16[16,3072]{1,0:T(8,128)(2,1)S(1)}, u32[]{:S(2)}, u32[]{:S(2)}) collective-permute-start(bf16[16,3072]{1,0:T(8,128)(2,1)} %refs_0_.5), channel_id=1, source_target_pairs={{0,4},{1,5},{2,6},{3,7},{4,0},{5,1},{6,2},{7,3},{8,12},{9,13},{10,... | collective-permute-start | bytes 294920 | tf_op jit(solution)/shard_map/ppermute | solution.py:318
  7.3 9.1 %collective-permute-start = (bf16[16,3072]{1,0:T(8,128)(2,1)}, bf16[16,3072]{1,0:T(8,128)(2,1)S(1)}, u32[]{:S(2)}, u32[]{:S(2)}) collective-permute-start(bf16[16,3072]{1,0:T(8,128)(2,1)} %refs_0_.5), channel_id=1, source_target_pairs={{0,2},{1,3},{2,4},{3,5},{4,6},{5,7},{6,0},{7,1},{8,10},{9,11},{10,... | collective-permute-start | bytes 294920 | tf_op jit(solution)/shard_map/ppermute | solution.py:318
  10.8 11.0 %collective-permute-start.6 = (bf16[16,3072]{1,0:T(8,128)(2,1)S(1)}, bf16[16,3072]{1,0:T(8,128)(2,1)S(1)}, u32[]{:S(2)}, u32[]{:S(2)}) collective-permute-start(bf16[16,3072]{1,0:T(8,128)(2,1)S(1)} %collective-permute-done.2.refs_6_), channel_id=1, source_target_pairs={{0,1},{1,0},{2,3},{3,2},{4,5},{5,4},{6,7},{7,6},{8,9},{9,8},{10,11... | collective-permute-start | bytes 294920 | tf_op jit(solution)/shard_map/ppermute | solution.py:313
  15.8 5.9 %collective-permute-start.5 = (bf16[16,3072]{1,0:T(8,128)(2,1)S(1)}, bf16[16,3072]{1,0:T(8,128)(2,1)S(1)}, u32[]{:S(2)}, u32[]{:S(2)}) collective-permute-start(bf16[16,3072]{1,0:T(8,128)(2,1)S(1)} %collective-permute-done.1.refs_4_), channel_id=1, source_target_pairs={{0,1},{1,0},{2,3},{3,2},{4,5},{5,4},{6,7},{7,6},{8,9},{9,8},{10,11... | collective-permute-start | bytes 294920 | tf_op jit(solution)/shard_map/ppermute | solution.py:313
  16.4 5.7 %collective-permute-start.4 = (bf16[16,3072]{1,0:T(8,128)(2,1)S(1)}, bf16[16,3072]{1,0:T(8,128)(2,1)S(1)}, u32[]{:S(2)}, u32[]{:S(2)}) collective-permute-start(bf16[16,3072]{1,0:T(8,128)(2,1)S(1)} %collective-permute-done.refs_2_), channel_id=1, source_target_pairs={{0,1},{1,0},{2,3},{3,2},{4,5},{5,4},{6,7},{7,6},{8,9},{9,8},{10,11... | collective-permute-start | bytes 294920 | tf_op jit(solution)/shard_map/ppermute | solution.py:313
  22.1 4.4 %copy-start = (bf16[16,3072]{1,0:T(8,128)(2,1)S(1)}, bf16[16,3072]{1,0:T(8,128)(2,1)}, u32[]{:S(2)}) copy-start(bf16[16,3072]{1,0:T(8,128)(2,1)} %refs_4_.1) | copy-start | bytes 294916
  26.4 14.9 %collective-permute-start.7 = (bf16[2,32,3072]{2,1,0:T(8,128)(2,1)S(1)}, bf16[2,32,3072]{2,1,0:T(8,128)(2,1)S(1)}, u32[]{:S(2)}, u32[]{:S(2)}) collective-permute-start(bf16[2,32,3072]{2,1,0:T(8,128)(2,1)S(1)} %get-tuple-element.55), channel_id=1, source_target_pairs={{0,8},{8,0},{16,24},{24,16},{1,9},{9,1},{17,25},{25,17},{2,10},{10... | collective-permute-start | bytes 1179656 | tf_op jit(solution)/shard_map/ppermute | solution.py:313
  26.5 6.3 %collective-permute-start.16 = (bf16[16,3072]{1,0:T(8,128)(2,1)S(1)}, bf16[16,3072]{1,0:T(8,128)(2,1)S(1)}, u32[]{:S(2)}, u32[]{:S(2)}) collective-permute-start(bf16[16,3072]{1,0:T(8,128)(2,1)S(1)} %copy-done), channel_id=1, source_target_pairs={{0,6},{1,7},{2,0},{3,1},{4,2},{5,3},{6,4},{7,5},{8,14},{9,15},{10,... | collective-permute-start | bytes 294920 | tf_op jit(solution)/shard_map/ppermute | solution.py:318
  29.5 9.7 %collective-permute-start.14 = (bf16[16,3072]{1,0:T(8,128)(2,1)S(1)}, bf16[16,3072]{1,0:T(8,128)(2,1)S(1)}, u32[]{:S(2)}, u32[]{:S(2)}) collective-permute-start(bf16[16,3072]{1,0:T(8,128)(2,1)S(1)} %copy-done), channel_id=1, source_target_pairs={{0,4},{1,5},{2,6},{3,7},{4,0},{5,1},{6,2},{7,3},{8,12},{9,13},{10,... | collective-permute-start | bytes 294920 | tf_op jit(solution)/shard_map/ppermute | solution.py:318
  29.5 10.1 %collective-permute-start.12 = (bf16[16,3072]{1,0:T(8,128)(2,1)S(1)}, bf16[16,3072]{1,0:T(8,128)(2,1)S(1)}, u32[]{:S(2)}, u32[]{:S(2)}) collective-permute-start(bf16[16,3072]{1,0:T(8,128)(2,1)S(1)} %copy-done), channel_id=1, source_target_pairs={{0,2},{1,3},{2,4},{3,5},{4,6},{5,7},{6,0},{7,1},{8,10},{9,11},{10,... | collective-permute-start | bytes 294920 | tf_op jit(solution)/shard_map/ppermute | solution.py:318
  30.2 11.2 %collective-permute-start.11 = (bf16[16,3072]{1,0:T(8,128)(2,1)S(1)}, bf16[16,3072]{1,0:T(8,128)(2,1)S(1)}, u32[]{:S(2)}, u32[]{:S(2)}) collective-permute-start(bf16[16,3072]{1,0:T(8,128)(2,1)S(1)} %copy-done), channel_id=1, source_target_pairs={{0,1},{1,0},{2,3},{3,2},{4,5},{5,4},{6,7},{7,6},{8,9},{9,8},{10,11... | collective-permute-start | bytes 294920 | tf_op jit(solution)/shard_map/ppermute | solution.py:313
  32.8 8.6 %collective-permute-start.17 = (bf16[16,3072]{1,0:T(8,128)(2,1)S(1)}, bf16[16,3072]{1,0:T(8,128)(2,1)S(1)}, u32[]{:S(2)}, u32[]{:S(2)}) collective-permute-start(bf16[16,3072]{1,0:T(8,128)(2,1)S(1)} %collective-permute-done.16.refs_6_.refs_10_), channel_id=1, source_target_pairs={{0,1},{1,0},{2,3},{3,2},{4,5},{5,4},{6,7},{7,6},{8,9},{9,8},{10,11... | collective-permute-start | bytes 294920 | tf_op jit(solution)/shard_map/ppermute | solution.py:313
  39.2 5.7 %collective-permute-start.15 = (bf16[16,3072]{1,0:T(8,128)(2,1)S(1)}, bf16[16,3072]{1,0:T(8,128)(2,1)S(1)}, u32[]{:S(2)}, u32[]{:S(2)}) collective-permute-start(bf16[16,3072]{1,0:T(8,128)(2,1)S(1)} %collective-permute-done.14.refs_4_.refs_8_), channel_id=1, source_target_pairs={{0,1},{1,0},{2,3},{3,2},{4,5},{5,4},{6,7},{7,6},{8,9},{9,8},{10,11... | collective-permute-start | bytes 294920 | tf_op jit(solution)/shard_map/ppermute | solution.py:313
  39.6 6.5 %collective-permute-start.13 = (bf16[16,3072]{1,0:T(8,128)(2,1)S(1)}, bf16[16,3072]{1,0:T(8,128)(2,1)S(1)}, u32[]{:S(2)}, u32[]{:S(2)}) collective-permute-start(bf16[16,3072]{1,0:T(8,128)(2,1)S(1)} %collective-permute-done.12.refs_2_.refs_6_), channel_id=1, source_target_pairs={{0,1},{1,0},{2,3},{3,2},{4,5},{5,4},{6,7},{7,6},{8,9},{9,8},{10,11... | collective-permute-start | bytes 294920 | tf_op jit(solution)/shard_map/ppermute | solution.py:313
  49.3 7.4 %collective-permute-start.18 = (bf16[2,32,3072]{2,1,0:T(8,128)(2,1)S(1)}, bf16[2,32,3072]{2,1,0:T(8,128)(2,1)S(1)}, u32[]{:S(2)}, u32[]{:S(2)}) collective-permute-start(bf16[2,32,3072]{2,1,0:T(8,128)(2,1)S(1)} %get-tuple-element.67), channel_id=1, source_target_pairs={{0,8},{8,0},{16,24},{24,16},{1,9},{9,1},{17,25},{25,17},{2,10},{10... | collective-permute-start | bytes 1179656 | tf_op jit(solution)/shard_map/ppermute | solution.py:313
  49.5 7.2 %collective-permute-start.8 = (bf16[32,3072]{1,0:T(8,128)(2,1)S(1)}, bf16[32,3072]{1,0:T(8,128)(2,1)S(1)}, u32[]{:S(2)}, u32[]{:S(2)}) collective-permute-start(bf16[32,3072]{1,0:T(8,128)(2,1)S(1)} %fusion.7), channel_id=1, source_target_pairs={{0,16},{8,24},{16,0},{24,8},{1,17},{9,25},{17,1},{25,9},{2,18},{10... | collective-permute-start | bytes 589832 | tf_op jit(solution)/shard_map/ppermute | solution.py:318
  56.8 7.8 %collective-permute-start.19 = (bf16[32,3072]{1,0:T(8,128)(2,1)S(1)}, bf16[32,3072]{1,0:T(8,128)(2,1)S(1)}, u32[]{:S(2)}, u32[]{:S(2)}) collective-permute-start(bf16[32,3072]{1,0:T(8,128)(2,1)S(1)} %fusion.8), channel_id=1, source_target_pairs={{0,16},{8,24},{16,0},{24,8},{1,17},{9,25},{17,1},{25,9},{2,18},{10... | collective-permute-start | bytes 589832 | tf_op jit(solution)/shard_map/ppermute | solution.py:318
  57.3 10.1 %collective-permute-start.10 = (bf16[32,3072]{1,0:T(8,128)(2,1)S(1)}, bf16[32,3072]{1,0:T(8,128)(2,1)S(1)}, u32[]{:S(2)}, u32[]{:S(2)}) collective-permute-start(bf16[32,3072]{1,0:T(8,128)(2,1)S(1)} %multiply_convert_fusion.refs_0_), channel_id=1, source_target_pairs={{0,16},{8,24},{16,0},{24,8},{1,17},{9,25},{17,1},{25,9},{2,18},{10... | collective-permute-start | bytes 589832 | tf_op jit(solution)/shard_map/ppermute | solution.py:318
  59.1 9.1 %collective-permute-start.9 = (bf16[32,3072]{1,0:T(8,128)(2,1)S(1)}, bf16[32,3072]{1,0:T(8,128)(2,1)S(1)}, u32[]{:S(2)}, u32[]{:S(2)}) collective-permute-start(bf16[32,3072]{1,0:T(8,128)(2,1)S(1)} %multiply_convert_fusion.refs_0_), channel_id=1, source_target_pairs={{0,8},{8,0},{16,24},{24,16},{1,9},{9,1},{17,25},{25,17},{2,10},{10... | collective-permute-start | bytes 589832 | tf_op jit(solution)/shard_map/ppermute | solution.py:313
  67.4 1.4 %collective-permute-start.20 = (bf16[32,3072]{1,0:T(8,128)(2,1)S(1)}, bf16[32,3072]{1,0:T(8,128)(2,1)S(1)}, u32[]{:S(2)}, u32[]{:S(2)}) collective-permute-start(bf16[32,3072]{1,0:T(8,128)(2,1)S(1)} %collective-permute-done.10.refs_2_), channel_id=1, source_target_pairs={{0,8},{8,0},{16,24},{24,16},{1,9},{9,1},{17,25},{25,17},{2,10},{10... | collective-permute-start | bytes 589832 | tf_op jit(solution)/shard_map/ppermute | solution.py:313
  67.4 7.3 %collective-permute-start.23 = (bf16[32,3072]{1,0:T(8,128)(2,1)S(1)}, bf16[32,3072]{1,0:T(8,128)(2,1)S(1)}, u32[]{:S(2)}, u32[]{:S(2)}) collective-permute-start(bf16[32,3072]{1,0:T(8,128)(2,1)S(1)} %fusion.6.refs_0_.refs_8_), channel_id=1, source_target_pairs={{0,16},{8,24},{16,0},{24,8},{1,17},{9,25},{17,1},{25,9},{2,18},{10... | collective-permute-start | bytes 589832 | tf_op jit(solution)/shard_map/ppermute | solution.py:318
  68.0 11.4 %collective-permute-start.22 = (bf16[32,3072]{1,0:T(8,128)(2,1)S(1)}, bf16[32,3072]{1,0:T(8,128)(2,1)S(1)}, u32[]{:S(2)}, u32[]{:S(2)}) collective-permute-start(bf16[32,3072]{1,0:T(8,128)(2,1)S(1)} %fusion.6.refs_0_.refs_8_), channel_id=1, source_target_pairs={{0,8},{8,0},{16,24},{24,16},{1,9},{9,1},{17,25},{25,17},{2,10},{10... | collective-permute-start | bytes 589832 | tf_op jit(solution)/shard_map/ppermute | solution.py:313
  74.7 4.6 %collective-permute-start.24 = (bf16[32,3072]{1,0:T(8,128)(2,1)S(1)}, bf16[32,3072]{1,0:T(8,128)(2,1)S(1)}, u32[]{:S(2)}, u32[]{:S(2)}) collective-permute-start(bf16[32,3072]{1,0:T(8,128)(2,1)S(1)} %collective-permute-done.23.refs_2_.refs_10_), channel_id=1, source_target_pairs={{0,8},{8,0},{16,24},{24,16},{1,9},{9,1},{17,25},{25,17},{2,10},{10... | collective-permute-start | bytes 589832 | tf_op jit(solution)/shard_map/ppermute | solution.py:313
  79.3 2.0 %copy-start.2 = (s32[1,1,288]{2,1,0:T(1,128)S(1)}, s32[1,1,288]{2,1,0:T(1,128)}, u32[]{:S(2)}) copy-start(s32[1,1,288]{2,1,0:T(1,128)} %slot_s.2) | copy-start | bytes 3460
  79.3 11.6 %collective-permute-start.21 = (bf16[4,16,3072]{2,1,0:T(8,128)(2,1)S(1)}, bf16[4,16,3072]{2,1,0:T(8,128)(2,1)S(1)}, u32[]{:S(2)}, u32[]{:S(2)}) collective-permute-start(bf16[4,16,3072]{2,1,0:T(8,128)(2,1)S(1)} %get-tuple-element.75), channel_id=1, source_target_pairs={{0,1},{1,0},{2,3},{3,2},{4,5},{5,4},{6,7},{7,6},{8,9},{9,8},{10,11... | collective-permute-start | bytes 1179656 | tf_op jit(solution)/shard_map/ppermute | solution.py:313
  81.3 29.8 %copy-start.3 = (s32[1,1,288]{2,1,0:T(1,128)S(1)}, s32[1,1,288]{2,1,0:T(1,128)}, u32[]{:S(2)}) copy-start(s32[1,1,288]{2,1,0:T(1,128)} %slot_s.3) | copy-start | bytes 3460
  90.9 8.6 %collective-permute-start.25 = (bf16[16,3072]{1,0:T(8,128)(2,1)S(1)}, bf16[16,3072]{1,0:T(8,128)(2,1)S(1)}, u32[]{:S(2)}, u32[]{:S(2)}) collective-permute-start(bf16[16,3072]{1,0:T(8,128)(2,1)S(1)} %get-tuple-element.97), channel_id=1, source_target_pairs={{0,6},{1,7},{2,0},{3,1},{4,2},{5,3},{6,4},{7,5},{8,14},{9,15},{10,... | collective-permute-start | bytes 294920 | tf_op jit(solution)/shard_map/ppermute | solution.py:318
  97.3 6.5 %collective-permute-start.27 = (bf16[16,3072]{1,0:T(8,128)(2,1)S(1)}, bf16[16,3072]{1,0:T(8,128)(2,1)S(1)}, u32[]{:S(2)}, u32[]{:S(2)}) collective-permute-start(bf16[16,3072]{1,0:T(8,128)(2,1)S(1)} %get-tuple-element.98), channel_id=1, source_target_pairs={{0,2},{1,3},{2,4},{3,5},{4,6},{5,7},{6,0},{7,1},{8,10},{9,11},{10,... | collective-permute-start | bytes 294920 | tf_op jit(solution)/shard_map/ppermute | solution.py:318
  97.3 8.2 %collective-permute-start.26 = (bf16[16,3072]{1,0:T(8,128)(2,1)S(1)}, bf16[16,3072]{1,0:T(8,128)(2,1)S(1)}, u32[]{:S(2)}, u32[]{:S(2)}) collective-permute-start(bf16[16,3072]{1,0:T(8,128)(2,1)S(1)} %get-tuple-element.99), channel_id=1, source_target_pairs={{0,4},{1,5},{2,6},{3,7},{4,0},{5,1},{6,2},{7,3},{8,12},{9,13},{10,... | collective-permute-start | bytes 294920 | tf_op jit(solution)/shard_map/ppermute | solution.py:318
  97.9 9.0 %collective-permute-start.28 = (bf16[4,16,3072]{2,1,0:T(8,128)(2,1)S(1)}, bf16[4,16,3072]{2,1,0:T(8,128)(2,1)S(1)}, u32[]{:S(2)}, u32[]{:S(2)}) collective-permute-start(bf16[4,16,3072]{2,1,0:T(8,128)(2,1)S(1)} %get-tuple-element.88), channel_id=1, source_target_pairs={{0,1},{1,0},{2,3},{3,2},{4,5},{5,4},{6,7},{7,6},{8,9},{9,8},{10,11... | collective-permute-start | bytes 1179656 | tf_op jit(solution)/shard_map/ppermute | solution.py:313
  107.0 12.8 %collective-permute-start.29 = (bf16[16,3072]{1,0:T(8,128)(2,1)S(1)}, bf16[16,3072]{1,0:T(8,128)(2,1)S(1)}, u32[]{:S(2)}, u32[]{:S(2)}) collective-permute-start(bf16[16,3072]{1,0:T(8,128)(2,1)S(1)} %get-tuple-element.94), channel_id=1, source_target_pairs={{0,6},{1,7},{2,0},{3,1},{4,2},{5,3},{6,4},{7,5},{8,14},{9,15},{10,... | collective-permute-start | bytes 294920 | tf_op jit(solution)/shard_map/ppermute | solution.py:318
  109.7 10.1 %collective-permute-start.31 = (bf16[16,3072]{1,0:T(8,128)(2,1)S(1)}, bf16[16,3072]{1,0:T(8,128)(2,1)S(1)}, u32[]{:S(2)}, u32[]{:S(2)}) collective-permute-start(bf16[16,3072]{1,0:T(8,128)(2,1)S(1)} %get-tuple-element.95), channel_id=1, source_target_pairs={{0,2},{1,3},{2,4},{3,5},{4,6},{5,7},{6,0},{7,1},{8,10},{9,11},{10,... | collective-permute-start | bytes 294920 | tf_op jit(solution)/shard_map/ppermute | solution.py:318
  109.7 10.1 %collective-permute-start.30 = (bf16[16,3072]{1,0:T(8,128)(2,1)S(1)}, bf16[16,3072]{1,0:T(8,128)(2,1)S(1)}, u32[]{:S(2)}, u32[]{:S(2)}) collective-permute-start(bf16[16,3072]{1,0:T(8,128)(2,1)S(1)} %get-tuple-element.96), channel_id=1, source_target_pairs={{0,4},{1,5},{2,6},{3,7},{4,0},{5,1},{6,2},{7,3},{8,12},{9,13},{10,... | collective-permute-start | bytes 294920 | tf_op jit(solution)/shard_map/ppermute | solution.py:318
